TPU v7x, 32 devices: a whole 2x2x4 slice. The times are simulated.
32 devices in a mesh: gx: 8 (over y, x, core), gy: 4 (over z).
Axes of the slice: x: 2, y: 2, z: 4, core: 2. Of those that a mesh axis runs over, the one named last changes fastest.
Arguments:
- grad_p: float32 [3, 128, 64, 128], P(None, 'gx', 'gy'), may hold values from -6 to 6
- grad_s: float32 [3, 128, 64, 128], P(None, 'gx', 'gy'), may hold values from -6 to 6
- acc_p: float32 [128, 64, 128], P('gx', 'gy'), may hold values from 0.2 to 2
- acc_s: float32 [128, 64, 128], P('gx', 'gy'), may hold values from 0.2 to 2
- trans_x: float32 [128, 64, 128], P('gx', 'gy'), may hold values from 0.1 to 10
- trans_y: float32 [128, 64, 128], P('gx', 'gy'), may hold values from 0.1 to 10
- trans_z: float32 [128, 64, 128], P('gx', 'gy'), may hold values from 0.1 to 10
- c_pp: float32 [3, 128, 64, 128], P(None, 'gx', 'gy'), may hold values from 0.05 to 0.5
- c_ss: float32 [3, 128, 64, 128], P(None, 'gx', 'gy'), may hold values from 0.2 to 2
- c_ps: float32 [3, 128, 64, 128], P(None, 'gx', 'gy'), may hold values from -0.2 to 0.2
- c_sp: float32 [3, 128, 64, 128], P(None, 'gx', 'gy'), may hold values from -0.5 to 0.5
- frac: float32 [3, 128, 64, 128], P(None, 'gx', 'gy'), may hold values from 0 to 0.5
- mobility: float32 [3, 128, 64, 128], P(None, 'gx', 'gy'), may hold values from 0.5 to 2
- rate_mis: float32 [64, 3], P(('gx', 'gy')), may hold values from -6 to 6
- bhp_mis: float32 [64, 3], P(('gx', 'gy')), may hold values from -6 to 6
- control: int32 [64, 3], P(('gx', 'gy')), may hold values from 0 to 1
- perf_well: int32 [4096], P(('gx', 'gy')), may hold values from 0 to 63
- perf_cell: int32 [4096], P(('gx', 'gy')), may hold values from 0 to 32767
- perf_wi: float32 [4096], P(('gx', 'gy')), may hold values from 1 to 10
Outputs:
- lam_p: float32 [128, 64, 128], P('gx', 'gy')
- lam_s: float32 [128, 64, 128], P('gx', 'gy')
- well_grad: float32 [64, 3], P(('gx', 'gy'))
Inputs may be any that keep to these rules, and one draw needn't show every extreme that they name: perf_cell indexes the block of the device that holds the slot, as (i * 16 + j) * 128 + k; slots may share a cell. `perf_well`: well w is held by the device of flat index w // 2 along gx+gy; a well's slots may lie on any devices.
All inputs are finite; a program needn't handle non-finite values.
Results may differ from a plain program's by a relative error of at most 0.0002.
Values sent between devices are 32-bit elements; how exact they have to be, the bound alone decides.
No kernel may reach another device: no remote copies, remote signals or barrier semaphores. Data moves between devices by JAX's collectives and lax.ppermute only.
A program may use at most 128 MiB of HBM per device.

v0:
```python
import jax
import jax.numpy as jnp
from jax import lax
from jax.sharding import PartitionSpec as P

SWEEPS = 8


omega_factor = 0.8


def passed_along(value, axis, by):
    length = lax.axis_size(axis)
    pairs = [(i, i + by) for i in range(length) if 0 <= i + by < length]
    return lax.ppermute(value, axis, pairs)


def padded_2(block, sides, width):
    for axis, dim in sides:
        count = lax.axis_size(axis)
        forward = [(i, i + 1) for i in range(count - 1)]
        backward = [(target, source) for source, target in forward]
        low = lax.ppermute(
            lax.slice_in_dim(block, block.shape[dim] - width, None, axis=dim), axis, forward
        )
        high = lax.ppermute(lax.slice_in_dim(block, 0, width, axis=dim), axis, backward)
        block = jnp.concatenate([low, block, high], axis=dim)
    return block


def neighbour_sum(fields, table):
    centre = fields[:, 1:-1, 1:-1, :]
    east = fields[:, 2:, 1:-1, :]
    west = fields[:, :-2, 1:-1, :]
    north = fields[:, 1:-1, 2:, :]
    south = fields[:, 1:-1, :-2, :]
    upper = jnp.pad(centre[..., 1:], ((0, 0), (0, 0), (0, 0), (0, 1)))
    lower = jnp.pad(centre[..., :-1], ((0, 0), (0, 0), (0, 0), (1, 0)))
    total = table[8] * east + table[9] * west
    total = total + table[10] * north + table[11] * south
    total = total + table[12] * upper + table[13] * lower
    return (centre, total)


def relax(fields, table):
    centre, beside_all = neighbour_sum(fields, table)
    weight_sum = table[14]
    laplace = weight_sum * centre - beside_all
    old_a = centre[0]
    old_b = centre[1]
    out_a = table[0] * old_a + laplace[0] + table[3] * old_b + table[4] * laplace[1]
    out_b = table[2] * old_a + table[1] * old_b + table[5] * laplace[1]
    new_a = old_a + table[15] * (table[6] - out_a)
    new_b = old_b + table[16] * (table[7] - out_b)
    return jnp.stack([new_a, new_b])


def local(
    grad_p,
    grad_s,
    acc_p,
    acc_s,
    trans_x,
    trans_y,
    trans_z,
    c_pp,
    c_ss,
    c_ps,
    c_sp,
    frac,
    mobility,
    rate_mis,
    bhp_mis,
    control,
    perf_well,
    perf_cell,
    perf_wi,
):
    rows_x, rows_y, layers = trans_x.shape
    steps = grad_p.shape[0]
    sweeps = SWEEPS
    cells = rows_x * rows_y * layers
    gx_at = lax.axis_index("gx")
    gy_at = lax.axis_index("gy")
    east_plane = passed_along(trans_x[0:1], "gx", -1)
    north_plane = passed_along(trans_y[:, 0:1], "gy", -1)
    first_x = lax.broadcasted_iota(jnp.int32, (rows_x, 1, 1), 0) + gx_at * rows_x > 0
    first_y = lax.broadcasted_iota(jnp.int32, (1, rows_y, 1), 1) + gy_at * rows_y > 0
    first_z = lax.broadcasted_iota(jnp.int32, (1, 1, layers), 2) > 0
    w_east = jnp.concatenate([trans_x[1:], east_plane], axis=0)
    w_west = jnp.where(first_x, trans_x, 0.0)
    w_north = jnp.concatenate([trans_y[:, 1:], north_plane], axis=1)
    w_south = jnp.where(first_y, trans_y, 0.0)
    w_up = jnp.pad(trans_z[:, :, 1:], ((0, 0), (0, 0), (0, 1)))
    w_down = jnp.where(first_z, trans_z, 0.0)
    weight_sum = w_east + w_west + w_north + w_south + w_up + w_down
    effective = jnp.where(control == 1, rate_mis, bhp_mis)
    all_rows = lax.all_gather(effective, ("gx", "gy"), axis=0, tiled=True)
    well_count = all_rows.shape[0]
    selector = (perf_well[:, None] == jnp.arange(well_count, dtype=jnp.int32)[None, :]).astype(
        jnp.float32
    )
    perf_rows = jnp.dot(selector, all_rows, precision=lax.Precision.HIGHEST)
    sources = (
        jnp.zeros((steps, cells), jnp.float32)
        .at[:, perf_cell]
        .add((perf_wi[:, None] * perf_rows).T)
    )
    sources = sources.reshape(steps, rows_x, rows_y, layers)
    multipliers = jnp.zeros((2, rows_x, rows_y, layers), jnp.float32)
    returned = [None] * steps
    for step_index in reversed(range(steps)):
        right_a = grad_p[step_index] + sources[step_index] + acc_p * multipliers[0]
        right_b = grad_s[step_index] + acc_s * multipliers[1]
        scale_a = omega_factor / (c_pp[step_index] + weight_sum)
        scale_b = omega_factor / (c_ss[step_index] + mobility[step_index] * weight_sum)
        table = jnp.stack(
            [
                c_pp[step_index],
                c_ss[step_index],
                c_ps[step_index],
                c_sp[step_index],
                frac[step_index],
                mobility[step_index],
                right_a,
                right_b,
                w_east,
                w_west,
                w_north,
                w_south,
                w_up,
                w_down,
                weight_sum,
                scale_a,
                scale_b,
            ]
        )
        for sweep_index in range(sweeps):
            padded = padded_2(multipliers, (("gx", 1), ("gy", 2)), 1)
            multipliers = relax(padded, table)
        flat_fields = multipliers.reshape(2, cells)
        at_cells = flat_fields[:, perf_cell]
        at_frac = frac[step_index].reshape(cells)[perf_cell]
        returned[step_index] = perf_wi * (at_cells[0] + at_frac * at_cells[1])
    contributions = jnp.stack(returned, axis=1)
    dense = jnp.dot(selector.T, contributions, precision=lax.Precision.HIGHEST)
    well_grad = lax.psum_scatter(dense, ("gx", "gy"), scatter_dimension=0, tiled=True)
    return (multipliers[0], multipliers[1], well_grad)


def solution(mesh):
    placed = (
        P(None, "gx", "gy", None),
        P(None, "gx", "gy", None),
        P("gx", "gy", None),
        P("gx", "gy", None),
        P("gx", "gy", None),
        P("gx", "gy", None),
        P("gx", "gy", None),
        P(None, "gx", "gy", None),
        P(None, "gx", "gy", None),
        P(None, "gx", "gy", None),
        P(None, "gx", "gy", None),
        P(None, "gx", "gy", None),
        P(None, "gx", "gy", None),
        P(("gx", "gy"), None),
        P(("gx", "gy"), None),
        P(("gx", "gy"), None),
        P(("gx", "gy")),
        P(("gx", "gy")),
        P(("gx", "gy")),
    )
    return jax.shard_map(
        local,
        mesh=mesh,
        in_specs=placed,
        out_specs=(P("gx", "gy", None), P("gx", "gy", None), P(("gx", "gy"), None)),
        check_vma=False,
    )
```

profile of v0, /device:TPU:0, one launch (start us, length us, event | category | flops | bytes accessed | tf_op | source)
XLA Modules:
  0.0 621.0 jit_solution(6534651151224634101)
XLA Ops:
  1.9 3.0 collective-permute-start.3
  10.5 71.9 %all-gather = f32[32,2,3]{2,1,0:T(2,128)S(1)} all-gather(f32[1,2,3]{2,1,0:T(2,128)S(1)} %fusion.643), channel_id=1, replica_groups=mesh['gx'=8,'gy'=4] {'gx','gy'}, dimensions={0}, use_global_device_ids=true | all-gather | bytes 792 | tf_op jit(solution)/shard_map/all_gather | solution.py:98
  83.4 7.8 %scatter_custom_fusion = f32[3,32768]{0,1:T(8,128)} fusion(s32[128]{0:T(128)S(1)} %compare_select_fusion, f32[128,3]{1,0:T(8,128)S(1)} %copy.30, f32[]{:T(128)} %constant.14.clone.1), kind=kCustom, calls=%fused_computation.10 | custom fusion | flops 384 | bytes 393220 | tf_op jit(solution)/shard_map/scatter-add | solution.py:107
  91.4 30.5 %slice_reduce_fusion = (f32[32768]{0:T(1024)S(1)}, f32[32768]{0:T(1024)S(1)}, f32[32768]{0:T(1024)S(1)}) fusion(f32[3,32768]{0,1:T(8,128)} %scatter_custom_fusion), kind=kLoop, calls=%fused_computation.7 | loop fusion | bytes 786432 | tf_op jit(solution)/shard_map/slice | solution.py:113
  123.6 4.5 collective-permute-start.5
  131.4 3.0 collective-permute-start.7
  136.6 4.8 collective-permute-start.9
  144.5 3.0 collective-permute-start.11
  149.7 4.8 collective-permute-start.13
  158.9 3.7 collective-permute-start.15
  164.7 4.5 collective-permute-start.17
  173.6 5.1 collective-permute-start.19
  180.9 4.7 collective-permute-start.21
  189.8 5.1 collective-permute-start.23
  197.1 4.5 collective-permute-start.25
  205.9 5.1 collective-permute-start.27
  213.2 4.5 collective-permute-start.29
  222.1 5.1 collective-permute-start.31
  229.4 4.5 collective-permute-start.33
  238.3 6.0 collective-permute-start.35
  246.5 4.5 collective-permute-start.37
  254.3 6.0 collective-permute-start.39
  262.5 4.5 collective-permute-start.41
  270.2 6.0 collective-permute-start.43
  278.4 4.5 collective-permute-start.45
  287.3 6.0 collective-permute-start.47
  295.5 4.5 collective-permute-start.49
  304.3 6.0 collective-permute-start.51
  312.5 4.5 collective-permute-start.53
  321.4 6.0 collective-permute-start.55
  329.6 4.5 collective-permute-start.57
  338.5 6.0 collective-permute-start.59
  346.7 4.5 collective-permute-start.61
  355.6 6.0 collective-permute-start.63
  363.8 4.5 collective-permute-start.65
  372.7 6.0 collective-permute-start.67
  380.9 4.5 collective-permute-start.69
  388.7 6.0 collective-permute-start.71
  396.9 4.5 collective-permute-start.73
  404.6 6.0 collective-permute-start.75
  412.8 4.5 collective-permute-start.77
  421.7 6.6 %collective-permute-start.79 = (f32[2,1,16,128]{3,2,1,0:T(8,128)}, f32[2,1,16,128]{3,2,1,0:T(8,128)}, u32[]{:S(2)}, u32[]{:S(2)}) collective-permute-start(f32[2,1,16,128]{3,2,1,0:T(8,128)} %get-tuple-element.147), channel_id=1, source_target_pairs={{0,4},{4,8},{8,12},{12,16},{16,20},{20,24},{24,28},{1,5},{5,9},{9,... | collective-permute-start | bytes 49160 | tf_op jit(solution)/shard_map/ppermute | solution.py:23
  428.9 2.5 gather_fusion.1
  431.4 2.5 gather_fusion.3
  433.9 2.5 gather_fusion.5
  438.7 4.5 collective-permute-start.81
  444.7 1.7 fusion.30
  450.2 6.6 %collective-permute-start.83 = (f32[2,1,16,128]{3,2,1,0:T(8,128)}, f32[2,1,16,128]{3,2,1,0:T(8,128)}, u32[]{:S(2)}, u32[]{:S(2)}) collective-permute-start(f32[2,1,16,128]{3,2,1,0:T(8,128)} %get-tuple-element.143), channel_id=1, source_target_pairs={{0,4},{4,8},{8,12},{12,16},{16,20},{20,24},{24,28},{1,5},{5,9},{9,... | collective-permute-start | bytes 49160 | tf_op jit(solution)/shard_map/ppermute | solution.py:23
  456.8 1.9 pad_maximum_fusion.307
  458.7 8.9 %copy.33 = f32[2,32768]{0,1:T(8,128)} copy(f32[2,32768]{1,0:T(2,128)} %pad_maximum_fusion.307) | data formatting | bytes 524288 | tf_op jit(solution)/shard_map/stack | solution.py:55
  467.6 7.1 %gather_fusion.4 = f32[128,2]{1,0:T(8,128)} fusion(f32[2,32768]{0,1:T(8,128)} %copy.33, s32[1024]{0:T(1024)} %pad_clamp_fusion), kind=kCustom, calls=%fused_computation.4 | custom fusion | bytes 2560 | tf_op jit(solution)/shard_map/gather | solution.py:142
  477.0 4.6 collective-permute-start.85
  487.3 5.5 collective-permute-start.87
  495.8 4.5 collective-permute-start.89
  505.7 6.6 %collective-permute-start.91 = (f32[2,1,16,128]{3,2,1,0:T(8,128)}, f32[2,1,16,128]{3,2,1,0:T(8,128)}, u32[]{:S(2)}, u32[]{:S(2)}) collective-permute-start(f32[2,1,16,128]{3,2,1,0:T(8,128)} %get-tuple-element.135), channel_id=1, source_target_pairs={{0,4},{4,8},{8,12},{12,16},{16,20},{20,24},{24,28},{1,5},{5,9},{9,... | collective-permute-start | bytes 49160 | tf_op jit(solution)/shard_map/ppermute | solution.py:23
  512.3 1.9 pad_maximum_fusion.306
  514.2 8.9 %copy.32 = f32[2,32768]{0,1:T(8,128)} copy(f32[2,32768]{1,0:T(2,128)} %pad_maximum_fusion.306) | data formatting | bytes 524288 | tf_op jit(solution)/shard_map/stack | solution.py:55
  523.1 7.1 %gather_fusion.2 = f32[128,2]{1,0:T(8,128)} fusion(f32[2,32768]{0,1:T(8,128)} %copy.32, s32[1024]{0:T(1024)} %pad_clamp_fusion), kind=kCustom, calls=%fused_computation.2 | custom fusion | bytes 2560 | tf_op jit(solution)/shard_map/gather | solution.py:142
  532.5 4.5 collective-permute-start.93
  542.8 4.5 collective-permute-start.95
  549.7 4.5 collective-permute-start.97
  557.4 8.4 %copy.31 = f32[2,32768]{0,1:T(8,128)} copy(f32[2,32768]{1,0:T(2,128)S(1)} %pad_maximum_fusion.305) | data formatting | bytes 524288 | tf_op jit(solution)/shard_map/stack | solution.py:55
  565.8 6.5 %gather_fusion = f32[128,2]{1,0:T(8,128)S(1)} fusion(f32[2,32768]{0,1:T(8,128)} %copy.31, s32[1024]{0:T(1024)} %pad_clamp_fusion), kind=kCustom, calls=%fused_computation | custom fusion | bytes 2560 | tf_op jit(solution)/shard_map/gather | solution.py:142
  572.9 47.6 %all-reduce.51 = f32[64,3]{1,0:T(8,128)S(1)} all-reduce(f32[64,3]{1,0:T(8,128)S(1)} %fusion.588), channel_id=2, replica_groups=mesh['gx'=8,'gy'=4] {'gx','gy'}, use_global_device_ids=true, to_apply=%region_1.2.clone | all-reduce | flops 192 | bytes 1536
  (366 shorter events, 161.0 us)
Async XLA Ops:
  0.6 121.5 %collective-permute-start.2 = (f32[2,1,16,128]{3,2,1,0:T(8,128)S(1)}, f32[2,1,16,128]{3,2,1,0:T(8,128)S(1)}, u32[]{:S(2)}, u32[]{:S(2)}) collective-permute-start(f32[2,1,16,128]{3,2,1,0:T(8,128)S(1)} %broadcast.163), channel_id=1, source_target_pairs={{4,0},{8,4},{12,8},{16,12},{20,16},{24,20},{28,24},{5,1},{9,5},{13... | collective-permute-start | bytes 49160 | tf_op jit(solution)/shard_map/ppermute | solution.py:26
  1.9 120.2 %collective-permute-start.3 = (f32[2,1,16,128]{3,2,1,0:T(8,128)S(1)}, f32[2,1,16,128]{3,2,1,0:T(8,128)S(1)}, u32[]{:S(2)}, u32[]{:S(2)}) collective-permute-start(f32[2,1,16,128]{3,2,1,0:T(8,128)S(1)} %broadcast.163), channel_id=1, source_target_pairs={{0,4},{4,8},{8,12},{12,16},{16,20},{20,24},{24,28},{1,5},{5,9},{9,... | collective-permute-start | bytes 49160 | tf_op jit(solution)/shard_map/ppermute | solution.py:23
  5.7 116.3 %collective-permute-start = (f32[1,16,128]{2,1,0:T(8,128)S(1)}, f32[1,16,128]{2,1,0:T(8,128)S(1)}, u32[]{:S(2)}, u32[]{:S(2)}) collective-permute-start(f32[1,16,128]{2,1,0:T(8,128)S(1)} %slice.1103), channel_id=1, source_target_pairs={{4,0},{8,4},{12,8},{16,12},{20,16},{24,20},{28,24},{5,1},{9,5},{13... | collective-permute-start | bytes 24584 | tf_op jit(solution)/shard_map/ppermute | solution.py:15
  7.8 114.2 %collective-permute-start.1 = (f32[16,1,128]{2,1,0:T(1,128)S(1)}, f32[16,1,128]{2,1,0:T(1,128)S(1)}, u32[]{:S(2)}, u32[]{:S(2)}) collective-permute-start(f32[16,1,128]{2,1,0:T(1,128)S(1)} %slice.1105), channel_id=1, source_target_pairs={{1,0},{2,1},{3,2},{5,4},{6,5},{7,6},{9,8},{10,9},{11,10},{13,12},{... | collective-permute-start | bytes 24584 | tf_op jit(solution)/shard_map/ppermute | solution.py:15
  123.6 6.0 collective-permute-start.5
  135.3 6.3 %collective-permute-start.8 = (f32[2,18,1,128]{3,2,1,0:T(1,128)S(1)}, f32[2,18,1,128]{3,2,1,0:T(1,128)S(1)}, u32[]{:S(2)}, u32[]{:S(2)}) collective-permute-start(f32[2,18,1,128]{3,2,1,0:T(1,128)S(1)} %get-tuple-element.125), channel_id=1, source_target_pairs={{1,0},{2,1},{3,2},{5,4},{6,5},{7,6},{9,8},{10,9},{11,10},{13,12},{... | collective-permute-start | bytes 55304 | tf_op jit(solution)/shard_map/ppermute | solution.py:26
  136.6 6.3 %collective-permute-start.9 = (f32[2,18,1,128]{3,2,1,0:T(1,128)S(1)}, f32[2,18,1,128]{3,2,1,0:T(1,128)S(1)}, u32[]{:S(2)}, u32[]{:S(2)}) collective-permute-start(f32[2,18,1,128]{3,2,1,0:T(1,128)S(1)} %get-tuple-element.126), channel_id=1, source_target_pairs={{0,1},{1,2},{2,3},{4,5},{5,6},{6,7},{8,9},{9,10},{10,11},{12,13},{... | collective-permute-start | bytes 55304 | tf_op jit(solution)/shard_map/ppermute | solution.py:23
  148.4 6.3 %collective-permute-start.12 = (f32[2,18,1,128]{3,2,1,0:T(1,128)S(1)}, f32[2,18,1,128]{3,2,1,0:T(1,128)S(1)}, u32[]{:S(2)}, u32[]{:S(2)}) collective-permute-start(f32[2,18,1,128]{3,2,1,0:T(1,128)S(1)} %get-tuple-element.123), channel_id=1, source_target_pairs={{1,0},{2,1},{3,2},{5,4},{6,5},{7,6},{9,8},{10,9},{11,10},{13,12},{... | collective-permute-start | bytes 55304 | tf_op jit(solution)/shard_map/ppermute | solution.py:26
  149.7 6.3 %collective-permute-start.13 = (f32[2,18,1,128]{3,2,1,0:T(1,128)S(1)}, f32[2,18,1,128]{3,2,1,0:T(1,128)S(1)}, u32[]{:S(2)}, u32[]{:S(2)}) collective-permute-start(f32[2,18,1,128]{3,2,1,0:T(1,128)S(1)} %get-tuple-element.124), channel_id=1, source_target_pairs={{0,1},{1,2},{2,3},{4,5},{5,6},{6,7},{8,9},{9,10},{10,11},{12,13},{... | collective-permute-start | bytes 55304 | tf_op jit(solution)/shard_map/ppermute | solution.py:23
  164.7 6.0 collective-permute-start.17
  172.3 6.5 %collective-permute-start.18 = (f32[2,1,16,128]{3,2,1,0:T(8,128)S(1)}, f32[2,1,16,128]{3,2,1,0:T(8,128)S(1)}, u32[]{:S(2)}, u32[]{:S(2)}) collective-permute-start(f32[2,1,16,128]{3,2,1,0:T(8,128)S(1)} %get-tuple-element.208), channel_id=1, source_target_pairs={{4,0},{8,4},{12,8},{16,12},{20,16},{24,20},{28,24},{5,1},{9,5},{13... | collective-permute-start | bytes 49160 | tf_op jit(solution)/shard_map/ppermute | solution.py:26
  179.6 6.2 collective-permute-start.20
  180.9 6.0 collective-permute-start.21
  188.5 6.5 %collective-permute-start.22 = (f32[2,1,16,128]{3,2,1,0:T(8,128)S(1)}, f32[2,1,16,128]{3,2,1,0:T(8,128)S(1)}, u32[]{:S(2)}, u32[]{:S(2)}) collective-permute-start(f32[2,1,16,128]{3,2,1,0:T(8,128)S(1)} %get-tuple-element.204), channel_id=1, source_target_pairs={{4,0},{8,4},{12,8},{16,12},{20,16},{24,20},{28,24},{5,1},{9,5},{13... | collective-permute-start | bytes 49160 | tf_op jit(solution)/shard_map/ppermute | solution.py:26
  197.1 6.0 collective-permute-start.25
  204.6 6.5 %collective-permute-start.26 = (f32[2,1,16,128]{3,2,1,0:T(8,128)S(1)}, f32[2,1,16,128]{3,2,1,0:T(8,128)S(1)}, u32[]{:S(2)}, u32[]{:S(2)}) collective-permute-start(f32[2,1,16,128]{3,2,1,0:T(8,128)S(1)} %get-tuple-element.200), channel_id=1, source_target_pairs={{4,0},{8,4},{12,8},{16,12},{20,16},{24,20},{28,24},{5,1},{9,5},{13... | collective-permute-start | bytes 49160 | tf_op jit(solution)/shard_map/ppermute | solution.py:26
  213.2 6.0 collective-permute-start.29
  220.8 6.5 %collective-permute-start.30 = (f32[2,1,16,128]{3,2,1,0:T(8,128)S(1)}, f32[2,1,16,128]{3,2,1,0:T(8,128)S(1)}, u32[]{:S(2)}, u32[]{:S(2)}) collective-permute-start(f32[2,1,16,128]{3,2,1,0:T(8,128)S(1)} %get-tuple-element.196), channel_id=1, source_target_pairs={{4,0},{8,4},{12,8},{16,12},{20,16},{24,20},{28,24},{5,1},{9,5},{13... | collective-permute-start | bytes 49160 | tf_op jit(solution)/shard_map/ppermute | solution.py:26
  229.4 6.0 collective-permute-start.33
  237.0 7.4 %collective-permute-start.34 = (f32[2,1,16,128]{3,2,1,0:T(8,128)S(1)}, f32[2,1,16,128]{3,2,1,0:T(8,128)S(1)}, u32[]{:S(2)}, u32[]{:S(2)}) collective-permute-start(f32[2,1,16,128]{3,2,1,0:T(8,128)S(1)} %get-tuple-element.192), channel_id=1, source_target_pairs={{4,0},{8,4},{12,8},{16,12},{20,16},{24,20},{28,24},{5,1},{9,5},{13... | collective-permute-start | bytes 49160 | tf_op jit(solution)/shard_map/ppermute | solution.py:26
  238.3 6.9 %collective-permute-start.35 = (f32[2,1,16,128]{3,2,1,0:T(8,128)S(1)}, f32[2,1,16,128]{3,2,1,0:T(8,128)S(1)}, u32[]{:S(2)}, u32[]{:S(2)}) collective-permute-start(f32[2,1,16,128]{3,2,1,0:T(8,128)S(1)} %get-tuple-element.191), channel_id=1, source_target_pairs={{0,4},{4,8},{8,12},{12,16},{16,20},{20,24},{24,28},{1,5},{5,9},{9,... | collective-permute-start | bytes 49160 | tf_op jit(solution)/shard_map/ppermute | solution.py:23
  246.5 6.0 collective-permute-start.37
  253.0 7.4 %collective-permute-start.38 = (f32[2,1,16,128]{3,2,1,0:T(8,128)S(1)}, f32[2,1,16,128]{3,2,1,0:T(8,128)S(1)}, u32[]{:S(2)}, u32[]{:S(2)}) collective-permute-start(f32[2,1,16,128]{3,2,1,0:T(8,128)S(1)} %get-tuple-element.188), channel_id=1, source_target_pairs={{4,0},{8,4},{12,8},{16,12},{20,16},{24,20},{28,24},{5,1},{9,5},{13... | collective-permute-start | bytes 49160 | tf_op jit(solution)/shard_map/ppermute | solution.py:26
  254.3 6.9 %collective-permute-start.39 = (f32[2,1,16,128]{3,2,1,0:T(8,128)S(1)}, f32[2,1,16,128]{3,2,1,0:T(8,128)S(1)}, u32[]{:S(2)}, u32[]{:S(2)}) collective-permute-start(f32[2,1,16,128]{3,2,1,0:T(8,128)S(1)} %get-tuple-element.187), channel_id=1, source_target_pairs={{0,4},{4,8},{8,12},{12,16},{16,20},{20,24},{24,28},{1,5},{5,9},{9,... | collective-permute-start | bytes 49160 | tf_op jit(solution)/shard_map/ppermute | solution.py:23
  268.9 7.4 %collective-permute-start.42 = (f32[2,1,16,128]{3,2,1,0:T(8,128)S(1)}, f32[2,1,16,128]{3,2,1,0:T(8,128)S(1)}, u32[]{:S(2)}, u32[]{:S(2)}) collective-permute-start(f32[2,1,16,128]{3,2,1,0:T(8,128)S(1)} %get-tuple-element.184), channel_id=1, source_target_pairs={{4,0},{8,4},{12,8},{16,12},{20,16},{24,20},{28,24},{5,1},{9,5},{13... | collective-permute-start | bytes 49160 | tf_op jit(solution)/shard_map/ppermute | solution.py:26
  270.2 6.9 %collective-permute-start.43 = (f32[2,1,16,128]{3,2,1,0:T(8,128)S(1)}, f32[2,1,16,128]{3,2,1,0:T(8,128)S(1)}, u32[]{:S(2)}, u32[]{:S(2)}) collective-permute-start(f32[2,1,16,128]{3,2,1,0:T(8,128)S(1)} %get-tuple-element.183), channel_id=1, source_target_pairs={{0,4},{4,8},{8,12},{12,16},{16,20},{20,24},{24,28},{1,5},{5,9},{9,... | collective-permute-start | bytes 49160 | tf_op jit(solution)/shard_map/ppermute | solution.py:23
  286.0 7.4 %collective-permute-start.46 = (f32[2,1,16,128]{3,2,1,0:T(8,128)S(1)}, f32[2,1,16,128]{3,2,1,0:T(8,128)S(1)}, u32[]{:S(2)}, u32[]{:S(2)}) collective-permute-start(f32[2,1,16,128]{3,2,1,0:T(8,128)S(1)} %get-tuple-element.180), channel_id=1, source_target_pairs={{4,0},{8,4},{12,8},{16,12},{20,16},{24,20},{28,24},{5,1},{9,5},{13... | collective-permute-start | bytes 49160 | tf_op jit(solution)/shard_map/ppermute | solution.py:26
  287.3 6.9 %collective-permute-start.47 = (f32[2,1,16,128]{3,2,1,0:T(8,128)S(1)}, f32[2,1,16,128]{3,2,1,0:T(8,128)S(1)}, u32[]{:S(2)}, u32[]{:S(2)}) collective-permute-start(f32[2,1,16,128]{3,2,1,0:T(8,128)S(1)} %get-tuple-element.179), channel_id=1, source_target_pairs={{0,4},{4,8},{8,12},{12,16},{16,20},{20,24},{24,28},{1,5},{5,9},{9,... | collective-permute-start | bytes 49160 | tf_op jit(solution)/shard_map/ppermute | solution.py:23
  295.5 6.0 collective-permute-start.49
  303.0 7.4 %collective-permute-start.50 = (f32[2,1,16,128]{3,2,1,0:T(8,128)S(1)}, f32[2,1,16,128]{3,2,1,0:T(8,128)S(1)}, u32[]{:S(2)}, u32[]{:S(2)}) collective-permute-start(f32[2,1,16,128]{3,2,1,0:T(8,128)S(1)} %get-tuple-element.176), channel_id=1, source_target_pairs={{4,0},{8,4},{12,8},{16,12},{20,16},{24,20},{28,24},{5,1},{9,5},{13... | collective-permute-start | bytes 49160 | tf_op jit(solution)/shard_map/ppermute | solution.py:26
  304.3 6.9 %collective-permute-start.51 = (f32[2,1,16,128]{3,2,1,0:T(8,128)S(1)}, f32[2,1,16,128]{3,2,1,0:T(8,128)S(1)}, u32[]{:S(2)}, u32[]{:S(2)}) collective-permute-start(f32[2,1,16,128]{3,2,1,0:T(8,128)S(1)} %get-tuple-element.175), channel_id=1, source_target_pairs={{0,4},{4,8},{8,12},{12,16},{16,20},{20,24},{24,28},{1,5},{5,9},{9,... | collective-permute-start | bytes 49160 | tf_op jit(solution)/shard_map/ppermute | solution.py:23
  312.5 6.0 collective-permute-start.53
  320.1 7.4 %collective-permute-start.54 = (f32[2,1,16,128]{3,2,1,0:T(8,128)S(1)}, f32[2,1,16,128]{3,2,1,0:T(8,128)S(1)}, u32[]{:S(2)}, u32[]{:S(2)}) collective-permute-start(f32[2,1,16,128]{3,2,1,0:T(8,128)S(1)} %get-tuple-element.172), channel_id=1, source_target_pairs={{4,0},{8,4},{12,8},{16,12},{20,16},{24,20},{28,24},{5,1},{9,5},{13... | collective-permute-start | bytes 49160 | tf_op jit(solution)/shard_map/ppermute | solution.py:26
  321.4 6.9 %collective-permute-start.55 = (f32[2,1,16,128]{3,2,1,0:T(8,128)S(1)}, f32[2,1,16,128]{3,2,1,0:T(8,128)S(1)}, u32[]{:S(2)}, u32[]{:S(2)}) collective-permute-start(f32[2,1,16,128]{3,2,1,0:T(8,128)S(1)} %get-tuple-element.171), channel_id=1, source_target_pairs={{0,4},{4,8},{8,12},{12,16},{16,20},{20,24},{24,28},{1,5},{5,9},{9,... | collective-permute-start | bytes 49160 | tf_op jit(solution)/shard_map/ppermute | solution.py:23
  329.6 6.0 collective-permute-start.57
  337.2 7.4 %collective-permute-start.58 = (f32[2,1,16,128]{3,2,1,0:T(8,128)S(1)}, f32[2,1,16,128]{3,2,1,0:T(8,128)S(1)}, u32[]{:S(2)}, u32[]{:S(2)}) collective-permute-start(f32[2,1,16,128]{3,2,1,0:T(8,128)S(1)} %get-tuple-element.168), channel_id=1, source_target_pairs={{4,0},{8,4},{12,8},{16,12},{20,16},{24,20},{28,24},{5,1},{9,5},{13... | collective-permute-start | bytes 49160 | tf_op jit(solution)/shard_map/ppermute | solution.py:26
  338.5 6.9 %collective-permute-start.59 = (f32[2,1,16,128]{3,2,1,0:T(8,128)S(1)}, f32[2,1,16,128]{3,2,1,0:T(8,128)S(1)}, u32[]{:S(2)}, u32[]{:S(2)}) collective-permute-start(f32[2,1,16,128]{3,2,1,0:T(8,128)S(1)} %get-tuple-element.167), channel_id=1, source_target_pairs={{0,4},{4,8},{8,12},{12,16},{16,20},{20,24},{24,28},{1,5},{5,9},{9,... | collective-permute-start | bytes 49160 | tf_op jit(solution)/shard_map/ppermute | solution.py:23
  346.7 6.0 collective-permute-start.61
  354.3 7.4 %collective-permute-start.62 = (f32[2,1,16,128]{3,2,1,0:T(8,128)S(1)}, f32[2,1,16,128]{3,2,1,0:T(8,128)S(1)}, u32[]{:S(2)}, u32[]{:S(2)}) collective-permute-start(f32[2,1,16,128]{3,2,1,0:T(8,128)S(1)} %get-tuple-element.164), channel_id=1, source_target_pairs={{4,0},{8,4},{12,8},{16,12},{20,16},{24,20},{28,24},{5,1},{9,5},{13... | collective-permute-start | bytes 49160 | tf_op jit(solution)/shard_map/ppermute | solution.py:26
  355.6 6.9 %collective-permute-start.63 = (f32[2,1,16,128]{3,2,1,0:T(8,128)S(1)}, f32[2,1,16,128]{3,2,1,0:T(8,128)S(1)}, u32[]{:S(2)}, u32[]{:S(2)}) collective-permute-start(f32[2,1,16,128]{3,2,1,0:T(8,128)S(1)} %get-tuple-element.163), channel_id=1, source_target_pairs={{0,4},{4,8},{8,12},{12,16},{16,20},{20,24},{24,28},{1,5},{5,9},{9,... | collective-permute-start | bytes 49160 | tf_op jit(solution)/shard_map/ppermute | solution.py:23
  363.8 6.0 collective-permute-start.65
  371.4 7.4 %collective-permute-start.66 = (f32[2,1,16,128]{3,2,1,0:T(8,128)S(1)}, f32[2,1,16,128]{3,2,1,0:T(8,128)S(1)}, u32[]{:S(2)}, u32[]{:S(2)}) collective-permute-start(f32[2,1,16,128]{3,2,1,0:T(8,128)S(1)} %get-tuple-element.160), channel_id=1, source_target_pairs={{4,0},{8,4},{12,8},{16,12},{20,16},{24,20},{28,24},{5,1},{9,5},{13... | collective-permute-start | bytes 49160 | tf_op jit(solution)/shard_map/ppermute | solution.py:26
  372.7 6.9 %collective-permute-start.67 = (f32[2,1,16,128]{3,2,1,0:T(8,128)S(1)}, f32[2,1,16,128]{3,2,1,0:T(8,128)S(1)}, u32[]{:S(2)}, u32[]{:S(2)}) collective-permute-start(f32[2,1,16,128]{3,2,1,0:T(8,128)S(1)} %get-tuple-element.159), channel_id=1, source_target_pairs={{0,4},{4,8},{8,12},{12,16},{16,20},{20,24},{24,28},{1,5},{5,9},{9,... | collective-permute-start | bytes 49160 | tf_op jit(solution)/shard_map/ppermute | solution.py:23
  387.4 7.4 %collective-permute-start.70 = (f32[2,1,16,128]{3,2,1,0:T(8,128)S(1)}, f32[2,1,16,128]{3,2,1,0:T(8,128)S(1)}, u32[]{:S(2)}, u32[]{:S(2)}) collective-permute-start(f32[2,1,16,128]{3,2,1,0:T(8,128)S(1)} %get-tuple-element.156), channel_id=1, source_target_pairs={{4,0},{8,4},{12,8},{16,12},{20,16},{24,20},{28,24},{5,1},{9,5},{13... | collective-permute-start | bytes 49160 | tf_op jit(solution)/shard_map/ppermute | solution.py:26
  388.7 6.9 %collective-permute-start.71 = (f32[2,1,16,128]{3,2,1,0:T(8,128)S(1)}, f32[2,1,16,128]{3,2,1,0:T(8,128)S(1)}, u32[]{:S(2)}, u32[]{:S(2)}) collective-permute-start(f32[2,1,16,128]{3,2,1,0:T(8,128)S(1)} %get-tuple-element.155), channel_id=1, source_target_pairs={{0,4},{4,8},{8,12},{12,16},{16,20},{20,24},{24,28},{1,5},{5,9},{9,... | collective-permute-start | bytes 49160 | tf_op jit(solution)/shard_map/ppermute | solution.py:23
  396.9 6.0 collective-permute-start.73
  403.3 8.1 %collective-permute-start.74 = (f32[2,1,16,128]{3,2,1,0:T(8,128)S(1)}, f32[2,1,16,128]{3,2,1,0:T(8,128)S(1)}, u32[]{:S(2)}, u32[]{:S(2)}) collective-permute-start(f32[2,1,16,128]{3,2,1,0:T(8,128)S(1)} %get-tuple-element.152), channel_id=1, source_target_pairs={{4,0},{8,4},{12,8},{16,12},{20,16},{24,20},{28,24},{5,1},{9,5},{13... | collective-permute-start | bytes 49160 | tf_op jit(solution)/shard_map/ppermute | solution.py:26
  404.6 6.9 %collective-permute-start.75 = (f32[2,1,16,128]{3,2,1,0:T(8,128)S(1)}, f32[2,1,16,128]{3,2,1,0:T(8,128)S(1)}, u32[]{:S(2)}, u32[]{:S(2)}) collective-permute-start(f32[2,1,16,128]{3,2,1,0:T(8,128)S(1)} %get-tuple-element.151), channel_id=1, source_target_pairs={{0,4},{4,8},{8,12},{12,16},{16,20},{20,24},{24,28},{1,5},{5,9},{9,... | collective-permute-start | bytes 49160 | tf_op jit(solution)/shard_map/ppermute | solution.py:23
  420.4 16.0 %collective-permute-start.78 = (f32[2,1,16,128]{3,2,1,0:T(8,128)}, f32[2,1,16,128]{3,2,1,0:T(8,128)S(1)}, u32[]{:S(2)}, u32[]{:S(2)}) collective-permute-start(f32[2,1,16,128]{3,2,1,0:T(8,128)} %get-tuple-element.148), channel_id=1, source_target_pairs={{4,0},{8,4},{12,8},{16,12},{20,16},{24,20},{28,24},{5,1},{9,5},{13... | collective-permute-start | bytes 49160 | tf_op jit(solution)/shard_map/ppermute | solution.py:26
  421.7 14.7 %collective-permute-start.79 = (f32[2,1,16,128]{3,2,1,0:T(8,128)}, f32[2,1,16,128]{3,2,1,0:T(8,128)}, u32[]{:S(2)}, u32[]{:S(2)}) collective-permute-start(f32[2,1,16,128]{3,2,1,0:T(8,128)} %get-tuple-element.147), channel_id=1, source_target_pairs={{0,4},{4,8},{8,12},{12,16},{16,20},{20,24},{24,28},{1,5},{5,9},{9,... | collective-permute-start | bytes 49160 | tf_op jit(solution)/shard_map/ppermute | solution.py:23
  437.4 7.1 %collective-permute-start.80 = (f32[2,18,1,128]{3,2,1,0:T(1,128)S(1)}, f32[2,18,1,128]{3,2,1,0:T(1,128)S(1)}, u32[]{:S(2)}, u32[]{:S(2)}) collective-permute-start(f32[2,18,1,128]{3,2,1,0:T(1,128)S(1)} %get-tuple-element.89), channel_id=1, source_target_pairs={{1,0},{2,1},{3,2},{5,4},{6,5},{7,6},{9,8},{10,9},{11,10},{13,12},{... | collective-permute-start | bytes 55304 | tf_op jit(solution)/shard_map/ppermute | solution.py:26
  448.9 25.9 %collective-permute-start.82 = (f32[2,1,16,128]{3,2,1,0:T(8,128)}, f32[2,1,16,128]{3,2,1,0:T(8,128)S(1)}, u32[]{:S(2)}, u32[]{:S(2)}) collective-permute-start(f32[2,1,16,128]{3,2,1,0:T(8,128)} %get-tuple-element.144), channel_id=1, source_target_pairs={{4,0},{8,4},{12,8},{16,12},{20,16},{24,20},{28,24},{5,1},{9,5},{13... | collective-permute-start | bytes 49160 | tf_op jit(solution)/shard_map/ppermute | solution.py:26
  450.2 24.6 %collective-permute-start.83 = (f32[2,1,16,128]{3,2,1,0:T(8,128)}, f32[2,1,16,128]{3,2,1,0:T(8,128)}, u32[]{:S(2)}, u32[]{:S(2)}) collective-permute-start(f32[2,1,16,128]{3,2,1,0:T(8,128)} %get-tuple-element.143), channel_id=1, source_target_pairs={{0,4},{4,8},{8,12},{12,16},{16,20},{20,24},{24,28},{1,5},{5,9},{9,... | collective-permute-start | bytes 49160 | tf_op jit(solution)/shard_map/ppermute | solution.py:23
  475.7 7.1 %collective-permute-start.84 = (f32[2,18,1,128]{3,2,1,0:T(1,128)S(1)}, f32[2,18,1,128]{3,2,1,0:T(1,128)S(1)}, u32[]{:S(2)}, u32[]{:S(2)}) collective-permute-start(f32[2,18,1,128]{3,2,1,0:T(1,128)S(1)} %get-tuple-element.87), channel_id=1, source_target_pairs={{1,0},{2,1},{3,2},{5,4},{6,5},{7,6},{9,8},{10,9},{11,10},{13,12},{... | collective-permute-start | bytes 55304 | tf_op jit(solution)/shard_map/ppermute | solution.py:26
  477.0 6.0 collective-permute-start.85
  486.0 8.4 %collective-permute-start.86 = (f32[2,1,16,128]{3,2,1,0:T(8,128)S(1)}, f32[2,1,16,128]{3,2,1,0:T(8,128)S(1)}, u32[]{:S(2)}, u32[]{:S(2)}) collective-permute-start(f32[2,1,16,128]{3,2,1,0:T(8,128)S(1)} %get-tuple-element.140), channel_id=1, source_target_pairs={{4,0},{8,4},{12,8},{16,12},{20,16},{24,20},{28,24},{5,1},{9,5},{13... | collective-permute-start | bytes 49160 | tf_op jit(solution)/shard_map/ppermute | solution.py:26
  487.3 7.2 %collective-permute-start.87 = (f32[2,1,16,128]{3,2,1,0:T(8,128)S(1)}, f32[2,1,16,128]{3,2,1,0:T(8,128)S(1)}, u32[]{:S(2)}, u32[]{:S(2)}) collective-permute-start(f32[2,1,16,128]{3,2,1,0:T(8,128)S(1)} %get-tuple-element.139), channel_id=1, source_target_pairs={{0,4},{4,8},{8,12},{12,16},{16,20},{20,24},{24,28},{1,5},{5,9},{9,... | collective-permute-start | bytes 49160 | tf_op jit(solution)/shard_map/ppermute | solution.py:23
  495.8 6.0 collective-permute-start.89
  504.4 25.8 %collective-permute-start.90 = (f32[2,1,16,128]{3,2,1,0:T(8,128)}, f32[2,1,16,128]{3,2,1,0:T(8,128)S(1)}, u32[]{:S(2)}, u32[]{:S(2)}) collective-permute-start(f32[2,1,16,128]{3,2,1,0:T(8,128)} %get-tuple-element.136), channel_id=1, source_target_pairs={{4,0},{8,4},{12,8},{16,12},{20,16},{24,20},{28,24},{5,1},{9,5},{13... | collective-permute-start | bytes 49160 | tf_op jit(solution)/shard_map/ppermute | solution.py:26
  505.7 24.6 %collective-permute-start.91 = (f32[2,1,16,128]{3,2,1,0:T(8,128)}, f32[2,1,16,128]{3,2,1,0:T(8,128)}, u32[]{:S(2)}, u32[]{:S(2)}) collective-permute-start(f32[2,1,16,128]{3,2,1,0:T(8,128)} %get-tuple-element.135), channel_id=1, source_target_pairs={{0,4},{4,8},{8,12},{12,16},{16,20},{20,24},{24,28},{1,5},{5,9},{9,... | collective-permute-start | bytes 49160 | tf_op jit(solution)/shard_map/ppermute | solution.py:23
  531.2 7.1 %collective-permute-start.92 = (f32[2,18,1,128]{3,2,1,0:T(1,128)S(1)}, f32[2,18,1,128]{3,2,1,0:T(1,128)S(1)}, u32[]{:S(2)}, u32[]{:S(2)}) collective-permute-start(f32[2,18,1,128]{3,2,1,0:T(1,128)S(1)} %get-tuple-element.83), channel_id=1, source_target_pairs={{1,0},{2,1},{3,2},{5,4},{6,5},{7,6},{9,8},{10,9},{11,10},{13,12},{... | collective-permute-start | bytes 55304 | tf_op jit(solution)/shard_map/ppermute | solution.py:26
  532.5 6.0 collective-permute-start.93
  541.5 6.9 %collective-permute-start.94 = (f32[2,1,16,128]{3,2,1,0:T(8,128)S(1)}, f32[2,1,16,128]{3,2,1,0:T(8,128)S(1)}, u32[]{:S(2)}, u32[]{:S(2)}) collective-permute-start(f32[2,1,16,128]{3,2,1,0:T(8,128)S(1)} %get-tuple-element.132), channel_id=1, source_target_pairs={{4,0},{8,4},{12,8},{16,12},{20,16},{24,20},{28,24},{5,1},{9,5},{13... | collective-permute-start | bytes 49160 | tf_op jit(solution)/shard_map/ppermute | solution.py:26
  549.7 6.0 collective-permute-start.97
  (71 other events, 1546.8 us)
where the time goes:
time: 625 us; the launch traced here: 621 us
  starting transfers between devices  304 us (49%)
  blocking collectives  119 us (19%)
  local copies, waits for them, and re-layouts  93.1 us (15%)
  other arithmetic  58.7 us (9%)
  waiting for transfers between devices  41.7 us (7%)
    ppermute x48, starting transfers between devices, padded_2(): lax.ppermute(lax.slice_in_dim(block, block.shape[dim] - width, None, axis...  240 us
    all_gather x1, blocking collectives, local(): all_rows = lax.all_gather(effective, ('gx', 'gy'), axis=0, tiled=True)  71.9 us
    ppermute x48, starting transfers between devices, padded_2(): lax.ppermute(lax.slice_in_dim(block, 0, width, axis=dim), axis, backward)  62 us
    unnamed x1, blocking collectives  47.6 us
    ppermute x48, waiting for transfers between devices, padded_2(): lax.ppermute(lax.slice_in_dim(block, block.shape[dim] - width, None, axis...  41.6 us
    slice x1, local copies, waits for them, and re-layouts, local(): right_a = grad_p[step_index] + sources[step_index] + acc_p * multipliers[0]  30.5 us
    another operation x3, local copies, waits for them, and re-layouts, relax(): return jnp.stack([new_a, new_b])  26.2 us
    add x23, other arithmetic, relax(): new_b = old_b + table[16] * (table[7] - out_b)  22.6 us
  transfers between devices with their start and end apart: 98, of which 42 were waited for; matrix products, arithmetic and copies ran while one was open for 15% of the time, Pallas kernels for 0%

commit v1 on v0

v1 whole, which is shorter than its diff:
```python
import functools

import jax
import jax.numpy as jnp
from jax import lax
from jax.experimental import pallas as pl
from jax.experimental.pallas import tpu as pltpu
from jax.sharding import PartitionSpec as P

SWEEPS = 8
OMEGA = 0.8
H = 8
HIGHEST = lax.Precision.HIGHEST
STEP_NAMES = 8


def shifted(value, axis, by):
    length = lax.axis_size(axis)
    pairs = [(i, i + by) for i in range(length) if 0 <= i + by < length]
    return lax.ppermute(value, axis, pairs)


def place_edges(dst, n, own, z_low, z_high, x_low, x_high):
    rx, ry, _ = own.shape
    dst[n, H : H + rx, H : H + ry, :] = own
    dst[n, H : H + rx, 0:H, :] = z_low
    dst[n, H : H + rx, H + ry : H + ry + H, :] = z_high
    dst[n, 0:H, 0 : ry + 2 * H, :] = x_low
    dst[n, H + rx : H + rx + H, 0 : ry + 2 * H, :] = x_high


def build_source(src, table_ref, ids_ref, step, steps, wells, rx, ry):
    f32 = jnp.float32
    count = table_ref.shape[0]
    rows_of = table_ref[:, 0, :]
    owner_iota = lax.broadcasted_iota(jnp.int32, (count, 128), 0)
    lane_iota = lax.broadcasted_iota(jnp.int32, (128, 128), 0)
    spans = ((0, H, rx - H), (H, rx, 0), (H + rx, H, 0))
    spans_y = ((0, H, ry - H), (H, ry, 0), (H + ry, H, 0))
    for dx in range(3):
        for dy in range(3):
            k = dx * 3 + dy
            at = ids_ref[k]
            live = ids_ref[9 + k].astype(f32)
            slot = table_ref[at]
            cell = slot[1:2, :].astype(jnp.int32)
            well = slot[2:3, :].astype(jnp.int32)
            wi = slot[3:4, :] * live
            owner = well // wells
            within = well - owner * wells
            hot = jnp.where(owner_iota == owner, 1.0, 0.0).astype(f32)
            rows = lax.dot_general(
                rows_of, hot, (((0,), (0,)), ((), ())), precision=HIGHEST,
                preferred_element_type=f32,
            )
            value = jnp.zeros((1, 128), f32)
            for u in range(wells):
                c = u * steps + step
                value = value + jnp.where(within == u, rows[c : c + 1, :], 0.0)
            value = value * wi
            lane = cell & 127
            row = cell >> 7
            by_lane = jnp.where(lane_iota == lane, value, 0.0)
            x0, nx, from_x = spans[dx]
            y0, ny, from_y = spans_y[dy]
            xi = lax.broadcasted_iota(jnp.int32, (nx, ny, 128), 0) + from_x
            yi = lax.broadcasted_iota(jnp.int32, (nx, ny, 128), 1) + from_y
            target = (xi * ry + yi).reshape(nx * ny, 128)
            by_row = jnp.where(target == row, 1.0, 0.0).astype(f32)
            part = lax.dot_general(
                by_row, by_lane, (((1,), (1,)), ((), ())), precision=HIGHEST,
                preferred_element_type=f32,
            )
            src[x0 : x0 + nx, y0 : y0 + ny, :] = part.reshape(nx, ny, 128)


def step_kernel(first, last, step, steps, wells, *refs):
    f32 = jnp.float32
    it = iter(refs)
    ids_ref, table_ref = next(it), next(it)
    own = [next(it) for _ in range(STEP_NAMES)]
    got = [next(it) for _ in range(4)]
    if first:
        own_geo = [next(it) for _ in range(3)]
    else:
        geo_in = next(it)
        own_acc = [next(it) for _ in range(2)] if step == steps - 2 else None
        acc_in = None if own_acc is not None else next(it)
        lam_own = next(it)
        lam_got = [next(it) for _ in range(4)]
        wells_in = next(it)
    if first:
        geo = next(it)
    else:
        geo = geo_in
    if last:
        out_a, out_b = next(it), next(it)
    else:
        out_lam, out_low, out_high = next(it), next(it), next(it)
        if not first:
            acc_out = next(it)
    out_wells = next(it)
    raw, coef, fields, src = next(it), next(it), next(it), next(it)

    rx, ry, nz = own[0].shape[-3:]
    ex, ey = rx + 2 * H, ry + 2 * H
    got_base = 3 if first else 0

    if first:
        for n in range(3):
            place_edges(geo, n, own_geo[n][...], *[g[n] for g in got])
        geo[1, :, ey : ey + 8, :] = jnp.zeros((ex, 8, nz), f32)

        lane = lax.broadcasted_iota(jnp.int32, (ey, nz), 1)

        def mask_z(x, _):
            geo[2, x, 0:ey, :] = jnp.where(lane == 0, 0.0, geo[2, x, 0:ey, :])
            return 0

        lax.fori_loop(0, ex, mask_z, 0)

        @pl.when(ids_ref[18] == 0)
        def _():
            geo[0, H, :, :] = jnp.zeros(geo.shape[2:], f32)

        @pl.when(ids_ref[19] == 0)
        def _():
            geo[1, :, H : H + 1, :] = jnp.zeros((ex, 1, nz), f32)

    for n in range(STEP_NAMES):
        place_edges(raw, n, own[n][0], *[g[got_base + n] for g in got])
    if not first:
        if own_acc is not None:
            acc = acc_out
            for n in range(2):
                place_edges(acc, n, own_acc[n][...], *[g[STEP_NAMES + n] for g in got])
        else:
            acc = acc_in

    build_source(src, table_ref, ids_ref, step, steps, wells, rx, ry)

    zero_pad = jnp.zeros((ex, 8, nz), f32)
    for buf in range(2):
        for f in range(2):
            fields[buf, f, :, 0:8, :] = zero_pad
            fields[buf, f, :, 8 + ey : 16 + ey, :] = zero_pad
            fields[buf, f, 0, 8 : 8 + ey, :] = jnp.zeros((ey, nz), f32)
            fields[buf, f, ex - 1, 8 : 8 + ey, :] = jnp.zeros((ey, nz), f32)

    if not first:
        for f in range(2):
            lo = 8 + H
            fields[0, f, H : H + rx, lo : lo + ry, :] = lam_own[f]
            fields[0, f, H : H + rx, 8:lo, :] = lam_got[0][f]
            fields[0, f, H : H + rx, lo + ry : lo + ry + H, :] = lam_got[1][f]
            fields[0, f, 0:H, 8 : 8 + ey, :] = lam_got[2][f]
            fields[0, f, H + rx : ex, 8 : 8 + ey, :] = lam_got[3][f]

    def prepare(x, _):
        tz = geo[2, x, 0:ey, :]
        total = (
            geo[0, x + 1, 0:ey, :]
            + geo[0, x, 0:ey, :]
            + geo[1, x, 1 : ey + 1, :]
            + geo[1, x, 0:ey, :]
            + pltpu.roll(tz, nz - 1, 1)
            + tz
        )
        c_pp, c_ss, c_ps, c_sp, frac, mob, g_p, g_s = [raw[n, x] for n in range(STEP_NAMES)]
        den_a = c_pp + total
        den_b = c_ss + mob * total
        s_a = jnp.where(den_a > 0, OMEGA / den_a, 0.0)
        s_b = jnp.where(den_b > 0, OMEGA / den_b, 0.0)
        r_a = g_p + src[x]
        r_b = g_s
        if not first:
            r_a = r_a + acc[0, x] * fields[0, 0, x, 8 : 8 + ey, :]
            r_b = r_b + acc[1, x] * fields[0, 1, x, 8 : 8 + ey, :]
        coef[0, x] = s_a
        coef[1, x] = r_a
        coef[2, x] = c_sp + frac * total
        coef[3, x] = s_b * r_b
        coef[4, x] = s_b * c_ps
        coef[5, x] = s_b * mob
        if first:
            fields[1, 0, x, 8 : 8 + ey, :] = s_a * r_a
            fields[1, 1, x, 8 : 8 + ey, :] = s_b * r_b
        return 0

    lax.fori_loop(0, ex - 1, prepare, 0)

    def sweep(number):
        old, new = (number - 1) % 2, number % 2
        y0, y1 = (H, H + ry) if number == SWEEPS else (0, ey)

        def body(x, _):
            def gather(f):
                def at(i, shift):
                    return fields[old, f, i, 8 + y0 + shift : 8 + y1 + shift, :]

                centre = at(x, 0)
                return (
                    centre, at(x + 1, 0), at(x - 1, 0), at(x, 1), at(x, -1),
                    pltpu.roll(centre, nz - 1, 1), pltpu.roll(centre, 1, 1),
                )

            tz = geo[2, x, y0:y1, :]
            weights = (
                geo[0, x + 1, y0:y1, :], geo[0, x, y0:y1, :],
                geo[1, x, y0 + 1 : y1 + 1, :], geo[1, x, y0:y1, :],
                pltpu.roll(tz, nz - 1, 1), tz,
            )

            def around(values):
                total = weights[0] * values[1]
                for w, v in zip(weights[1:], values[2:]):
                    total = total + w * v
                return total

            va, vb = gather(0), gather(1)
            n_a, n_b = around(va), around(vb)
            a, b = va[0], vb[0]

            def co(n):
                return coef[n, x, y0:y1, :]

            frac = raw[4, x, y0:y1, :]
            fields[new, 0, x, 8 + y0 : 8 + y1, :] = (1.0 - OMEGA) * a + co(0) * (
                co(1) + n_a - co(2) * b + frac * n_b
            )
            fields[new, 1, x, 8 + y0 : 8 + y1, :] = (
                (1.0 - OMEGA) * b + co(3) - co(4) * a + co(5) * n_b
            )
            return 0

        lax.fori_loop(number, ex - number, body, 0)

    for number in range(2 if first else 1, SWEEPS + 1):
        sweep(number)

    end = SWEEPS % 2
    lo = 8 + H
    lam = [fields[end, f, H : H + rx, lo : lo + ry, :] for f in range(2)]
    if last:
        out_a[...] = lam[0]
        out_b[...] = lam[1]
    else:
        for f in range(2):
            out_lam[f] = lam[f]
            out_low[f] = fields[end, f, H : H + rx, lo : lo + H, :]
            out_high[f] = fields[end, f, H : H + rx, lo + ry - H : lo + ry, :]

    mix = (lam[0] + own[4][0] * lam[1]).reshape(rx * ry, nz)
    slot = table_ref[ids_ref[4]]
    cell = slot[1:2, :].astype(jnp.int32)
    well = slot[2:3, :].astype(jnp.int32)
    wi = slot[3:4, :]
    row = cell >> 7
    lane = cell & 127
    by_row = jnp.where(
        lax.broadcasted_iota(jnp.int32, (rx * ry, 128), 0) == row, 1.0, 0.0
    ).astype(f32)
    picked = lax.dot_general(
        mix, by_row, (((0,), (0,)), ((), ())), precision=HIGHEST, preferred_element_type=f32
    )
    sub = lax.broadcasted_iota(jnp.int32, (128, 128), 0)
    values = jnp.sum(jnp.where(sub == lane, picked, 0.0), axis=0, keepdims=True) * wi
    count = table_ref.shape[0]
    owner = well // wells
    column = (well - owner * wells) * steps + step
    spread = jnp.where(sub == column, values, 0.0)
    hot = jnp.where(
        lax.broadcasted_iota(jnp.int32, (count, 128), 0) == owner, 1.0, 0.0
    ).astype(f32)
    dense = lax.dot_general(
        hot, spread, (((1,), (1,)), ((), ())), precision=HIGHEST, preferred_element_type=f32
    )
    if not first:
        dense = dense + wells_in[...]
    out_wells[...] = dense


def whole(shape):
    return pl.BlockSpec(memory_space=pltpu.VMEM)


def run_step(first, last, step, steps, wells, ids, table, own, got, more, shapes):
    f32 = jnp.float32
    rx, ry, nz = shapes
    ex, ey = rx + 2 * H, ry + 2 * H
    vmem = pl.BlockSpec(memory_space=pltpu.VMEM)
    pick = pl.BlockSpec((1, rx, ry, nz), lambda i: (step, 0, 0, 0))
    in_specs = [pl.BlockSpec(memory_space=pltpu.SMEM), vmem] + [pick] * STEP_NAMES
    in_specs += [vmem] * (len(got) + len(more))
    sds = jax.ShapeDtypeStruct
    out_shape = []
    if first:
        out_shape.append(sds((3, ex, ey + 8, nz), f32))
    if last:
        out_shape += [sds((rx, ry, nz), f32)] * 2
    else:
        out_shape.append(sds((2, rx, ry, nz), f32))
        out_shape += [sds((2, rx, H, nz), f32)] * 2
        if not first:
            out_shape.append(sds((2, ex, ey, nz), f32))
    out_shape.append(sds((table.shape[0], 128), f32))
    return pl.pallas_call(
        functools.partial(step_kernel, first, last, step, steps, wells),
        grid=(1,),
        in_specs=in_specs,
        out_specs=[vmem] * len(out_shape),
        out_shape=out_shape,
        scratch_shapes=[
            pltpu.VMEM((STEP_NAMES, ex, ey, nz), f32),
            pltpu.VMEM((6, ex, ey, nz), f32),
            pltpu.VMEM((2, 2, ex, ey + 16, nz), f32),
            pltpu.VMEM((ex, ey, nz), f32),
        ],
        compiler_params=pltpu.CompilerParams(vmem_limit_bytes=48 * 1024 * 1024),
        name="step" + str(step),
    )(ids, table, *own, *got, *more)


def exchange(blocks):
    z_low = shifted(blocks[:, :, -H:, :], "gy", 1)
    z_high = shifted(blocks[:, :, :H, :], "gy", -1)
    return z_low, z_high, *exchange_x(blocks, z_low, z_high)


def exchange_x(blocks, z_low, z_high):
    rx = blocks.shape[1]
    x_low = shifted(
        jnp.concatenate([s[:, rx - H :] for s in (z_low, blocks, z_high)], axis=2), "gx", 1
    )
    x_high = shifted(
        jnp.concatenate([s[:, :H] for s in (z_low, blocks, z_high)], axis=2), "gx", -1
    )
    return x_low, x_high


def local(
    grad_p, grad_s, acc_p, acc_s, trans_x, trans_y, trans_z, c_pp, c_ss, c_ps, c_sp,
    frac, mobility, rate_mis, bhp_mis, control, perf_well, perf_cell, perf_wi,
):
    f32 = jnp.float32
    shapes = trans_x.shape
    rx, ry, nz = shapes
    steps = grad_p.shape[0]
    wells = rate_mis.shape[0]
    n_x, n_y = lax.axis_size("gx"), lax.axis_size("gy")
    devices = n_x * n_y
    gx_at, gy_at = lax.axis_index("gx"), lax.axis_index("gy")
    own = [c_pp, c_ss, c_ps, c_sp, frac, mobility, grad_p, grad_s]

    effective = jnp.where(control == 1, rate_mis, bhp_mis).reshape(1, wells * steps)
    effective = jnp.pad(effective, ((0, 0), (0, 128 - wells * steps)))
    mine = jnp.concatenate(
        [effective, perf_cell.astype(f32)[None], perf_well.astype(f32)[None], perf_wi[None]]
    )
    table = lax.all_to_all(
        jnp.broadcast_to(mine[None], (devices, 4, 128)), ("gx", "gy"), 0, 0, tiled=True
    )

    ids, live = [], []
    for dx in (-1, 0, 1):
        for dy in (-1, 0, 1):
            x, y = gx_at + dx, gy_at + dy
            inside = (x >= 0) & (x < n_x) & (y >= 0) & (y < n_y)
            ids.append(jnp.where(inside, x * n_y + y, 0))
            live.append(inside.astype(jnp.int32))
    ids = jnp.stack(ids + live + [gx_at, gy_at]).astype(jnp.int32)

    lam = None
    geo = acc = dense = None
    for step in reversed(range(steps)):
        first, last = step == steps - 1, step == 0
        group = [a[step] for a in own]
        if first:
            group = [trans_x, trans_y, trans_z] + group
        elif step == steps - 2:
            group = group + [acc_p, acc_s]
        got = exchange(jnp.stack(group))
        if first:
            more = [trans_x, trans_y, trans_z]
        else:
            lam_all, low, high = lam
            z_low = shifted(high, "gy", 1)
            z_high = shifted(low, "gy", -1)
            x_low, x_high = exchange_x(lam_all, z_low, z_high)
            more = [geo] + ([acc_p, acc_s] if step == steps - 2 else [acc])
            more += [lam_all, z_low, z_high, x_low, x_high, dense]
        outs = run_step(first, last, step, steps, wells, ids, table, own, got, more, shapes)
        if first:
            geo = outs[0]
            lam = outs[1:4]
        elif not last:
            lam = outs[0:3]
            acc = outs[3]
        dense = outs[-1]
    out_a, out_b = outs[0], outs[1]
    parts = lax.all_to_all(dense[:, None, :], ("gx", "gy"), 0, 0, tiled=True)
    well_grad = jnp.sum(parts, axis=(0, 1))[: wells * steps].reshape(wells, steps)
    return out_a, out_b, well_grad


def solution(mesh):
    cells3 = P("gx", "gy", None)
    cells4 = P(None, "gx", "gy", None)
    flat = ("gx", "gy")
    placed = (cells4,) * 2 + (cells3,) * 5 + (cells4,) * 6 + (P(flat, None),) * 3 + (P(flat),) * 3
    return jax.shard_map(
        local,
        mesh=mesh,
        in_specs=placed,
        out_specs=(cells3, cells3, P(flat, None)),
        check_vma=False,
    )
```

time: 625 us -> 221 us (0.35)
  starting transfers between devices: 304 us -> 65.5 us
  blocking collectives: 119 us -> 22.3 us
  Pallas kernels: 0 us -> 79.1 us
  local copies, waits for them, and re-layouts: 93.1 us -> 26.6 us
  other arithmetic: 58.7 us -> 5.38 us
  waiting for transfers between devices: 41.7 us -> 19.7 us
    ppermute x98 -> x20, starting transfers between devices: 304 us -> 58.6 us  [shifted(): return lax.ppermute(value, axis, pairs)]
    pallas_call x0 -> x3, Pallas kernels: none -> 79.1 us  [run_step(): pl.pallas_call(functools.partial(step_kernel, first, last, step, steps, w...]
    all_gather x1 -> x0, blocking collectives: 71.9 us -> none  [local(): all_rows = lax.all_gather(effective, ('gx', 'gy'), axis=0, tiled=True)]
    unnamed x1 -> x0, blocking collectives: 47.6 us -> none
    gather x6 -> x0, local copies, waits for them, and re-layouts: 28.2 us -> none  [the longest x3 20.8 us: local(): at_cells = flat_fields[:, perf_cell]]
    another operation x5 -> x2, local copies, waits for them, and re-layouts: 26.2 us -> 0.76 us  [the longest x1 0.66 us: local(): got = exchange(jnp.stack(group))]
    add x26 -> x0, other arithmetic: 23 us -> none  [the longest x23 22.6 us: relax(): new_b = old_b + table[16] * (table[7] - out_b)]
    all_to_all x0 -> x1, blocking collectives: none -> 22.3 us  [local(): parts = lax.all_to_all(dense[:, None, :], ('gx', 'gy'), 0, 0, tiled=True)]
  transfers between devices with their start and end apart: 98 -> 21, of which waited for: 42 -> 7; matrix products, arithmetic and copies ran while one was open for 15% -> 9% of each run, Pallas kernels for 0% -> 24%
where the time goes in v1:
time: 221 us; the launch traced here: 220 us
  Pallas kernels  79.1 us (36%)
  starting transfers between devices  65.5 us (30%)
  local copies, waits for them, and re-layouts  26.6 us (12%)
  blocking collectives  22.3 us (10%)
  waiting for transfers between devices  19.7 us (9%)
  other arithmetic  5.38 us (2%)
    pallas_call x3, Pallas kernels, run_step(): pl.pallas_call(functools.partial(step_kernel, first, last, step, steps, w...  79.1 us
    ppermute x20, starting transfers between devices, shifted(): return lax.ppermute(value, axis, pairs)  58.6 us
    all_to_all x1, blocking collectives, local(): parts = lax.all_to_all(dense[:, None, :], ('gx', 'gy'), 0, 0, tiled=True)  22.3 us
    ppermute x20, waiting for transfers between devices, shifted(): return lax.ppermute(value, axis, pairs)  19.7 us
    unnamed x90, local copies, waits for them, and re-layouts  10.6 us
    slice x15, local copies, waits for them, and re-layouts, exchange_x(): s[:, :H]  8.95 us
    all_to_all x1, starting transfers between devices, local(): lax.all_to_all(jnp.broadcast_to(mine[None], (devices, 4, 128)), ('gx', 'g...  6.85 us
    slice x3, local copies, waits for them, and re-layouts, exchange(): z_high = shifted(blocks[:, :, :H, :], 'gy', -1)  4.93 us
  transfers between devices with their start and end apart: 21, of which 7 were waited for; matrix products, arithmetic and copies ran while one was open for 9% of the time, Pallas kernels for 24%

profile of v1, /device:TPU:0, one launch (start us, length us, event | category | flops | bytes accessed | tf_op | source)
XLA Modules:
  0.0 220.0 jit_solution(3239514835679374223)
XLA Ops:
  0.7 1.0 bitcast_dynamic-update-slice_fusion.4
  1.7 1.0 bitcast_dynamic-update-slice_fusion.3
  2.6 0.9 bitcast_dynamic-update-slice_fusion.2
  3.6 1.1 slice_dynamic-update-slice_fusion.7
  4.9 0.8 copy-done.5
  5.8 0.1 copy-done.7
  6.0 1.1 copy-done.19
  7.0 1.1 copy-done.20
  8.2 1.3 fusion.3
  9.5 0.2 copy-done.17
  9.7 5.8 %collective-permute-start.4 = (f32[11,16,8,128]{3,2,1,0:T(8,128)}, f32[11,16,8,128]{3,2,1,0:T(8,128)}, u32[]{:S(2)}, u32[]{:S(2)}) collective-permute-start(f32[11,16,8,128]{3,2,1,0:T(8,128)} %get-tuple-element.32), channel_id=1, source_target_pairs={{0,1},{1,2},{2,3},{4,5},{5,6},{6,7},{8,9},{9,10},{10,11},{12,13},{... | collective-permute-start | bytes 2162696 | tf_op jit(solution)/shard_map/ppermute | solution.py:20
  15.5 1.3 collective-permute-start.5
  17.0 0.6 broadcast_in_dim.21
  17.6 6.8 %all-to-all-start = ((f32[32,4,128]{2,1,0:T(4,128)}), f32[32,4,128]{2,1,0:T(4,128)S(1)}, u32[]{:S(2)}, u32[]{:S(2)}) async-start(f32[32,4,128]{2,1,0:T(4,128)} %broadcast_in_dim.21), calls=%async_computation | async-start | bytes 131072 | tf_op jit(solution)/shard_map/all_to_all | solution.py:360
  24.5 0.7 bitcast_dynamic-update-slice_fusion.1
  25.1 0.7 bitcast_dynamic-update-slice_fusion
  25.8 2.5 %fusion.5 = (f32[10,16,8,128]{3,2,1,0:T(8,128)}, f32[10,16,8,128]{3,2,1,0:T(8,128)}) fusion(f32[10,16,16,128]{3,2,1,0:T(8,128)} %bitcast_dynamic-update-slice_fusion), kind=kLoop, calls=%fused_computation.49 | loop fusion | bytes 2621440 | tf_op jit(solution)/shard_map/slice | solution.py:326
  28.3 4.5 %collective-permute-start.8 = (f32[10,16,8,128]{3,2,1,0:T(8,128)}, f32[10,16,8,128]{3,2,1,0:T(8,128)}, u32[]{:S(2)}, u32[]{:S(2)}) collective-permute-start(f32[10,16,8,128]{3,2,1,0:T(8,128)} %get-tuple-element.36), channel_id=1, source_target_pairs={{0,1},{1,2},{2,3},{4,5},{5,6},{6,7},{8,9},{9,10},{10,11},{12,13},{... | collective-permute-start | bytes 1966088 | tf_op jit(solution)/shard_map/ppermute | solution.py:20
  32.9 1.3 collective-permute-start.9
  34.2 1.1 fusion.7
  35.2 5.3 %collective-permute-start = (f32[8,16,8,128]{3,2,1,0:T(8,128)}, f32[8,16,8,128]{3,2,1,0:T(8,128)}, u32[]{:S(2)}, u32[]{:S(2)}) collective-permute-start(f32[8,16,8,128]{3,2,1,0:T(8,128)} %get-tuple-element.40), channel_id=1, source_target_pairs={{0,1},{1,2},{2,3},{4,5},{5,6},{6,7},{8,9},{9,10},{10,11},{12,13},{... | collective-permute-start | bytes 1572872 | tf_op jit(solution)/shard_map/ppermute | solution.py:20
  40.7 1.5 fusion.4
  42.2 0.3 copy-done.18
  42.6 1.2 fusion.8
  43.7 1.2 fusion.9
  44.9 1.3 pad_maximum_fusion.1
  46.2 1.3 collective-permute-start.7
  47.5 1.3 pad_maximum_fusion
  48.8 4.3 %collective-permute-start.6 = (f32[11,8,32,128]{3,2,1,0:T(8,128)}, f32[11,8,32,128]{3,2,1,0:T(8,128)}, u32[]{:S(2)}, u32[]{:S(2)}) collective-permute-start(f32[11,8,32,128]{3,2,1,0:T(8,128)} %pad_maximum_fusion), channel_id=1, source_target_pairs={{0,4},{4,8},{8,12},{12,16},{16,20},{20,24},{24,28},{1,5},{5,9},{9,... | collective-permute-start | bytes 4325384 | tf_op jit(solution)/shard_map/ppermute | solution.py:20
  53.1 1.0 fusion.6
  54.1 3.7 %collective-permute-done.refs_10_ = f32[8,16,8,128]{3,2,1,0:T(8,128)} collective-permute-done((f32[8,16,8,128]{3,2,1,0:T(8,128)}, f32[8,16,8,128]{3,2,1,0:T(8,128)}, u32[]{:S(2)}, u32[]{:S(2)}) %collective-permute-start) | collective-permute-done | bytes 524320 | tf_op jit(solution)/shard_map/ppermute | solution.py:20
  57.8 1.3 collective-permute-start.1
  59.1 1.9 fusion.12
  61.0 1.1 fusion.10
  62.2 1.2 pad_maximum_fusion.3
  63.5 1.3 collective-permute-start.11
  64.8 1.3 pad_maximum_fusion.2
  66.0 4.1 %collective-permute-start.10 = (f32[10,8,32,128]{3,2,1,0:T(8,128)}, f32[10,8,32,128]{3,2,1,0:T(8,128)}, u32[]{:S(2)}, u32[]{:S(2)}) collective-permute-start(f32[10,8,32,128]{3,2,1,0:T(8,128)} %pad_maximum_fusion.2), channel_id=1, source_target_pairs={{0,4},{4,8},{8,12},{12,16},{16,20},{20,24},{24,28},{1,5},{5,9},{9,... | collective-permute-start | bytes 3932168 | tf_op jit(solution)/shard_map/ppermute | solution.py:20
  70.1 3.5 %collective-permute-done.1.refs_11_ = f32[8,16,8,128]{3,2,1,0:T(8,128)S(1)} collective-permute-done((f32[8,16,8,128]{3,2,1,0:T(8,128)S(1)}, f32[8,16,8,128]{3,2,1,0:T(8,128)S(1)}, u32[]{:S(2)}, u32[]{:S(2)}) %collective-permute-start.1) | collective-permute-done | bytes 524320 | tf_op jit(solution)/shard_map/ppermute | solution.py:20
  73.6 0.9 fusion.13
  74.5 0.8 copy-done.8
  75.3 0.9 copy-done.12
  76.2 24.7 %step2.1 = (f32[3,32,40,128]{3,2,1,0:T(8,128)}, f32[2,16,16,128]{3,2,1,0:T(8,128)S(1)}, f32[2,16,8,128]{3,2,1,0:T(8,128)S(1)}, f32[2,16,8,128]{3,2,1,0:T(8,128)S(1)}, f32[32,128]{1,0:T(8,128)S(1)}) custom-call(s32[20]{0:T(128)S(1)} %stack.143.refs_0_, f32[32,4,128]{2,1,0:T(4,128)S(1)} %all-to-all-done.refs_1_, f32[3,16,16,128]{3,2,1,0:T(8,128)S(1)} %copy-done, ...), custom_call_target="tpu_custom_call" | custom-call | tf_op jit(solution)/shard_map/step2/pallas_call | solution.py:307
  100.9 3.8 %collective-permute-start.12 = (f32[2,16,8,128]{3,2,1,0:T(8,128)S(1)}, f32[2,16,8,128]{3,2,1,0:T(8,128)S(1)}, u32[]{:S(2)}, u32[]{:S(2)}) collective-permute-start(f32[2,16,8,128]{3,2,1,0:T(8,128)S(1)} %get-tuple-element.18), channel_id=1, source_target_pairs={{0,1},{1,2},{2,3},{4,5},{5,6},{6,7},{8,9},{9,10},{10,11},{12,13},{... | collective-permute-start | bytes 393224 | tf_op jit(solution)/shard_map/ppermute | solution.py:20
  104.7 1.3 collective-permute-start.13
  106.0 1.9 collective-permute-done.12.refs_18_
  108.0 4.1 %collective-permute-done.13.refs_19_ = f32[2,16,8,128]{3,2,1,0:T(8,128)S(1)} collective-permute-done((f32[2,16,8,128]{3,2,1,0:T(8,128)S(1)}, f32[2,16,8,128]{3,2,1,0:T(8,128)S(1)}, u32[]{:S(2)}, u32[]{:S(2)}) %collective-permute-start.13) | collective-permute-done | bytes 131104 | tf_op jit(solution)/shard_map/ppermute | solution.py:20
  112.2 1.4 collective-permute-start.15
  113.6 3.0 %collective-permute-start.14 = (f32[2,8,32,128]{3,2,1,0:T(8,128)S(1)}, f32[2,8,32,128]{3,2,1,0:T(8,128)S(1)}, u32[]{:S(2)}, u32[]{:S(2)}) collective-permute-start(f32[2,8,32,128]{3,2,1,0:T(8,128)S(1)} %pad_maximum_fusion.6), channel_id=1, source_target_pairs={{0,4},{4,8},{8,12},{12,16},{16,20},{20,24},{24,28},{1,5},{5,9},{9,... | collective-permute-start | bytes 786440 | tf_op jit(solution)/shard_map/ppermute | solution.py:20
  116.7 0.1 pad_maximum_fusion.5
  116.8 1.4 collective-permute-start.3
  118.4 3.2 %collective-permute-start.2 = (f32[8,8,32,128]{3,2,1,0:T(8,128)S(1)}, f32[8,8,32,128]{3,2,1,0:T(8,128)S(1)}, u32[]{:S(2)}, u32[]{:S(2)}) collective-permute-start(f32[8,8,32,128]{3,2,1,0:T(8,128)S(1)} %pad_maximum_fusion.4), channel_id=1, source_target_pairs={{0,4},{4,8},{8,12},{12,16},{16,20},{20,24},{24,28},{1,5},{5,9},{9,... | collective-permute-start | bytes 3145736 | tf_op jit(solution)/shard_map/ppermute | solution.py:20
  121.6 27.6 %step1.1 = (f32[2,16,16,128]{3,2,1,0:T(8,128)S(1)}, f32[2,16,8,128]{3,2,1,0:T(8,128)S(1)}, f32[2,16,8,128]{3,2,1,0:T(8,128)S(1)}, f32[2,32,32,128]{3,2,1,0:T(8,128)}, f32[32,128]{1,0:T(8,128)S(1)}) custom-call(s32[20]{0:T(128)S(1)} %stack.143.refs_0_, f32[32,4,128]{2,1,0:T(4,128)S(1)} %all-to-all-done.refs_1_, f32[3,16,16,128]{3,2,1,0:T(8,128)S(1)} %copy-done, ...), custom_call_target="tpu_custom_call" | custom-call | tf_op jit(solution)/shard_map/step1/pallas_call | solution.py:307
  149.2 3.6 %collective-permute-start.16 = (f32[2,16,8,128]{3,2,1,0:T(8,128)S(1)}, f32[2,16,8,128]{3,2,1,0:T(8,128)S(1)}, u32[]{:S(2)}, u32[]{:S(2)}) collective-permute-start(f32[2,16,8,128]{3,2,1,0:T(8,128)S(1)} %get-tuple-element.23), channel_id=1, source_target_pairs={{0,1},{1,2},{2,3},{4,5},{5,6},{6,7},{8,9},{9,10},{10,11},{12,13},{... | collective-permute-start | bytes 393224 | tf_op jit(solution)/shard_map/ppermute | solution.py:20
  152.8 1.3 collective-permute-start.17
  154.1 1.2 collective-permute-done.16.refs_17_
  155.3 4.4 %collective-permute-done.17.refs_18_ = f32[2,16,8,128]{3,2,1,0:T(8,128)S(1)} collective-permute-done((f32[2,16,8,128]{3,2,1,0:T(8,128)S(1)}, f32[2,16,8,128]{3,2,1,0:T(8,128)S(1)}, u32[]{:S(2)}, u32[]{:S(2)}) %collective-permute-start.17) | collective-permute-done | bytes 131104 | tf_op jit(solution)/shard_map/ppermute | solution.py:20
  159.7 1.3 collective-permute-start.19
  161.0 7.8 %collective-permute-start.18 = (f32[2,8,32,128]{3,2,1,0:T(8,128)S(1)}, f32[2,8,32,128]{3,2,1,0:T(8,128)S(1)}, u32[]{:S(2)}, u32[]{:S(2)}) collective-permute-start(f32[2,8,32,128]{3,2,1,0:T(8,128)S(1)} %pad_maximum_fusion.8), channel_id=1, source_target_pairs={{0,4},{4,8},{8,12},{12,16},{16,20},{20,24},{24,28},{1,5},{5,9},{9,... | collective-permute-start | bytes 786440 | tf_op jit(solution)/shard_map/ppermute | solution.py:20
  168.9 0.9 collective-permute-done.18.refs_19_
  169.9 0.3 copy-done.31
  170.2 26.8 %step0.1 = (f32[16,16,128]{2,1,0:T(8,128)}, f32[16,16,128]{2,1,0:T(8,128)}, f32[32,128]{1,0:T(8,128)S(1)}) custom-call(s32[20]{0:T(128)S(1)} %stack.143.refs_0_, f32[32,4,128]{2,1,0:T(4,128)S(1)} %all-to-all-done.refs_1_, f32[3,16,16,128]{3,2,1,0:T(8,128)S(1)} %copy-done, f32[3,16,16,128]{3,2,1,0:T(8,128)S(1)} %copy-done.1, ...), custom_call_target="tpu_custom_call" | custom-call | tf_op jit(solution)/shard_map/step0/pallas_call | solution.py:307
  197.0 22.3 %all_to_all.10 = f32[32,1,128]{2,1,0:T(1,128)S(1)} all-to-all(f32[32,1,128]{2,1,0:T(1,128)S(1)} %bitcast.39), channel_id=1, replica_groups=mesh['gx'=8,'gy'=4] {'gx','gy'}, dimensions={0} | all-to-all | bytes 32768 | tf_op jit(solution)/shard_map/all_to_all | solution.py:401
  219.3 0.6 reshape.14
  (109 shorter events, 1.2 us)
Async XLA Ops:
  0.6 4.0 %copy-start.1 = (f32[3,16,16,128]{3,2,1,0:T(8,128)S(1)}, f32[3,16,16,128]{3,2,1,0:T(8,128)}, u32[]{:S(2)}) copy-start(f32[3,16,16,128]{3,2,1,0:T(8,128)} %refs_3_.5) | copy-start | bytes 1179652
  0.6 4.1 %copy-start.2 = (f32[3,16,16,128]{3,2,1,0:T(8,128)S(1)}, f32[3,16,16,128]{3,2,1,0:T(8,128)}, u32[]{:S(2)}) copy-start(f32[3,16,16,128]{3,2,1,0:T(8,128)} %refs_4_.5) | copy-start | bytes 1179652
  1.6 3.1 %copy-start.3 = (f32[3,16,16,128]{3,2,1,0:T(8,128)S(1)}, f32[3,16,16,128]{3,2,1,0:T(8,128)}, u32[]{:S(2)}) copy-start(f32[3,16,16,128]{3,2,1,0:T(8,128)} %refs_5_.5) | copy-start | bytes 1179652
  3.5 1.3 copy-start.4
  4.7 1.0 copy-start.5
  4.7 1.1 copy-start.6
  4.8 1.1 copy-start.7
  6.0 1.1 copy-start.19
  7.0 1.1 copy-start.20
  8.1 1.6 copy-start.17
  8.1 8.7 %copy-start.33 = (f32[2,3]{1,0:T(2,128)S(1)}, f32[2,3]{1,0:T(2,128)}, u32[]{:S(2)}) copy-start(f32[2,3]{1,0:T(2,128)} %param.32) | copy-start | bytes 76
  8.1 8.7 %copy-start.34 = (f32[2,3]{1,0:T(2,128)S(1)}, f32[2,3]{1,0:T(2,128)}, u32[]{:S(2)}) copy-start(f32[2,3]{1,0:T(2,128)} %param.33) | copy-start | bytes 76
  8.1 8.7 %copy-start.35 = (s32[2,3]{1,0:T(2,128)S(1)}, s32[2,3]{1,0:T(2,128)}, u32[]{:S(2)}) copy-start(s32[2,3]{1,0:T(2,128)} %param.34) | copy-start | bytes 76
  8.1 8.8 %copy-start.36 = (s32[128]{0:T(128)S(1)}, s32[128]{0:T(128)}, u32[]{:S(2)}) copy-start(s32[128]{0:T(128)} %param.35) | copy-start | bytes 1540
  8.1 8.8 %copy-start.37 = (s32[128]{0:T(128)S(1)}, s32[128]{0:T(128)}, u32[]{:S(2)}) copy-start(s32[128]{0:T(128)} %param.36) | copy-start | bytes 1540
  8.1 8.8 %copy-start.38 = (f32[128]{0:T(128)S(1)}, f32[128]{0:T(128)}, u32[]{:S(2)}) copy-start(f32[128]{0:T(128)} %param.37) | copy-start | bytes 1540
  8.1 16.3 %copy-start.13 = (f32[16,16,128]{2,1,0:T(8,128)S(1)}, f32[16,16,128]{2,1,0:T(8,128)}, u32[]{:S(2)}) copy-start(f32[16,16,128]{2,1,0:T(8,128)} %refs_15_.3) | copy-start | bytes 393220
  8.1 17.0 %copy-start.15 = (f32[16,16,128]{2,1,0:T(8,128)S(1)}, f32[16,16,128]{2,1,0:T(8,128)}, u32[]{:S(2)}) copy-start(f32[16,16,128]{2,1,0:T(8,128)} %refs_16_.3) | copy-start | bytes 393220
  9.7 32.9 %collective-permute-start.4 = (f32[11,16,8,128]{3,2,1,0:T(8,128)}, f32[11,16,8,128]{3,2,1,0:T(8,128)}, u32[]{:S(2)}, u32[]{:S(2)}) collective-permute-start(f32[11,16,8,128]{3,2,1,0:T(8,128)} %get-tuple-element.32), channel_id=1, source_target_pairs={{0,1},{1,2},{2,3},{4,5},{5,6},{6,7},{8,9},{9,10},{10,11},{12,13},{... | collective-permute-start | bytes 2162696 | tf_op jit(solution)/shard_map/ppermute | solution.py:20
  15.5 28.2 %collective-permute-start.5 = (f32[11,16,8,128]{3,2,1,0:T(8,128)}, f32[11,16,8,128]{3,2,1,0:T(8,128)}, u32[]{:S(2)}, u32[]{:S(2)}) collective-permute-start(f32[11,16,8,128]{3,2,1,0:T(8,128)} %get-tuple-element.31), channel_id=1, source_target_pairs={{1,0},{2,1},{3,2},{5,4},{6,5},{7,6},{9,8},{10,9},{11,10},{13,12},{... | collective-permute-start | bytes 2162696 | tf_op jit(solution)/shard_map/ppermute | solution.py:20
  17.6 57.7 %all-to-all-start = ((f32[32,4,128]{2,1,0:T(4,128)}), f32[32,4,128]{2,1,0:T(4,128)S(1)}, u32[]{:S(2)}, u32[]{:S(2)}) async-start(f32[32,4,128]{2,1,0:T(4,128)} %broadcast_in_dim.21), calls=%async_computation | async-start | bytes 131072 | tf_op jit(solution)/shard_map/all_to_all | solution.py:360
  25.1 9.0 %copy-start.21 = (f32[8,16,16,128]{3,2,1,0:T(8,128)S(1)}, f32[8,16,16,128]{3,2,1,0:T(8,128)}, u32[]{:S(2)}) copy-start(f32[8,16,16,128]{3,2,1,0:T(8,128)} %copy-done.20) | copy-start | bytes 3145732
  28.3 32.7 %collective-permute-start.8 = (f32[10,16,8,128]{3,2,1,0:T(8,128)}, f32[10,16,8,128]{3,2,1,0:T(8,128)}, u32[]{:S(2)}, u32[]{:S(2)}) collective-permute-start(f32[10,16,8,128]{3,2,1,0:T(8,128)} %get-tuple-element.36), channel_id=1, source_target_pairs={{0,1},{1,2},{2,3},{4,5},{5,6},{6,7},{8,9},{9,10},{10,11},{12,13},{... | collective-permute-start | bytes 1966088 | tf_op jit(solution)/shard_map/ppermute | solution.py:20
  32.9 29.3 %collective-permute-start.9 = (f32[10,16,8,128]{3,2,1,0:T(8,128)}, f32[10,16,8,128]{3,2,1,0:T(8,128)S(1)}, u32[]{:S(2)}, u32[]{:S(2)}) collective-permute-start(f32[10,16,8,128]{3,2,1,0:T(8,128)} %get-tuple-element.35), channel_id=1, source_target_pairs={{1,0},{2,1},{3,2},{5,4},{6,5},{7,6},{9,8},{10,9},{11,10},{13,12},{... | collective-permute-start | bytes 1966088 | tf_op jit(solution)/shard_map/ppermute | solution.py:20
  35.2 22.6 %collective-permute-start = (f32[8,16,8,128]{3,2,1,0:T(8,128)}, f32[8,16,8,128]{3,2,1,0:T(8,128)}, u32[]{:S(2)}, u32[]{:S(2)}) collective-permute-start(f32[8,16,8,128]{3,2,1,0:T(8,128)} %get-tuple-element.40), channel_id=1, source_target_pairs={{0,1},{1,2},{2,3},{4,5},{5,6},{6,7},{8,9},{9,10},{10,11},{12,13},{... | collective-permute-start | bytes 1572872 | tf_op jit(solution)/shard_map/ppermute | solution.py:20
  40.7 1.8 copy-start.18
  46.2 29.1 %collective-permute-start.7 = (f32[11,8,32,128]{3,2,1,0:T(8,128)}, f32[11,8,32,128]{3,2,1,0:T(8,128)}, u32[]{:S(2)}, u32[]{:S(2)}) collective-permute-start(f32[11,8,32,128]{3,2,1,0:T(8,128)} %pad_maximum_fusion.1), channel_id=1, source_target_pairs={{4,0},{8,4},{12,8},{16,12},{20,16},{24,20},{28,24},{5,1},{9,5},{13... | collective-permute-start | bytes 4325384 | tf_op jit(solution)/shard_map/ppermute | solution.py:20
  47.5 5.6 %copy-start.22 = (f32[8,16,16,128]{3,2,1,0:T(8,128)S(1)}, f32[8,16,16,128]{3,2,1,0:T(8,128)}, u32[]{:S(2)}) copy-start(f32[8,16,16,128]{3,2,1,0:T(8,128)} %copy-done.20) | copy-start | bytes 3145732
  48.8 9.1 %copy-start.32 = (f32[8,16,8,128]{3,2,1,0:T(8,128)S(1)}, f32[8,16,8,128]{3,2,1,0:T(8,128)}, u32[]{:S(2)}) copy-start(f32[8,16,8,128]{3,2,1,0:T(8,128)} %get-tuple-element.39) | copy-start | bytes 1572868
  48.8 26.5 %collective-permute-start.6 = (f32[11,8,32,128]{3,2,1,0:T(8,128)}, f32[11,8,32,128]{3,2,1,0:T(8,128)}, u32[]{:S(2)}, u32[]{:S(2)}) collective-permute-start(f32[11,8,32,128]{3,2,1,0:T(8,128)} %pad_maximum_fusion), channel_id=1, source_target_pairs={{0,4},{4,8},{8,12},{12,16},{16,20},{20,24},{24,28},{1,5},{5,9},{9,... | collective-permute-start | bytes 4325384 | tf_op jit(solution)/shard_map/ppermute | solution.py:20
  57.8 15.8 %collective-permute-start.1 = (f32[8,16,8,128]{3,2,1,0:T(8,128)S(1)}, f32[8,16,8,128]{3,2,1,0:T(8,128)S(1)}, u32[]{:S(2)}, u32[]{:S(2)}) collective-permute-start(f32[8,16,8,128]{3,2,1,0:T(8,128)S(1)} %copy-done.32), channel_id=1, source_target_pairs={{1,0},{2,1},{3,2},{5,4},{6,5},{7,6},{9,8},{10,9},{11,10},{13,12},{... | collective-permute-start | bytes 1572872 | tf_op jit(solution)/shard_map/ppermute | solution.py:20
  62.2 1.3 copy-start.23
  63.5 55.0 %collective-permute-start.11 = (f32[10,8,32,128]{3,2,1,0:T(8,128)}, f32[10,8,32,128]{3,2,1,0:T(8,128)}, u32[]{:S(2)}, u32[]{:S(2)}) collective-permute-start(f32[10,8,32,128]{3,2,1,0:T(8,128)} %pad_maximum_fusion.3), channel_id=1, source_target_pairs={{4,0},{8,4},{12,8},{16,12},{20,16},{24,20},{28,24},{5,1},{9,5},{13... | collective-permute-start | bytes 3932168 | tf_op jit(solution)/shard_map/ppermute | solution.py:20
  64.7 10.5 %copy-start = (f32[3,16,16,128]{3,2,1,0:T(8,128)S(1)}, f32[3,16,16,128]{3,2,1,0:T(8,128)}, u32[]{:S(2)}) copy-start(f32[3,16,16,128]{3,2,1,0:T(8,128)} %refs_2_.5) | copy-start | bytes 1179652
  64.8 10.5 %copy-start.10 = (f32[16,16,128]{2,1,0:T(8,128)S(1)}, f32[16,16,128]{2,1,0:T(8,128)}, u32[]{:S(2)}) copy-start(f32[16,16,128]{2,1,0:T(8,128)} %refs_14_.1) | copy-start | bytes 393220
  64.8 10.5 %copy-start.11 = (f32[16,16,128]{2,1,0:T(8,128)S(1)}, f32[16,16,128]{2,1,0:T(8,128)}, u32[]{:S(2)}) copy-start(f32[16,16,128]{2,1,0:T(8,128)} %refs_15_.2) | copy-start | bytes 393220
  66.0 55.5 %collective-permute-start.10 = (f32[10,8,32,128]{3,2,1,0:T(8,128)}, f32[10,8,32,128]{3,2,1,0:T(8,128)}, u32[]{:S(2)}, u32[]{:S(2)}) collective-permute-start(f32[10,8,32,128]{3,2,1,0:T(8,128)} %pad_maximum_fusion.2), channel_id=1, source_target_pairs={{0,4},{4,8},{8,12},{12,16},{16,20},{20,24},{24,28},{1,5},{5,9},{9,... | collective-permute-start | bytes 3932168 | tf_op jit(solution)/shard_map/ppermute | solution.py:20
  74.5 0.8 copy-start.8
  75.3 0.9 copy-start.12
  100.9 15.7 %copy-start.25 = (f32[8,8,16,128]{3,2,1,0:T(8,128)S(1)}, f32[8,8,16,128]{3,2,1,0:T(8,128)}, u32[]{:S(2)}) copy-start(f32[8,8,16,128]{3,2,1,0:T(8,128)} %get-tuple-element.37) | copy-start | bytes 1572868
  100.9 15.8 %copy-start.27 = (f32[8,8,8,128]{3,2,1,0:T(8,128)S(1)}, f32[8,8,8,128]{3,2,1,0:T(8,128)}, u32[]{:S(2)}) copy-start(f32[8,8,8,128]{3,2,1,0:T(8,128)} %get-tuple-element.49) | copy-start | bytes 786436
  100.9 15.8 %copy-start.29 = (f32[8,8,8,128]{3,2,1,0:T(8,128)S(1)}, f32[8,8,8,128]{3,2,1,0:T(8,128)}, u32[]{:S(2)}) copy-start(f32[8,8,8,128]{3,2,1,0:T(8,128)} %get-tuple-element.51) | copy-start | bytes 786436
  100.9 7.0 %collective-permute-start.12 = (f32[2,16,8,128]{3,2,1,0:T(8,128)S(1)}, f32[2,16,8,128]{3,2,1,0:T(8,128)S(1)}, u32[]{:S(2)}, u32[]{:S(2)}) collective-permute-start(f32[2,16,8,128]{3,2,1,0:T(8,128)S(1)} %get-tuple-element.18), channel_id=1, source_target_pairs={{0,1},{1,2},{2,3},{4,5},{5,6},{6,7},{8,9},{9,10},{10,11},{12,13},{... | collective-permute-start | bytes 393224 | tf_op jit(solution)/shard_map/ppermute | solution.py:20
  104.7 7.4 %collective-permute-start.13 = (f32[2,16,8,128]{3,2,1,0:T(8,128)S(1)}, f32[2,16,8,128]{3,2,1,0:T(8,128)S(1)}, u32[]{:S(2)}, u32[]{:S(2)}) collective-permute-start(f32[2,16,8,128]{3,2,1,0:T(8,128)S(1)} %get-tuple-element.19), channel_id=1, source_target_pairs={{1,0},{2,1},{3,2},{5,4},{6,5},{7,6},{9,8},{10,9},{11,10},{13,12},{... | collective-permute-start | bytes 393224 | tf_op jit(solution)/shard_map/ppermute | solution.py:20
  112.1 6.1 %copy-start.24 = (f32[8,8,16,128]{3,2,1,0:T(8,128)S(1)}, f32[8,8,16,128]{3,2,1,0:T(8,128)}, u32[]{:S(2)}) copy-start(f32[8,8,16,128]{3,2,1,0:T(8,128)} %get-tuple-element.38) | copy-start | bytes 1572868
  112.1 6.1 %copy-start.26 = (f32[8,8,8,128]{3,2,1,0:T(8,128)S(1)}, f32[8,8,8,128]{3,2,1,0:T(8,128)}, u32[]{:S(2)}) copy-start(f32[8,8,8,128]{3,2,1,0:T(8,128)} %get-tuple-element.50) | copy-start | bytes 786436
  112.1 6.1 %copy-start.28 = (f32[8,8,8,128]{3,2,1,0:T(8,128)S(1)}, f32[8,8,8,128]{3,2,1,0:T(8,128)}, u32[]{:S(2)}) copy-start(f32[8,8,8,128]{3,2,1,0:T(8,128)} %get-tuple-element.52) | copy-start | bytes 786436
  112.2 9.4 %collective-permute-start.15 = (f32[2,8,32,128]{3,2,1,0:T(8,128)S(1)}, f32[2,8,32,128]{3,2,1,0:T(8,128)S(1)}, u32[]{:S(2)}, u32[]{:S(2)}) collective-permute-start(f32[2,8,32,128]{3,2,1,0:T(8,128)S(1)} %pad_maximum_fusion.7), channel_id=1, source_target_pairs={{4,0},{8,4},{12,8},{16,12},{20,16},{24,20},{28,24},{5,1},{9,5},{13... | collective-permute-start | bytes 786440 | tf_op jit(solution)/shard_map/ppermute | solution.py:20
  113.6 8.0 %collective-permute-start.14 = (f32[2,8,32,128]{3,2,1,0:T(8,128)S(1)}, f32[2,8,32,128]{3,2,1,0:T(8,128)S(1)}, u32[]{:S(2)}, u32[]{:S(2)}) collective-permute-start(f32[2,8,32,128]{3,2,1,0:T(8,128)S(1)} %pad_maximum_fusion.6), channel_id=1, source_target_pairs={{0,4},{4,8},{8,12},{12,16},{16,20},{20,24},{24,28},{1,5},{5,9},{9,... | collective-permute-start | bytes 786440 | tf_op jit(solution)/shard_map/ppermute | solution.py:20
  116.8 4.8 %copy-start.14 = (f32[16,16,128]{2,1,0:T(8,128)S(1)}, f32[16,16,128]{2,1,0:T(8,128)}, u32[]{:S(2)}) copy-start(f32[16,16,128]{2,1,0:T(8,128)} %refs_15_.3) | copy-start | bytes 393220
  116.8 4.8 %copy-start.16 = (f32[16,16,128]{2,1,0:T(8,128)S(1)}, f32[16,16,128]{2,1,0:T(8,128)}, u32[]{:S(2)}) copy-start(f32[16,16,128]{2,1,0:T(8,128)} %refs_16_.3) | copy-start | bytes 393220
  116.8 52.0 %collective-permute-start.3 = (f32[8,8,32,128]{3,2,1,0:T(8,128)S(1)}, f32[8,8,32,128]{3,2,1,0:T(8,128)S(1)}, u32[]{:S(2)}, u32[]{:S(2)}) collective-permute-start(f32[8,8,32,128]{3,2,1,0:T(8,128)S(1)} %pad_maximum_fusion.5), channel_id=1, source_target_pairs={{4,0},{8,4},{12,8},{16,12},{20,16},{24,20},{28,24},{5,1},{9,5},{13... | collective-permute-start | bytes 3145736 | tf_op jit(solution)/shard_map/ppermute | solution.py:20
  118.4 50.5 %collective-permute-start.2 = (f32[8,8,32,128]{3,2,1,0:T(8,128)S(1)}, f32[8,8,32,128]{3,2,1,0:T(8,128)S(1)}, u32[]{:S(2)}, u32[]{:S(2)}) collective-permute-start(f32[8,8,32,128]{3,2,1,0:T(8,128)S(1)} %pad_maximum_fusion.4), channel_id=1, source_target_pairs={{0,4},{4,8},{8,12},{12,16},{16,20},{20,24},{24,28},{1,5},{5,9},{9,... | collective-permute-start | bytes 3145736 | tf_op jit(solution)/shard_map/ppermute | solution.py:20
  149.2 21.0 %copy-start.9 = (f32[8,16,8,128]{3,2,1,0:T(8,128)S(1)}, f32[8,16,8,128]{3,2,1,0:T(8,128)}, u32[]{:S(2)}) copy-start(f32[8,16,8,128]{3,2,1,0:T(8,128)} %copy-done.8) | copy-start | bytes 1572868
  149.2 6.1 %collective-permute-start.16 = (f32[2,16,8,128]{3,2,1,0:T(8,128)S(1)}, f32[2,16,8,128]{3,2,1,0:T(8,128)S(1)}, u32[]{:S(2)}, u32[]{:S(2)}) collective-permute-start(f32[2,16,8,128]{3,2,1,0:T(8,128)S(1)} %get-tuple-element.23), channel_id=1, source_target_pairs={{0,1},{1,2},{2,3},{4,5},{5,6},{6,7},{8,9},{9,10},{10,11},{12,13},{... | collective-permute-start | bytes 393224 | tf_op jit(solution)/shard_map/ppermute | solution.py:20
  152.8 6.9 %collective-permute-start.17 = (f32[2,16,8,128]{3,2,1,0:T(8,128)S(1)}, f32[2,16,8,128]{3,2,1,0:T(8,128)S(1)}, u32[]{:S(2)}, u32[]{:S(2)}) collective-permute-start(f32[2,16,8,128]{3,2,1,0:T(8,128)S(1)} %get-tuple-element.24), channel_id=1, source_target_pairs={{1,0},{2,1},{3,2},{5,4},{6,5},{7,6},{9,8},{10,9},{11,10},{13,12},{... | collective-permute-start | bytes 393224 | tf_op jit(solution)/shard_map/ppermute | solution.py:20
  159.7 9.2 %collective-permute-start.19 = (f32[2,8,32,128]{3,2,1,0:T(8,128)S(1)}, f32[2,8,32,128]{3,2,1,0:T(8,128)S(1)}, u32[]{:S(2)}, u32[]{:S(2)}) collective-permute-start(f32[2,8,32,128]{3,2,1,0:T(8,128)S(1)} %pad_maximum_fusion.9), channel_id=1, source_target_pairs={{4,0},{8,4},{12,8},{16,12},{20,16},{24,20},{28,24},{5,1},{9,5},{13... | collective-permute-start | bytes 786440 | tf_op jit(solution)/shard_map/ppermute | solution.py:20
  161.0 8.8 %collective-permute-start.18 = (f32[2,8,32,128]{3,2,1,0:T(8,128)S(1)}, f32[2,8,32,128]{3,2,1,0:T(8,128)S(1)}, u32[]{:S(2)}, u32[]{:S(2)}) collective-permute-start(f32[2,8,32,128]{3,2,1,0:T(8,128)S(1)} %pad_maximum_fusion.8), channel_id=1, source_target_pairs={{0,4},{4,8},{8,12},{12,16},{16,20},{20,24},{24,28},{1,5},{5,9},{9,... | collective-permute-start | bytes 786440 | tf_op jit(solution)/shard_map/ppermute | solution.py:20
  168.9 1.0 copy-start.30
  168.9 1.3 copy-start.31

commit v2 on v0

v2 whole, which is shorter than its diff:
```python
import functools

import jax
import jax.numpy as jnp
from jax import lax
from jax.experimental import pallas as pl
from jax.experimental.pallas import tpu as pltpu
from jax.sharding import PartitionSpec as P

SWEEPS = 8
OMEGA = 0.8
KEEP = 1.0 - OMEGA
H = 8
V = 4
HIGHEST = lax.Precision.HIGHEST
F32 = jnp.float32
BF16 = jnp.bfloat16

VMEM = pl.BlockSpec(memory_space=pltpu.VMEM)
SMEM = pl.BlockSpec(memory_space=pltpu.SMEM)
ANY = pl.BlockSpec(memory_space=pl.ANY)


def sds(*shape):
    return jax.ShapeDtypeStruct(shape, F32)


def params():
    return pltpu.CompilerParams(vmem_limit_bytes=40 * 1024 * 1024)


def shifted(value, axis, by):
    length = lax.axis_size(axis)
    pairs = [(i, i + by) for i in range(length) if 0 <= i + by < length]
    return lax.ppermute(value, axis, pairs)


def copy_kernel(plan, n_in, *refs):
    ins, outs, sems = refs[:n_in], refs[n_in:-1], refs[-1]
    copies = [
        pltpu.make_async_copy(ins[i].at[s], outs[o].at[d], sems.at[k])
        for k, (i, s, o, d) in enumerate(plan)
    ]
    for c in copies:
        c.start()
    for c in copies:
        c.wait()


def copied(name, ins, plan, outs):
    return pl.pallas_call(
        functools.partial(copy_kernel, plan, len(ins)),
        in_specs=[ANY] * len(ins),
        out_specs=[ANY] * len(outs),
        out_shape=outs,
        scratch_shapes=[pltpu.SemaphoreType.DMA((len(plan),))],
        name=name,
    )(*ins)


def rows(at, size):
    return slice(at, at + size)


ALL = slice(None)


def pack_z(name, arrays, at, dims, after=()):
    rx, ry, nz = dims
    plan = []
    for n, lead in enumerate(at):
        pre = () if lead is None else (lead,)
        plan.append((n, pre + (ALL, rows(0, H)), 0, (n,)))
        plan.append((n, pre + (ALL, rows(ry - H, H)), 1, (n,)))
    count = len(arrays)
    return copied(name, list(arrays) + list(after), plan, [sds(count, rx, H, nz)] * 2)


def pack_x_edges(name, arrays, at, dims):
    rx, ry, nz = dims
    plan = []
    for n, lead in enumerate(at):
        pre = () if lead is None else (lead,)
        plan.append((n, pre + (rows(0, H),), 0, (n,)))
        plan.append((n, pre + (rows(rx - H, H),), 1, (n,)))
    return copied(name, arrays, plan, [sds(len(arrays), H, ry, nz)] * 2)


def pack_corners(name, z_low, z_high):
    count, rx, _, nz = z_low.shape
    plan = []
    for o, x in ((0, 0), (1, rx - H)):
        for i in (0, 1):
            plan.append((i, (ALL, rows(x, H)), o, (ALL, ALL, rows(i * H, H))))
    return copied(name, [z_low, z_high], plan, [sds(count, H, 2 * H, nz)] * 2)


def pack_x(name, arrays, at, z_low, z_high, dims):
    rx, ry, nz = dims
    count = z_low.shape[0]
    plan = []
    base = len(arrays)
    for o, x in ((0, 0), (1, rx - H)):
        plan.append((base, (ALL, rows(x, H)), o, (ALL, ALL, rows(0, H))))
        plan.append((base + 1, (ALL, rows(x, H)), o, (ALL, ALL, rows(H + ry, H))))
        if at is None:
            plan.append((0, (ALL, rows(x, H)), o, (ALL, ALL, rows(H, ry))))
        else:
            for n, lead in enumerate(at):
                pre = () if lead is None else (lead,)
                plan.append((n, pre + (rows(x, H),), o, (n, ALL, rows(H, ry))))
    return copied(
        name, list(arrays) + [z_low, z_high], plan, [sds(count, H, ry + 2 * H, nz)] * 2
    )


def source_kernel(steps, wells, ry, ids_ref, table_ref, src_ref):
    count = table_ref.shape[0]
    rx = src_ref.shape[1] // 3
    of_wells = table_ref[:, 0, :]
    owner_iota = lax.broadcasted_iota(jnp.int32, (count, 128), 0)
    sub = lax.broadcasted_iota(jnp.int32, (128, 128), 0)
    row_iota = lax.broadcasted_iota(jnp.int32, (rx * ry, 128), 0)

    def block(k, _):
        slot = table_ref[ids_ref[k]]
        cell = slot[1:2, :].astype(jnp.int32)
        well = slot[2:3, :].astype(jnp.int32)
        wi = slot[3:4, :] * ids_ref[9 + k].astype(F32)
        owner = well // wells
        within = well - owner * wells
        hot = jnp.where(owner_iota == owner, 1.0, 0.0).astype(F32)
        found = lax.dot_general(
            of_wells, hot, (((0,), (0,)), ((), ())), precision=HIGHEST,
            preferred_element_type=F32,
        )
        by_row = jnp.where(row_iota == (cell >> 7), 1.0, 0.0).astype(BF16)
        in_lane = sub == (cell & 127)
        dx = k // 3
        dy = k - 3 * dx
        for step in range(steps):
            value = jnp.zeros((1, 128), F32)
            for u in range(wells):
                c = u * steps + step
                value = value + jnp.where(within == u, found[c : c + 1, :], 0.0)
            value = value * wi
            part = None
            for _ in range(3):
                piece = value.astype(BF16)
                value = value - piece.astype(F32)
                by_lane = jnp.where(in_lane, piece.astype(F32), 0.0).astype(BF16)
                add = lax.dot_general(
                    by_row, by_lane, (((1,), (1,)), ((), ())), preferred_element_type=F32
                )
                part = add if part is None else part + add
            src_ref[
                step, pl.ds(pl.multiple_of(dx * rx, rx), rx),
                pl.ds(pl.multiple_of(dy * ry, ry), ry), :,
            ] = part.reshape(rx, ry, 128)
        return 0

    lax.fori_loop(0, 9, block, 0)


def by_v(ref, lead, x, offset=0):
    return jnp.stack(
        [ref[(*lead, x, pl.ds(offset + v, 8, stride=V), slice(None))] for v in range(V)]
    )


def up_v(value):
    return jnp.concatenate([value[1:], pltpu.roll(value[0], 7, 0)[None]])


def down_v(value):
    return jnp.concatenate([pltpu.roll(value[V - 1], 1, 0)[None], value[:-1]])


def roll_z(value, by):
    return pltpu.roll(value, by, 2)


def fill(dst, base, own, leads, z_low, z_high, x_low, x_high, corners, offset=0):
    count = len(own)
    rx, ry = own[0].shape[-3], own[0].shape[-2]

    def middle(x, _):
        for n in range(count):
            pre = () if leads[n] is None else (leads[n],)
            dst[base + n, H + x, 0:H, :] = z_low[offset + n, x]
            dst[base + n, H + x, H : H + ry, :] = own[n][pre + (x,)]
            dst[base + n, H + x, H + ry : 2 * H + ry, :] = z_high[offset + n, x]
        return 0

    lax.fori_loop(0, rx, middle, 0)

    def outer(x, _):
        for n in range(count):
            for at, edge, corner in (
                (x, x_low, corners and corners[0]),
                (H + rx + x, x_high, corners and corners[1]),
            ):
                if corner is None:
                    dst[base + n, at, :, :] = edge[offset + n, x]
                else:
                    dst[base + n, at, 0:H, :] = corner[offset + n, x, 0:H]
                    dst[base + n, at, H : H + ry, :] = edge[offset + n, x]
                    dst[base + n, at, H + ry : 2 * H + ry, :] = corner[offset + n, x, H : 2 * H]
        return 0

    lax.fori_loop(0, H, outer, 0)


SA, RA, PC, FR, RB, QC, MC, AA, AB = range(9)
TX, TY, TZ, TU, WS = range(5)


def coefficients(raw, base, src_ref, step, x, total, src_x, src_y):
    c_pp, c_ss, c_ps, c_sp, frac, mob, g_p, g_s = [by_v(raw, (base + n,), x) for n in range(8)]
    den_a = c_pp + total
    den_b = c_ss + mob * total
    s_a = jnp.where(den_a > 0, OMEGA / den_a, 0.0)
    s_b = jnp.where(den_b > 0, OMEGA / den_b, 0.0)
    r_a = g_p + by_v(src_ref, (step,), x + src_x, src_y)
    return s_a, r_a, c_sp + frac * total, frac, s_b * g_s, s_b * c_ps, s_b * mob, s_b


def sweeps(coef, geo, fields, lin, begin, ex):
    def sweep(number):
        old, new = (number - 1) % 2, number % 2

        def body(x, _):
            tx_up, tx_low = geo[TX, x + 1], geo[TX, x]
            ty_low = geo[TY, x]
            ty_up = up_v(ty_low)
            tz_low, tz_up = geo[TZ, x], geo[TU, x]

            def around(f):
                c = fields[old, f, x]
                total = tx_up * fields[old, f, x + 1] + tx_low * fields[old, f, x - 1]
                total = total + (ty_up * up_v(c) + ty_low * down_v(c))
                total = total + (tz_up * roll_z(c, 127) + tz_low * roll_z(c, 1))
                return c, total

            a, n_a = around(0)
            b, n_b = around(1)
            new_a = KEEP * a + coef[SA, x] * (
                (coef[RA, x] + n_a) + (coef[FR, x] * n_b - coef[PC, x] * b)
            )
            new_b = (KEEP * b + coef[RB, x]) + (coef[MC, x] * n_b - coef[QC, x] * a)
            if number == SWEEPS:
                for v in range(V):
                    lin[0, x, pl.ds(v, 8, stride=V), :] = new_a[v]
                    lin[1, x, pl.ds(v, 8, stride=V), :] = new_b[v]
            else:
                fields[new, 0, x] = new_a
                fields[new, 1, x] = new_b
            return 0

        lax.fori_loop(number, ex - number, body, 0, unroll=2)

    for number in range(begin, SWEEPS + 1):
        sweep(number)


def finish(last, step, steps, wells, lin, frac, ids_ref, table_ref, column_ref, before, outs):
    rx, ry, nz = frac.shape[-3:]
    out_wells = outs[-1]

    def copy(x, _):
        for f in range(2):
            row = lin[f, H + x, H : H + ry, :]
            if last:
                outs[f][x] = row
            else:
                outs[0][f, x] = row
                outs[1][f, x] = row[0:H]
                outs[2][f, x] = row[ry - H :]
        return 0

    lax.fori_loop(0, rx, copy, 0, unroll=2)
    mix = lin[0, H : H + rx, H : H + ry, :] + frac[0] * lin[1, H : H + rx, H : H + ry, :]
    mix = mix.reshape(rx * ry, nz)
    cell = column_ref[:, 1:2].astype(jnp.int32)
    by_row = jnp.where(
        lax.broadcasted_iota(jnp.int32, (128, rx * ry), 1) == (cell >> 7), 1.0, 0.0
    ).astype(BF16)
    picked = None
    for _ in range(3):
        piece = mix.astype(BF16)
        mix = mix - piece.astype(F32)
        add = jnp.dot(by_row, piece, preferred_element_type=F32)
        picked = add if picked is None else picked + add
    lane = lax.broadcasted_iota(jnp.int32, (128, 128), 1)
    values = jnp.sum(jnp.where(lane == (cell & 127), picked, 0.0), axis=1, keepdims=True)
    values = values * column_ref[:, 3:4]
    well = column_ref[:, 2:3].astype(jnp.int32)
    owner = well // wells
    spread = jnp.where(lane == (well - owner * wells) * steps + step, values, 0.0)
    flat = table_ref[ids_ref[4]][2:3, :].astype(jnp.int32) // wells
    count = table_ref.shape[0]
    hot = jnp.where(
        lax.broadcasted_iota(jnp.int32, (count, 128), 0) == flat, 1.0, 0.0
    ).astype(F32)
    dense = jnp.dot(hot, spread, precision=HIGHEST, preferred_element_type=F32)
    if before is not None:
        dense = dense + before[...]
    out_wells[...] = dense


def first_kernel(step, steps, wells, *refs):
    ids_ref, table_ref, column_ref, src_ref = refs[:4]
    own_geo, own = refs[4:7], refs[7:15]
    z_low, z_high, x_low, x_high, c_low, c_high = refs[15:21]
    geo = refs[21]
    outs = refs[22:26]
    raw, coef, fields, lin = refs[26:]
    rx, ry, nz = own[0].shape[-3:]
    ex = rx + 2 * H
    got = (z_low, z_high, x_low, x_high, (c_low, c_high))
    fill(raw, 0, own_geo + own, [None] * 3 + [0] * 8, *got)

    @pl.when(ids_ref[18] == 0)
    def _():
        raw[0, H, :, :] = jnp.zeros(raw.shape[2:], F32)

    @pl.when(ids_ref[19] == 0)
    def _():
        def clear(x, _):
            raw[1, x, H : H + 1, :] = jnp.zeros((1, nz), F32)
            return 0

        lax.fori_loop(0, ex, clear, 0)

    def geometry(x, _):
        lane = lax.broadcasted_iota(jnp.int32, (V, 8, nz), 2)
        tz = jnp.where(lane == 0, 0.0, by_v(raw, (2,), x))
        geo[TX, x] = by_v(raw, (0,), x)
        geo[TY, x] = by_v(raw, (1,), x)
        geo[TZ, x] = tz
        geo[TU, x] = roll_z(tz, 127)
        return 0

    lax.fori_loop(0, ex, geometry, 0)

    def prepare(x, _):
        ty = geo[TY, x]
        total = (
            (geo[TX, x + 1] + geo[TX, x]) + (up_v(ty) + ty) + (geo[TU, x] + geo[TZ, x])
        )
        geo[WS, x] = total
        s_a, r_a, p, frac, r_b, q, m, _ = coefficients(
            raw, 3, src_ref, step, x, total, rx - H, ry - H
        )
        coef[SA, x] = s_a
        coef[RA, x] = r_a
        coef[PC, x] = p
        coef[FR, x] = frac
        coef[RB, x] = r_b
        coef[QC, x] = q
        coef[MC, x] = m
        fields[1, 0, x] = s_a * r_a
        fields[1, 1, x] = r_b
        return 0

    lax.fori_loop(0, ex - 1, prepare, 0)
    sweeps(coef, geo, fields, lin, 2, ex)
    finish(False, step, steps, wells, lin, own[4], ids_ref, table_ref, column_ref, None, outs)


def prepare_kernel(step, with_acc, *refs):
    src_ref, geo = refs[:2]
    own = refs[2:10]
    at = 10
    acc = ()
    if with_acc:
        acc = refs[10:12]
        at = 12
    got = refs[at : at + 4]
    at += 4
    if not with_acc:
        acc_raw = refs[at]
        at += 1
    coef = refs[at]
    raw = refs[-1]
    rx, ry, nz = own[0].shape[-3:]
    ex = rx + 2 * H
    fill(raw, 0, own, [0] * 8, *got, None)
    if with_acc:
        acc_raw = refs[at + 1]
        fill(acc_raw, 0, acc, [None] * 2, *got, None, offset=8)

    def prepare(x, _):
        s_a, r_a, p, frac, r_b, q, m, s_b = coefficients(
            raw, 0, src_ref, step, x, geo[WS, x], rx - H, ry - H
        )
        coef[SA, x] = s_a
        coef[RA, x] = r_a
        coef[PC, x] = p
        coef[FR, x] = frac
        coef[RB, x] = r_b
        coef[QC, x] = q
        coef[MC, x] = m
        coef[AA, x] = by_v(acc_raw, (0,), x)
        coef[AB, x] = s_b * by_v(acc_raw, (1,), x)
        return 0

    lax.fori_loop(0, ex - 1, prepare, 0)


def sweep_kernel(last, step, steps, wells, *refs):
    ids_ref, table_ref, column_ref, coef, geo, frac, lam = refs[:7]
    got = refs[7:11]
    before = refs[11]
    outs = refs[12:-3]
    now, fields, lin = refs[-3:]
    rx, ry, nz = frac.shape[-3:]
    ex = rx + 2 * H
    fill(lin, 0, [lam.at[0], lam.at[1]], [None] * 2, *got, None)

    def begin(x, _):
        a, b = by_v(lin, (0,), x), by_v(lin, (1,), x)
        fields[0, 0, x] = a
        fields[0, 1, x] = b
        now[0, x] = coef[RA, x] + coef[AA, x] * a
        now[1, x] = coef[RB, x] + coef[AB, x] * b
        return 0

    lax.fori_loop(0, ex, begin, 0)

    class Joined:
        def __getitem__(self, at):
            n, x = at
            return now[0, x] if n == RA else now[1, x] if n == RB else coef[n, x]

    sweeps(Joined(), geo, fields, lin, 1, ex)
    finish(last, step, steps, wells, lin, frac, ids_ref, table_ref, column_ref, before, outs)


def local(
    grad_p, grad_s, acc_p, acc_s, trans_x, trans_y, trans_z, c_pp, c_ss, c_ps, c_sp,
    frac, mobility, rate_mis, bhp_mis, control, perf_well, perf_cell, perf_wi,
):
    dims = rx, ry, nz = trans_x.shape
    ex, ey = rx + 2 * H, ry + 2 * H
    steps = grad_p.shape[0]
    wells = rate_mis.shape[0]
    n_x, n_y = lax.axis_size("gx"), lax.axis_size("gy")
    devices = n_x * n_y
    gx_at, gy_at = lax.axis_index("gx"), lax.axis_index("gy")
    own = [c_pp, c_ss, c_ps, c_sp, frac, mobility, grad_p, grad_s]
    geo_own = [trans_x, trans_y, trans_z]
    top = steps - 1

    def sent(low, high, axis):
        return shifted(high, axis, 1), shifted(low, axis, -1)

    group = geo_own + own
    at = [None] * 3 + [top] * 8
    z_got = sent(*pack_z("pack_z2", group, at, dims), "gy")
    x_got = sent(*pack_x_edges("pack_x2", group, at, dims), "gx")

    effective = jnp.where(control == 1, rate_mis, bhp_mis).reshape(1, wells * steps)
    effective = jnp.pad(effective, ((0, 0), (0, 128 - wells * steps)))
    mine = jnp.concatenate(
        [effective, perf_cell.astype(F32)[None], perf_well.astype(F32)[None], perf_wi[None]]
    )
    table = lax.all_to_all(
        jnp.broadcast_to(mine[None], (devices, 4, 128)), ("gx", "gy"), 0, 0, tiled=True
    )
    column = mine.T

    ids, live = [], []
    for dx in (-1, 0, 1):
        for dy in (-1, 0, 1):
            x, y = gx_at + dx, gy_at + dy
            inside = (x >= 0) & (x < n_x) & (y >= 0) & (y < n_y)
            ids.append(jnp.where(inside, x * n_y + y, 0))
            live.append(inside.astype(jnp.int32))
    ids = jnp.stack(ids + live + [gx_at, gy_at]).astype(jnp.int32)

    src = pl.pallas_call(
        functools.partial(source_kernel, steps, wells, ry),
        in_specs=[SMEM, VMEM],
        out_specs=VMEM,
        out_shape=sds(steps, 3 * rx, 3 * ry, nz),
        compiler_params=params(),
        name="sources",
    )(ids, table)

    c_got = sent(*pack_corners("pack_c2", *z_got), "gx")

    def pick(step):
        return pl.BlockSpec((1, rx, ry, nz), lambda i: (step, 0, 0, 0))

    ext = (ex, V, 8, nz)
    lam_out = [sds(2, rx, ry, nz), sds(2, rx, H, nz), sds(2, rx, H, nz)]
    well_out = sds(devices, 128)

    geo, lam, low, high, dense = pl.pallas_call(
        functools.partial(first_kernel, top, steps, wells),
        grid=(1,),
        in_specs=[SMEM] + [VMEM] * 6 + [pick(top)] * 8 + [VMEM] * 6,
        out_specs=[VMEM] * 5,
        out_shape=[sds(5, *ext)] + lam_out + [well_out],
        scratch_shapes=[
            pltpu.VMEM((11, ex, ey, nz), F32),
            pltpu.VMEM((7, *ext), F32),
            pltpu.VMEM((2, 2, *ext), F32),
            pltpu.VMEM((2, ex, ey, nz), F32),
        ],
        compiler_params=params(),
        name="step_top",
    )(ids, table, column, src, *geo_own, *own, *z_got, *x_got, *c_got)

    acc_raw = None
    after = z_got
    for step in reversed(range(top)):
        last = step == 0
        with_acc = step == top - 1
        group = own + ([acc_p, acc_s] if with_acc else [])
        at = [step] * 8 + ([None] * 2 if with_acc else [])
        g_z = sent(*pack_z("pack_z", group, at, dims, after), "gy")
        g_x = sent(*pack_x("pack_x", group, at, *g_z, dims), "gx")
        after = g_z

        outs = [sds(9, *ext)] + ([sds(2, ex, ey, nz)] if with_acc else [])
        made = pl.pallas_call(
            functools.partial(prepare_kernel, step, with_acc),
            grid=(1,),
            in_specs=[VMEM] * 2 + [pick(step)] * 8 + [VMEM] * (6 if with_acc else 5),
            out_specs=[VMEM] * len(outs),
            out_shape=outs,
            scratch_shapes=[pltpu.VMEM((8, ex, ey, nz), F32)],
            compiler_params=params(),
            name="prepare",
        )(src, geo, *own, *((acc_p, acc_s) if with_acc else ()), *g_z, *g_x,
          *(() if with_acc else (acc_raw,)))
        coef = made[0]
        if with_acc:
            acc_raw = made[1]

        l_z = sent(low, high, "gy")
        l_x = sent(*pack_x("pack_lam", [lam], None, *l_z, dims), "gx")
        outs = [sds(rx, ry, nz)] * 2 if last else lam_out
        outs = pl.pallas_call(
            functools.partial(sweep_kernel, last, step, steps, wells),
            grid=(1,),
            in_specs=[SMEM] + [VMEM] * 4 + [pick(step)] + [VMEM] * 6,
            out_specs=[VMEM] * (len(outs) + 1),
            out_shape=outs + [well_out],
            scratch_shapes=[
                pltpu.VMEM((2, *ext), F32),
                pltpu.VMEM((2, 2, *ext), F32),
                pltpu.VMEM((2, ex, ey, nz), F32),
            ],
            compiler_params=params(),
            name="step",
        )(ids, table, column, coef, geo, frac, lam, *l_z, *l_x, dense)
        dense = outs[-1]
        if not last:
            lam, low, high = outs[:3]

    parts = lax.all_to_all(dense[:, None, :], ("gx", "gy"), 0, 0, tiled=True)
    well_grad = jnp.sum(parts, axis=(0, 1))[: wells * steps].reshape(wells, steps)
    return outs[0], outs[1], well_grad


def solution(mesh):
    cells3 = P("gx", "gy", None)
    cells4 = P(None, "gx", "gy", None)
    flat = ("gx", "gy")
    placed = (cells4,) * 2 + (cells3,) * 5 + (cells4,) * 6 + (P(flat, None),) * 3 + (P(flat),) * 3
    return jax.shard_map(
        local,
        mesh=mesh,
        in_specs=placed,
        out_specs=(cells3, cells3, P(flat, None)),
        check_vma=False,
    )
```

time: 625 us -> 640 us (1.024)
  Pallas kernels: 0 us -> 446 us
  starting transfers between devices: 304 us -> 63.4 us
  blocking collectives: 119 us -> 14.7 us
  other arithmetic: 58.7 us -> 0.07 us
  local copies, waits for them, and re-layouts: 93.1 us -> 61.7 us
  waiting for transfers between devices: 41.7 us -> 49.9 us
    pallas_call x0 -> x15, Pallas kernels: none -> 446 us  [the longest x9 388 us: copied(): pl.pallas_call(functools.partial(copy_kernel, plan, len(ins)), in_specs=[...]
    ppermute x98 -> x22, starting transfers between devices: 304 us -> 54.4 us  [shifted(): return lax.ppermute(value, axis, pairs)]
    all_gather x1 -> x0, blocking collectives: 71.9 us -> none  [local(): all_rows = lax.all_gather(effective, ('gx', 'gy'), axis=0, tiled=True)]
    unnamed x73 -> x168, local copies, waits for them, and re-layouts: 2.64 us -> 59.5 us
    unnamed x1 -> x0, blocking collectives: 47.6 us -> none
    slice x11 -> x0, local copies, waits for them, and re-layouts: 35.8 us -> none  [the longest x1 30.5 us: local(): right_a = grad_p[step_index] + sources[step_index] + acc_p * multipliers[0]]
    gather x6 -> x0, local copies, waits for them, and re-layouts: 28.2 us -> none  [the longest x3 20.8 us: local(): at_cells = flat_fields[:, perf_cell]]
    another operation x5 -> x1, local copies, waits for them, and re-layouts: 26.2 us -> 0.09 us  [local(): ids = jnp.stack(ids + live + [gx_at, gy_at]).astype(jnp.int32)]
  transfers between devices with their start and end apart: 98 -> 23, of which waited for: 42 -> 7; matrix products, arithmetic and copies ran while one was open for 15% -> 0% of each run, Pallas kernels for 0% -> 54%
where the time goes in v2:
time: 640 us; the launch traced here: 638 us
  Pallas kernels  446 us (70%)
  starting transfers between devices  63.4 us (10%)
  local copies, waits for them, and re-layouts  61.7 us (10%)
  waiting for transfers between devices  49.9 us (8%)
  blocking collectives  14.7 us (2%)
    pallas_call x9, Pallas kernels, copied(): pl.pallas_call(functools.partial(copy_kernel, plan, len(ins)), in_specs=[...  388 us
    unnamed x168, local copies, waits for them, and re-layouts  59.5 us
    ppermute x22, starting transfers between devices, shifted(): return lax.ppermute(value, axis, pairs)  54.4 us
    ppermute x22, waiting for transfers between devices, shifted(): return lax.ppermute(value, axis, pairs)  33.7 us
    pallas_call x2, Pallas kernels, local(): pl.pallas_call(functools.partial(sweep_kernel, last, step, steps, wells),...  25.7 us
    all_to_all x1, waiting for transfers between devices, local(): lax.all_to_all(jnp.broadcast_to(mine[None], (devices, 4, 128)), ('gx', 'g...  16.2 us
    pallas_call x1, Pallas kernels, local(): pl.pallas_call(functools.partial(first_kernel, top, steps, wells), grid=(...  15.6 us
    all_to_all x1, blocking collectives, local(): parts = lax.all_to_all(dense[:, None, :], ('gx', 'gy'), 0, 0, tiled=True)  14.7 us
  transfers between devices with their start and end apart: 23, of which 7 were waited for; matrix products, arithmetic and copies ran while one was open for 0% of the time, Pallas kernels for 54%

profile of v2, /device:TPU:0, one launch (start us, length us, event | category | flops | bytes accessed | tf_op | source)
XLA Modules:
  0.0 637.7 jit_solution(5876683156286738886)
XLA Ops:
  0.6 45.0 %pack_z2.1 = (f32[11,16,8,128]{3,2,1,0:T(8,128)}, f32[11,16,8,128]{3,2,1,0:T(8,128)}) custom-call(f32[16,16,128]{2,1,0:T(8,128)} %refs_4_.11, f32[16,16,128]{2,1,0:T(8,128)} %refs_5_.13, f32[16,16,128]{2,1,0:T(8,128)} %refs_6_.11, f32[3,16,16,128]{3,2,1,0:T(8,128)} %refs_2_.15, f32[3,16,16,128]{3,2,1,0:T(8,128)} %refs_3_.15, f32[3,16,16,128]{3,2,1,0:T(8,128)} %refs_4_.17, ...), custom_call_target="tpu_custom_call" | custom-call | tf_op jit(solution)/shard_map/pack_z2/pallas_call | solution.py:51
  45.6 5.0 collective-permute-start
  50.6 1.3 collective-permute-start.1
  51.9 14.3 %collective-permute-done.refs_0_.refs_15_.refs_10_ = f32[11,16,8,128]{3,2,1,0:T(8,128)S(1)} collective-permute-done((f32[11,16,8,128]{3,2,1,0:T(8,128)}, f32[11,16,8,128]{3,2,1,0:T(8,128)S(1)}, u32[]{:S(2)}, u32[]{:S(2)}) %collective-permute-start) | collective-permute-done | bytes 720928 | tf_op jit(solution)/shard_map/ppermute | solution.py:35
  66.2 4.0 collective-permute-done.1.refs_1_.refs_16_.refs_11_
  71.2 41.0 %pack_z.2 = (f32[10,16,8,128]{3,2,1,0:T(8,128)}, f32[10,16,8,128]{3,2,1,0:T(8,128)}) custom-call(f32[3,16,16,128]{3,2,1,0:T(8,128)} %refs_2_.15, f32[3,16,16,128]{3,2,1,0:T(8,128)} %refs_3_.15, f32[3,16,16,128]{3,2,1,0:T(8,128)} %refs_4_.17, f32[3,16,16,128]{3,2,1,0:T(8,128)} %refs_5_.19, f32[3,16,16,128]{3,2,1,0:T(8,128)} %refs_5_.21, ...), custom_call_target="tpu_custom_call" | custom-call | tf_op jit(solution)/shard_map/pack_z/pallas_call | solution.py:51
  112.2 3.5 collective-permute-start.6
  115.7 1.3 collective-permute-start.7
  117.0 45.0 %pack_x2.1 = (f32[11,8,16,128]{3,2,1,0:T(8,128)}, f32[11,8,16,128]{3,2,1,0:T(8,128)}) custom-call(f32[16,16,128]{2,1,0:T(8,128)} %refs_4_.11, f32[16,16,128]{2,1,0:T(8,128)} %refs_5_.13, f32[16,16,128]{2,1,0:T(8,128)} %refs_6_.11, f32[3,16,16,128]{3,2,1,0:T(8,128)} %refs_2_.15, f32[3,16,16,128]{3,2,1,0:T(8,128)} %refs_3_.15, f32[3,16,16,128]{3,2,1,0:T(8,128)} %refs_4_.17, ...), custom_call_target="tpu_custom_call" | custom-call | tf_op jit(solution)/shard_map/pack_x2/pallas_call | solution.py:51
  161.9 1.3 collective-permute-start.2
  165.0 33.0 %pack_z.3 = (f32[8,16,8,128]{3,2,1,0:T(8,128)}, f32[8,16,8,128]{3,2,1,0:T(8,128)}) custom-call(f32[3,16,16,128]{3,2,1,0:T(8,128)} %refs_2_.15, f32[3,16,16,128]{3,2,1,0:T(8,128)} %refs_3_.15, f32[3,16,16,128]{3,2,1,0:T(8,128)} %refs_4_.17, f32[3,16,16,128]{3,2,1,0:T(8,128)} %refs_5_.19, f32[3,16,16,128]{3,2,1,0:T(8,128)} %refs_5_.21, ...), custom_call_target="tpu_custom_call" | custom-call | tf_op jit(solution)/shard_map/pack_z/pallas_call | solution.py:51
  198.0 4.6 collective-permute-start.8
  202.7 1.4 collective-permute-start.9
  204.1 80.7 %pack_x.3 = (f32[10,8,32,128]{3,2,1,0:T(8,128)}, f32[10,8,32,128]{3,2,1,0:T(8,128)}) custom-call(f32[3,16,16,128]{3,2,1,0:T(8,128)} %refs_2_.15, f32[3,16,16,128]{3,2,1,0:T(8,128)} %refs_3_.15, f32[3,16,16,128]{3,2,1,0:T(8,128)} %refs_4_.17, f32[3,16,16,128]{3,2,1,0:T(8,128)} %refs_5_.19, f32[3,16,16,128]{3,2,1,0:T(8,128)} %refs_5_.21, ...), custom_call_target="tpu_custom_call" | custom-call | tf_op jit(solution)/shard_map/pack_x/pallas_call | solution.py:51
  284.8 4.9 collective-permute-start.12
  289.7 1.4 collective-permute-start.3
  291.1 44.8 %pack_c2.1 = (f32[11,8,16,128]{3,2,1,0:T(8,128)}, f32[11,8,16,128]{3,2,1,0:T(8,128)}) custom-call(f32[11,16,8,128]{3,2,1,0:T(8,128)} %copy-done.34, f32[11,16,8,128]{3,2,1,0:T(8,128)} %copy-done.36), custom_call_target="tpu_custom_call" | custom-call | tf_op jit(solution)/shard_map/pack_c2/pallas_call | solution.py:51
  336.8 3.1 collective-permute-start.4
  339.9 1.3 collective-permute-start.13
  341.2 1.3 collective-permute-start.5
  342.7 64.8 %pack_x.2 = (f32[8,8,32,128]{3,2,1,0:T(8,128)}, f32[8,8,32,128]{3,2,1,0:T(8,128)}) custom-call(f32[3,16,16,128]{3,2,1,0:T(8,128)} %refs_2_.15, f32[3,16,16,128]{3,2,1,0:T(8,128)} %refs_3_.15, f32[3,16,16,128]{3,2,1,0:T(8,128)} %refs_4_.17, f32[3,16,16,128]{3,2,1,0:T(8,128)} %refs_5_.19, f32[3,16,16,128]{3,2,1,0:T(8,128)} %refs_5_.21, ...), custom_call_target="tpu_custom_call" | custom-call | tf_op jit(solution)/shard_map/pack_x/pallas_call | solution.py:51
  407.5 4.6 collective-permute-start.10
  412.1 1.3 collective-permute-start.11
  414.1 9.0 %all-to-all-start = ((f32[32,4,128]{2,1,0:T(4,128)}), f32[32,4,128]{2,1,0:T(4,128)S(1)}, u32[]{:S(2)}, u32[]{:S(2)}) async-start(f32[32,4,128]{2,1,0:T(4,128)} %broadcast_in_dim.21), calls=%async_computation | async-start | bytes 131072 | tf_op jit(solution)/shard_map/all_to_all | solution.py:468
  424.0 16.2 %all-to-all-done.table_ref.refs_1_ = f32[32,4,128]{2,1,0:T(4,128)S(1)} async-done(((f32[32,4,128]{2,1,0:T(4,128)}), f32[32,4,128]{2,1,0:T(4,128)S(1)}, u32[]{:S(2)}, u32[]{:S(2)}) %all-to-all-start) | async-done | bytes 65568 | tf_op jit(solution)/shard_map/all_to_all | solution.py:468
  440.2 6.6 %sources.1.refs_3_.refs_0_ = f32[3,48,48,128]{3,2,1,0:T(8,128)S(1)} custom-call(s32[20]{0:T(128)S(1)} %stack.119.ids_ref.refs_0_, f32[32,4,128]{2,1,0:T(4,128)S(1)} %all-to-all-done.table_ref.refs_1_), custom_call_target="tpu_custom_call" | custom-call | tf_op jit(solution)/shard_map/sources/pallas_call | solution.py:482
  446.8 1.8 copy-done
  449.5 1.0 copy-done.2
  457.5 1.1 copy-done.35
  458.6 1.1 copy-done.37
  463.2 1.1 copy-done.66
  464.3 1.1 copy-done.68
  465.5 1.1 copy-done.70
  466.6 1.1 copy-done.72
  467.7 15.6 %step_top.1 = (f32[5,32,4,8,128]{4,3,2,1,0:T(8,128)S(1)}, f32[2,16,16,128]{3,2,1,0:T(8,128)S(1)}, f32[2,16,8,128]{3,2,1,0:T(8,128)S(1)}, f32[2,16,8,128]{3,2,1,0:T(8,128)S(1)}, f32[32,128]{1,0:T(8,128)S(1)}) custom-call(s32[20]{0:T(128)S(1)} %stack.119.ids_ref.refs_0_, f32[32,4,128]{2,1,0:T(4,128)S(1)} %copy-done.48, f32[128,4]{1,0:T(8,128)S(1)} %bitcast.30, ...), custom_call_target="tpu_custom_call" | custom-call | tf_op jit(solution)/shard_map/step_top/pallas_call | solution.py:500
  483.3 1.6 copy-done.7
  486.1 5.0 collective-permute-start.14
  491.1 2.4 collective-permute-done.14.refs_1_.refs_7_
  493.5 1.3 collective-permute-start.15
  494.8 6.2 collective-permute-done.15.refs_2_.refs_8_
  501.0 17.0 %pack_lam.2 = (f32[2,8,32,128]{3,2,1,0:T(8,128)}, f32[2,8,32,128]{3,2,1,0:T(8,128)}) custom-call(f32[2,16,16,128]{3,2,1,0:T(8,128)} %copy-done.63, f32[2,16,8,128]{3,2,1,0:T(8,128)} %collective-permute-done.14.refs_1_.refs_7_, f32[2,16,8,128]{3,2,1,0:T(8,128)} %collective-permute-done.15.refs_2_.refs_8_), custom_call_target="tpu_custom_call" | custom-call | tf_op jit(solution)/shard_map/pack_lam/pallas_call | solution.py:51
  518.1 1.3 collective-permute-start.16
  519.4 1.3 collective-permute-start.17
  521.7 1.7 copy-done.8
  530.4 1.1 copy-done.39
  531.5 1.1 copy-done.41
  534.5 5.3 prepare.2
  539.8 2.6 copy-done.42
  542.5 12.7 %step.2 = (f32[2,16,16,128]{3,2,1,0:T(8,128)S(1)}, f32[2,16,8,128]{3,2,1,0:T(8,128)S(1)}, f32[2,16,8,128]{3,2,1,0:T(8,128)S(1)}, f32[32,128]{1,0:T(8,128)S(1)}) custom-call(s32[20]{0:T(128)S(1)} %copy-done.76, f32[32,4,128]{2,1,0:T(4,128)S(1)} %copy-done.49, f32[128,4]{1,0:T(8,128)S(1)} %bitcast.31, f32[9,32,4,8,128]{4,3,2,1,0:T(8,128)S(1)} %copy-done.42, ...), custom_call_target="tpu_custom_call" | custom-call | tf_op jit(solution)/shard_map/step/pallas_call | solution.py:546
  555.8 4.6 collective-permute-start.18
  560.4 1.3 collective-permute-start.19
  561.7 1.2 collective-permute-done.18.refs_1_.refs_7_
  562.9 5.5 collective-permute-done.19.refs_2_.refs_8_
  568.3 17.0 %pack_lam.3 = (f32[2,8,32,128]{3,2,1,0:T(8,128)}, f32[2,8,32,128]{3,2,1,0:T(8,128)}) custom-call(f32[2,16,16,128]{3,2,1,0:T(8,128)} %copy-done.61, f32[2,16,8,128]{3,2,1,0:T(8,128)} %collective-permute-done.18.refs_1_.refs_7_, f32[2,16,8,128]{3,2,1,0:T(8,128)} %collective-permute-done.19.refs_2_.refs_8_), custom_call_target="tpu_custom_call" | custom-call | tf_op jit(solution)/shard_map/pack_lam/pallas_call | solution.py:51
  585.4 2.2 collective-permute-start.20
  587.6 1.3 collective-permute-start.21
  589.9 1.7 copy-done.10
  598.6 1.0 copy-done.44
  599.6 1.0 copy-done.46
  600.7 1.2 copy-done.60
  601.9 4.9 prepare.3.refs_3_
  606.9 2.3 copy-done.33
  609.3 13.0 %step.3 = (f32[16,16,128]{2,1,0:T(8,128)}, f32[16,16,128]{2,1,0:T(8,128)}, f32[32,128]{1,0:T(8,128)S(1)}) custom-call(s32[20]{0:T(128)S(1)} %copy-done.77, f32[32,4,128]{2,1,0:T(4,128)S(1)} %copy-done.50, f32[128,4]{1,0:T(8,128)S(1)} %bitcast.32, f32[9,32,4,8,128]{4,3,2,1,0:T(8,128)S(1)} %copy-done.33, f32[5,32,4,8,128]{4,3,2,1,0:T(8,128)S(1)} %copy-done.11, ...), custom_call_target="tpu_custom_call" | custom-call | tf_op jit(solution)/shard_map/step/pallas_call | solution.py:546
  622.3 14.7 %all_to_all.10 = f32[32,1,128]{2,1,0:T(1,128)S(1)} all-to-all(f32[32,1,128]{2,1,0:T(1,128)S(1)} %bitcast.33), channel_id=1, replica_groups=mesh['gx'=8,'gy'=4] {'gx','gy'}, dimensions={0} | all-to-all | bytes 32768 | tf_op jit(solution)/shard_map/all_to_all | solution.py:564
  (175 shorter events, 36.9 us)
Async XLA Ops:
  45.6 20.6 %collective-permute-start = (f32[11,16,8,128]{3,2,1,0:T(8,128)}, f32[11,16,8,128]{3,2,1,0:T(8,128)S(1)}, u32[]{:S(2)}, u32[]{:S(2)}) collective-permute-start(f32[11,16,8,128]{3,2,1,0:T(8,128)} %get-tuple-element.35), channel_id=1, source_target_pairs={{0,1},{1,2},{2,3},{4,5},{5,6},{6,7},{8,9},{9,10},{10,11},{12,13},{... | collective-permute-start | bytes 2162696 | tf_op jit(solution)/shard_map/ppermute | solution.py:35
  50.6 19.7 %collective-permute-start.1 = (f32[11,16,8,128]{3,2,1,0:T(8,128)}, f32[11,16,8,128]{3,2,1,0:T(8,128)S(1)}, u32[]{:S(2)}, u32[]{:S(2)}) collective-permute-start(f32[11,16,8,128]{3,2,1,0:T(8,128)} %get-tuple-element.36), channel_id=1, source_target_pairs={{1,0},{2,1},{3,2},{5,4},{6,5},{7,6},{9,8},{10,9},{11,10},{13,12},{... | collective-permute-start | bytes 2162696 | tf_op jit(solution)/shard_map/ppermute | solution.py:35
  66.2 4.1 copy-start.34
  112.2 51.1 %collective-permute-start.6 = (f32[10,16,8,128]{3,2,1,0:T(8,128)}, f32[10,16,8,128]{3,2,1,0:T(8,128)S(1)}, u32[]{:S(2)}, u32[]{:S(2)}) collective-permute-start(f32[10,16,8,128]{3,2,1,0:T(8,128)} %get-tuple-element.42), channel_id=1, source_target_pairs={{0,1},{1,2},{2,3},{4,5},{5,6},{6,7},{8,9},{9,10},{10,11},{12,13},{... | collective-permute-start | bytes 1966088 | tf_op jit(solution)/shard_map/ppermute | solution.py:35
  115.7 47.7 %collective-permute-start.7 = (f32[10,16,8,128]{3,2,1,0:T(8,128)}, f32[10,16,8,128]{3,2,1,0:T(8,128)S(1)}, u32[]{:S(2)}, u32[]{:S(2)}) collective-permute-start(f32[10,16,8,128]{3,2,1,0:T(8,128)} %get-tuple-element.43), channel_id=1, source_target_pairs={{1,0},{2,1},{3,2},{5,4},{6,5},{7,6},{9,8},{10,9},{11,10},{13,12},{... | collective-permute-start | bytes 1966088 | tf_op jit(solution)/shard_map/ppermute | solution.py:35
  161.9 174.0 %collective-permute-start.2 = (f32[11,8,16,128]{3,2,1,0:T(8,128)}, f32[11,8,16,128]{3,2,1,0:T(8,128)S(1)}, u32[]{:S(2)}, u32[]{:S(2)}) collective-permute-start(f32[11,8,16,128]{3,2,1,0:T(8,128)} %get-tuple-element.37), channel_id=1, source_target_pairs={{0,4},{4,8},{8,12},{12,16},{16,20},{20,24},{24,28},{1,5},{5,9},{9,... | collective-permute-start | bytes 2162696 | tf_op jit(solution)/shard_map/ppermute | solution.py:35
  198.0 141.9 %collective-permute-start.8 = (f32[8,16,8,128]{3,2,1,0:T(8,128)}, f32[8,16,8,128]{3,2,1,0:T(8,128)S(1)}, u32[]{:S(2)}, u32[]{:S(2)}) collective-permute-start(f32[8,16,8,128]{3,2,1,0:T(8,128)} %get-tuple-element.44), channel_id=1, source_target_pairs={{0,1},{1,2},{2,3},{4,5},{5,6},{6,7},{8,9},{9,10},{10,11},{12,13},{... | collective-permute-start | bytes 1572872 | tf_op jit(solution)/shard_map/ppermute | solution.py:35
  202.6 139.9 %copy-start.78 = (f32[2,3]{1,0:T(2,128)S(1)}, f32[2,3]{1,0:T(2,128)}, u32[]{:S(2)}) copy-start(f32[2,3]{1,0:T(2,128)} %param.32) | copy-start | bytes 76
  202.6 139.9 %copy-start.79 = (f32[2,3]{1,0:T(2,128)S(1)}, f32[2,3]{1,0:T(2,128)}, u32[]{:S(2)}) copy-start(f32[2,3]{1,0:T(2,128)} %param.33) | copy-start | bytes 76
  202.6 139.9 %copy-start.80 = (s32[2,3]{1,0:T(2,128)S(1)}, s32[2,3]{1,0:T(2,128)}, u32[]{:S(2)}) copy-start(s32[2,3]{1,0:T(2,128)} %param.34) | copy-start | bytes 76
  202.6 140.0 %copy-start.81 = (s32[128]{0:T(128)S(1)}, s32[128]{0:T(128)}, u32[]{:S(2)}) copy-start(s32[128]{0:T(128)} %param.35) | copy-start | bytes 1540
  202.6 140.0 %copy-start.82 = (s32[128]{0:T(128)S(1)}, s32[128]{0:T(128)}, u32[]{:S(2)}) copy-start(s32[128]{0:T(128)} %param.36) | copy-start | bytes 1540
  202.7 138.5 %collective-permute-start.9 = (f32[8,16,8,128]{3,2,1,0:T(8,128)}, f32[8,16,8,128]{3,2,1,0:T(8,128)S(1)}, u32[]{:S(2)}, u32[]{:S(2)}) collective-permute-start(f32[8,16,8,128]{3,2,1,0:T(8,128)} %get-tuple-element.45), channel_id=1, source_target_pairs={{1,0},{2,1},{3,2},{5,4},{6,5},{7,6},{9,8},{10,9},{11,10},{13,12},{... | collective-permute-start | bytes 1572872 | tf_op jit(solution)/shard_map/ppermute | solution.py:35
  284.8 234.6 %collective-permute-start.12 = (f32[10,8,32,128]{3,2,1,0:T(8,128)}, f32[10,8,32,128]{3,2,1,0:T(8,128)}, u32[]{:S(2)}, u32[]{:S(2)}) collective-permute-start(f32[10,8,32,128]{3,2,1,0:T(8,128)} %get-tuple-element.48), channel_id=1, source_target_pairs={{0,4},{4,8},{8,12},{12,16},{16,20},{20,24},{24,28},{1,5},{5,9},{9,... | collective-permute-start | bytes 3932168 | tf_op jit(solution)/shard_map/ppermute | solution.py:35
  289.7 123.7 %copy-start.83 = (f32[128]{0:T(128)S(1)}, f32[128]{0:T(128)}, u32[]{:S(2)}) copy-start(f32[128]{0:T(128)} %param.37) | copy-start | bytes 1540
  289.7 117.8 %collective-permute-start.3 = (f32[11,8,16,128]{3,2,1,0:T(8,128)}, f32[11,8,16,128]{3,2,1,0:T(8,128)S(1)}, u32[]{:S(2)}, u32[]{:S(2)}) collective-permute-start(f32[11,8,16,128]{3,2,1,0:T(8,128)} %get-tuple-element.38), channel_id=1, source_target_pairs={{4,0},{8,4},{12,8},{16,12},{20,16},{24,20},{28,24},{5,1},{9,5},{13... | collective-permute-start | bytes 2162696 | tf_op jit(solution)/shard_map/ppermute | solution.py:35
  336.8 75.3 %collective-permute-start.4 = (f32[11,8,16,128]{3,2,1,0:T(8,128)}, f32[11,8,16,128]{3,2,1,0:T(8,128)S(1)}, u32[]{:S(2)}, u32[]{:S(2)}) collective-permute-start(f32[11,8,16,128]{3,2,1,0:T(8,128)} %get-tuple-element.39), channel_id=1, source_target_pairs={{0,4},{4,8},{8,12},{12,16},{16,20},{20,24},{24,28},{1,5},{5,9},{9,... | collective-permute-start | bytes 2162696 | tf_op jit(solution)/shard_map/ppermute | solution.py:35
  339.9 2.8 copy-start.43
  339.9 180.8 %collective-permute-start.13 = (f32[10,8,32,128]{3,2,1,0:T(8,128)}, f32[10,8,32,128]{3,2,1,0:T(8,128)}, u32[]{:S(2)}, u32[]{:S(2)}) collective-permute-start(f32[10,8,32,128]{3,2,1,0:T(8,128)} %get-tuple-element.49), channel_id=1, source_target_pairs={{4,0},{8,4},{12,8},{16,12},{20,16},{24,20},{28,24},{5,1},{9,5},{13... | collective-permute-start | bytes 3932168 | tf_op jit(solution)/shard_map/ppermute | solution.py:35
  341.2 1.5 copy-start.45
  341.2 107.4 %collective-permute-start.5 = (f32[11,8,16,128]{3,2,1,0:T(8,128)}, f32[11,8,16,128]{3,2,1,0:T(8,128)S(1)}, u32[]{:S(2)}, u32[]{:S(2)}) collective-permute-start(f32[11,8,16,128]{3,2,1,0:T(8,128)} %get-tuple-element.40), channel_id=1, source_target_pairs={{4,0},{8,4},{12,8},{16,12},{20,16},{24,20},{28,24},{5,1},{9,5},{13... | collective-permute-start | bytes 2162696 | tf_op jit(solution)/shard_map/ppermute | solution.py:35
  407.5 41.1 %copy-start.67 = (f32[11,8,16,128]{3,2,1,0:T(8,128)}, f32[11,8,16,128]{3,2,1,0:T(8,128)S(1)}, u32[]{:S(2)}) copy-start(f32[11,8,16,128]{3,2,1,0:T(8,128)S(1)} %collective-permute-done.3.refs_18_) | copy-start | bytes 2162692
  407.5 181.4 %collective-permute-start.10 = (f32[8,8,32,128]{3,2,1,0:T(8,128)}, f32[8,8,32,128]{3,2,1,0:T(8,128)}, u32[]{:S(2)}, u32[]{:S(2)}) collective-permute-start(f32[8,8,32,128]{3,2,1,0:T(8,128)} %get-tuple-element.46), channel_id=1, source_target_pairs={{0,4},{4,8},{8,12},{12,16},{16,20},{20,24},{24,28},{1,5},{5,9},{9,... | collective-permute-start | bytes 3145736 | tf_op jit(solution)/shard_map/ppermute | solution.py:35
  412.1 36.5 %copy-start.69 = (f32[11,8,16,128]{3,2,1,0:T(8,128)}, f32[11,8,16,128]{3,2,1,0:T(8,128)S(1)}, u32[]{:S(2)}) copy-start(f32[11,8,16,128]{3,2,1,0:T(8,128)S(1)} %collective-permute-done.4.refs_19_) | copy-start | bytes 2162692
  412.1 176.7 %collective-permute-start.11 = (f32[8,8,32,128]{3,2,1,0:T(8,128)}, f32[8,8,32,128]{3,2,1,0:T(8,128)}, u32[]{:S(2)}, u32[]{:S(2)}) collective-permute-start(f32[8,8,32,128]{3,2,1,0:T(8,128)} %get-tuple-element.47), channel_id=1, source_target_pairs={{4,0},{8,4},{12,8},{16,12},{20,16},{24,20},{28,24},{5,1},{9,5},{13... | collective-permute-start | bytes 3145736 | tf_op jit(solution)/shard_map/ppermute | solution.py:35
  414.1 26.1 %all-to-all-start = ((f32[32,4,128]{2,1,0:T(4,128)}), f32[32,4,128]{2,1,0:T(4,128)S(1)}, u32[]{:S(2)}, u32[]{:S(2)}) async-start(f32[32,4,128]{2,1,0:T(4,128)} %broadcast_in_dim.21), calls=%async_computation | async-start | bytes 131072 | tf_op jit(solution)/shard_map/all_to_all | solution.py:468
  424.0 59.3 %copy-start.75 = (s32[20]{0:T(128)}, s32[20]{0:T(128)S(1)}, u32[]{:S(2)}) copy-start(s32[20]{0:T(128)S(1)} %stack.119.ids_ref.refs_0_) | copy-start | bytes 244
  440.2 8.4 %copy-start.47 = (f32[32,4,128]{2,1,0:T(4,128)}, f32[32,4,128]{2,1,0:T(4,128)S(1)}, u32[]{:S(2)}) copy-start(f32[32,4,128]{2,1,0:T(4,128)S(1)} %all-to-all-done.table_ref.refs_1_) | copy-start | bytes 196612
  440.2 9.3 %copy-start.56 = (f32[4,128]{0,1:T(8,128)S(1)}, f32[4,128]{0,1:T(8,128)}, u32[]{:S(2)}) copy-start(f32[4,128]{0,1:T(8,128)} %copy.27) | copy-start | bytes 6148
  446.8 1.8 copy-start
  457.5 1.1 copy-start.35
  458.6 1.1 copy-start.37
  463.2 1.1 copy-start.66
  464.3 1.1 copy-start.68
  465.5 1.1 copy-start.70
  467.7 53.0 %copy-start.1 = (f32[3,48,48,128]{3,2,1,0:T(8,128)S(1)}, f32[3,48,48,128]{3,2,1,0:T(8,128)}, u32[]{:S(2)}) copy-start(f32[3,48,48,128]{3,2,1,0:T(8,128)} %copy-done) | copy-start | bytes 10616836
  483.3 1.6 copy-start.7
  486.1 7.4 %collective-permute-start.14 = (f32[2,16,8,128]{3,2,1,0:T(8,128)S(1)}, f32[2,16,8,128]{3,2,1,0:T(8,128)}, u32[]{:S(2)}, u32[]{:S(2)}) collective-permute-start(f32[2,16,8,128]{3,2,1,0:T(8,128)S(1)} %get-tuple-element.53), channel_id=1, source_target_pairs={{0,1},{1,2},{2,3},{4,5},{5,6},{6,7},{8,9},{9,10},{10,11},{12,13},{... | collective-permute-start | bytes 393224 | tf_op jit(solution)/shard_map/ppermute | solution.py:35
  493.5 7.5 %collective-permute-start.15 = (f32[2,16,8,128]{3,2,1,0:T(8,128)S(1)}, f32[2,16,8,128]{3,2,1,0:T(8,128)}, u32[]{:S(2)}, u32[]{:S(2)}) collective-permute-start(f32[2,16,8,128]{3,2,1,0:T(8,128)S(1)} %get-tuple-element.54), channel_id=1, source_target_pairs={{1,0},{2,1},{3,2},{5,4},{6,5},{7,6},{9,8},{10,9},{11,10},{13,12},{... | collective-permute-start | bytes 393224 | tf_op jit(solution)/shard_map/ppermute | solution.py:35
  518.1 21.6 %collective-permute-start.16 = (f32[2,8,32,128]{3,2,1,0:T(8,128)}, f32[2,8,32,128]{3,2,1,0:T(8,128)S(1)}, u32[]{:S(2)}, u32[]{:S(2)}) collective-permute-start(f32[2,8,32,128]{3,2,1,0:T(8,128)} %get-tuple-element.55), channel_id=1, source_target_pairs={{0,4},{4,8},{8,12},{12,16},{16,20},{20,24},{24,28},{1,5},{5,9},{9,... | collective-permute-start | bytes 786440 | tf_op jit(solution)/shard_map/ppermute | solution.py:35
  519.4 20.3 %collective-permute-start.17 = (f32[2,8,32,128]{3,2,1,0:T(8,128)}, f32[2,8,32,128]{3,2,1,0:T(8,128)S(1)}, u32[]{:S(2)}, u32[]{:S(2)}) collective-permute-start(f32[2,8,32,128]{3,2,1,0:T(8,128)} %get-tuple-element.56), channel_id=1, source_target_pairs={{4,0},{8,4},{12,8},{16,12},{20,16},{24,20},{28,24},{5,1},{9,5},{13... | collective-permute-start | bytes 786440 | tf_op jit(solution)/shard_map/ppermute | solution.py:35
  521.7 1.7 copy-start.8
  534.4 5.3 copy-start.4
  534.4 5.3 copy-start.9
  534.4 5.3 copy-start.49
  534.4 5.3 copy-start.57
  534.4 5.3 copy-start.64
  534.5 5.3 copy-start.74
  534.5 5.3 copy-start.76
  539.7 15.4 %copy-start.59 = (f32[2,32,32,128]{3,2,1,0:T(8,128)}, f32[2,32,32,128]{3,2,1,0:T(8,128)S(1)}, u32[]{:S(2)}) copy-start(f32[2,32,32,128]{3,2,1,0:T(8,128)S(1)} %get-tuple-element.50.refs_14_) | copy-start | bytes 3145732
  539.8 2.7 copy-start.42
  555.8 7.0 %collective-permute-start.18 = (f32[2,16,8,128]{3,2,1,0:T(8,128)S(1)}, f32[2,16,8,128]{3,2,1,0:T(8,128)}, u32[]{:S(2)}, u32[]{:S(2)}) collective-permute-start(f32[2,16,8,128]{3,2,1,0:T(8,128)S(1)} %get-tuple-element.59), channel_id=1, source_target_pairs={{0,1},{1,2},{2,3},{4,5},{5,6},{6,7},{8,9},{9,10},{10,11},{12,13},{... | collective-permute-start | bytes 393224 | tf_op jit(solution)/shard_map/ppermute | solution.py:35
  560.4 7.9 %collective-permute-start.19 = (f32[2,16,8,128]{3,2,1,0:T(8,128)S(1)}, f32[2,16,8,128]{3,2,1,0:T(8,128)}, u32[]{:S(2)}, u32[]{:S(2)}) collective-permute-start(f32[2,16,8,128]{3,2,1,0:T(8,128)S(1)} %get-tuple-element.60), channel_id=1, source_target_pairs={{1,0},{2,1},{3,2},{5,4},{6,5},{7,6},{9,8},{10,9},{11,10},{13,12},{... | collective-permute-start | bytes 393224 | tf_op jit(solution)/shard_map/ppermute | solution.py:35
  585.4 21.5 %collective-permute-start.20 = (f32[2,8,32,128]{3,2,1,0:T(8,128)}, f32[2,8,32,128]{3,2,1,0:T(8,128)S(1)}, u32[]{:S(2)}, u32[]{:S(2)}) collective-permute-start(f32[2,8,32,128]{3,2,1,0:T(8,128)} %get-tuple-element.61), channel_id=1, source_target_pairs={{0,4},{4,8},{8,12},{12,16},{16,20},{20,24},{24,28},{1,5},{5,9},{9,... | collective-permute-start | bytes 786440 | tf_op jit(solution)/shard_map/ppermute | solution.py:35
  587.6 19.3 %collective-permute-start.21 = (f32[2,8,32,128]{3,2,1,0:T(8,128)}, f32[2,8,32,128]{3,2,1,0:T(8,128)S(1)}, u32[]{:S(2)}, u32[]{:S(2)}) collective-permute-start(f32[2,8,32,128]{3,2,1,0:T(8,128)} %get-tuple-element.62), channel_id=1, source_target_pairs={{4,0},{8,4},{12,8},{16,12},{20,16},{24,20},{28,24},{5,1},{9,5},{13... | collective-permute-start | bytes 786440 | tf_op jit(solution)/shard_map/ppermute | solution.py:35
  589.9 1.7 copy-start.10
  600.7 1.2 copy-start.60
  601.9 5.0 copy-start.6
  601.9 5.0 copy-start.11
  601.9 5.0 copy-start.50
  601.9 5.0 copy-start.58
  601.9 5.0 copy-start.62
  601.9 5.0 copy-start.77
  606.9 2.3 copy-start.33
  (43 other events, 40.9 us)

commit v3 on v2

v3 whole, which is shorter than its diff:
```python
import functools

import jax
import jax.numpy as jnp
from jax import lax
from jax.experimental import pallas as pl
from jax.experimental.pallas import tpu as pltpu
from jax.sharding import PartitionSpec as P

SWEEPS = 8
OMEGA = 0.8
KEEP = 1.0 - OMEGA
H = 8
V = 4
HIGHEST = lax.Precision.HIGHEST
F32 = jnp.float32
BF16 = jnp.bfloat16

VMEM = pl.BlockSpec(memory_space=pltpu.VMEM)
ANY = pl.BlockSpec(memory_space=pl.ANY)
HBM = pl.BlockSpec(memory_space=pltpu.HBM)


def sds(*shape):
    return jax.ShapeDtypeStruct(shape, F32)


def params(mib):
    return pltpu.CompilerParams(vmem_limit_bytes=mib * 1024 * 1024)


def call(kernel, ins, outs, name, mib, specs=None, scratch=()):
    return pl.pallas_call(
        kernel,
        in_specs=specs or [VMEM] * len(ins),
        out_specs=[VMEM] * len(outs),
        out_shape=outs,
        scratch_shapes=list(scratch),
        compiler_params=params(mib),
        name=name,
    )(*ins)


def shifted(value, axis, by):
    length = lax.axis_size(axis)
    pairs = [(i, i + by) for i in range(length) if 0 <= i + by < length]
    return lax.ppermute(value, axis, pairs)


def load_kernel(leads, split, *refs):
    count = len(leads)
    ins, (top, rest, y_low, y_high, x_low, x_high), sems = refs[:count], refs[count:-1], refs[-1]
    rx, ry = top.shape[1:3]
    copies = []
    for n, lead in enumerate(leads):
        to = top.at[n] if n < split else rest.at[n - split]
        copies.append(
            pltpu.make_async_copy(
                ins[n] if lead is None else ins[n].at[lead], to, sems.at[n]
            )
        )
    for c in copies:
        c.start()
    for c in copies[:split]:
        c.wait()
    edges_body(top, y_low, y_high, x_low, x_high)
    for c in copies[split:]:
        c.wait()


def edges_body(own, y_low, y_high, x_low, x_high):
    rx, ry = own.shape[1:3]

    def one(n, _):
        y_low[n] = own[n, :, 0:H, :]
        y_high[n] = own[n, :, ry - H :, :]
        x_low[n] = own[n, 0:H]
        x_high[n] = own[n, rx - H :]
        return 0

    lax.fori_loop(0, own.shape[0], one, 0)


def edge_shapes(n, dims):
    rx, ry, nz = dims
    return [sds(n, rx, H, nz)] * 2 + [sds(n, H, ry, nz)] * 2


def load(arrays, leads, split, dims):
    n = len(leads)
    return pl.pallas_call(
        functools.partial(load_kernel, leads, split),
        in_specs=[HBM] * n,
        out_specs=[VMEM] * 6,
        out_shape=[sds(split, *dims), sds(n - split, *dims)] + edge_shapes(split, dims),
        scratch_shapes=[pltpu.SemaphoreType.DMA((n,))],
        name="load",
    )(*arrays)


def edges_kernel(own, *refs):
    edges_body(own, *refs[-4:])


def fold(rows_of, high):
    tiles = []
    for dx in range(1, 5):
        near, far = rows_of(dx), rows_of(8 - dx)
        sub = lax.broadcasted_iota(jnp.int32, near.shape, 0)
        if high:
            tiles.append(jnp.where(sub < 8 - dx, near, pltpu.roll(far, 8 - dx, 0)))
        else:
            tiles.append(jnp.where(sub >= dx, near, pltpu.roll(far, dx, 0)))
    return tiles


def unfold(tile, dx, high):
    return tile, pltpu.roll(tile, dx if high else 8 - dx, 0)


def corner_tiles(n, z_low, z_high, put):
    rx = z_low.shape[1]
    for side in (0, 1):
        for high, z in ((False, z_low), (True, z_high)):

            def rows_of(dx):
                return z[n, dx - 1 if side == 0 else rx - dx]

            for t, tile in enumerate(fold(rows_of, high)):
                put(side, int(high), t, tile)


def corner_kernel(z_low, z_high, *refs):
    outs = refs[-2:]

    def one(n, _):
        def put(side, y, t, tile):
            outs[side][n, t, y * H : (y + 1) * H, :] = tile

        corner_tiles(n, z_low, z_high, put)
        return 0

    lax.fori_loop(0, z_low.shape[0], one, 0)


def pack_corners(name, z_low, z_high, after):
    count, _, _, nz = z_low.shape
    return call(
        corner_kernel, [z_low, z_high, *after], [sds(count, 4, 2 * H, nz)] * 2, name, 4,
        [VMEM] * 2 + [ANY] * len(after),
    )


def widen_kernel(own, z_low, z_high, *outs):
    rx = own.shape[1]

    def one(n, _):
        def put(side, y, t, tile):
            outs[side][n, H + t, y * H : (y + 1) * H, :] = tile

        corner_tiles(n, z_low, z_high, put)
        outs[0][n, 0:H] = own[n, 0:H]
        outs[1][n, 0:H] = own[n, rx - H :]
        return 0

    lax.fori_loop(0, own.shape[0], one, 0)


def widen(own, z_low, z_high):
    count, rx, ry, nz = own.shape
    return call(widen_kernel, [own, z_low, z_high], [sds(count, H + 4, ry, nz)] * 2, "widen", 4)


def table_kernel(steps, rate, bhp, control, perf_well, perf_cell, perf_wi, _, out):
    wells = rate.shape[0]
    effective = jnp.where(control[...] == 1, rate[...], bhp[...])
    lane = lax.broadcasted_iota(jnp.int32, (1, 128), 1)
    row = jnp.zeros((1, 128), F32)
    for u in range(wells):
        for n in range(steps):
            row = jnp.where(lane == u * steps + n, effective[u : u + 1, n : n + 1], row)
    mine = jnp.concatenate(
        [row, perf_cell[...].astype(F32), perf_well[...].astype(F32), perf_wi[...]]
    )
    out[...] = jnp.broadcast_to(mine[None], out.shape)


def spot():
    n_x, n_y = lax.axis_size("gx"), lax.axis_size("gy")
    x, y = lax.axis_index("gx"), lax.axis_index("gy")
    return x, y, n_x, n_y


def source_kernel(steps, wells, ry, table_ref, src_ref):
    here_x, here_y, n_x, n_y = spot()
    count = table_ref.shape[0]
    rx = src_ref.shape[1] // 3
    of_wells = table_ref[:, 0, :]
    owner_iota = lax.broadcasted_iota(jnp.int32, (count, 128), 0)
    sub = lax.broadcasted_iota(jnp.int32, (128, 128), 0)
    row_iota = lax.broadcasted_iota(jnp.int32, (rx * ry, 128), 0)

    def block(k, _):
        dx = k // 3
        dy = k - 3 * dx
        at_x, at_y = here_x + dx - 1, here_y + dy - 1
        inside = (at_x >= 0) & (at_x < n_x) & (at_y >= 0) & (at_y < n_y)
        slot = table_ref[jnp.where(inside, at_x * n_y + at_y, 0)]
        cell = slot[1:2, :].astype(jnp.int32)
        well = slot[2:3, :].astype(jnp.int32)
        wi = slot[3:4, :] * inside.astype(F32)
        owner = well // wells
        within = well - owner * wells
        hot = jnp.where(owner_iota == owner, 1.0, 0.0).astype(F32)
        found = lax.dot_general(
            of_wells, hot, (((0,), (0,)), ((), ())), precision=HIGHEST,
            preferred_element_type=F32,
        )
        by_row = jnp.where(row_iota == (cell >> 7), 1.0, 0.0).astype(BF16)
        in_lane = sub == (cell & 127)
        for step in range(steps):
            value = jnp.zeros((1, 128), F32)
            for u in range(wells):
                c = u * steps + step
                value = value + jnp.where(within == u, found[c : c + 1, :], 0.0)
            value = value * wi
            part = None
            for _ in range(3):
                piece = value.astype(BF16)
                value = value - piece.astype(F32)
                by_lane = jnp.where(in_lane, piece.astype(F32), 0.0).astype(BF16)
                add = lax.dot_general(
                    by_row, by_lane, (((1,), (1,)), ((), ())), preferred_element_type=F32
                )
                part = add if part is None else part + add
            src_ref[
                step, pl.ds(pl.multiple_of(dx * rx, rx), rx),
                pl.ds(pl.multiple_of(dy * ry, ry), ry), :,
            ] = part.reshape(rx, ry, 128)
        return 0

    lax.fori_loop(0, 9, block, 0)


def by_v(ref, lead, x, offset=0):
    return jnp.stack(
        [ref[(*lead, x, pl.ds(offset + v, 8, stride=V), slice(None))] for v in range(V)]
    )


def up_v(value):
    return jnp.concatenate([value[1:], pltpu.roll(value[0], 7, 0)[None]])


def down_v(value):
    return jnp.concatenate([pltpu.roll(value[V - 1], 1, 0)[None], value[:-1]])


def roll_z(value, by):
    return pltpu.roll(value, by, 2)


def fill(dst, own, z_low, z_high, x_edges, corners, base, first=0):
    count, (rx, ry, nz) = dst.shape[0], own.shape[1:]

    def one(n, _):
        m = n + first
        dst[n, H : H + rx, 0:H, :] = z_low[m]
        dst[n, H : H + rx, H : H + ry, :] = own[m]
        dst[n, H : H + rx, H + ry : 2 * H + ry, :] = z_high[m]
        for side in (0, 1):
            at = side * (H + rx)
            dst[n, at : at + H, H : H + ry, :] = x_edges[side][m, 0:H]
            for y in (0, 1):
                to = y * (H + ry)
                for t in range(4):
                    tile = corners[side][m, base + t, y * H : (y + 1) * H, :]
                    near, far = unfold(tile, t + 1, y == 1)
                    for dx, row in ((t + 1, near), (7 - t, far)):
                        x = H - dx if side == 0 else H + rx + dx - 1
                        dst[n, x, to : to + H, :] = row
                x = 0 if side == 0 else 2 * H + rx - 1
                dst[n, x, to : to + H, :] = jnp.zeros((H, nz), F32)
        return 0

    lax.fori_loop(0, count, one, 0)


SA, RA, PC, FR, RB, QC, MC, AA, AB = range(9)
TX, TY, TZ, TU, WS = range(5)


def coefficients(raw, base, src_ref, step, x, total, src_x, src_y):
    c_pp, c_ss, c_ps, c_sp, frac, mob, g_p, g_s = [by_v(raw, (base + n,), x) for n in range(8)]
    den_a = c_pp + total
    den_b = c_ss + mob * total
    s_a = jnp.where(den_a > 0, OMEGA / den_a, 0.0)
    s_b = jnp.where(den_b > 0, OMEGA / den_b, 0.0)
    r_a = g_p + by_v(src_ref, (step,), x + src_x, src_y)
    return s_a, r_a, c_sp + frac * total, frac, s_b * g_s, s_b * c_ps, s_b * mob, s_b


BLOCK = 2
UNROLL = 4


def sweeps(coef, geo, bufs, lin, begin, ex):
    def work(number, x, count):
        old, new = bufs[(number - 1) % 2], bufs[number % 2]
        tx = [geo[TX, x + r] for r in range(count + 1)]
        values = [[old[f][x - 1 + r] for r in range(count + 2)] for f in range(2)]
        results = []
        for r in range(count):
            at = x + r
            ty = geo[TY, at]
            ty_up = up_v(ty)
            tz, tz_up = geo[TZ, at], geo[TU, at]

            def around(v):
                c = v[r + 1]
                total = tx[r + 1] * v[r + 2] + tx[r] * v[r]
                total = total + (ty_up * up_v(c) + ty * down_v(c))
                total = total + (tz_up * roll_z(c, 127) + tz * roll_z(c, 1))
                return c, total

            a, n_a = around(values[0])
            b, n_b = around(values[1])
            new_a = KEEP * a + coef[SA, at] * (
                (coef[RA, at] + n_a) + (coef[FR, at] * n_b - coef[PC, at] * b)
            )
            new_b = (KEEP * b + coef[RB, at]) + (coef[MC, at] * n_b - coef[QC, at] * a)
            results.append((new_a, new_b))
        for r in range(count):
            for f in range(2):
                if number == SWEEPS:
                    for v in range(V):
                        lin[f, x + r, pl.ds(v, 8, stride=V), :] = results[r][f][v]
                else:
                    new[f][x + r] = results[r][f]

    for number in range(begin, SWEEPS + 1):
        size = BLOCK * UNROLL
        total = ex - 2 * number

        def many(i, _):
            for u in range(UNROLL):
                work(number, number + i * size + u * BLOCK, BLOCK)
            return 0

        lax.fori_loop(0, total // size, many, 0)
        for at in range(total - total % size, total, BLOCK):
            work(number, number + at, BLOCK)


def finish(last, step, steps, wells, lin, frac, table_ref, before, outs):
    rx, ry, nz = frac.shape[-3:]
    out_wells = outs[-1]

    def copy(x, _):
        for f in range(2):
            row = lin[f, H + x, H : H + ry, :]
            if last:
                outs[f][x] = row
            else:
                outs[0][f, x] = row
                outs[1][f, x] = row[0:H]
                outs[2][f, x] = row[ry - H :]
        return 0

    lax.fori_loop(0, rx, copy, 0, unroll=2)
    mix = lin[0, H : H + rx, H : H + ry, :] + frac[...] * lin[1, H : H + rx, H : H + ry, :]
    mix = mix.reshape(rx * ry, nz)
    here_x, here_y, _, n_y = spot()
    slot = table_ref[here_x * n_y + here_y]
    lane = lax.broadcasted_iota(jnp.int32, (128, 128), 1)
    diagonal = lax.broadcasted_iota(jnp.int32, (128, 128), 0) == lane

    def upright(row):
        return jnp.sum(jnp.where(diagonal, row, 0.0), axis=1, keepdims=True)

    cell = upright(slot[1:2, :]).astype(jnp.int32)
    well = upright(slot[2:3, :]).astype(jnp.int32)
    wi = upright(slot[3:4, :])
    by_row = jnp.where(
        lax.broadcasted_iota(jnp.int32, (128, rx * ry), 1) == (cell >> 7), 1.0, 0.0
    ).astype(BF16)
    picked = None
    for _ in range(3):
        piece = mix.astype(BF16)
        mix = mix - piece.astype(F32)
        add = jnp.dot(by_row, piece, preferred_element_type=F32)
        picked = add if picked is None else picked + add
    values = jnp.sum(jnp.where(lane == (cell & 127), picked, 0.0), axis=1, keepdims=True)
    values = values * wi
    owner = well // wells
    spread = jnp.where(lane == (well - owner * wells) * steps + step, values, 0.0)
    flat = slot[2:3, :].astype(jnp.int32) // wells
    count = table_ref.shape[0]
    hot = jnp.where(
        lax.broadcasted_iota(jnp.int32, (count, 128), 0) == flat, 1.0, 0.0
    ).astype(F32)
    dense = jnp.dot(hot, spread, precision=HIGHEST, preferred_element_type=F32)
    if before is not None:
        dense = dense + before[...]
    out_wells[...] = dense


def first_kernel(step, steps, wells, *refs):
    table_ref, src_ref, own, z_low, z_high, x_low, x_high, c_low, c_high = refs[:9]
    geo = refs[9]
    outs = refs[10:14]
    raw, coef, fa0, fb0, fa1, fb1, lin = refs[14:]
    rx, ry, nz = own.shape[1:]
    ex = rx + 2 * H
    fill(raw, own, z_low, z_high, (x_low, x_high), (c_low, c_high), 0)
    here_x, here_y, _, _ = spot()

    @pl.when(here_x == 0)
    def _():
        raw[0, H, :, :] = jnp.zeros(raw.shape[2:], F32)

    @pl.when(here_y == 0)
    def _():
        def clear(x, _):
            raw[1, x, H : H + 1, :] = jnp.zeros((1, nz), F32)
            return 0

        lax.fori_loop(0, ex, clear, 0)

    def geometry(x, _):
        lane = lax.broadcasted_iota(jnp.int32, (V, 8, nz), 2)
        tz = jnp.where(lane == 0, 0.0, by_v(raw, (2,), x))
        geo[TX, x] = by_v(raw, (0,), x)
        geo[TY, x] = by_v(raw, (1,), x)
        geo[TZ, x] = tz
        geo[TU, x] = roll_z(tz, 127)
        return 0

    lax.fori_loop(0, ex, geometry, 0, unroll=4)

    def prepare(x, _):
        ty = geo[TY, x]
        total = (
            (geo[TX, x + 1] + geo[TX, x]) + (up_v(ty) + ty) + (geo[TU, x] + geo[TZ, x])
        )
        geo[WS, x] = total
        s_a, r_a, p, frac, r_b, q, m, _ = coefficients(
            raw, 3, src_ref, step, x, total, rx - H, ry - H
        )
        coef[SA, x] = s_a
        coef[RA, x] = r_a
        coef[PC, x] = p
        coef[FR, x] = frac
        coef[RB, x] = r_b
        coef[QC, x] = q
        coef[MC, x] = m
        fa1[x] = s_a * r_a
        fb1[x] = r_b
        return 0

    lax.fori_loop(0, ex - 1, prepare, 0)
    sweeps(coef, geo, ((fa0, fb0), (fa1, fb1)), lin, 2, ex)
    finish(False, step, steps, wells, lin, own.at[7], table_ref, None, outs)


def prepare_kernel(step, first, with_acc, *refs):
    src_ref, geo, own, z_low, z_high, x_low, x_high, c_low, c_high = refs[:9]
    if with_acc:
        coef, acc_out, raw = refs[9:]
    else:
        acc, coef, raw = refs[9:]
    rx, ry, nz = own.shape[1:]
    ex = rx + 2 * H
    fill(raw, own, z_low, z_high, (x_low, x_high), (c_low, c_high), 0, first)

    def prepare(x, _):
        s_a, r_a, p, frac, r_b, q, m, s_b = coefficients(
            raw, 0, src_ref, step, x, geo[WS, x], rx - H, ry - H
        )
        coef[SA, x] = s_a
        coef[RA, x] = r_a
        coef[PC, x] = p
        coef[FR, x] = frac
        coef[RB, x] = r_b
        coef[QC, x] = q
        coef[MC, x] = m
        if with_acc:
            a, b = by_v(raw, (8,), x), by_v(raw, (9,), x)
            acc_out[0, x] = a
            acc_out[1, x] = b
        else:
            a, b = acc[0, x], acc[1, x]
        coef[AA, x] = a
        coef[AB, x] = s_b * b
        return 0

    lax.fori_loop(0, ex - 1, prepare, 0)


def sweep_kernel(last, step, frac_at, steps, wells, *refs):
    table_ref, coef, geo, own, lam, z_low, z_high, x_low, x_high, before = refs[:10]
    outs = refs[10:-6]
    now, fa0, fb0, fa1, fb1, lin = refs[-6:]
    rx, ry, nz = own.shape[1:]
    ex = rx + 2 * H
    fill(lin, lam, z_low, z_high, (x_low, x_high), (x_low, x_high), H)

    def begin(x, _):
        a, b = by_v(lin, (0,), x), by_v(lin, (1,), x)
        fa0[x] = a
        fb0[x] = b
        now[0, x] = coef[RA, x] + coef[AA, x] * a
        now[1, x] = coef[RB, x] + coef[AB, x] * b
        return 0

    lax.fori_loop(0, ex, begin, 0, unroll=4)

    class Joined:
        def __getitem__(self, at):
            n, x = at
            return now[0, x] if n == RA else now[1, x] if n == RB else coef[n, x]

    sweeps(Joined(), geo, ((fa0, fb0), (fa1, fb1)), lin, 1, ex)
    finish(last, step, steps, wells, lin, own.at[frac_at], table_ref, before, outs)


def local(
    grad_p, grad_s, acc_p, acc_s, trans_x, trans_y, trans_z, c_pp, c_ss, c_ps, c_sp,
    frac, mobility, rate_mis, bhp_mis, control, perf_well, perf_cell, perf_wi,
):
    dims = rx, ry, nz = trans_x.shape
    ex, ey = rx + 2 * H, ry + 2 * H
    steps = grad_p.shape[0]
    wells = rate_mis.shape[0]
    devices = lax.axis_size("gx") * lax.axis_size("gy")
    own = [c_pp, c_ss, c_ps, c_sp, frac, mobility, grad_p, grad_s]
    top = steps - 1

    def sent(low, high, axis):
        return shifted(high, axis, 1), shifted(low, axis, -1)

    arrays = [trans_x, trans_y, trans_z] + own
    leads = [None] * 3 + [top] * 8
    split = len(arrays)
    places = {}
    for step in reversed(range(top)):
        places[step] = len(arrays) - split
        arrays += own
        leads += [step] * 8
        if step == top - 1:
            arrays += [acc_p, acc_s]
            leads += [None] * 2
    blocks, more, y_low, y_high, e_low, e_high = load(arrays, leads, split, dims)

    z_got = sent(y_low, y_high, "gy")
    x_got = sent(e_low, e_high, "gx")

    mine = call(
        functools.partial(table_kernel, steps),
        [rate_mis, bhp_mis, control] + [p[None] for p in (perf_well, perf_cell, perf_wi)]
        + [y_low], [sds(devices, 4, 128)], "table", 4, [VMEM] * 6 + [ANY],
    )[0]
    table = lax.all_to_all(mine, ("gx", "gy"), 0, 0, tiled=True)
    src = call(
        functools.partial(source_kernel, steps, wells, ry), [table],
        [sds(steps, 3 * rx, 3 * ry, nz)], "sources", 8,
    )[0]

    corners = pack_corners("corners", *z_got, (*x_got, table))
    c_got = sent(*corners, "gx")

    edges = call(
        edges_kernel, [more, *corners, src], edge_shapes(len(arrays) - split, dims), "edges", 4,
        [VMEM] + [ANY] * 3,
    )
    m_z = sent(*edges[:2], "gy")
    m_x = sent(*edges[2:], "gx")

    ext = (ex, V, 8, nz)
    lam_out = [sds(2, rx, ry, nz), sds(2, rx, H, nz), sds(2, rx, H, nz)]
    well_out = sds(devices, 128)
    fields = [pltpu.VMEM(ext, F32)] * 4 + [pltpu.VMEM((2, ex, ey, nz), F32)]

    geo, lam, low, high, dense = call(
        functools.partial(first_kernel, top, steps, wells),
        [table, src, blocks, *z_got, *x_got, *c_got],
        [sds(5, *ext)] + lam_out + [well_out], "step_top", 16,
        scratch=[pltpu.VMEM((split, ex, ey, nz), F32), pltpu.VMEM((7, *ext), F32)] + fields,
    )

    m_c = sent(*pack_corners("corners_more", *m_z, (low,)), "gx")

    acc = None
    for step in reversed(range(top)):
        last = step == 0
        with_acc = step == top - 1
        at = places[step]
        made = call(
            functools.partial(prepare_kernel, step, at, with_acc),
            [src, geo, more, *m_z, *m_x, *m_c] + ([] if with_acc else [acc]),
            [sds(9, *ext)] + ([sds(2, *ext)] if with_acc else []), "prepare", 8,
            scratch=[pltpu.VMEM((10 if with_acc else 8, ex, ey, nz), F32)],
        )
        coef = made[0]
        if with_acc:
            acc = made[1]

        l_z = sent(low, high, "gy")
        l_x = sent(*widen(lam, *l_z), "gx")
        outs = [sds(rx, ry, nz)] * 2 if last else lam_out
        outs = call(
            functools.partial(sweep_kernel, last, step, at + 4, steps, wells),
            [table, coef, geo, more, lam, *l_z, *l_x, dense],
            outs + [well_out], "step", 8, scratch=[pltpu.VMEM((2, *ext), F32)] + fields,
        )
        dense = outs[-1]
        if not last:
            lam, low, high = outs[:3]

    parts = lax.all_to_all(dense[:, None, :], ("gx", "gy"), 0, 0, tiled=True)
    well_grad = jnp.sum(parts, axis=(0, 1))[: wells * steps].reshape(wells, steps)
    return outs[0], outs[1], well_grad


def solution(mesh):
    cells3 = P("gx", "gy", None)
    cells4 = P(None, "gx", "gy", None)
    flat = ("gx", "gy")
    placed = (cells4,) * 2 + (cells3,) * 5 + (cells4,) * 6 + (P(flat, None),) * 3 + (P(flat),) * 3
    return jax.shard_map(
        local,
        mesh=mesh,
        in_specs=placed,
        out_specs=(cells3, cells3, P(flat, None)),
        check_vma=False,
    )
```

time: 640 us -> 175 us (0.27)
  Pallas kernels: 446 us -> 33.5 us
  local copies, waits for them, and re-layouts: 61.7 us -> 3.27 us
  blocking collectives: 14.7 us -> 38.7 us
  waiting for transfers between devices: 49.9 us -> 39.5 us
    pallas_call x15 -> x13, Pallas kernels: 446 us -> 33.5 us  [the longest x12 28.3 us: call(): pl.pallas_call(kernel, in_specs=specs or [VMEM] * len(ins), out_specs=[VM...]
    unnamed x168 -> x18, local copies, waits for them, and re-layouts: 59.5 us -> 2.63 us
    all_to_all x0 -> x1, blocking collectives: none -> 24.2 us  [local(): table = lax.all_to_all(mine, ('gx', 'gy'), 0, 0, tiled=True)]
    all_to_all x1 -> x0, waiting for transfers between devices: 16.2 us -> none  [local(): lax.all_to_all(jnp.broadcast_to(mine[None], (devices, 4, 128)), ('gx', 'g...]
    all_to_all x1 -> x0, starting transfers between devices: 9.01 us -> none  [local(): lax.all_to_all(jnp.broadcast_to(mine[None], (devices, 4, 128)), ('gx', 'g...]
    ppermute x22 -> x20, waiting for transfers between devices: 33.7 us -> 39.5 us  [shifted(): return lax.ppermute(value, axis, pairs)]
    ppermute x22 -> x20, starting transfers between devices: 54.4 us -> 58.2 us  [shifted(): return lax.ppermute(value, axis, pairs)]
  transfers between devices with their start and end apart: 23 -> 20, of which waited for: 7 -> 7; matrix products, arithmetic and copies ran while one was open for 0% -> 0% of each run, Pallas kernels for 54% -> 9%
where the time goes in v3:
time: 175 us; the launch traced here: 174 us
  starting transfers between devices  58.2 us (33%)
  waiting for transfers between devices  39.5 us (23%)
  blocking collectives  38.7 us (22%)
  Pallas kernels  33.5 us (19%)
  local copies, waits for them, and re-layouts  3.27 us (2%)
    ppermute x20, starting transfers between devices, shifted(): return lax.ppermute(value, axis, pairs)  58.2 us
    ppermute x20, waiting for transfers between devices, shifted(): return lax.ppermute(value, axis, pairs)  39.5 us
    pallas_call x12, Pallas kernels, call(): pl.pallas_call(kernel, in_specs=specs or [VMEM] * len(ins), out_specs=[VM...  28.3 us
    all_to_all x1, blocking collectives, local(): table = lax.all_to_all(mine, ('gx', 'gy'), 0, 0, tiled=True)  24.2 us
    all_to_all x1, blocking collectives, local(): parts = lax.all_to_all(dense[:, None, :], ('gx', 'gy'), 0, 0, tiled=True)  14.5 us
    pallas_call x1, Pallas kernels, load(): pl.pallas_call(functools.partial(load_kernel, leads, split), in_specs=[HB...  5.2 us
  transfers between devices with their start and end apart: 20, of which 7 were waited for; matrix products, arithmetic and copies ran while one was open for 0% of the time, Pallas kernels for 9%

profile of v3, /device:TPU:0, one launch (start us, length us, event | category | flops | bytes accessed | tf_op | source)
XLA Modules:
  0.0 174.4 jit_solution(17316484021076288854)
XLA Ops:
  0.6 0.0 copy-start.8
  0.6 0.0 copy-start.7
  0.7 0.0 copy-start.6
  0.7 0.0 copy-start.5
  0.7 0.0 copy-start.4
  0.7 0.0 copy-start.3
  0.7 5.2 %load.1 = (f32[11,16,16,128]{3,2,1,0:T(8,128)}, f32[18,16,16,128]{3,2,1,0:T(8,128)}, f32[11,16,8,128]{3,2,1,0:T(8,128)}, f32[11,16,8,128]{3,2,1,0:T(8,128)}, f32...) custom-call(f32[16,16,128]{2,1,0:T(8,128)} %refs_0_.1, f32[16,16,128]{2,1,0:T(8,128)} %refs_1_.1, ...), custom_call_target="tpu_custom_call" | custom-call | tf_op jit(solution)/shard_map/load/pallas_call | solution.py:91
  5.9 5.0 %collective-permute-start = (f32[11,16,8,128]{3,2,1,0:T(8,128)}, f32[11,16,8,128]{3,2,1,0:T(8,128)S(1)}, u32[]{:S(2)}, u32[]{:S(2)}) collective-permute-start(f32[11,16,8,128]{3,2,1,0:T(8,128)} %get-tuple-element.37), channel_id=1, source_target_pairs={{0,1},{1,2},{2,3},{4,5},{5,6},{6,7},{8,9},{9,10},{10,11},{12,13},{... | collective-permute-start | bytes 2162696 | tf_op jit(solution)/shard_map/ppermute | solution.py:47
  10.9 1.5 collective-permute-start.2
  12.4 1.3 collective-permute-start.3
  13.7 1.3 collective-permute-start.1
  15.1 1.1 copy-done.2
  16.2 0.1 table.1
  16.3 24.2 %all_to_all.10.table_ref.refs_2_.refs_0_ = f32[32,4,128]{2,1,0:T(4,128)S(1)} all-to-all(f32[32,4,128]{2,1,0:T(4,128)S(1)} %table.1), channel_id=1, replica_groups=mesh['gx'=8,'gy'=4] {'gx','gy'}, dimensions={0} | all-to-all | bytes 131072 | tf_op jit(solution)/shard_map/all_to_all | solution.py:563
  40.4 6.0 %sources.1.refs_1_.refs_2_.refs_0_ = f32[3,48,48,128]{3,2,1,0:T(8,128)S(1)} custom-call(f32[32,4,128]{2,1,0:T(4,128)S(1)} %all_to_all.10.table_ref.refs_2_.refs_0_), custom_call_target="tpu_custom_call" | custom-call | tf_op jit(solution)/shard_map/sources/pallas_call | solution.py:33
  46.5 0.0 copy-start
  46.5 0.0 collective-permute-done.z_low.refs_3_
  46.5 0.0 collective-permute-done.2.refs_0_.refs_5_
  46.5 0.0 collective-permute-done.3.refs_1_.refs_6_
  46.5 0.0 collective-permute-done.1.z_high.refs_4_
  46.5 0.1 corners.1
  46.6 1.5 copy-done
  48.1 0.3 edges.1
  48.5 2.4 %collective-permute-start.6 = (f32[18,16,8,128]{3,2,1,0:T(8,128)S(1)}, f32[18,16,8,128]{3,2,1,0:T(8,128)S(1)}, u32[]{:S(2)}, u32[]{:S(2)}) collective-permute-start(f32[18,16,8,128]{3,2,1,0:T(8,128)S(1)} %get-tuple-element.44), channel_id=1, source_target_pairs={{0,1},{1,2},{2,3},{4,5},{5,6},{6,7},{8,9},{9,10},{10,11},{12,13},{... | collective-permute-start | bytes 3538952 | tf_op jit(solution)/shard_map/ppermute | solution.py:47
  50.8 1.3 collective-permute-start.7
  52.1 1.8 %collective-permute-start.8 = (f32[18,8,16,128]{3,2,1,0:T(8,128)S(1)}, f32[18,8,16,128]{3,2,1,0:T(8,128)S(1)}, u32[]{:S(2)}, u32[]{:S(2)}) collective-permute-start(f32[18,8,16,128]{3,2,1,0:T(8,128)S(1)} %get-tuple-element.46), channel_id=1, source_target_pairs={{0,4},{4,8},{8,12},{12,16},{16,20},{20,24},{24,28},{1,5},{5,9},{9,... | collective-permute-start | bytes 3538952 | tf_op jit(solution)/shard_map/ppermute | solution.py:47
  54.0 3.6 %collective-permute-start.4 = (f32[11,4,16,128]{3,2,1,0:T(8,128)S(1)}, f32[11,4,16,128]{3,2,1,0:T(8,128)S(1)}, u32[]{:S(2)}, u32[]{:S(2)}) collective-permute-start(f32[11,4,16,128]{3,2,1,0:T(8,128)S(1)} %get-tuple-element.40.refs_1_), channel_id=1, source_target_pairs={{0,4},{4,8},{8,12},{12,16},{16,20},{20,24},{24,28},{1,5},{5,9},{9,... | collective-permute-start | bytes 1081352 | tf_op jit(solution)/shard_map/ppermute | solution.py:47
  57.6 1.3 collective-permute-start.9
  58.9 0.0 collective-permute-done.4.refs_7_
  58.9 1.3 collective-permute-start.5
  60.2 15.5 %collective-permute-done.5.refs_8_ = f32[11,4,16,128]{3,2,1,0:T(8,128)S(1)} collective-permute-done((f32[11,4,16,128]{3,2,1,0:T(8,128)S(1)}, f32[11,4,16,128]{3,2,1,0:T(8,128)S(1)}, u32[]{:S(2)}, u32[]{:S(2)}) %collective-permute-start.5) | collective-permute-done | bytes 360480 | tf_op jit(solution)/shard_map/ppermute | solution.py:47
  75.7 7.1 %step_top.1 = (f32[5,32,4,8,128]{4,3,2,1,0:T(8,128)S(1)}, f32[2,16,16,128]{3,2,1,0:T(8,128)S(1)}, f32[2,16,8,128]{3,2,1,0:T(8,128)S(1)}, f32[2,16,8,128]{3,2,1,0:T(8,128)S(1)}, f32[32,128]{1,0:T(8,128)S(1)}) custom-call(f32[32,4,128]{2,1,0:T(4,128)S(1)} %all_to_all.10.table_ref.refs_2_.refs_0_, f32[3,48,48,128]{3,2,1,0:T(8,128)S(1)} %sources.1.refs_1_.refs_2_.refs_0_, ...), custom_call_target="tpu_custom_call" | custom-call | tf_op jit(solution)/shard_map/step_top/pallas_call | solution.py:33
  82.8 0.0 collective-permute-done.6.z_low.refs_3_
  82.8 0.0 collective-permute-done.7.z_high.refs_4_
  82.9 0.2 corners_more.1
  83.1 16.8 %collective-permute-start.10 = (f32[18,4,16,128]{3,2,1,0:T(8,128)S(1)}, f32[18,4,16,128]{3,2,1,0:T(8,128)S(1)}, u32[]{:S(2)}, u32[]{:S(2)}) collective-permute-start(f32[18,4,16,128]{3,2,1,0:T(8,128)S(1)} %get-tuple-element.49), channel_id=1, source_target_pairs={{0,4},{4,8},{8,12},{12,16},{16,20},{20,24},{24,28},{1,5},{5,9},{9,... | collective-permute-start | bytes 1769480 | tf_op jit(solution)/shard_map/ppermute | solution.py:47
  99.9 1.3 collective-permute-start.11
  101.2 4.4 %collective-permute-start.12 = (f32[2,16,8,128]{3,2,1,0:T(8,128)S(1)}, f32[2,16,8,128]{3,2,1,0:T(8,128)S(1)}, u32[]{:S(2)}, u32[]{:S(2)}) collective-permute-start(f32[2,16,8,128]{3,2,1,0:T(8,128)S(1)} %get-tuple-element.54), channel_id=1, source_target_pairs={{0,1},{1,2},{2,3},{4,5},{5,6},{6,7},{8,9},{9,10},{10,11},{12,13},{... | collective-permute-start | bytes 393224 | tf_op jit(solution)/shard_map/ppermute | solution.py:47
  105.6 3.7 %collective-permute-done.12.z_low.refs_5_ = f32[2,16,8,128]{3,2,1,0:T(8,128)S(1)} collective-permute-done((f32[2,16,8,128]{3,2,1,0:T(8,128)S(1)}, f32[2,16,8,128]{3,2,1,0:T(8,128)S(1)}, u32[]{:S(2)}, u32[]{:S(2)}) %collective-permute-start.12) | collective-permute-done | bytes 131104 | tf_op jit(solution)/shard_map/ppermute | solution.py:47
  109.3 1.3 collective-permute-start.13
  110.6 6.9 %collective-permute-done.13.z_high.refs_6_ = f32[2,16,8,128]{3,2,1,0:T(8,128)S(1)} collective-permute-done((f32[2,16,8,128]{3,2,1,0:T(8,128)S(1)}, f32[2,16,8,128]{3,2,1,0:T(8,128)S(1)}, u32[]{:S(2)}, u32[]{:S(2)}) %collective-permute-start.13) | collective-permute-done | bytes 131104 | tf_op jit(solution)/shard_map/ppermute | solution.py:47
  117.5 1.5 collective-permute-start.14
  119.0 0.0 collective-permute-done.8.refs_5_
  119.0 1.3 collective-permute-start.15
  120.3 0.0 collective-permute-done.9.refs_6_
  120.3 0.0 collective-permute-done.10.refs_7_
  120.3 0.0 collective-permute-done.11.refs_8_
  120.4 1.1 prepare.2
  121.4 0.0 collective-permute-done.14.refs_7_
  121.4 6.1 %collective-permute-done.15.refs_8_ = f32[2,12,16,128]{3,2,1,0:T(8,128)S(1)} collective-permute-done((f32[2,12,16,128]{3,2,1,0:T(8,128)S(1)}, f32[2,12,16,128]{3,2,1,0:T(8,128)S(1)}, u32[]{:S(2)}, u32[]{:S(2)}) %collective-permute-start.15) | collective-permute-done | bytes 196640 | tf_op jit(solution)/shard_map/ppermute | solution.py:47
  127.5 6.0 %step.2 = (f32[2,16,16,128]{3,2,1,0:T(8,128)S(1)}, f32[2,16,8,128]{3,2,1,0:T(8,128)S(1)}, f32[2,16,8,128]{3,2,1,0:T(8,128)S(1)}, f32[32,128]{1,0:T(8,128)S(1)}) custom-call(f32[32,4,128]{2,1,0:T(4,128)S(1)} %all_to_all.10.table_ref.refs_2_.refs_0_, f32[9,32,4,8,128]{4,3,2,1,0:T(8,128)S(1)} %get-tuple-element.52.refs_1_, ...), custom_call_target="tpu_custom_call" | custom-call | tf_op jit(solution)/shard_map/step/pallas_call | solution.py:33
  133.5 3.6 %collective-permute-start.16 = (f32[2,16,8,128]{3,2,1,0:T(8,128)S(1)}, f32[2,16,8,128]{3,2,1,0:T(8,128)S(1)}, u32[]{:S(2)}, u32[]{:S(2)}) collective-permute-start(f32[2,16,8,128]{3,2,1,0:T(8,128)S(1)} %get-tuple-element.59), channel_id=1, source_target_pairs={{0,1},{1,2},{2,3},{4,5},{5,6},{6,7},{8,9},{9,10},{10,11},{12,13},{... | collective-permute-start | bytes 393224 | tf_op jit(solution)/shard_map/ppermute | solution.py:47
  137.2 1.3 collective-permute-start.17
  138.5 1.2 collective-permute-done.16.z_low.refs_5_
  139.7 4.4 %collective-permute-done.17.z_high.refs_6_ = f32[2,16,8,128]{3,2,1,0:T(8,128)S(1)} collective-permute-done((f32[2,16,8,128]{3,2,1,0:T(8,128)S(1)}, f32[2,16,8,128]{3,2,1,0:T(8,128)S(1)}, u32[]{:S(2)}, u32[]{:S(2)}) %collective-permute-start.17) | collective-permute-done | bytes 131104 | tf_op jit(solution)/shard_map/ppermute | solution.py:47
  144.1 4.6 %collective-permute-start.18 = (f32[2,12,16,128]{3,2,1,0:T(8,128)S(1)}, f32[2,12,16,128]{3,2,1,0:T(8,128)S(1)}, u32[]{:S(2)}, u32[]{:S(2)}) collective-permute-start(f32[2,12,16,128]{3,2,1,0:T(8,128)S(1)} %get-tuple-element.61), channel_id=1, source_target_pairs={{0,4},{4,8},{8,12},{12,16},{16,20},{20,24},{24,28},{1,5},{5,9},{9,... | collective-permute-start | bytes 589832 | tf_op jit(solution)/shard_map/ppermute | solution.py:47
  148.7 1.3 collective-permute-start.19
  150.0 1.0 prepare.3.refs_1_
  151.0 0.0 collective-permute-done.18.refs_7_
  151.0 1.8 %collective-permute-done.19.refs_8_ = f32[2,12,16,128]{3,2,1,0:T(8,128)S(1)} collective-permute-done((f32[2,12,16,128]{3,2,1,0:T(8,128)S(1)}, f32[2,12,16,128]{3,2,1,0:T(8,128)S(1)}, u32[]{:S(2)}, u32[]{:S(2)}) %collective-permute-start.19) | collective-permute-done | bytes 196640 | tf_op jit(solution)/shard_map/ppermute | solution.py:47
  152.8 6.3 %step.3 = (f32[16,16,128]{2,1,0:T(8,128)}, f32[16,16,128]{2,1,0:T(8,128)}, f32[32,128]{1,0:T(8,128)S(1)}) custom-call(f32[32,4,128]{2,1,0:T(4,128)S(1)} %all_to_all.10.table_ref.refs_2_.refs_0_, f32[9,32,4,8,128]{4,3,2,1,0:T(8,128)S(1)} %prepare.3.refs_1_, f32[5,32,4,8,128]{4,3,2,1,0:T(8,128)S(1)} %get-tuple-element.42.refs_1_.refs_2_, ...), custom_call_target="tpu_custom_call" | custom-call | tf_op jit(solution)/shard_map/step/pallas_call | solution.py:33
  159.1 14.5 %all_to_all.11 = f32[32,1,128]{2,1,0:T(1,128)S(1)} all-to-all(f32[32,1,128]{2,1,0:T(1,128)S(1)} %bitcast.7), channel_id=1, replica_groups=mesh['gx'=8,'gy'=4] {'gx','gy'}, dimensions={0} | all-to-all | bytes 32768 | tf_op jit(solution)/shard_map/all_to_all | solution.py:620
  173.7 0.1 reduce_sum.9
  173.7 0.6 reshape.9
  (11 shorter events, 0.1 us)
Async XLA Ops:
  0.6 14.4 %copy-start.8 = (f32[128]{0:T(128)S(1)}, f32[128]{0:T(128)}, u32[]{:S(2)}) copy-start(f32[128]{0:T(128)} %param.37) | copy-start | bytes 1540
  0.6 14.4 %copy-start.7 = (s32[128]{0:T(128)S(1)}, s32[128]{0:T(128)}, u32[]{:S(2)}) copy-start(s32[128]{0:T(128)} %param.36) | copy-start | bytes 1540
  0.7 14.4 %copy-start.6 = (s32[128]{0:T(128)S(1)}, s32[128]{0:T(128)}, u32[]{:S(2)}) copy-start(s32[128]{0:T(128)} %param.35) | copy-start | bytes 1540
  0.7 14.4 %copy-start.5 = (s32[2,3]{1,0:T(2,128)S(1)}, s32[2,3]{1,0:T(2,128)}, u32[]{:S(2)}) copy-start(s32[2,3]{1,0:T(2,128)} %control.1) | copy-start | bytes 76
  0.7 14.4 %copy-start.4 = (f32[2,3]{1,0:T(2,128)S(1)}, f32[2,3]{1,0:T(2,128)}, u32[]{:S(2)}) copy-start(f32[2,3]{1,0:T(2,128)} %bhp.1) | copy-start | bytes 76
  0.7 14.4 %copy-start.3 = (f32[2,3]{1,0:T(2,128)S(1)}, f32[2,3]{1,0:T(2,128)}, u32[]{:S(2)}) copy-start(f32[2,3]{1,0:T(2,128)} %rate.1) | copy-start | bytes 76
  5.9 40.6 %collective-permute-start = (f32[11,16,8,128]{3,2,1,0:T(8,128)}, f32[11,16,8,128]{3,2,1,0:T(8,128)S(1)}, u32[]{:S(2)}, u32[]{:S(2)}) collective-permute-start(f32[11,16,8,128]{3,2,1,0:T(8,128)} %get-tuple-element.37), channel_id=1, source_target_pairs={{0,1},{1,2},{2,3},{4,5},{5,6},{6,7},{8,9},{9,10},{10,11},{12,13},{... | collective-permute-start | bytes 2162696 | tf_op jit(solution)/shard_map/ppermute | solution.py:47
  10.9 35.6 %collective-permute-start.2 = (f32[11,8,16,128]{3,2,1,0:T(8,128)}, f32[11,8,16,128]{3,2,1,0:T(8,128)S(1)}, u32[]{:S(2)}, u32[]{:S(2)}) collective-permute-start(f32[11,8,16,128]{3,2,1,0:T(8,128)} %get-tuple-element.38), channel_id=1, source_target_pairs={{0,4},{4,8},{8,12},{12,16},{16,20},{20,24},{24,28},{1,5},{5,9},{9,... | collective-permute-start | bytes 2162696 | tf_op jit(solution)/shard_map/ppermute | solution.py:47
  12.4 34.1 %collective-permute-start.3 = (f32[11,8,16,128]{3,2,1,0:T(8,128)}, f32[11,8,16,128]{3,2,1,0:T(8,128)S(1)}, u32[]{:S(2)}, u32[]{:S(2)}) collective-permute-start(f32[11,8,16,128]{3,2,1,0:T(8,128)} %get-tuple-element.39), channel_id=1, source_target_pairs={{4,0},{8,4},{12,8},{16,12},{20,16},{24,20},{28,24},{5,1},{9,5},{13... | collective-permute-start | bytes 2162696 | tf_op jit(solution)/shard_map/ppermute | solution.py:47
  13.7 32.8 %collective-permute-start.1 = (f32[11,16,8,128]{3,2,1,0:T(8,128)}, f32[11,16,8,128]{3,2,1,0:T(8,128)S(1)}, u32[]{:S(2)}, u32[]{:S(2)}) collective-permute-start(f32[11,16,8,128]{3,2,1,0:T(8,128)} %get-tuple-element.35._), channel_id=1, source_target_pairs={{1,0},{2,1},{3,2},{5,4},{6,5},{7,6},{9,8},{10,9},{11,10},{13,12},{... | collective-permute-start | bytes 2162696 | tf_op jit(solution)/shard_map/ppermute | solution.py:47
  15.1 1.1 copy-start.2
  46.5 1.7 copy-start
  48.1 27.6 %copy-start.1 = (f32[11,16,16,128]{3,2,1,0:T(8,128)S(1)}, f32[11,16,16,128]{3,2,1,0:T(8,128)}, u32[]{:S(2)}) copy-start(f32[11,16,16,128]{3,2,1,0:T(8,128)} %get-tuple-element.36.refs_2_) | copy-start | bytes 4325380
  48.5 34.4 %collective-permute-start.6 = (f32[18,16,8,128]{3,2,1,0:T(8,128)S(1)}, f32[18,16,8,128]{3,2,1,0:T(8,128)S(1)}, u32[]{:S(2)}, u32[]{:S(2)}) collective-permute-start(f32[18,16,8,128]{3,2,1,0:T(8,128)S(1)} %get-tuple-element.44), channel_id=1, source_target_pairs={{0,1},{1,2},{2,3},{4,5},{5,6},{6,7},{8,9},{9,10},{10,11},{12,13},{... | collective-permute-start | bytes 3538952 | tf_op jit(solution)/shard_map/ppermute | solution.py:47
  50.8 32.0 %collective-permute-start.7 = (f32[18,16,8,128]{3,2,1,0:T(8,128)S(1)}, f32[18,16,8,128]{3,2,1,0:T(8,128)S(1)}, u32[]{:S(2)}, u32[]{:S(2)}) collective-permute-start(f32[18,16,8,128]{3,2,1,0:T(8,128)S(1)} %get-tuple-element.45), channel_id=1, source_target_pairs={{1,0},{2,1},{3,2},{5,4},{6,5},{7,6},{9,8},{10,9},{11,10},{13,12},{... | collective-permute-start | bytes 3538952 | tf_op jit(solution)/shard_map/ppermute | solution.py:47
  52.1 66.9 %collective-permute-start.8 = (f32[18,8,16,128]{3,2,1,0:T(8,128)S(1)}, f32[18,8,16,128]{3,2,1,0:T(8,128)S(1)}, u32[]{:S(2)}, u32[]{:S(2)}) collective-permute-start(f32[18,8,16,128]{3,2,1,0:T(8,128)S(1)} %get-tuple-element.46), channel_id=1, source_target_pairs={{0,4},{4,8},{8,12},{12,16},{16,20},{20,24},{24,28},{1,5},{5,9},{9,... | collective-permute-start | bytes 3538952 | tf_op jit(solution)/shard_map/ppermute | solution.py:47
  54.0 4.9 %collective-permute-start.4 = (f32[11,4,16,128]{3,2,1,0:T(8,128)S(1)}, f32[11,4,16,128]{3,2,1,0:T(8,128)S(1)}, u32[]{:S(2)}, u32[]{:S(2)}) collective-permute-start(f32[11,4,16,128]{3,2,1,0:T(8,128)S(1)} %get-tuple-element.40.refs_1_), channel_id=1, source_target_pairs={{0,4},{4,8},{8,12},{12,16},{16,20},{20,24},{24,28},{1,5},{5,9},{9,... | collective-permute-start | bytes 1081352 | tf_op jit(solution)/shard_map/ppermute | solution.py:47
  57.6 62.7 %collective-permute-start.9 = (f32[18,8,16,128]{3,2,1,0:T(8,128)S(1)}, f32[18,8,16,128]{3,2,1,0:T(8,128)S(1)}, u32[]{:S(2)}, u32[]{:S(2)}) collective-permute-start(f32[18,8,16,128]{3,2,1,0:T(8,128)S(1)} %get-tuple-element.47), channel_id=1, source_target_pairs={{4,0},{8,4},{12,8},{16,12},{20,16},{24,20},{28,24},{5,1},{9,5},{13... | collective-permute-start | bytes 3538952 | tf_op jit(solution)/shard_map/ppermute | solution.py:47
  58.9 16.8 %collective-permute-start.5 = (f32[11,4,16,128]{3,2,1,0:T(8,128)S(1)}, f32[11,4,16,128]{3,2,1,0:T(8,128)S(1)}, u32[]{:S(2)}, u32[]{:S(2)}) collective-permute-start(f32[11,4,16,128]{3,2,1,0:T(8,128)S(1)} %get-tuple-element.41.refs_0_), channel_id=1, source_target_pairs={{4,0},{8,4},{12,8},{16,12},{20,16},{24,20},{28,24},{5,1},{9,5},{13... | collective-permute-start | bytes 1081352 | tf_op jit(solution)/shard_map/ppermute | solution.py:47
  83.1 37.3 %collective-permute-start.10 = (f32[18,4,16,128]{3,2,1,0:T(8,128)S(1)}, f32[18,4,16,128]{3,2,1,0:T(8,128)S(1)}, u32[]{:S(2)}, u32[]{:S(2)}) collective-permute-start(f32[18,4,16,128]{3,2,1,0:T(8,128)S(1)} %get-tuple-element.49), channel_id=1, source_target_pairs={{0,4},{4,8},{8,12},{12,16},{16,20},{20,24},{24,28},{1,5},{5,9},{9,... | collective-permute-start | bytes 1769480 | tf_op jit(solution)/shard_map/ppermute | solution.py:47
  99.9 20.4 %collective-permute-start.11 = (f32[18,4,16,128]{3,2,1,0:T(8,128)S(1)}, f32[18,4,16,128]{3,2,1,0:T(8,128)S(1)}, u32[]{:S(2)}, u32[]{:S(2)}) collective-permute-start(f32[18,4,16,128]{3,2,1,0:T(8,128)S(1)} %get-tuple-element.50), channel_id=1, source_target_pairs={{4,0},{8,4},{12,8},{16,12},{20,16},{24,20},{28,24},{5,1},{9,5},{13... | collective-permute-start | bytes 1769480 | tf_op jit(solution)/shard_map/ppermute | solution.py:47
  101.2 8.1 %collective-permute-start.12 = (f32[2,16,8,128]{3,2,1,0:T(8,128)S(1)}, f32[2,16,8,128]{3,2,1,0:T(8,128)S(1)}, u32[]{:S(2)}, u32[]{:S(2)}) collective-permute-start(f32[2,16,8,128]{3,2,1,0:T(8,128)S(1)} %get-tuple-element.54), channel_id=1, source_target_pairs={{0,1},{1,2},{2,3},{4,5},{5,6},{6,7},{8,9},{9,10},{10,11},{12,13},{... | collective-permute-start | bytes 393224 | tf_op jit(solution)/shard_map/ppermute | solution.py:47
  109.3 8.1 %collective-permute-start.13 = (f32[2,16,8,128]{3,2,1,0:T(8,128)S(1)}, f32[2,16,8,128]{3,2,1,0:T(8,128)S(1)}, u32[]{:S(2)}, u32[]{:S(2)}) collective-permute-start(f32[2,16,8,128]{3,2,1,0:T(8,128)S(1)} %get-tuple-element.48.refs_0_), channel_id=1, source_target_pairs={{1,0},{2,1},{3,2},{5,4},{6,5},{7,6},{9,8},{10,9},{11,10},{13,12},{... | collective-permute-start | bytes 393224 | tf_op jit(solution)/shard_map/ppermute | solution.py:47
  117.5 3.9 %collective-permute-start.14 = (f32[2,12,16,128]{3,2,1,0:T(8,128)S(1)}, f32[2,12,16,128]{3,2,1,0:T(8,128)S(1)}, u32[]{:S(2)}, u32[]{:S(2)}) collective-permute-start(f32[2,12,16,128]{3,2,1,0:T(8,128)S(1)} %get-tuple-element.55), channel_id=1, source_target_pairs={{0,4},{4,8},{8,12},{12,16},{16,20},{20,24},{24,28},{1,5},{5,9},{9,... | collective-permute-start | bytes 589832 | tf_op jit(solution)/shard_map/ppermute | solution.py:47
  119.0 8.5 %collective-permute-start.15 = (f32[2,12,16,128]{3,2,1,0:T(8,128)S(1)}, f32[2,12,16,128]{3,2,1,0:T(8,128)S(1)}, u32[]{:S(2)}, u32[]{:S(2)}) collective-permute-start(f32[2,12,16,128]{3,2,1,0:T(8,128)S(1)} %get-tuple-element.56), channel_id=1, source_target_pairs={{4,0},{8,4},{12,8},{16,12},{20,16},{24,20},{28,24},{5,1},{9,5},{13... | collective-permute-start | bytes 589832 | tf_op jit(solution)/shard_map/ppermute | solution.py:47
  133.5 6.2 %collective-permute-start.16 = (f32[2,16,8,128]{3,2,1,0:T(8,128)S(1)}, f32[2,16,8,128]{3,2,1,0:T(8,128)S(1)}, u32[]{:S(2)}, u32[]{:S(2)}) collective-permute-start(f32[2,16,8,128]{3,2,1,0:T(8,128)S(1)} %get-tuple-element.59), channel_id=1, source_target_pairs={{0,1},{1,2},{2,3},{4,5},{5,6},{6,7},{8,9},{9,10},{10,11},{12,13},{... | collective-permute-start | bytes 393224 | tf_op jit(solution)/shard_map/ppermute | solution.py:47
  137.2 6.9 %collective-permute-start.17 = (f32[2,16,8,128]{3,2,1,0:T(8,128)S(1)}, f32[2,16,8,128]{3,2,1,0:T(8,128)S(1)}, u32[]{:S(2)}, u32[]{:S(2)}) collective-permute-start(f32[2,16,8,128]{3,2,1,0:T(8,128)S(1)} %get-tuple-element.60), channel_id=1, source_target_pairs={{1,0},{2,1},{3,2},{5,4},{6,5},{7,6},{9,8},{10,9},{11,10},{13,12},{... | collective-permute-start | bytes 393224 | tf_op jit(solution)/shard_map/ppermute | solution.py:47
  144.1 7.0 %collective-permute-start.18 = (f32[2,12,16,128]{3,2,1,0:T(8,128)S(1)}, f32[2,12,16,128]{3,2,1,0:T(8,128)S(1)}, u32[]{:S(2)}, u32[]{:S(2)}) collective-permute-start(f32[2,12,16,128]{3,2,1,0:T(8,128)S(1)} %get-tuple-element.61), channel_id=1, source_target_pairs={{0,4},{4,8},{8,12},{12,16},{16,20},{20,24},{24,28},{1,5},{5,9},{9,... | collective-permute-start | bytes 589832 | tf_op jit(solution)/shard_map/ppermute | solution.py:47
  148.7 4.1 %collective-permute-start.19 = (f32[2,12,16,128]{3,2,1,0:T(8,128)S(1)}, f32[2,12,16,128]{3,2,1,0:T(8,128)S(1)}, u32[]{:S(2)}, u32[]{:S(2)}) collective-permute-start(f32[2,12,16,128]{3,2,1,0:T(8,128)S(1)} %get-tuple-element.62), channel_id=1, source_target_pairs={{4,0},{8,4},{12,8},{16,12},{20,16},{24,20},{28,24},{5,1},{9,5},{13... | collective-permute-start | bytes 589832 | tf_op jit(solution)/shard_map/ppermute | solution.py:47

commit v4 on v3

--- a/solution.py
+++ b/solution.py
@@ -47,59 +47,43 @@
     return lax.ppermute(value, axis, pairs)
 
 
-def load_kernel(leads, split, *refs):
+def load_kernel(leads, *refs):
     count = len(leads)
-    ins, (top, rest, y_low, y_high, x_low, x_high), sems = refs[:count], refs[count:-1], refs[-1]
-    rx, ry = top.shape[1:3]
-    copies = []
-    for n, lead in enumerate(leads):
-        to = top.at[n] if n < split else rest.at[n - split]
-        copies.append(
-            pltpu.make_async_copy(
-                ins[n] if lead is None else ins[n].at[lead], to, sems.at[n]
-            )
+    ins, (own, y_low, y_high, x_low, x_high, token), sems = refs[:count], refs[count:-1], refs[-1]
+    token[...] = jnp.zeros(token.shape, F32)
+    rx, ry = own.shape[1:3]
+    copies = [
+        pltpu.make_async_copy(
+            ins[n] if lead is None else ins[n].at[lead], own.at[n], sems.at[n]
         )
+        for n, lead in enumerate(leads)
+    ]
     for c in copies:
         c.start()
-    for c in copies[:split]:
-        c.wait()
-    edges_body(top, y_low, y_high, x_low, x_high)
-    for c in copies[split:]:
-        c.wait()
-
-
-def edges_body(own, y_low, y_high, x_low, x_high):
-    rx, ry = own.shape[1:3]
-
-    def one(n, _):
+
+    def one(n):
         y_low[n] = own[n, :, 0:H, :]
         y_high[n] = own[n, :, ry - H :, :]
         x_low[n] = own[n, 0:H]
         x_high[n] = own[n, rx - H :]
-        return 0
-
-    lax.fori_loop(0, own.shape[0], one, 0)
-
-
-def edge_shapes(n, dims):
+
+    for n, c in enumerate(copies):
+        c.wait()
+        one(n)
+
+
+def load(arrays, leads, dims):
+    n = len(leads)
     rx, ry, nz = dims
-    return [sds(n, rx, H, nz)] * 2 + [sds(n, H, ry, nz)] * 2
-
-
-def load(arrays, leads, split, dims):
-    n = len(leads)
     return pl.pallas_call(
-        functools.partial(load_kernel, leads, split),
+        functools.partial(load_kernel, leads),
         in_specs=[HBM] * n,
         out_specs=[VMEM] * 6,
-        out_shape=[sds(split, *dims), sds(n - split, *dims)] + edge_shapes(split, dims),
+        out_shape=[sds(n, *dims)] + [sds(n, rx, H, nz)] * 2 + [sds(n, H, ry, nz)] * 2
+        + [sds(8, 128)],
         scratch_shapes=[pltpu.SemaphoreType.DMA((n,))],
         name="load",
     )(*arrays)
-
-
-def edges_kernel(own, *refs):
-    edges_body(own, *refs[-4:])
 
 
 def fold(rows_of, high):
@@ -130,23 +114,24 @@
                 put(side, int(high), t, tile)
 
 
-def corner_kernel(z_low, z_high, *refs):
+def corner_kernel(first, z_low, z_high, *refs):
     outs = refs[-2:]
 
     def one(n, _):
         def put(side, y, t, tile):
             outs[side][n, t, y * H : (y + 1) * H, :] = tile
 
-        corner_tiles(n, z_low, z_high, put)
-        return 0
-
-    lax.fori_loop(0, z_low.shape[0], one, 0)
-
-
-def pack_corners(name, z_low, z_high, after):
-    count, _, _, nz = z_low.shape
+        corner_tiles(n + first, z_low, z_high, put)
+        return 0
+
+    lax.fori_loop(0, outs[0].shape[0], one, 0)
+
+
+def pack_corners(name, z_low, z_high, first, count, after):
+    nz = z_low.shape[-1]
     return call(
-        corner_kernel, [z_low, z_high, *after], [sds(count, 4, 2 * H, nz)] * 2, name, 4,
+        functools.partial(corner_kernel, first), [z_low, z_high, *after],
+        [sds(count, 4, 2 * H, nz)] * 2, name, 4,
         [VMEM] * 2 + [ANY] * len(after),
     )
 
@@ -191,7 +176,7 @@
     return x, y, n_x, n_y
 
 
-def source_kernel(steps, wells, ry, table_ref, src_ref):
+def source_kernel(steps, wells, ry, table_ref, _, src_ref):
     here_x, here_y, n_x, n_y = spot()
     count = table_ref.shape[0]
     rx = src_ref.shape[1] // 3
@@ -260,7 +245,7 @@
     return pltpu.roll(value, by, 2)
 
 
-def fill(dst, own, z_low, z_high, x_edges, corners, base, first=0):
+def fill(dst, own, z_low, z_high, x_edges, corners, base, first=0, corner_first=0):
     count, (rx, ry, nz) = dst.shape[0], own.shape[1:]
 
     def one(n, _):
@@ -274,7 +259,7 @@
             for y in (0, 1):
                 to = y * (H + ry)
                 for t in range(4):
-                    tile = corners[side][m, base + t, y * H : (y + 1) * H, :]
+                    tile = corners[side][n + corner_first, base + t, y * H : (y + 1) * H, :]
                     near, far = unfold(tile, t + 1, y == 1)
                     for dx, row in ((t + 1, near), (7 - t, far)):
                         x = H - dx if side == 0 else H + rx + dx - 1
@@ -463,7 +448,7 @@
     finish(False, step, steps, wells, lin, own.at[7], table_ref, None, outs)
 
 
-def prepare_kernel(step, first, with_acc, *refs):
+def prepare_kernel(step, first, corner_first, with_acc, *refs):
     src_ref, geo, own, z_low, z_high, x_low, x_high, c_low, c_high = refs[:9]
     if with_acc:
         coef, acc_out, raw = refs[9:]
@@ -471,7 +456,7 @@
         acc, coef, raw = refs[9:]
     rx, ry, nz = own.shape[1:]
     ex = rx + 2 * H
-    fill(raw, own, z_low, z_high, (x_low, x_high), (c_low, c_high), 0, first)
+    fill(raw, own, z_low, z_high, (x_low, x_high), (c_low, c_high), 0, first, corner_first)
 
     def prepare(x, _):
         s_a, r_a, p, frac, r_b, q, m, s_b = coefficients(
@@ -544,13 +529,13 @@
     split = len(arrays)
     places = {}
     for step in reversed(range(top)):
-        places[step] = len(arrays) - split
+        places[step] = len(arrays)
         arrays += own
         leads += [step] * 8
         if step == top - 1:
             arrays += [acc_p, acc_s]
             leads += [None] * 2
-    blocks, more, y_low, y_high, e_low, e_high = load(arrays, leads, split, dims)
+    blocks, y_low, y_high, e_low, e_high, token = load(arrays, leads, dims)
 
     z_got = sent(y_low, y_high, "gy")
     x_got = sent(e_low, e_high, "gx")
@@ -558,23 +543,18 @@
     mine = call(
         functools.partial(table_kernel, steps),
         [rate_mis, bhp_mis, control] + [p[None] for p in (perf_well, perf_cell, perf_wi)]
-        + [y_low], [sds(devices, 4, 128)], "table", 4, [VMEM] * 6 + [ANY],
+        + [token], [sds(devices, 4, 128)], "table", 4, [VMEM] * 6 + [ANY],
     )[0]
     table = lax.all_to_all(mine, ("gx", "gy"), 0, 0, tiled=True)
+
+    corners = pack_corners("corners", *z_got, 0, split, (*x_got, table))
+    c_got = sent(*corners, "gx")
     src = call(
-        functools.partial(source_kernel, steps, wells, ry), [table],
-        [sds(steps, 3 * rx, 3 * ry, nz)], "sources", 8,
+        functools.partial(source_kernel, steps, wells, ry), [table, corners[0]],
+        [sds(steps, 3 * rx, 3 * ry, nz)], "sources", 8, [VMEM, ANY],
     )[0]
-
-    corners = pack_corners("corners", *z_got, (*x_got, table))
-    c_got = sent(*corners, "gx")
-
-    edges = call(
-        edges_kernel, [more, *corners, src], edge_shapes(len(arrays) - split, dims), "edges", 4,
-        [VMEM] + [ANY] * 3,
-    )
-    m_z = sent(*edges[:2], "gy")
-    m_x = sent(*edges[2:], "gx")
+    rest = len(arrays) - split
+    m_c = sent(*pack_corners("corners_more", *z_got, split, rest, (src,)), "gx")
 
     ext = (ex, V, 8, nz)
     lam_out = [sds(2, rx, ry, nz), sds(2, rx, H, nz), sds(2, rx, H, nz)]
@@ -588,16 +568,14 @@
         scratch=[pltpu.VMEM((split, ex, ey, nz), F32), pltpu.VMEM((7, *ext), F32)] + fields,
     )
 
-    m_c = sent(*pack_corners("corners_more", *m_z, (low,)), "gx")
-
     acc = None
     for step in reversed(range(top)):
         last = step == 0
         with_acc = step == top - 1
         at = places[step]
         made = call(
-            functools.partial(prepare_kernel, step, at, with_acc),
-            [src, geo, more, *m_z, *m_x, *m_c] + ([] if with_acc else [acc]),
+            functools.partial(prepare_kernel, step, at, at - split, with_acc),
+            [src, geo, blocks, *z_got, *x_got, *m_c] + ([] if with_acc else [acc]),
             [sds(9, *ext)] + ([sds(2, *ext)] if with_acc else []), "prepare", 8,
             scratch=[pltpu.VMEM((10 if with_acc else 8, ex, ey, nz), F32)],
         )
@@ -610,7 +588,7 @@
         outs = [sds(rx, ry, nz)] * 2 if last else lam_out
         outs = call(
             functools.partial(sweep_kernel, last, step, at + 4, steps, wells),
-            [table, coef, geo, more, lam, *l_z, *l_x, dense],
+            [table, coef, geo, blocks, lam, *l_z, *l_x, dense],
             outs + [well_out], "step", 8, scratch=[pltpu.VMEM((2, *ext), F32)] + fields,
         )
         dense = outs[-1]

time: 175 us -> 154 us (0.88)
  waiting for transfers between devices: 39.5 us -> 17.4 us
  blocking collectives: 38.7 us -> 60.8 us
  starting transfers between devices: 58.2 us -> 37.8 us
  local copies, waits for them, and re-layouts: 3.27 us -> 1.36 us
    ppermute x20 -> x16, waiting for transfers between devices: 39.5 us -> 17.4 us  [shifted(): return lax.ppermute(value, axis, pairs)]
    all_to_all x1, blocking collectives: 24.2 us -> 44.7 us  [local(): table = lax.all_to_all(mine, ('gx', 'gy'), 0, 0, tiled=True)]
    ppermute x20 -> x16, starting transfers between devices: 58.2 us -> 37.8 us  [shifted(): return lax.ppermute(value, axis, pairs)]
    unnamed x18 -> x16, local copies, waits for them, and re-layouts: 2.63 us -> 0.71 us
    pallas_call x12 -> x11, Pallas kernels: 28.3 us -> 28 us  [call(): pl.pallas_call(kernel, in_specs=specs or [VMEM] * len(ins), out_specs=[VM...]
  transfers between devices with their start and end apart: 20 -> 16, of which waited for: 7 -> 6; matrix products, arithmetic and copies ran while one was open for 0% -> 0% of each run, Pallas kernels for 9% -> 10%
where the time goes in v4:
time: 154 us; the launch traced here: 153 us
  blocking collectives  60.8 us (39%)
  starting transfers between devices  37.8 us (25%)
  Pallas kernels  34.6 us (22%)
  waiting for transfers between devices  17.4 us (11%)
    all_to_all x1, blocking collectives, local(): table = lax.all_to_all(mine, ('gx', 'gy'), 0, 0, tiled=True)  44.7 us
    ppermute x16, starting transfers between devices, shifted(): return lax.ppermute(value, axis, pairs)  37.8 us
    pallas_call x11, Pallas kernels, call(): pl.pallas_call(kernel, in_specs=specs or [VMEM] * len(ins), out_specs=[VM...  28 us
    ppermute x16, waiting for transfers between devices, shifted(): return lax.ppermute(value, axis, pairs)  17.4 us
    all_to_all x1, blocking collectives, local(): parts = lax.all_to_all(dense[:, None, :], ('gx', 'gy'), 0, 0, tiled=True)  16.1 us
    pallas_call x1, Pallas kernels, load(): pl.pallas_call(functools.partial(load_kernel, leads), in_specs=[HBM] * n,...  6.68 us
  transfers between devices with their start and end apart: 16, of which 6 were waited for; matrix products, arithmetic and copies ran while one was open for 0% of the time, Pallas kernels for 10%

profile of v4, /device:TPU:0, one launch (start us, length us, event | category | flops | bytes accessed | tf_op | source)
XLA Modules:
  0.0 153.1 jit_solution(7240866700359382234)
XLA Ops:
  0.6 0.0 copy-start.7
  0.6 0.0 copy-start.6
  0.7 0.0 copy-start.5
  0.7 0.0 copy-start.4
  0.7 0.0 copy-start.3
  0.7 0.0 copy-start.2
  0.7 6.7 %load.1 = (f32[29,16,16,128]{3,2,1,0:T(8,128)}, f32[29,16,8,128]{3,2,1,0:T(8,128)}, f32[29,16,8,128]{3,2,1,0:T(8,128)}, f32[29,8,16,128]{3,2,1,0:T(8,128)}, f32[...) custom-call(f32[16,16,128]{2,1,0:T(8,128)} %refs_0_.1, f32[16,16,128]{2,1,0:T(8,128)} %refs_1_.1, f32[16,16,128]{2,1,0:T(8,128)} %refs_2_.1, ...), custom_call_target="tpu_custom_call" | custom-call | tf_op jit(solution)/shard_map/load/pallas_call | solution.py:78
  7.4 5.0 %collective-permute-start = (f32[29,16,8,128]{3,2,1,0:T(8,128)}, f32[29,16,8,128]{3,2,1,0:T(8,128)S(1)}, u32[]{:S(2)}, u32[]{:S(2)}) collective-permute-start(f32[29,16,8,128]{3,2,1,0:T(8,128)} %get-tuple-element.32), channel_id=1, source_target_pairs={{0,1},{1,2},{2,3},{4,5},{5,6},{6,7},{8,9},{9,10},{10,11},{12,13},{... | collective-permute-start | bytes 5701640 | tf_op jit(solution)/shard_map/ppermute | solution.py:47
  12.4 1.3 collective-permute-start.1
  13.7 1.6 %collective-permute-start.2 = (f32[29,8,16,128]{3,2,1,0:T(8,128)}, f32[29,8,16,128]{3,2,1,0:T(8,128)S(1)}, u32[]{:S(2)}, u32[]{:S(2)}) collective-permute-start(f32[29,8,16,128]{3,2,1,0:T(8,128)} %get-tuple-element.34), channel_id=1, source_target_pairs={{0,4},{4,8},{8,12},{12,16},{16,20},{20,24},{24,28},{1,5},{5,9},{9,... | collective-permute-start | bytes 5701640 | tf_op jit(solution)/shard_map/ppermute | solution.py:47
  15.3 1.3 collective-permute-start.3
  16.6 0.0 copy-done.7
  16.6 0.0 copy-done.6
  16.7 0.0 copy-done.5
  16.7 0.0 copy-done.4
  16.7 0.0 copy-done.3
  16.7 0.0 copy-done.2
  16.7 0.0 copy-start.1
  16.7 0.7 copy-done.1
  17.4 0.1 table.1
  17.5 44.7 %all_to_all.10.refs_2_.table_ref.refs_0_ = f32[32,4,128]{2,1,0:T(4,128)S(1)} all-to-all(f32[32,4,128]{2,1,0:T(4,128)S(1)} %table.1), channel_id=1, replica_groups=mesh['gx'=8,'gy'=4] {'gx','gy'}, dimensions={0} | all-to-all | bytes 131072 | tf_op jit(solution)/shard_map/all_to_all | solution.py:548
  62.1 0.0 collective-permute-done.z_low.refs_3_
  62.1 0.0 collective-permute-done.1.z_high.refs_4_
  62.1 0.0 collective-permute-done.2.refs_0_.refs_5_
  62.1 0.0 collective-permute-done.3.refs_1_.refs_6_
  62.2 0.1 corners.1
  62.3 1.5 collective-permute-start.4
  63.8 1.3 collective-permute-start.5
  65.1 6.0 %sources.1.refs_1_.refs_0_ = f32[3,48,48,128]{3,2,1,0:T(8,128)S(1)} custom-call(f32[32,4,128]{2,1,0:T(4,128)S(1)} %all_to_all.10.refs_2_.table_ref.refs_0_, f32[11,4,16,128]{3,2,1,0:T(8,128)S(1)} %get-tuple-element.36._), custom_call_target="tpu_custom_call" | custom-call | tf_op jit(solution)/shard_map/sources/pallas_call | solution.py:33
  71.2 0.0 copy-start
  71.2 0.2 corners_more.1
  71.4 4.0 %collective-permute-start.6 = (f32[18,4,16,128]{3,2,1,0:T(8,128)S(1)}, f32[18,4,16,128]{3,2,1,0:T(8,128)S(1)}, u32[]{:S(2)}, u32[]{:S(2)}) collective-permute-start(f32[18,4,16,128]{3,2,1,0:T(8,128)S(1)} %get-tuple-element.40), channel_id=1, source_target_pairs={{0,4},{4,8},{8,12},{12,16},{16,20},{20,24},{24,28},{1,5},{5,9},{9,... | collective-permute-start | bytes 1769480 | tf_op jit(solution)/shard_map/ppermute | solution.py:47
  75.3 1.3 collective-permute-start.7
  76.6 0.0 collective-permute-done.4.refs_7_
  76.7 0.0 collective-permute-done.5.refs_8_
  76.7 0.0 copy-done
  76.7 7.1 %step_top.1 = (f32[5,32,4,8,128]{4,3,2,1,0:T(8,128)S(1)}, f32[2,16,16,128]{3,2,1,0:T(8,128)S(1)}, f32[2,16,8,128]{3,2,1,0:T(8,128)S(1)}, f32[2,16,8,128]{3,2,1,0:T(8,128)S(1)}, f32[32,128]{1,0:T(8,128)S(1)}) custom-call(f32[32,4,128]{2,1,0:T(4,128)S(1)} %all_to_all.10.refs_2_.table_ref.refs_0_, f32[3,48,48,128]{3,2,1,0:T(8,128)S(1)} %sources.1.refs_1_.refs_0_, ...), custom_call_target="tpu_custom_call" | custom-call | tf_op jit(solution)/shard_map/step_top/pallas_call | solution.py:33
  83.8 4.3 %collective-permute-start.8 = (f32[2,16,8,128]{3,2,1,0:T(8,128)S(1)}, f32[2,16,8,128]{3,2,1,0:T(8,128)S(1)}, u32[]{:S(2)}, u32[]{:S(2)}) collective-permute-start(f32[2,16,8,128]{3,2,1,0:T(8,128)S(1)} %get-tuple-element.45), channel_id=1, source_target_pairs={{0,1},{1,2},{2,3},{4,5},{5,6},{6,7},{8,9},{9,10},{10,11},{12,13},{... | collective-permute-start | bytes 393224 | tf_op jit(solution)/shard_map/ppermute | solution.py:47
  88.1 1.3 collective-permute-start.9
  89.4 1.2 collective-permute-done.8.z_low.refs_5_
  90.6 4.7 %collective-permute-done.9.z_high.refs_6_ = f32[2,16,8,128]{3,2,1,0:T(8,128)S(1)} collective-permute-done((f32[2,16,8,128]{3,2,1,0:T(8,128)S(1)}, f32[2,16,8,128]{3,2,1,0:T(8,128)S(1)}, u32[]{:S(2)}, u32[]{:S(2)}) %collective-permute-start.9) | collective-permute-done | bytes 131104 | tf_op jit(solution)/shard_map/ppermute | solution.py:47
  95.3 2.8 %collective-permute-start.10 = (f32[2,12,16,128]{3,2,1,0:T(8,128)S(1)}, f32[2,12,16,128]{3,2,1,0:T(8,128)S(1)}, u32[]{:S(2)}, u32[]{:S(2)}) collective-permute-start(f32[2,12,16,128]{3,2,1,0:T(8,128)S(1)} %get-tuple-element.47), channel_id=1, source_target_pairs={{0,4},{4,8},{8,12},{12,16},{16,20},{20,24},{24,28},{1,5},{5,9},{9,... | collective-permute-start | bytes 589832 | tf_op jit(solution)/shard_map/ppermute | solution.py:47
  98.1 1.3 collective-permute-start.11
  99.4 0.0 collective-permute-done.6.refs_7_
  99.4 0.0 collective-permute-done.7.refs_8_
  99.4 1.1 prepare.2
  100.5 0.0 collective-permute-done.10.refs_7_
  100.5 4.2 %collective-permute-done.11.refs_8_ = f32[2,12,16,128]{3,2,1,0:T(8,128)S(1)} collective-permute-done((f32[2,12,16,128]{3,2,1,0:T(8,128)S(1)}, f32[2,12,16,128]{3,2,1,0:T(8,128)S(1)}, u32[]{:S(2)}, u32[]{:S(2)}) %collective-permute-start.11) | collective-permute-done | bytes 196640 | tf_op jit(solution)/shard_map/ppermute | solution.py:47
  104.7 6.0 %step.2 = (f32[2,16,16,128]{3,2,1,0:T(8,128)S(1)}, f32[2,16,8,128]{3,2,1,0:T(8,128)S(1)}, f32[2,16,8,128]{3,2,1,0:T(8,128)S(1)}, f32[32,128]{1,0:T(8,128)S(1)}) custom-call(f32[32,4,128]{2,1,0:T(4,128)S(1)} %all_to_all.10.refs_2_.table_ref.refs_0_, f32[9,32,4,8,128]{4,3,2,1,0:T(8,128)S(1)} %get-tuple-element.43.refs_1_, ...), custom_call_target="tpu_custom_call" | custom-call | tf_op jit(solution)/shard_map/step/pallas_call | solution.py:33
  110.7 3.4 %collective-permute-start.12 = (f32[2,16,8,128]{3,2,1,0:T(8,128)S(1)}, f32[2,16,8,128]{3,2,1,0:T(8,128)S(1)}, u32[]{:S(2)}, u32[]{:S(2)}) collective-permute-start(f32[2,16,8,128]{3,2,1,0:T(8,128)S(1)} %get-tuple-element.51), channel_id=1, source_target_pairs={{0,1},{1,2},{2,3},{4,5},{5,6},{6,7},{8,9},{9,10},{10,11},{12,13},{... | collective-permute-start | bytes 393224 | tf_op jit(solution)/shard_map/ppermute | solution.py:47
  114.1 1.3 collective-permute-start.13
  115.4 1.2 collective-permute-done.12.z_low.refs_5_
  116.6 4.4 %collective-permute-done.13.z_high.refs_6_ = f32[2,16,8,128]{3,2,1,0:T(8,128)S(1)} collective-permute-done((f32[2,16,8,128]{3,2,1,0:T(8,128)S(1)}, f32[2,16,8,128]{3,2,1,0:T(8,128)S(1)}, u32[]{:S(2)}, u32[]{:S(2)}) %collective-permute-start.13) | collective-permute-done | bytes 131104 | tf_op jit(solution)/shard_map/ppermute | solution.py:47
  121.0 4.9 %collective-permute-start.14 = (f32[2,12,16,128]{3,2,1,0:T(8,128)S(1)}, f32[2,12,16,128]{3,2,1,0:T(8,128)S(1)}, u32[]{:S(2)}, u32[]{:S(2)}) collective-permute-start(f32[2,12,16,128]{3,2,1,0:T(8,128)S(1)} %get-tuple-element.53), channel_id=1, source_target_pairs={{0,4},{4,8},{8,12},{12,16},{16,20},{20,24},{24,28},{1,5},{5,9},{9,... | collective-permute-start | bytes 589832 | tf_op jit(solution)/shard_map/ppermute | solution.py:47
  125.8 1.3 collective-permute-start.15
  127.1 1.0 prepare.3.refs_1_
  128.1 0.0 collective-permute-done.14.refs_7_
  128.2 1.8 %collective-permute-done.15.refs_8_ = f32[2,12,16,128]{3,2,1,0:T(8,128)S(1)} collective-permute-done((f32[2,12,16,128]{3,2,1,0:T(8,128)S(1)}, f32[2,12,16,128]{3,2,1,0:T(8,128)S(1)}, u32[]{:S(2)}, u32[]{:S(2)}) %collective-permute-start.15) | collective-permute-done | bytes 196640 | tf_op jit(solution)/shard_map/ppermute | solution.py:47
  129.9 6.3 %step.3 = (f32[16,16,128]{2,1,0:T(8,128)}, f32[16,16,128]{2,1,0:T(8,128)}, f32[32,128]{1,0:T(8,128)S(1)}) custom-call(f32[32,4,128]{2,1,0:T(4,128)S(1)} %all_to_all.10.refs_2_.table_ref.refs_0_, f32[9,32,4,8,128]{4,3,2,1,0:T(8,128)S(1)} %prepare.3.refs_1_, f32[5,32,4,8,128]{4,3,2,1,0:T(8,128)S(1)} %get-tuple-element.39.refs_1_.refs_2_, ...), custom_call_target="tpu_custom_call" | custom-call | tf_op jit(solution)/shard_map/step/pallas_call | solution.py:33
  136.3 16.1 %all_to_all.11 = f32[32,1,128]{2,1,0:T(1,128)S(1)} all-to-all(f32[32,1,128]{2,1,0:T(1,128)S(1)} %bitcast.7), channel_id=1, replica_groups=mesh['gx'=8,'gy'=4] {'gx','gy'}, dimensions={0} | all-to-all | bytes 32768 | tf_op jit(solution)/shard_map/all_to_all | solution.py:598
  152.4 0.1 reduce_sum.9
  152.5 0.6 reshape.9
  (2 shorter events, 0.1 us)
Async XLA Ops:
  0.6 16.0 %copy-start.7 = (f32[128]{0:T(128)S(1)}, f32[128]{0:T(128)}, u32[]{:S(2)}) copy-start(f32[128]{0:T(128)} %param.37) | copy-start | bytes 1540
  0.6 16.0 %copy-start.6 = (s32[128]{0:T(128)S(1)}, s32[128]{0:T(128)}, u32[]{:S(2)}) copy-start(s32[128]{0:T(128)} %param.36) | copy-start | bytes 1540
  0.7 16.0 %copy-start.5 = (s32[128]{0:T(128)S(1)}, s32[128]{0:T(128)}, u32[]{:S(2)}) copy-start(s32[128]{0:T(128)} %param.35) | copy-start | bytes 1540
  0.7 16.0 %copy-start.4 = (s32[2,3]{1,0:T(2,128)S(1)}, s32[2,3]{1,0:T(2,128)}, u32[]{:S(2)}) copy-start(s32[2,3]{1,0:T(2,128)} %control.1) | copy-start | bytes 76
  0.7 16.0 %copy-start.3 = (f32[2,3]{1,0:T(2,128)S(1)}, f32[2,3]{1,0:T(2,128)}, u32[]{:S(2)}) copy-start(f32[2,3]{1,0:T(2,128)} %bhp.1) | copy-start | bytes 76
  0.7 16.0 %copy-start.2 = (f32[2,3]{1,0:T(2,128)S(1)}, f32[2,3]{1,0:T(2,128)}, u32[]{:S(2)}) copy-start(f32[2,3]{1,0:T(2,128)} %rate.1) | copy-start | bytes 76
  7.4 54.8 %collective-permute-start = (f32[29,16,8,128]{3,2,1,0:T(8,128)}, f32[29,16,8,128]{3,2,1,0:T(8,128)S(1)}, u32[]{:S(2)}, u32[]{:S(2)}) collective-permute-start(f32[29,16,8,128]{3,2,1,0:T(8,128)} %get-tuple-element.32), channel_id=1, source_target_pairs={{0,1},{1,2},{2,3},{4,5},{5,6},{6,7},{8,9},{9,10},{10,11},{12,13},{... | collective-permute-start | bytes 5701640 | tf_op jit(solution)/shard_map/ppermute | solution.py:47
  12.4 49.7 %collective-permute-start.1 = (f32[29,16,8,128]{3,2,1,0:T(8,128)}, f32[29,16,8,128]{3,2,1,0:T(8,128)S(1)}, u32[]{:S(2)}, u32[]{:S(2)}) collective-permute-start(f32[29,16,8,128]{3,2,1,0:T(8,128)} %get-tuple-element.33), channel_id=1, source_target_pairs={{1,0},{2,1},{3,2},{5,4},{6,5},{7,6},{9,8},{10,9},{11,10},{13,12},{... | collective-permute-start | bytes 5701640 | tf_op jit(solution)/shard_map/ppermute | solution.py:47
  13.7 48.4 %collective-permute-start.2 = (f32[29,8,16,128]{3,2,1,0:T(8,128)}, f32[29,8,16,128]{3,2,1,0:T(8,128)S(1)}, u32[]{:S(2)}, u32[]{:S(2)}) collective-permute-start(f32[29,8,16,128]{3,2,1,0:T(8,128)} %get-tuple-element.34), channel_id=1, source_target_pairs={{0,4},{4,8},{8,12},{12,16},{16,20},{20,24},{24,28},{1,5},{5,9},{9,... | collective-permute-start | bytes 5701640 | tf_op jit(solution)/shard_map/ppermute | solution.py:47
  15.3 46.8 %collective-permute-start.3 = (f32[29,8,16,128]{3,2,1,0:T(8,128)}, f32[29,8,16,128]{3,2,1,0:T(8,128)S(1)}, u32[]{:S(2)}, u32[]{:S(2)}) collective-permute-start(f32[29,8,16,128]{3,2,1,0:T(8,128)} %get-tuple-element.35), channel_id=1, source_target_pairs={{4,0},{8,4},{12,8},{16,12},{20,16},{24,20},{28,24},{5,1},{9,5},{13... | collective-permute-start | bytes 5701640 | tf_op jit(solution)/shard_map/ppermute | solution.py:47
  16.7 0.7 copy-start.1
  62.3 14.4 %collective-permute-start.4 = (f32[11,4,16,128]{3,2,1,0:T(8,128)S(1)}, f32[11,4,16,128]{3,2,1,0:T(8,128)S(1)}, u32[]{:S(2)}, u32[]{:S(2)}) collective-permute-start(f32[11,4,16,128]{3,2,1,0:T(8,128)S(1)} %get-tuple-element.38), channel_id=1, source_target_pairs={{0,4},{4,8},{8,12},{12,16},{16,20},{20,24},{24,28},{1,5},{5,9},{9,... | collective-permute-start | bytes 1081352 | tf_op jit(solution)/shard_map/ppermute | solution.py:47
  63.8 12.8 %collective-permute-start.5 = (f32[11,4,16,128]{3,2,1,0:T(8,128)S(1)}, f32[11,4,16,128]{3,2,1,0:T(8,128)S(1)}, u32[]{:S(2)}, u32[]{:S(2)}) collective-permute-start(f32[11,4,16,128]{3,2,1,0:T(8,128)S(1)} %get-tuple-element.36._), channel_id=1, source_target_pairs={{4,0},{8,4},{12,8},{16,12},{20,16},{24,20},{28,24},{5,1},{9,5},{13... | collective-permute-start | bytes 1081352 | tf_op jit(solution)/shard_map/ppermute | solution.py:47
  71.2 5.5 %copy-start = (f32[29,16,16,128]{3,2,1,0:T(8,128)S(1)}, f32[29,16,16,128]{3,2,1,0:T(8,128)}, u32[]{:S(2)}) copy-start(f32[29,16,16,128]{3,2,1,0:T(8,128)} %get-tuple-element.37.refs_2_.refs_3_) | copy-start | bytes 11403268
  71.4 28.1 %collective-permute-start.6 = (f32[18,4,16,128]{3,2,1,0:T(8,128)S(1)}, f32[18,4,16,128]{3,2,1,0:T(8,128)S(1)}, u32[]{:S(2)}, u32[]{:S(2)}) collective-permute-start(f32[18,4,16,128]{3,2,1,0:T(8,128)S(1)} %get-tuple-element.40), channel_id=1, source_target_pairs={{0,4},{4,8},{8,12},{12,16},{16,20},{20,24},{24,28},{1,5},{5,9},{9,... | collective-permute-start | bytes 1769480 | tf_op jit(solution)/shard_map/ppermute | solution.py:47
  75.3 24.1 %collective-permute-start.7 = (f32[18,4,16,128]{3,2,1,0:T(8,128)S(1)}, f32[18,4,16,128]{3,2,1,0:T(8,128)S(1)}, u32[]{:S(2)}, u32[]{:S(2)}) collective-permute-start(f32[18,4,16,128]{3,2,1,0:T(8,128)S(1)} %get-tuple-element.41), channel_id=1, source_target_pairs={{4,0},{8,4},{12,8},{16,12},{20,16},{24,20},{28,24},{5,1},{9,5},{13... | collective-permute-start | bytes 1769480 | tf_op jit(solution)/shard_map/ppermute | solution.py:47
  83.8 6.8 %collective-permute-start.8 = (f32[2,16,8,128]{3,2,1,0:T(8,128)S(1)}, f32[2,16,8,128]{3,2,1,0:T(8,128)S(1)}, u32[]{:S(2)}, u32[]{:S(2)}) collective-permute-start(f32[2,16,8,128]{3,2,1,0:T(8,128)S(1)} %get-tuple-element.45), channel_id=1, source_target_pairs={{0,1},{1,2},{2,3},{4,5},{5,6},{6,7},{8,9},{9,10},{10,11},{12,13},{... | collective-permute-start | bytes 393224 | tf_op jit(solution)/shard_map/ppermute | solution.py:47
  88.1 7.2 %collective-permute-start.9 = (f32[2,16,8,128]{3,2,1,0:T(8,128)S(1)}, f32[2,16,8,128]{3,2,1,0:T(8,128)S(1)}, u32[]{:S(2)}, u32[]{:S(2)}) collective-permute-start(f32[2,16,8,128]{3,2,1,0:T(8,128)S(1)} %get-tuple-element.46), channel_id=1, source_target_pairs={{1,0},{2,1},{3,2},{5,4},{6,5},{7,6},{9,8},{10,9},{11,10},{13,12},{... | collective-permute-start | bytes 393224 | tf_op jit(solution)/shard_map/ppermute | solution.py:47
  95.3 5.2 %collective-permute-start.10 = (f32[2,12,16,128]{3,2,1,0:T(8,128)S(1)}, f32[2,12,16,128]{3,2,1,0:T(8,128)S(1)}, u32[]{:S(2)}, u32[]{:S(2)}) collective-permute-start(f32[2,12,16,128]{3,2,1,0:T(8,128)S(1)} %get-tuple-element.47), channel_id=1, source_target_pairs={{0,4},{4,8},{8,12},{12,16},{16,20},{20,24},{24,28},{1,5},{5,9},{9,... | collective-permute-start | bytes 589832 | tf_op jit(solution)/shard_map/ppermute | solution.py:47
  98.1 6.6 %collective-permute-start.11 = (f32[2,12,16,128]{3,2,1,0:T(8,128)S(1)}, f32[2,12,16,128]{3,2,1,0:T(8,128)S(1)}, u32[]{:S(2)}, u32[]{:S(2)}) collective-permute-start(f32[2,12,16,128]{3,2,1,0:T(8,128)S(1)} %get-tuple-element.48), channel_id=1, source_target_pairs={{4,0},{8,4},{12,8},{16,12},{20,16},{24,20},{28,24},{5,1},{9,5},{13... | collective-permute-start | bytes 589832 | tf_op jit(solution)/shard_map/ppermute | solution.py:47
  110.7 5.9 %collective-permute-start.12 = (f32[2,16,8,128]{3,2,1,0:T(8,128)S(1)}, f32[2,16,8,128]{3,2,1,0:T(8,128)S(1)}, u32[]{:S(2)}, u32[]{:S(2)}) collective-permute-start(f32[2,16,8,128]{3,2,1,0:T(8,128)S(1)} %get-tuple-element.51), channel_id=1, source_target_pairs={{0,1},{1,2},{2,3},{4,5},{5,6},{6,7},{8,9},{9,10},{10,11},{12,13},{... | collective-permute-start | bytes 393224 | tf_op jit(solution)/shard_map/ppermute | solution.py:47
  114.1 6.9 %collective-permute-start.13 = (f32[2,16,8,128]{3,2,1,0:T(8,128)S(1)}, f32[2,16,8,128]{3,2,1,0:T(8,128)S(1)}, u32[]{:S(2)}, u32[]{:S(2)}) collective-permute-start(f32[2,16,8,128]{3,2,1,0:T(8,128)S(1)} %get-tuple-element.52), channel_id=1, source_target_pairs={{1,0},{2,1},{3,2},{5,4},{6,5},{7,6},{9,8},{10,9},{11,10},{13,12},{... | collective-permute-start | bytes 393224 | tf_op jit(solution)/shard_map/ppermute | solution.py:47
  121.0 7.2 %collective-permute-start.14 = (f32[2,12,16,128]{3,2,1,0:T(8,128)S(1)}, f32[2,12,16,128]{3,2,1,0:T(8,128)S(1)}, u32[]{:S(2)}, u32[]{:S(2)}) collective-permute-start(f32[2,12,16,128]{3,2,1,0:T(8,128)S(1)} %get-tuple-element.53), channel_id=1, source_target_pairs={{0,4},{4,8},{8,12},{12,16},{16,20},{20,24},{24,28},{1,5},{5,9},{9,... | collective-permute-start | bytes 589832 | tf_op jit(solution)/shard_map/ppermute | solution.py:47
  125.8 4.1 %collective-permute-start.15 = (f32[2,12,16,128]{3,2,1,0:T(8,128)S(1)}, f32[2,12,16,128]{3,2,1,0:T(8,128)S(1)}, u32[]{:S(2)}, u32[]{:S(2)}) collective-permute-start(f32[2,12,16,128]{3,2,1,0:T(8,128)S(1)} %get-tuple-element.54), channel_id=1, source_target_pairs={{4,0},{8,4},{12,8},{16,12},{20,16},{24,20},{28,24},{5,1},{9,5},{13... | collective-permute-start | bytes 589832 | tf_op jit(solution)/shard_map/ppermute | solution.py:47

commit v5 on v4

--- a/solution.py
+++ b/solution.py
@@ -15,6 +15,7 @@
 HIGHEST = lax.Precision.HIGHEST
 F32 = jnp.float32
 BF16 = jnp.bfloat16
+FLOPS = 1e9
 
 VMEM = pl.BlockSpec(memory_space=pltpu.VMEM)
 ANY = pl.BlockSpec(memory_space=pl.ANY)
@@ -27,6 +28,16 @@
 
 def params(mib):
     return pltpu.CompilerParams(vmem_limit_bytes=mib * 1024 * 1024)
+
+
+TIMES = {"step_top": 7, "step": 6, "sources": 3, "prepare": 1.5}
+
+
+def estimate(name):
+    work = TIMES.get(name, 0.5)
+    return pl.CostEstimate(
+        flops=int(work * FLOPS), bytes_accessed=int(work * 3.0e6), transcendentals=0
+    )
 
 
 def call(kernel, ins, outs, name, mib, specs=None, scratch=()):
@@ -37,6 +48,7 @@
         out_shape=outs,
         scratch_shapes=list(scratch),
         compiler_params=params(mib),
+        cost_estimate=estimate(name),
         name=name,
     )(*ins)
 
@@ -49,9 +61,7 @@
 
 def load_kernel(leads, *refs):
     count = len(leads)
-    ins, (own, y_low, y_high, x_low, x_high, token), sems = refs[:count], refs[count:-1], refs[-1]
-    token[...] = jnp.zeros(token.shape, F32)
-    rx, ry = own.shape[1:3]
+    ins, (own, y_low, y_high, x_low, x_high), sems = refs[:count], refs[-6:-1], refs[-1]
     copies = [
         pltpu.make_async_copy(
             ins[n] if lead is None else ins[n].at[lead], own.at[n], sems.at[n]
@@ -60,30 +70,71 @@
     ]
     for c in copies:
         c.start()
-
-    def one(n):
-        y_low[n] = own[n, :, 0:H, :]
-        y_high[n] = own[n, :, ry - H :, :]
-        x_low[n] = own[n, 0:H]
-        x_high[n] = own[n, rx - H :]
-
-    for n, c in enumerate(copies):
+    for c in copies:
         c.wait()
-        one(n)
-
-
-def load(arrays, leads, dims):
+    y_edges(own, y_low, y_high)
+    x_edges(own, x_low, x_high)
+
+
+def y_edges(own, low, high):
+    ry = own.shape[2]
+
+    def one(n, _):
+        low[n] = own[n, :, 0:H, :]
+        high[n] = own[n, :, ry - H :, :]
+        return 0
+
+    lax.fori_loop(0, own.shape[0], one, 0)
+
+
+def x_edges(own, low, high):
+    rx = own.shape[1]
+
+    def one(n, _):
+        low[n] = own[n, 0:H]
+        high[n] = own[n, rx - H :]
+        return 0
+
+    lax.fori_loop(0, own.shape[0], one, 0)
+
+
+def load(arrays, leads, dims, after):
     n = len(leads)
     rx, ry, nz = dims
     return pl.pallas_call(
         functools.partial(load_kernel, leads),
-        in_specs=[HBM] * n,
-        out_specs=[VMEM] * 6,
-        out_shape=[sds(n, *dims)] + [sds(n, rx, H, nz)] * 2 + [sds(n, H, ry, nz)] * 2
-        + [sds(8, 128)],
+        in_specs=[HBM] * n + [ANY] * len(after),
+        out_specs=[VMEM] * 5,
+        out_shape=[sds(n, *dims)] + [sds(n, rx, H, nz)] * 2 + [sds(n, H, ry, nz)] * 2,
         scratch_shapes=[pltpu.SemaphoreType.DMA((n,))],
         name="load",
-    )(*arrays)
+    )(*arrays, *after)
+
+
+def more_kernel(leads, *refs):
+    count = len(leads)
+    ins, (own, y_low, y_high), sems = refs[:count], refs[-4:-1], refs[-1]
+    copies = [
+        pltpu.make_async_copy(
+            ins[n] if lead is None else ins[n].at[lead], own.at[n], sems.at[n]
+        )
+        for n, lead in enumerate(leads)
+    ]
+    for c in copies:
+        c.start()
+    for c in copies:
+        c.wait()
+    y_edges(own, y_low, y_high)
+
+
+def more(arrays, leads, dims, after):
+    n = len(leads)
+    rx, ry, nz = dims
+    return call(
+        functools.partial(more_kernel, leads), list(arrays) + list(after),
+        [sds(n, *dims)] + [sds(n, rx, H, nz)] * 2, "more", 4,
+        [ANY] * (n + len(after)), [pltpu.SemaphoreType.DMA((n,))],
+    )
 
 
 def fold(rows_of, high):
@@ -114,29 +165,30 @@
                 put(side, int(high), t, tile)
 
 
-def corner_kernel(first, z_low, z_high, *refs):
+def corner_kernel(z_low, z_high, *refs):
     outs = refs[-2:]
 
     def one(n, _):
         def put(side, y, t, tile):
             outs[side][n, t, y * H : (y + 1) * H, :] = tile
 
-        corner_tiles(n + first, z_low, z_high, put)
-        return 0
-
-    lax.fori_loop(0, outs[0].shape[0], one, 0)
-
-
-def pack_corners(name, z_low, z_high, first, count, after):
-    nz = z_low.shape[-1]
+        corner_tiles(n, z_low, z_high, put)
+        return 0
+
+    lax.fori_loop(0, z_low.shape[0], one, 0)
+
+
+def pack_corners(name, z_low, z_high, after):
+    count, _, _, nz = z_low.shape
     return call(
-        functools.partial(corner_kernel, first), [z_low, z_high, *after],
+        corner_kernel, [z_low, z_high, *after],
         [sds(count, 4, 2 * H, nz)] * 2, name, 4,
         [VMEM] * 2 + [ANY] * len(after),
     )
 
 
-def widen_kernel(own, z_low, z_high, *outs):
+def widen_kernel(own, z_low, z_high, *refs):
+    outs = refs[-2:]
     rx = own.shape[1]
 
     def one(n, _):
@@ -151,22 +203,30 @@
     lax.fori_loop(0, own.shape[0], one, 0)
 
 
-def widen(own, z_low, z_high):
+def widen(own, z_low, z_high, after=()):
     count, rx, ry, nz = own.shape
-    return call(widen_kernel, [own, z_low, z_high], [sds(count, H + 4, ry, nz)] * 2, "widen", 4)
-
-
-def table_kernel(steps, rate, bhp, control, perf_well, perf_cell, perf_wi, _, out):
+    return call(
+        widen_kernel, [own, z_low, z_high, *after], [sds(count, H + 4, ry, nz)] * 2, "widen", 4,
+        [VMEM] * 3 + [ANY] * len(after),
+    )
+
+
+def table_kernel(steps, *refs):
+    ins, out, held, sems = refs[:6], refs[6], refs[7:13], refs[13]
+    copies = [pltpu.make_async_copy(i, h, sems.at[n]) for n, (i, h) in enumerate(zip(ins, held))]
+    for c in copies:
+        c.start()
+    for c in copies:
+        c.wait()
+    rate, bhp, control, perf_well, perf_cell, perf_wi = [h[...] for h in held]
     wells = rate.shape[0]
-    effective = jnp.where(control[...] == 1, rate[...], bhp[...])
+    effective = jnp.where(control == 1, rate, bhp)
     lane = lax.broadcasted_iota(jnp.int32, (1, 128), 1)
     row = jnp.zeros((1, 128), F32)
     for u in range(wells):
         for n in range(steps):
             row = jnp.where(lane == u * steps + n, effective[u : u + 1, n : n + 1], row)
-    mine = jnp.concatenate(
-        [row, perf_cell[...].astype(F32), perf_well[...].astype(F32), perf_wi[...]]
-    )
+    mine = jnp.concatenate([row, perf_cell.astype(F32), perf_well.astype(F32), perf_wi])
     out[...] = jnp.broadcast_to(mine[None], out.shape)
 
 
@@ -176,7 +236,7 @@
     return x, y, n_x, n_y
 
 
-def source_kernel(steps, wells, ry, table_ref, _, src_ref):
+def source_kernel(wanted, steps, wells, ry, table_ref, _, src_ref):
     here_x, here_y, n_x, n_y = spot()
     count = table_ref.shape[0]
     rx = src_ref.shape[1] // 3
@@ -203,7 +263,7 @@
         )
         by_row = jnp.where(row_iota == (cell >> 7), 1.0, 0.0).astype(BF16)
         in_lane = sub == (cell & 127)
-        for step in range(steps):
+        for place, step in enumerate(wanted):
             value = jnp.zeros((1, 128), F32)
             for u in range(wells):
                 c = u * steps + step
@@ -219,7 +279,7 @@
                 )
                 part = add if part is None else part + add
             src_ref[
-                step, pl.ds(pl.multiple_of(dx * rx, rx), rx),
+                place, pl.ds(pl.multiple_of(dx * rx, rx), rx),
                 pl.ds(pl.multiple_of(dy * ry, ry), ry), :,
             ] = part.reshape(rx, ry, 128)
         return 0
@@ -245,21 +305,20 @@
     return pltpu.roll(value, by, 2)
 
 
-def fill(dst, own, z_low, z_high, x_edges, corners, base, first=0, corner_first=0):
+def fill(dst, own, z_low, z_high, x_edges, corners, base):
     count, (rx, ry, nz) = dst.shape[0], own.shape[1:]
 
     def one(n, _):
-        m = n + first
-        dst[n, H : H + rx, 0:H, :] = z_low[m]
-        dst[n, H : H + rx, H : H + ry, :] = own[m]
-        dst[n, H : H + rx, H + ry : 2 * H + ry, :] = z_high[m]
+        dst[n, H : H + rx, 0:H, :] = z_low[n]
+        dst[n, H : H + rx, H : H + ry, :] = own[n]
+        dst[n, H : H + rx, H + ry : 2 * H + ry, :] = z_high[n]
         for side in (0, 1):
             at = side * (H + rx)
-            dst[n, at : at + H, H : H + ry, :] = x_edges[side][m, 0:H]
+            dst[n, at : at + H, H : H + ry, :] = x_edges[side][n, 0:H]
             for y in (0, 1):
                 to = y * (H + ry)
                 for t in range(4):
-                    tile = corners[side][n + corner_first, base + t, y * H : (y + 1) * H, :]
+                    tile = corners[side][n, base + t, y * H : (y + 1) * H, :]
                     near, far = unfold(tile, t + 1, y == 1)
                     for dx, row in ((t + 1, near), (7 - t, far)):
                         x = H - dx if side == 0 else H + rx + dx - 1
@@ -430,7 +489,7 @@
         )
         geo[WS, x] = total
         s_a, r_a, p, frac, r_b, q, m, _ = coefficients(
-            raw, 3, src_ref, step, x, total, rx - H, ry - H
+            raw, 3, src_ref, 0, x, total, rx - H, ry - H
         )
         coef[SA, x] = s_a
         coef[RA, x] = r_a
@@ -448,15 +507,15 @@
     finish(False, step, steps, wells, lin, own.at[7], table_ref, None, outs)
 
 
-def prepare_kernel(step, first, corner_first, with_acc, *refs):
-    src_ref, geo, own, z_low, z_high, x_low, x_high, c_low, c_high = refs[:9]
+def prepare_kernel(step, with_acc, *refs):
+    src_ref, geo, own, z_low, z_high, x_low, x_high = refs[:7]
     if with_acc:
-        coef, acc_out, raw = refs[9:]
+        coef, acc_out, raw = refs[7:]
     else:
-        acc, coef, raw = refs[9:]
+        acc, coef, raw = refs[7:]
     rx, ry, nz = own.shape[1:]
     ex = rx + 2 * H
-    fill(raw, own, z_low, z_high, (x_low, x_high), (c_low, c_high), 0, first, corner_first)
+    fill(raw, own, z_low, z_high, (x_low, x_high), (x_low, x_high), H)
 
     def prepare(x, _):
         s_a, r_a, p, frac, r_b, q, m, s_b = coefficients(
@@ -482,7 +541,7 @@
     lax.fori_loop(0, ex - 1, prepare, 0)
 
 
-def sweep_kernel(last, step, frac_at, steps, wells, *refs):
+def sweep_kernel(last, step, steps, wells, *refs):
     table_ref, coef, geo, own, lam, z_low, z_high, x_low, x_high, before = refs[:10]
     outs = refs[10:-6]
     now, fa0, fb0, fa1, fb1, lin = refs[-6:]
@@ -506,7 +565,7 @@
             return now[0, x] if n == RA else now[1, x] if n == RB else coef[n, x]
 
     sweeps(Joined(), geo, ((fa0, fb0), (fa1, fb1)), lin, 1, ex)
-    finish(last, step, steps, wells, lin, own.at[frac_at], table_ref, before, outs)
+    finish(last, step, steps, wells, lin, own.at[4], table_ref, before, outs)
 
 
 def local(
@@ -527,34 +586,40 @@
     arrays = [trans_x, trans_y, trans_z] + own
     leads = [None] * 3 + [top] * 8
     split = len(arrays)
-    places = {}
-    for step in reversed(range(top)):
-        places[step] = len(arrays)
-        arrays += own
-        leads += [step] * 8
-        if step == top - 1:
-            arrays += [acc_p, acc_s]
-            leads += [None] * 2
-    blocks, y_low, y_high, e_low, e_high, token = load(arrays, leads, dims)
-
+    small = [rate_mis, bhp_mis, control] + [p[None] for p in (perf_well, perf_cell, perf_wi)]
+    mine = pl.pallas_call(
+        functools.partial(table_kernel, steps),
+        in_specs=[HBM] * 6,
+        out_specs=VMEM,
+        out_shape=sds(devices, 4, 128),
+        scratch_shapes=[pltpu.VMEM(p.shape, p.dtype) for p in small]
+        + [pltpu.SemaphoreType.DMA((6,))],
+        name="table",
+    )(*small)
+    table = lax.all_to_all(mine, ("gx", "gy"), 0, 0, tiled=True)
+
+    blocks, y_low, y_high, e_low, e_high = load(arrays, leads, dims, (table,))
     z_got = sent(y_low, y_high, "gy")
     x_got = sent(e_low, e_high, "gx")
 
-    mine = call(
-        functools.partial(table_kernel, steps),
-        [rate_mis, bhp_mis, control] + [p[None] for p in (perf_well, perf_cell, perf_wi)]
-        + [token], [sds(devices, 4, 128)], "table", 4, [VMEM] * 6 + [ANY],
-    )[0]
-    table = lax.all_to_all(mine, ("gx", "gy"), 0, 0, tiled=True)
-
-    corners = pack_corners("corners", *z_got, 0, split, (*x_got, table))
+    def sources(wanted, after):
+        return call(
+            functools.partial(source_kernel, wanted, steps, wells, ry), [table, after],
+            [sds(len(wanted), 3 * rx, 3 * ry, nz)], "sources", 8, [VMEM, ANY],
+        )[0]
+
+    def others(step, after):
+        with_acc = step == top - 1
+        arrays = own + ([acc_p, acc_s] if with_acc else [])
+        leads = [step] * 8 + ([None] * 2 if with_acc else [])
+        held, low, high = more(arrays, leads, dims, (after,))
+        return held, sent(low, high, "gy"), low
+
+    ready = {top - 1: others(top - 1, blocks)}
+    corners = pack_corners("corners", *z_got, (*x_got, ready[top - 1][2]))
     c_got = sent(*corners, "gx")
-    src = call(
-        functools.partial(source_kernel, steps, wells, ry), [table, corners[0]],
-        [sds(steps, 3 * rx, 3 * ry, nz)], "sources", 8, [VMEM, ANY],
-    )[0]
-    rest = len(arrays) - split
-    m_c = sent(*pack_corners("corners_more", *z_got, split, rest, (src,)), "gx")
+    src = sources((top,), corners[0])
+    sides = {top - 1: sent(*widen(*ready[top - 1][:1], *ready[top - 1][1], (src,)), "gx")}
 
     ext = (ex, V, 8, nz)
     lam_out = [sds(2, rx, ry, nz), sds(2, rx, H, nz), sds(2, rx, H, nz)]
@@ -569,13 +634,18 @@
     )
 
     acc = None
+    src = None
     for step in reversed(range(top)):
         last = step == 0
         with_acc = step == top - 1
-        at = places[step]
+        if src is None:
+            src = sources(tuple(range(top)), low)
+        held, m_z, _ = ready[step]
+        if step not in sides:
+            sides[step] = sent(*widen(held, *m_z, (low,)), "gx")
         made = call(
-            functools.partial(prepare_kernel, step, at, at - split, with_acc),
-            [src, geo, blocks, *z_got, *x_got, *m_c] + ([] if with_acc else [acc]),
+            functools.partial(prepare_kernel, step, with_acc),
+            [src, geo, held, *m_z, *sides[step]] + ([] if with_acc else [acc]),
             [sds(9, *ext)] + ([sds(2, *ext)] if with_acc else []), "prepare", 8,
             scratch=[pltpu.VMEM((10 if with_acc else 8, ex, ey, nz), F32)],
         )
@@ -583,12 +653,14 @@
         if with_acc:
             acc = made[1]
 
+        if not last:
+            ready[step - 1] = others(step - 1, low)
         l_z = sent(low, high, "gy")
         l_x = sent(*widen(lam, *l_z), "gx")
         outs = [sds(rx, ry, nz)] * 2 if last else lam_out
         outs = call(
-            functools.partial(sweep_kernel, last, step, at + 4, steps, wells),
-            [table, coef, geo, blocks, lam, *l_z, *l_x, dense],
+            functools.partial(sweep_kernel, last, step, steps, wells),
+            [table, coef, geo, held, lam, *l_z, *l_x, dense],
             outs + [well_out], "step", 8, scratch=[pltpu.VMEM((2, *ext), F32)] + fields,
         )
         dense = outs[-1]

time: 154 us -> 151 us (0.981)
  blocking collectives: 60.8 us -> 28.7 us
  starting transfers between devices: 37.8 us -> 51.1 us
  waiting for transfers between devices: 17.4 us -> 26 us
  Pallas kernels: 34.6 us -> 40.9 us
    all_to_all x1, blocking collectives: 44.7 us -> 14.9 us  [local(): table = lax.all_to_all(mine, ('gx', 'gy'), 0, 0, tiled=True)]
    ppermute x16 -> x22, starting transfers between devices: 37.8 us -> 51.1 us  [shifted(): return lax.ppermute(value, axis, pairs)]
    ppermute x16 -> x22, waiting for transfers between devices: 17.4 us -> 26 us  [shifted(): return lax.ppermute(value, axis, pairs)]
    pallas_call x11 -> x14, Pallas kernels: 28 us -> 35.6 us  [call(): pl.pallas_call(kernel, in_specs=specs or [VMEM] * len(ins), out_specs=[VM...]
    all_to_all x1, blocking collectives: 16.1 us -> 13.8 us  [local(): parts = lax.all_to_all(dense[:, None, :], ('gx', 'gy'), 0, 0, tiled=True)]
    pallas_call x1 -> x2, Pallas kernels: 6.68 us -> 5.37 us  [the longest x1 3.76 us: load(): pl.pallas_call(functools.partial(load_kernel, leads), in_specs=[HBM] * n...]
  transfers between devices with their start and end apart: 16 -> 22, of which waited for: 6 -> 8; matrix products, arithmetic and copies ran while one was open for 0% -> 0% of each run, Pallas kernels for 10% -> 19%
where the time goes in v5:
time: 151 us; the launch traced here: 150 us
  starting transfers between devices  51.1 us (34%)
  Pallas kernels  40.9 us (27%)
  blocking collectives  28.7 us (19%)
  waiting for transfers between devices  26 us (17%)
  local copies, waits for them, and re-layouts  2.07 us (1%)
    ppermute x22, starting transfers between devices, shifted(): return lax.ppermute(value, axis, pairs)  51.1 us
    pallas_call x14, Pallas kernels, call(): pl.pallas_call(kernel, in_specs=specs or [VMEM] * len(ins), out_specs=[VM...  35.6 us
    ppermute x22, waiting for transfers between devices, shifted(): return lax.ppermute(value, axis, pairs)  26 us
    all_to_all x1, blocking collectives, local(): table = lax.all_to_all(mine, ('gx', 'gy'), 0, 0, tiled=True)  14.9 us
    all_to_all x1, blocking collectives, local(): parts = lax.all_to_all(dense[:, None, :], ('gx', 'gy'), 0, 0, tiled=True)  13.8 us
    pallas_call x1, Pallas kernels, load(): pl.pallas_call(functools.partial(load_kernel, leads), in_specs=[HBM] * n...  3.76 us
  transfers between devices with their start and end apart: 22, of which 8 were waited for; matrix products, arithmetic and copies ran while one was open for 0% of the time, Pallas kernels for 19%

profile of v5, /device:TPU:0, one launch (start us, length us, event | category | flops | bytes accessed | tf_op | source)
XLA Modules:
  0.0 150.0 jit_solution(17945816587383257746)
XLA Ops:
  0.6 0.0 copy-start.6
  0.6 0.0 copy-start.7
  0.7 0.0 copy-start
  0.7 0.0 copy-start.1
  0.7 0.0 copy-start.2
  0.7 0.0 copy-start.3
  0.7 0.0 copy-start.4
  0.7 0.0 copy-start.5
  0.8 1.6 %table.1 = f32[32,4,128]{2,1,0:T(4,128)} custom-call(f32[2,3]{1,0:T(2,128)} %refs_0_.4, f32[2,3]{1,0:T(2,128)} %refs_1_.4, s32[2,3]{1,0:T(2,128)} %refs_2_.4, s32[1,128]{1,0:T(1,128)} %bitcast.8, s32[1,128]{1,0:T(1,128)} %bitcast.9, f32[1,128]{1,0:T(1,128)} %bitcast.10), custom_call_target="tpu_custom_call" | custom-call | tf_op jit(solution)/shard_map/table/pallas_call | solution.py:590
  2.4 14.9 %all_to_all.10.refs_11_.table_ref.refs_0_ = f32[32,4,128]{2,1,0:T(4,128)} all-to-all(f32[32,4,128]{2,1,0:T(4,128)} %table.1), channel_id=1, replica_groups=mesh['gx'=8,'gy'=4] {'gx','gy'}, dimensions={0} | all-to-all | bytes 131072 | tf_op jit(solution)/shard_map/all_to_all | solution.py:599
  17.3 3.8 %load.1 = (f32[11,16,16,128]{3,2,1,0:T(8,128)}, f32[11,16,8,128]{3,2,1,0:T(8,128)}, f32[11,16,8,128]{3,2,1,0:T(8,128)}, f32[11,8,16,128]{3,2,1,0:T(8,128)}, f32[11,8,16,128]{3,2,1,0:T(8,128)}) custom-call(f32[16,16,128]{2,1,0:T(8,128)} %refs_0_.5, f32[16,16,128]{2,1,0:T(8,128)} %refs_1_.5, f32[16,16,128]{2,1,0:T(8,128)} %refs_2_.5, ...), custom_call_target="tpu_custom_call" | custom-call | tf_op jit(solution)/shard_map/load/pallas_call | solution.py:104
  21.1 2.2 %collective-permute-start = (f32[11,16,8,128]{3,2,1,0:T(8,128)}, f32[11,16,8,128]{3,2,1,0:T(8,128)S(1)}, u32[]{:S(2)}, u32[]{:S(2)}) collective-permute-start(f32[11,16,8,128]{3,2,1,0:T(8,128)} %get-tuple-element.38), channel_id=1, source_target_pairs={{0,1},{1,2},{2,3},{4,5},{5,6},{6,7},{8,9},{9,10},{10,11},{12,13},{... | collective-permute-start | bytes 2162696 | tf_op jit(solution)/shard_map/ppermute | solution.py:59
  23.2 1.3 collective-permute-start.1
  24.5 1.8 %collective-permute-start.2 = (f32[11,8,16,128]{3,2,1,0:T(8,128)}, f32[11,8,16,128]{3,2,1,0:T(8,128)S(1)}, u32[]{:S(2)}, u32[]{:S(2)}) collective-permute-start(f32[11,8,16,128]{3,2,1,0:T(8,128)} %get-tuple-element.40), channel_id=1, source_target_pairs={{0,4},{4,8},{8,12},{12,16},{16,20},{20,24},{24,28},{1,5},{5,9},{9,... | collective-permute-start | bytes 2162696 | tf_op jit(solution)/shard_map/ppermute | solution.py:59
  26.3 1.3 collective-permute-start.3
  27.7 1.4 copy-done.8
  29.1 1.9 %more.2 = (f32[10,16,16,128]{3,2,1,0:T(8,128)S(1)}, f32[10,16,8,128]{3,2,1,0:T(8,128)S(1)}, f32[10,16,8,128]{3,2,1,0:T(8,128)S(1)}) custom-call(f32[3,16,16,128]{3,2,1,0:T(8,128)S(1)} %copy-done, f32[3,16,16,128]{3,2,1,0:T(8,128)S(1)} %copy-done.1, f32[3,16,16,128]{3,2,1,0:T(8,128)S(1)} %copy-done.2, f32[3,16,16,128]{3,2,1,0:T(8,128)S(1)} %copy-done.3, ...), custom_call_target="tpu_custom_call" | custom-call | flops 500000000 | bytes 1500000 | tf_op jit(solution)/shard_map/more/pallas_call | solution.py:44
  31.0 1.4 collective-permute-start.9
  32.4 6.8 %collective-permute-done.z_low.refs_3_ = f32[11,16,8,128]{3,2,1,0:T(8,128)S(1)} collective-permute-done((f32[11,16,8,128]{3,2,1,0:T(8,128)}, f32[11,16,8,128]{3,2,1,0:T(8,128)S(1)}, u32[]{:S(2)}, u32[]{:S(2)}) %collective-permute-start) | collective-permute-done | bytes 720928 | tf_op jit(solution)/shard_map/ppermute | solution.py:59
  39.2 4.3 %collective-permute-start.8 = (f32[10,16,8,128]{3,2,1,0:T(8,128)S(1)}, f32[10,16,8,128]{3,2,1,0:T(8,128)S(1)}, u32[]{:S(2)}, u32[]{:S(2)}) collective-permute-start(f32[10,16,8,128]{3,2,1,0:T(8,128)S(1)} %get-tuple-element.52), channel_id=1, source_target_pairs={{0,1},{1,2},{2,3},{4,5},{5,6},{6,7},{8,9},{9,10},{10,11},{12,13},{... | collective-permute-start | bytes 1966088 | tf_op jit(solution)/shard_map/ppermute | solution.py:59
  43.5 0.9 collective-permute-done.1.z_high.refs_4_
  44.4 0.1 corners.1
  44.5 1.3 collective-permute-start.5
  45.8 3.5 %collective-permute-start.4 = (f32[11,4,16,128]{3,2,1,0:T(8,128)S(1)}, f32[11,4,16,128]{3,2,1,0:T(8,128)S(1)}, u32[]{:S(2)}, u32[]{:S(2)}) collective-permute-start(f32[11,4,16,128]{3,2,1,0:T(8,128)S(1)} %get-tuple-element.45), channel_id=1, source_target_pairs={{0,4},{4,8},{8,12},{12,16},{16,20},{20,24},{24,28},{1,5},{5,9},{9,... | collective-permute-start | bytes 1081352 | tf_op jit(solution)/shard_map/ppermute | solution.py:59
  49.3 5.0 %sources.2.refs_1_.refs_0_ = f32[1,48,48,128]{3,2,1,0:T(8,128)S(1)} custom-call(f32[32,4,128]{2,1,0:T(4,128)S(1)} %copy-done.10, f32[11,4,16,128]{3,2,1,0:T(8,128)S(1)} %get-tuple-element.44._), custom_call_target="tpu_custom_call" | custom-call | flops 3000000000 | bytes 9000000 | tf_op jit(solution)/shard_map/sources/pallas_call | solution.py:44
  54.3 3.0 %collective-permute-done.9.z_high.refs_4_ = f32[10,16,8,128]{3,2,1,0:T(8,128)S(1)} collective-permute-done((f32[10,16,8,128]{3,2,1,0:T(8,128)S(1)}, f32[10,16,8,128]{3,2,1,0:T(8,128)S(1)}, u32[]{:S(2)}, u32[]{:S(2)}) %collective-permute-start.9) | collective-permute-done | bytes 655392 | tf_op jit(solution)/shard_map/ppermute | solution.py:59
  57.3 0.0 collective-permute-done.8.z_low.refs_3_
  57.3 0.2 widen.4
  57.5 1.4 collective-permute-start.10
  58.8 1.3 collective-permute-start.11
  60.1 0.0 collective-permute-done.5.refs_8_
  60.1 0.0 collective-permute-done.4.refs_7_
  60.1 7.1 %step_top.1 = (f32[5,32,4,8,128]{4,3,2,1,0:T(8,128)S(1)}, f32[2,16,16,128]{3,2,1,0:T(8,128)S(1)}, f32[2,16,8,128]{3,2,1,0:T(8,128)S(1)}, f32[2,16,8,128]{3,2,1,0:T(8,128)S(1)}, f32[32,128]{1,0:T(8,128)S(1)}) custom-call(f32[32,4,128]{2,1,0:T(4,128)S(1)} %copy-done.10, f32[1,48,48,128]{3,2,1,0:T(8,128)S(1)} %sources.2.refs_1_.refs_0_, ...), custom_call_target="tpu_custom_call" | custom-call | flops 7000000000 | bytes 21000000 | tf_op jit(solution)/shard_map/step_top/pallas_call | solution.py:44
  67.3 3.9 %collective-permute-start.12 = (f32[2,16,8,128]{3,2,1,0:T(8,128)S(1)}, f32[2,16,8,128]{3,2,1,0:T(8,128)S(1)}, u32[]{:S(2)}, u32[]{:S(2)}) collective-permute-start(f32[2,16,8,128]{3,2,1,0:T(8,128)S(1)} %get-tuple-element.57), channel_id=1, source_target_pairs={{0,1},{1,2},{2,3},{4,5},{5,6},{6,7},{8,9},{9,10},{10,11},{12,13},{... | collective-permute-start | bytes 393224 | tf_op jit(solution)/shard_map/ppermute | solution.py:59
  71.2 1.3 collective-permute-start.13
  72.5 1.5 %more.3 = (f32[8,16,16,128]{3,2,1,0:T(8,128)S(1)}, f32[8,16,8,128]{3,2,1,0:T(8,128)S(1)}, f32[8,16,8,128]{3,2,1,0:T(8,128)S(1)}) custom-call(f32[3,16,16,128]{3,2,1,0:T(8,128)S(1)} %copy-done, f32[3,16,16,128]{3,2,1,0:T(8,128)S(1)} %copy-done.1, f32[3,16,16,128]{3,2,1,0:T(8,128)S(1)} %copy-done.2, f32[3,16,16,128]{3,2,1,0:T(8,128)S(1)} %copy-done.3, ...), custom_call_target="tpu_custom_call" | custom-call | flops 500000000 | bytes 1500000 | tf_op jit(solution)/shard_map/more/pallas_call | solution.py:44
  74.0 4.6 %collective-permute-start.6 = (f32[8,16,8,128]{3,2,1,0:T(8,128)S(1)}, f32[8,16,8,128]{3,2,1,0:T(8,128)S(1)}, u32[]{:S(2)}, u32[]{:S(2)}) collective-permute-start(f32[8,16,8,128]{3,2,1,0:T(8,128)S(1)} %get-tuple-element.49), channel_id=1, source_target_pairs={{0,1},{1,2},{2,3},{4,5},{5,6},{6,7},{8,9},{9,10},{10,11},{12,13},{... | collective-permute-start | bytes 1572872 | tf_op jit(solution)/shard_map/ppermute | solution.py:59
  78.6 0.0 collective-permute-done.12.z_low.refs_5_
  78.6 0.2 collective-permute-done.13.z_high.refs_6_
  78.9 2.7 %collective-permute-start.14 = (f32[2,12,16,128]{3,2,1,0:T(8,128)S(1)}, f32[2,12,16,128]{3,2,1,0:T(8,128)S(1)}, u32[]{:S(2)}, u32[]{:S(2)}) collective-permute-start(f32[2,12,16,128]{3,2,1,0:T(8,128)S(1)} %get-tuple-element.58), channel_id=1, source_target_pairs={{0,4},{4,8},{8,12},{12,16},{16,20},{20,24},{24,28},{1,5},{5,9},{9,... | collective-permute-start | bytes 589832 | tf_op jit(solution)/shard_map/ppermute | solution.py:59
  81.7 1.3 collective-permute-start.15
  83.0 5.2 %sources.3.refs_0_ = f32[2,48,48,128]{3,2,1,0:T(8,128)S(1)} custom-call(f32[32,4,128]{2,1,0:T(4,128)S(1)} %copy-done.10, f32[2,16,8,128]{3,2,1,0:T(8,128)S(1)} %get-tuple-element.46._.refs_8_), custom_call_target="tpu_custom_call" | custom-call | flops 3000000000 | bytes 9000000 | tf_op jit(solution)/shard_map/sources/pallas_call | solution.py:44
  88.2 0.0 collective-permute-done.10.refs_5_
  88.2 1.3 collective-permute-start.7
  89.5 0.0 collective-permute-done.11.refs_6_
  89.5 1.1 prepare.2
  90.6 0.0 collective-permute-done.15.refs_8_
  90.6 6.0 %step.2 = (f32[2,16,16,128]{3,2,1,0:T(8,128)S(1)}, f32[2,16,8,128]{3,2,1,0:T(8,128)S(1)}, f32[2,16,8,128]{3,2,1,0:T(8,128)S(1)}, f32[32,128]{1,0:T(8,128)S(1)}) custom-call(f32[32,4,128]{2,1,0:T(4,128)S(1)} %copy-done.10, f32[9,32,4,8,128]{4,3,2,1,0:T(8,128)S(1)} %get-tuple-element.55.refs_1_, f32[5,32,4,8,128]{4,3,2,1,0:T(8,128)S(1)} %get-tuple-element.47.refs_1_.refs_2_, ...), custom_call_target="tpu_custom_call" | custom-call | flops 6000000000 | bytes 18000000 | tf_op jit(solution)/shard_map/step/pallas_call | solution.py:44
  96.6 6.0 %collective-permute-done.7.z_high.refs_4_ = f32[8,16,8,128]{3,2,1,0:T(8,128)S(1)} collective-permute-done((f32[8,16,8,128]{3,2,1,0:T(8,128)S(1)}, f32[8,16,8,128]{3,2,1,0:T(8,128)S(1)}, u32[]{:S(2)}, u32[]{:S(2)}) %collective-permute-start.7) | collective-permute-done | bytes 524320 | tf_op jit(solution)/shard_map/ppermute | solution.py:59
  102.6 0.1 widen.6
  102.8 4.0 %collective-permute-start.16 = (f32[8,12,16,128]{3,2,1,0:T(8,128)S(1)}, f32[8,12,16,128]{3,2,1,0:T(8,128)S(1)}, u32[]{:S(2)}, u32[]{:S(2)}) collective-permute-start(f32[8,12,16,128]{3,2,1,0:T(8,128)S(1)} %get-tuple-element.62), channel_id=1, source_target_pairs={{0,4},{4,8},{8,12},{12,16},{16,20},{20,24},{24,28},{1,5},{5,9},{9,... | collective-permute-start | bytes 2359304 | tf_op jit(solution)/shard_map/ppermute | solution.py:59
  106.8 1.3 collective-permute-start.17
  108.1 2.2 %collective-permute-start.18 = (f32[2,16,8,128]{3,2,1,0:T(8,128)S(1)}, f32[2,16,8,128]{3,2,1,0:T(8,128)S(1)}, u32[]{:S(2)}, u32[]{:S(2)}) collective-permute-start(f32[2,16,8,128]{3,2,1,0:T(8,128)S(1)} %get-tuple-element.66), channel_id=1, source_target_pairs={{0,1},{1,2},{2,3},{4,5},{5,6},{6,7},{8,9},{9,10},{10,11},{12,13},{... | collective-permute-start | bytes 393224 | tf_op jit(solution)/shard_map/ppermute | solution.py:59
  110.4 1.3 collective-permute-start.19
  111.7 1.2 collective-permute-done.18.z_low.refs_5_
  112.9 4.4 %collective-permute-done.19.z_high.refs_6_ = f32[2,16,8,128]{3,2,1,0:T(8,128)S(1)} collective-permute-done((f32[2,16,8,128]{3,2,1,0:T(8,128)S(1)}, f32[2,16,8,128]{3,2,1,0:T(8,128)S(1)}, u32[]{:S(2)}, u32[]{:S(2)}) %collective-permute-start.19) | collective-permute-done | bytes 131104 | tf_op jit(solution)/shard_map/ppermute | solution.py:59
  117.3 5.9 %collective-permute-start.20 = (f32[2,12,16,128]{3,2,1,0:T(8,128)S(1)}, f32[2,12,16,128]{3,2,1,0:T(8,128)S(1)}, u32[]{:S(2)}, u32[]{:S(2)}) collective-permute-start(f32[2,12,16,128]{3,2,1,0:T(8,128)S(1)} %get-tuple-element.67), channel_id=1, source_target_pairs={{0,4},{4,8},{8,12},{12,16},{16,20},{20,24},{24,28},{1,5},{5,9},{9,... | collective-permute-start | bytes 589832 | tf_op jit(solution)/shard_map/ppermute | solution.py:59
  123.2 1.5 collective-permute-start.21
  124.7 1.0 prepare.3.refs_1_
  125.7 3.5 %collective-permute-done.21.refs_8_ = f32[2,12,16,128]{3,2,1,0:T(8,128)S(1)} collective-permute-done((f32[2,12,16,128]{3,2,1,0:T(8,128)S(1)}, f32[2,12,16,128]{3,2,1,0:T(8,128)S(1)}, u32[]{:S(2)}, u32[]{:S(2)}) %collective-permute-start.21) | collective-permute-done | bytes 196640 | tf_op jit(solution)/shard_map/ppermute | solution.py:59
  129.2 6.3 %step.3 = (f32[16,16,128]{2,1,0:T(8,128)}, f32[16,16,128]{2,1,0:T(8,128)}, f32[32,128]{1,0:T(8,128)S(1)}) custom-call(f32[32,4,128]{2,1,0:T(4,128)S(1)} %copy-done.10, f32[9,32,4,8,128]{4,3,2,1,0:T(8,128)S(1)} %prepare.3.refs_1_, f32[5,32,4,8,128]{4,3,2,1,0:T(8,128)S(1)} %get-tuple-element.47.refs_1_.refs_2_, ...), custom_call_target="tpu_custom_call" | custom-call | flops 6000000000 | bytes 18000000 | tf_op jit(solution)/shard_map/step/pallas_call | solution.py:44
  135.5 13.8 %all_to_all.11 = f32[32,1,128]{2,1,0:T(1,128)S(1)} all-to-all(f32[32,1,128]{2,1,0:T(1,128)S(1)} %bitcast.7), channel_id=1, replica_groups=mesh['gx'=8,'gy'=4] {'gx','gy'}, dimensions={0} | all-to-all | bytes 32768 | tf_op jit(solution)/shard_map/all_to_all | solution.py:670
  149.3 0.1 reduce_sum.9
  149.3 0.6 reshape.9
  (26 shorter events, 0.1 us)
Async XLA Ops:
  0.6 27.0 %copy-start.6 = (f32[3,16,16,128]{3,2,1,0:T(8,128)S(1)}, f32[3,16,16,128]{3,2,1,0:T(8,128)}, u32[]{:S(2)}) copy-start(f32[3,16,16,128]{3,2,1,0:T(8,128)} %refs_6_.5) | copy-start | bytes 1179652
  0.6 27.0 %copy-start.7 = (f32[3,16,16,128]{3,2,1,0:T(8,128)S(1)}, f32[3,16,16,128]{3,2,1,0:T(8,128)}, u32[]{:S(2)}) copy-start(f32[3,16,16,128]{3,2,1,0:T(8,128)} %refs_7_.5) | copy-start | bytes 1179652
  0.7 27.0 %copy-start = (f32[3,16,16,128]{3,2,1,0:T(8,128)S(1)}, f32[3,16,16,128]{3,2,1,0:T(8,128)}, u32[]{:S(2)}) copy-start(f32[3,16,16,128]{3,2,1,0:T(8,128)} %refs_0_.7) | copy-start | bytes 1179652
  0.7 27.0 %copy-start.1 = (f32[3,16,16,128]{3,2,1,0:T(8,128)S(1)}, f32[3,16,16,128]{3,2,1,0:T(8,128)}, u32[]{:S(2)}) copy-start(f32[3,16,16,128]{3,2,1,0:T(8,128)} %refs_1_.7) | copy-start | bytes 1179652
  0.7 27.0 %copy-start.2 = (f32[3,16,16,128]{3,2,1,0:T(8,128)S(1)}, f32[3,16,16,128]{3,2,1,0:T(8,128)}, u32[]{:S(2)}) copy-start(f32[3,16,16,128]{3,2,1,0:T(8,128)} %refs_2_.7) | copy-start | bytes 1179652
  0.7 27.0 %copy-start.3 = (f32[3,16,16,128]{3,2,1,0:T(8,128)S(1)}, f32[3,16,16,128]{3,2,1,0:T(8,128)}, u32[]{:S(2)}) copy-start(f32[3,16,16,128]{3,2,1,0:T(8,128)} %refs_3_.5) | copy-start | bytes 1179652
  0.7 27.0 %copy-start.4 = (f32[3,16,16,128]{3,2,1,0:T(8,128)S(1)}, f32[3,16,16,128]{3,2,1,0:T(8,128)}, u32[]{:S(2)}) copy-start(f32[3,16,16,128]{3,2,1,0:T(8,128)} %refs_4_.5) | copy-start | bytes 1179652
  0.7 27.0 %copy-start.5 = (f32[3,16,16,128]{3,2,1,0:T(8,128)S(1)}, f32[3,16,16,128]{3,2,1,0:T(8,128)}, u32[]{:S(2)}) copy-start(f32[3,16,16,128]{3,2,1,0:T(8,128)} %refs_5_.5) | copy-start | bytes 1179652
  0.7 27.0 %copy-start.11 = (f32[16,16,128]{2,1,0:T(8,128)S(1)}, f32[16,16,128]{2,1,0:T(8,128)}, u32[]{:S(2)}) copy-start(f32[16,16,128]{2,1,0:T(8,128)} %refs_8_.3) | copy-start | bytes 393220
  0.7 27.0 %copy-start.12 = (f32[16,16,128]{2,1,0:T(8,128)S(1)}, f32[16,16,128]{2,1,0:T(8,128)}, u32[]{:S(2)}) copy-start(f32[16,16,128]{2,1,0:T(8,128)} %refs_9_.3) | copy-start | bytes 393220
  21.1 18.1 %collective-permute-start = (f32[11,16,8,128]{3,2,1,0:T(8,128)}, f32[11,16,8,128]{3,2,1,0:T(8,128)S(1)}, u32[]{:S(2)}, u32[]{:S(2)}) collective-permute-start(f32[11,16,8,128]{3,2,1,0:T(8,128)} %get-tuple-element.38), channel_id=1, source_target_pairs={{0,1},{1,2},{2,3},{4,5},{5,6},{6,7},{8,9},{9,10},{10,11},{12,13},{... | collective-permute-start | bytes 2162696 | tf_op jit(solution)/shard_map/ppermute | solution.py:59
  23.2 21.1 %collective-permute-start.1 = (f32[11,16,8,128]{3,2,1,0:T(8,128)}, f32[11,16,8,128]{3,2,1,0:T(8,128)S(1)}, u32[]{:S(2)}, u32[]{:S(2)}) collective-permute-start(f32[11,16,8,128]{3,2,1,0:T(8,128)} %get-tuple-element.39), channel_id=1, source_target_pairs={{1,0},{2,1},{3,2},{5,4},{6,5},{7,6},{9,8},{10,9},{11,10},{13,12},{... | collective-permute-start | bytes 2162696 | tf_op jit(solution)/shard_map/ppermute | solution.py:59
  24.5 19.8 %collective-permute-start.2 = (f32[11,8,16,128]{3,2,1,0:T(8,128)}, f32[11,8,16,128]{3,2,1,0:T(8,128)S(1)}, u32[]{:S(2)}, u32[]{:S(2)}) collective-permute-start(f32[11,8,16,128]{3,2,1,0:T(8,128)} %get-tuple-element.40), channel_id=1, source_target_pairs={{0,4},{4,8},{8,12},{12,16},{16,20},{20,24},{24,28},{1,5},{5,9},{9,... | collective-permute-start | bytes 2162696 | tf_op jit(solution)/shard_map/ppermute | solution.py:59
  26.3 18.0 %collective-permute-start.3 = (f32[11,8,16,128]{3,2,1,0:T(8,128)}, f32[11,8,16,128]{3,2,1,0:T(8,128)S(1)}, u32[]{:S(2)}, u32[]{:S(2)}) collective-permute-start(f32[11,8,16,128]{3,2,1,0:T(8,128)} %get-tuple-element.41), channel_id=1, source_target_pairs={{4,0},{8,4},{12,8},{16,12},{20,16},{24,20},{28,24},{5,1},{9,5},{13... | collective-permute-start | bytes 2162696 | tf_op jit(solution)/shard_map/ppermute | solution.py:59
  27.7 1.4 copy-start.8
  31.0 18.3 %copy-start.10 = (f32[32,4,128]{2,1,0:T(4,128)S(1)}, f32[32,4,128]{2,1,0:T(4,128)}, u32[]{:S(2)}) copy-start(f32[32,4,128]{2,1,0:T(4,128)} %all_to_all.10.refs_11_.table_ref.refs_0_) | copy-start | bytes 196612
  31.0 26.3 %collective-permute-start.9 = (f32[10,16,8,128]{3,2,1,0:T(8,128)S(1)}, f32[10,16,8,128]{3,2,1,0:T(8,128)S(1)}, u32[]{:S(2)}, u32[]{:S(2)}) collective-permute-start(f32[10,16,8,128]{3,2,1,0:T(8,128)S(1)} %get-tuple-element.43.refs_2_), channel_id=1, source_target_pairs={{1,0},{2,1},{3,2},{5,4},{6,5},{7,6},{9,8},{10,9},{11,10},{13,12},{... | collective-permute-start | bytes 1966088 | tf_op jit(solution)/shard_map/ppermute | solution.py:59
  39.2 18.1 %collective-permute-start.8 = (f32[10,16,8,128]{3,2,1,0:T(8,128)S(1)}, f32[10,16,8,128]{3,2,1,0:T(8,128)S(1)}, u32[]{:S(2)}, u32[]{:S(2)}) collective-permute-start(f32[10,16,8,128]{3,2,1,0:T(8,128)S(1)} %get-tuple-element.52), channel_id=1, source_target_pairs={{0,1},{1,2},{2,3},{4,5},{5,6},{6,7},{8,9},{9,10},{10,11},{12,13},{... | collective-permute-start | bytes 1966088 | tf_op jit(solution)/shard_map/ppermute | solution.py:59
  44.5 15.6 %collective-permute-start.5 = (f32[11,4,16,128]{3,2,1,0:T(8,128)S(1)}, f32[11,4,16,128]{3,2,1,0:T(8,128)S(1)}, u32[]{:S(2)}, u32[]{:S(2)}) collective-permute-start(f32[11,4,16,128]{3,2,1,0:T(8,128)S(1)} %get-tuple-element.44._), channel_id=1, source_target_pairs={{4,0},{8,4},{12,8},{16,12},{20,16},{24,20},{28,24},{5,1},{9,5},{13... | collective-permute-start | bytes 1081352 | tf_op jit(solution)/shard_map/ppermute | solution.py:59
  45.8 14.3 %collective-permute-start.4 = (f32[11,4,16,128]{3,2,1,0:T(8,128)S(1)}, f32[11,4,16,128]{3,2,1,0:T(8,128)S(1)}, u32[]{:S(2)}, u32[]{:S(2)}) collective-permute-start(f32[11,4,16,128]{3,2,1,0:T(8,128)S(1)} %get-tuple-element.45), channel_id=1, source_target_pairs={{0,4},{4,8},{8,12},{12,16},{16,20},{20,24},{24,28},{1,5},{5,9},{9,... | collective-permute-start | bytes 1081352 | tf_op jit(solution)/shard_map/ppermute | solution.py:59
  54.3 5.8 %copy-start.9 = (f32[11,16,16,128]{3,2,1,0:T(8,128)S(1)}, f32[11,16,16,128]{3,2,1,0:T(8,128)}, u32[]{:S(2)}) copy-start(f32[11,16,16,128]{3,2,1,0:T(8,128)} %get-tuple-element.42.refs_10_.refs_2_) | copy-start | bytes 4325380
  57.5 30.7 %collective-permute-start.10 = (f32[10,12,16,128]{3,2,1,0:T(8,128)S(1)}, f32[10,12,16,128]{3,2,1,0:T(8,128)S(1)}, u32[]{:S(2)}, u32[]{:S(2)}) collective-permute-start(f32[10,12,16,128]{3,2,1,0:T(8,128)S(1)} %get-tuple-element.53), channel_id=1, source_target_pairs={{0,4},{4,8},{8,12},{12,16},{16,20},{20,24},{24,28},{1,5},{5,9},{9,... | collective-permute-start | bytes 2949128 | tf_op jit(solution)/shard_map/ppermute | solution.py:59
  58.8 30.7 %collective-permute-start.11 = (f32[10,12,16,128]{3,2,1,0:T(8,128)S(1)}, f32[10,12,16,128]{3,2,1,0:T(8,128)S(1)}, u32[]{:S(2)}, u32[]{:S(2)}) collective-permute-start(f32[10,12,16,128]{3,2,1,0:T(8,128)S(1)} %get-tuple-element.54), channel_id=1, source_target_pairs={{4,0},{8,4},{12,8},{16,12},{20,16},{24,20},{28,24},{5,1},{9,5},{13... | collective-permute-start | bytes 2949128 | tf_op jit(solution)/shard_map/ppermute | solution.py:59
  67.3 11.3 %collective-permute-start.12 = (f32[2,16,8,128]{3,2,1,0:T(8,128)S(1)}, f32[2,16,8,128]{3,2,1,0:T(8,128)S(1)}, u32[]{:S(2)}, u32[]{:S(2)}) collective-permute-start(f32[2,16,8,128]{3,2,1,0:T(8,128)S(1)} %get-tuple-element.57), channel_id=1, source_target_pairs={{0,1},{1,2},{2,3},{4,5},{5,6},{6,7},{8,9},{9,10},{10,11},{12,13},{... | collective-permute-start | bytes 393224 | tf_op jit(solution)/shard_map/ppermute | solution.py:59
  71.2 7.7 %collective-permute-start.13 = (f32[2,16,8,128]{3,2,1,0:T(8,128)S(1)}, f32[2,16,8,128]{3,2,1,0:T(8,128)S(1)}, u32[]{:S(2)}, u32[]{:S(2)}) collective-permute-start(f32[2,16,8,128]{3,2,1,0:T(8,128)S(1)} %get-tuple-element.46._.refs_8_), channel_id=1, source_target_pairs={{1,0},{2,1},{3,2},{5,4},{6,5},{7,6},{9,8},{10,9},{11,10},{13,12},{... | collective-permute-start | bytes 393224 | tf_op jit(solution)/shard_map/ppermute | solution.py:59
  74.0 22.6 %collective-permute-start.6 = (f32[8,16,8,128]{3,2,1,0:T(8,128)S(1)}, f32[8,16,8,128]{3,2,1,0:T(8,128)S(1)}, u32[]{:S(2)}, u32[]{:S(2)}) collective-permute-start(f32[8,16,8,128]{3,2,1,0:T(8,128)S(1)} %get-tuple-element.49), channel_id=1, source_target_pairs={{0,1},{1,2},{2,3},{4,5},{5,6},{6,7},{8,9},{9,10},{10,11},{12,13},{... | collective-permute-start | bytes 1572872 | tf_op jit(solution)/shard_map/ppermute | solution.py:59
  78.9 11.7 %collective-permute-start.14 = (f32[2,12,16,128]{3,2,1,0:T(8,128)S(1)}, f32[2,12,16,128]{3,2,1,0:T(8,128)S(1)}, u32[]{:S(2)}, u32[]{:S(2)}) collective-permute-start(f32[2,12,16,128]{3,2,1,0:T(8,128)S(1)} %get-tuple-element.58), channel_id=1, source_target_pairs={{0,4},{4,8},{8,12},{12,16},{16,20},{20,24},{24,28},{1,5},{5,9},{9,... | collective-permute-start | bytes 589832 | tf_op jit(solution)/shard_map/ppermute | solution.py:59
  81.7 9.0 %collective-permute-start.15 = (f32[2,12,16,128]{3,2,1,0:T(8,128)S(1)}, f32[2,12,16,128]{3,2,1,0:T(8,128)S(1)}, u32[]{:S(2)}, u32[]{:S(2)}) collective-permute-start(f32[2,12,16,128]{3,2,1,0:T(8,128)S(1)} %get-tuple-element.59), channel_id=1, source_target_pairs={{4,0},{8,4},{12,8},{16,12},{20,16},{24,20},{28,24},{5,1},{9,5},{13... | collective-permute-start | bytes 589832 | tf_op jit(solution)/shard_map/ppermute | solution.py:59
  88.2 14.4 %collective-permute-start.7 = (f32[8,16,8,128]{3,2,1,0:T(8,128)S(1)}, f32[8,16,8,128]{3,2,1,0:T(8,128)S(1)}, u32[]{:S(2)}, u32[]{:S(2)}) collective-permute-start(f32[8,16,8,128]{3,2,1,0:T(8,128)S(1)} %get-tuple-element.50), channel_id=1, source_target_pairs={{1,0},{2,1},{3,2},{5,4},{6,5},{7,6},{9,8},{10,9},{11,10},{13,12},{... | collective-permute-start | bytes 1572872 | tf_op jit(solution)/shard_map/ppermute | solution.py:59
  102.8 21.9 %collective-permute-start.16 = (f32[8,12,16,128]{3,2,1,0:T(8,128)S(1)}, f32[8,12,16,128]{3,2,1,0:T(8,128)S(1)}, u32[]{:S(2)}, u32[]{:S(2)}) collective-permute-start(f32[8,12,16,128]{3,2,1,0:T(8,128)S(1)} %get-tuple-element.62), channel_id=1, source_target_pairs={{0,4},{4,8},{8,12},{12,16},{16,20},{20,24},{24,28},{1,5},{5,9},{9,... | collective-permute-start | bytes 2359304 | tf_op jit(solution)/shard_map/ppermute | solution.py:59
  106.8 17.8 %collective-permute-start.17 = (f32[8,12,16,128]{3,2,1,0:T(8,128)S(1)}, f32[8,12,16,128]{3,2,1,0:T(8,128)S(1)}, u32[]{:S(2)}, u32[]{:S(2)}) collective-permute-start(f32[8,12,16,128]{3,2,1,0:T(8,128)S(1)} %get-tuple-element.63), channel_id=1, source_target_pairs={{4,0},{8,4},{12,8},{16,12},{20,16},{24,20},{28,24},{5,1},{9,5},{13... | collective-permute-start | bytes 2359304 | tf_op jit(solution)/shard_map/ppermute | solution.py:59
  108.1 4.7 %collective-permute-start.18 = (f32[2,16,8,128]{3,2,1,0:T(8,128)S(1)}, f32[2,16,8,128]{3,2,1,0:T(8,128)S(1)}, u32[]{:S(2)}, u32[]{:S(2)}) collective-permute-start(f32[2,16,8,128]{3,2,1,0:T(8,128)S(1)} %get-tuple-element.66), channel_id=1, source_target_pairs={{0,1},{1,2},{2,3},{4,5},{5,6},{6,7},{8,9},{9,10},{10,11},{12,13},{... | collective-permute-start | bytes 393224 | tf_op jit(solution)/shard_map/ppermute | solution.py:59
  110.4 6.9 %collective-permute-start.19 = (f32[2,16,8,128]{3,2,1,0:T(8,128)S(1)}, f32[2,16,8,128]{3,2,1,0:T(8,128)S(1)}, u32[]{:S(2)}, u32[]{:S(2)}) collective-permute-start(f32[2,16,8,128]{3,2,1,0:T(8,128)S(1)} %get-tuple-element.61.refs_0_), channel_id=1, source_target_pairs={{1,0},{2,1},{3,2},{5,4},{6,5},{7,6},{9,8},{10,9},{11,10},{13,12},{... | collective-permute-start | bytes 393224 | tf_op jit(solution)/shard_map/ppermute | solution.py:59
  117.3 8.4 %collective-permute-start.20 = (f32[2,12,16,128]{3,2,1,0:T(8,128)S(1)}, f32[2,12,16,128]{3,2,1,0:T(8,128)S(1)}, u32[]{:S(2)}, u32[]{:S(2)}) collective-permute-start(f32[2,12,16,128]{3,2,1,0:T(8,128)S(1)} %get-tuple-element.67), channel_id=1, source_target_pairs={{0,4},{4,8},{8,12},{12,16},{16,20},{20,24},{24,28},{1,5},{5,9},{9,... | collective-permute-start | bytes 589832 | tf_op jit(solution)/shard_map/ppermute | solution.py:59
  123.2 6.0 %collective-permute-start.21 = (f32[2,12,16,128]{3,2,1,0:T(8,128)S(1)}, f32[2,12,16,128]{3,2,1,0:T(8,128)S(1)}, u32[]{:S(2)}, u32[]{:S(2)}) collective-permute-start(f32[2,12,16,128]{3,2,1,0:T(8,128)S(1)} %get-tuple-element.68), channel_id=1, source_target_pairs={{4,0},{8,4},{12,8},{16,12},{20,16},{24,20},{28,24},{5,1},{9,5},{13... | collective-permute-start | bytes 589832 | tf_op jit(solution)/shard_map/ppermute | solution.py:59

commit v6 on v5

--- a/solution.py
+++ b/solution.py
@@ -61,7 +61,8 @@
 
 def load_kernel(leads, *refs):
     count = len(leads)
-    ins, (own, y_low, y_high, x_low, x_high), sems = refs[:count], refs[-6:-1], refs[-1]
+    ins, (own, y_low, y_high, token), sems = refs[:count], refs[-5:-1], refs[-1]
+    token[...] = jnp.zeros(token.shape, F32)
     copies = [
         pltpu.make_async_copy(
             ins[n] if lead is None else ins[n].at[lead], own.at[n], sems.at[n]
@@ -73,7 +74,6 @@
     for c in copies:
         c.wait()
     y_edges(own, y_low, y_high)
-    x_edges(own, x_low, x_high)
 
 
 def y_edges(own, low, high):
@@ -82,17 +82,6 @@
     def one(n, _):
         low[n] = own[n, :, 0:H, :]
         high[n] = own[n, :, ry - H :, :]
-        return 0
-
-    lax.fori_loop(0, own.shape[0], one, 0)
-
-
-def x_edges(own, low, high):
-    rx = own.shape[1]
-
-    def one(n, _):
-        low[n] = own[n, 0:H]
-        high[n] = own[n, rx - H :]
         return 0
 
     lax.fori_loop(0, own.shape[0], one, 0)
@@ -104,36 +93,35 @@
     return pl.pallas_call(
         functools.partial(load_kernel, leads),
         in_specs=[HBM] * n + [ANY] * len(after),
-        out_specs=[VMEM] * 5,
-        out_shape=[sds(n, *dims)] + [sds(n, rx, H, nz)] * 2 + [sds(n, H, ry, nz)] * 2,
+        out_specs=[VMEM] * 4,
+        out_shape=[sds(n, *dims)] + [sds(n, rx, H, nz)] * 2 + [sds(8, 128)],
         scratch_shapes=[pltpu.SemaphoreType.DMA((n,))],
         name="load",
     )(*arrays, *after)
 
 
-def more_kernel(leads, *refs):
-    count = len(leads)
-    ins, (own, y_low, y_high), sems = refs[:count], refs[-4:-1], refs[-1]
-    copies = [
-        pltpu.make_async_copy(
-            ins[n] if lead is None else ins[n].at[lead], own.at[n], sems.at[n]
-        )
-        for n, lead in enumerate(leads)
-    ]
-    for c in copies:
-        c.start()
-    for c in copies:
-        c.wait()
-    y_edges(own, y_low, y_high)
-
-
-def more(arrays, leads, dims, after):
-    n = len(leads)
+def more_kernel(plan, count, *refs):
+    ins, holders, (y_low, y_high) = refs[:count], refs[count + 1 : -2], refs[-2:]
+    rx, ry = y_low.shape[1], holders[0].shape[2]
+
+    def row(x, _):
+        for n, (i, lead, h, m) in enumerate(plan):
+            value = ins[i][x] if lead is None else ins[i][lead, x]
+            holders[h][m, x] = value
+            y_low[n, x] = value[0:H]
+            y_high[n, x] = value[ry - H :]
+        return 0
+
+    lax.fori_loop(0, rx, row, 0)
+
+
+def more(arrays, plan, sizes, dims, after):
+    n = len(plan)
     rx, ry, nz = dims
     return call(
-        functools.partial(more_kernel, leads), list(arrays) + list(after),
-        [sds(n, *dims)] + [sds(n, rx, H, nz)] * 2, "more", 4,
-        [ANY] * (n + len(after)), [pltpu.SemaphoreType.DMA((n,))],
+        functools.partial(more_kernel, plan, len(arrays)), list(arrays) + [after],
+        [sds(m, *dims) for m in sizes] + [sds(n, rx, H, nz)] * 2, "more", 4,
+        [VMEM] * len(arrays) + [ANY],
     )
 
 
@@ -165,29 +153,7 @@
                 put(side, int(high), t, tile)
 
 
-def corner_kernel(z_low, z_high, *refs):
-    outs = refs[-2:]
-
-    def one(n, _):
-        def put(side, y, t, tile):
-            outs[side][n, t, y * H : (y + 1) * H, :] = tile
-
-        corner_tiles(n, z_low, z_high, put)
-        return 0
-
-    lax.fori_loop(0, z_low.shape[0], one, 0)
-
-
-def pack_corners(name, z_low, z_high, after):
-    count, _, _, nz = z_low.shape
-    return call(
-        corner_kernel, [z_low, z_high, *after],
-        [sds(count, 4, 2 * H, nz)] * 2, name, 4,
-        [VMEM] * 2 + [ANY] * len(after),
-    )
-
-
-def widen_kernel(own, z_low, z_high, *refs):
+def widen_kernel(first, own, z_low, z_high, *refs):
     outs = refs[-2:]
     rx = own.shape[1]
 
@@ -195,7 +161,7 @@
         def put(side, y, t, tile):
             outs[side][n, H + t, y * H : (y + 1) * H, :] = tile
 
-        corner_tiles(n, z_low, z_high, put)
+        corner_tiles(n + first, z_low, z_high, put)
         outs[0][n, 0:H] = own[n, 0:H]
         outs[1][n, 0:H] = own[n, rx - H :]
         return 0
@@ -203,10 +169,11 @@
     lax.fori_loop(0, own.shape[0], one, 0)
 
 
-def widen(own, z_low, z_high, after=()):
+def widen(own, z_low, z_high, after=(), first=0):
     count, rx, ry, nz = own.shape
     return call(
-        widen_kernel, [own, z_low, z_high, *after], [sds(count, H + 4, ry, nz)] * 2, "widen", 4,
+        functools.partial(widen_kernel, first), [own, z_low, z_high, *after],
+        [sds(count, H + 4, ry, nz)] * 2, "widen", 4,
         [VMEM] * 3 + [ANY] * len(after),
     )
 
@@ -236,61 +203,59 @@
     return x, y, n_x, n_y
 
 
-def source_kernel(wanted, steps, wells, ry, table_ref, _, src_ref):
+def source_kernel(steps, wells, table_ref, _, src_ref):
     here_x, here_y, n_x, n_y = spot()
     count = table_ref.shape[0]
-    rx = src_ref.shape[1] // 3
+    rx, ry = src_ref.shape[1] - 2 * H, src_ref.shape[2] - 2 * H
     of_wells = table_ref[:, 0, :]
+    columns = [
+        jnp.broadcast_to(of_wells[:, c : c + 1], (count, 128)) for c in range(wells * steps)
+    ]
     owner_iota = lax.broadcasted_iota(jnp.int32, (count, 128), 0)
     sub = lax.broadcasted_iota(jnp.int32, (128, 128), 0)
-    row_iota = lax.broadcasted_iota(jnp.int32, (rx * ry, 128), 0)
-
-    def block(k, _):
-        dx = k // 3
-        dy = k - 3 * dx
-        at_x, at_y = here_x + dx - 1, here_y + dy - 1
-        inside = (at_x >= 0) & (at_x < n_x) & (at_y >= 0) & (at_y < n_y)
-        slot = table_ref[jnp.where(inside, at_x * n_y + at_y, 0)]
-        cell = slot[1:2, :].astype(jnp.int32)
-        well = slot[2:3, :].astype(jnp.int32)
-        wi = slot[3:4, :] * inside.astype(F32)
-        owner = well // wells
-        within = well - owner * wells
-        hot = jnp.where(owner_iota == owner, 1.0, 0.0).astype(F32)
-        found = lax.dot_general(
-            of_wells, hot, (((0,), (0,)), ((), ())), precision=HIGHEST,
-            preferred_element_type=F32,
-        )
-        by_row = jnp.where(row_iota == (cell >> 7), 1.0, 0.0).astype(BF16)
-        in_lane = sub == (cell & 127)
-        for place, step in enumerate(wanted):
-            value = jnp.zeros((1, 128), F32)
-            for u in range(wells):
-                c = u * steps + step
-                value = value + jnp.where(within == u, found[c : c + 1, :], 0.0)
-            value = value * wi
-            part = None
-            for _ in range(3):
-                piece = value.astype(BF16)
-                value = value - piece.astype(F32)
-                by_lane = jnp.where(in_lane, piece.astype(F32), 0.0).astype(BF16)
-                add = lax.dot_general(
-                    by_row, by_lane, (((1,), (1,)), ((), ())), preferred_element_type=F32
+
+    def spans(length):
+        return ((0, H, length - H), (H, length, 0), (H + length, H, 0))
+
+    for dx, (x0, size_x, from_x) in enumerate(spans(rx)):
+        for dy, (y0, size_y, from_y) in enumerate(spans(ry)):
+            at_x, at_y = here_x + dx - 1, here_y + dy - 1
+            inside = (at_x >= 0) & (at_x < n_x) & (at_y >= 0) & (at_y < n_y)
+            slot = table_ref[jnp.where(inside, at_x * n_y + at_y, 0)]
+            cell = slot[1:2, :].astype(jnp.int32)
+            well = slot[2:3, :].astype(jnp.int32)
+            wi = slot[3:4, :] * inside.astype(F32)
+            owner = well // wells
+            within = well - owner * wells
+            hot = owner_iota == owner
+            in_lane = sub == (cell & 127)
+            pieces = []
+            for step in range(steps):
+                chosen = columns[step]
+                for u in range(1, wells):
+                    chosen = jnp.where(within == u, columns[u * steps + step], chosen)
+                value = jnp.sum(jnp.where(hot, chosen, 0.0), axis=0, keepdims=True) * wi
+                high = value.astype(BF16).astype(F32)
+                for piece in (high, value - high):
+                    pieces.append(jnp.where(in_lane, piece, 0.0).astype(BF16))
+            xi = lax.broadcasted_iota(jnp.int32, (size_x, size_y, 128), 0) + from_x
+            yi = lax.broadcasted_iota(jnp.int32, (size_x, size_y, 128), 1) + from_y
+            target = (xi * ry + yi).reshape(size_x * size_y, 128)
+            by_row = jnp.where(target == (cell >> 7), 1.0, 0.0).astype(BF16)
+            found = lax.dot_general(
+                by_row, jnp.concatenate(pieces), (((1,), (1,)), ((), ())),
+                preferred_element_type=F32,
+            )
+            for step in range(steps):
+                part = found[:, step * 256 : step * 256 + 128]
+                part = part + found[:, step * 256 + 128 : step * 256 + 256]
+                src_ref[step, x0 : x0 + size_x, y0 : y0 + size_y, :] = part.reshape(
+                    size_x, size_y, 128
                 )
-                part = add if part is None else part + add
-            src_ref[
-                place, pl.ds(pl.multiple_of(dx * rx, rx), rx),
-                pl.ds(pl.multiple_of(dy * ry, ry), ry), :,
-            ] = part.reshape(rx, ry, 128)
-        return 0
-
-    lax.fori_loop(0, 9, block, 0)
-
-
-def by_v(ref, lead, x, offset=0):
-    return jnp.stack(
-        [ref[(*lead, x, pl.ds(offset + v, 8, stride=V), slice(None))] for v in range(V)]
-    )
+
+
+def by_v(ref, lead, x):
+    return jnp.stack([ref[(*lead, x, pl.ds(v, 8, stride=V), slice(None))] for v in range(V)])
 
 
 def up_v(value):
@@ -305,20 +270,20 @@
     return pltpu.roll(value, by, 2)
 
 
-def fill(dst, own, z_low, z_high, x_edges, corners, base):
+def fill(dst, own, z_low, z_high, sides, first=0):
     count, (rx, ry, nz) = dst.shape[0], own.shape[1:]
 
     def one(n, _):
-        dst[n, H : H + rx, 0:H, :] = z_low[n]
+        dst[n, H : H + rx, 0:H, :] = z_low[n + first]
         dst[n, H : H + rx, H : H + ry, :] = own[n]
-        dst[n, H : H + rx, H + ry : 2 * H + ry, :] = z_high[n]
+        dst[n, H : H + rx, H + ry : 2 * H + ry, :] = z_high[n + first]
         for side in (0, 1):
             at = side * (H + rx)
-            dst[n, at : at + H, H : H + ry, :] = x_edges[side][n, 0:H]
+            dst[n, at : at + H, H : H + ry, :] = sides[side][n, 0:H]
             for y in (0, 1):
                 to = y * (H + ry)
                 for t in range(4):
-                    tile = corners[side][n, base + t, y * H : (y + 1) * H, :]
+                    tile = sides[side][n, H + t, y * H : (y + 1) * H, :]
                     near, far = unfold(tile, t + 1, y == 1)
                     for dx, row in ((t + 1, near), (7 - t, far)):
                         x = H - dx if side == 0 else H + rx + dx - 1
@@ -334,13 +299,13 @@
 TX, TY, TZ, TU, WS = range(5)
 
 
-def coefficients(raw, base, src_ref, step, x, total, src_x, src_y):
+def coefficients(raw, base, src_ref, step, x, total):
     c_pp, c_ss, c_ps, c_sp, frac, mob, g_p, g_s = [by_v(raw, (base + n,), x) for n in range(8)]
     den_a = c_pp + total
     den_b = c_ss + mob * total
     s_a = jnp.where(den_a > 0, OMEGA / den_a, 0.0)
     s_b = jnp.where(den_b > 0, OMEGA / den_b, 0.0)
-    r_a = g_p + by_v(src_ref, (step,), x + src_x, src_y)
+    r_a = g_p + by_v(src_ref, (step,), x)
     return s_a, r_a, c_sp + frac * total, frac, s_b * g_s, s_b * c_ps, s_b * mob, s_b
 
 
@@ -450,13 +415,13 @@
 
 
 def first_kernel(step, steps, wells, *refs):
-    table_ref, src_ref, own, z_low, z_high, x_low, x_high, c_low, c_high = refs[:9]
-    geo = refs[9]
-    outs = refs[10:14]
-    raw, coef, fa0, fb0, fa1, fb1, lin = refs[14:]
+    table_ref, src_ref, own, z_low, z_high, x_low, x_high = refs[:7]
+    geo = refs[7]
+    outs = refs[8:12]
+    raw, coef, fa0, fb0, fa1, fb1, lin = refs[12:]
     rx, ry, nz = own.shape[1:]
     ex = rx + 2 * H
-    fill(raw, own, z_low, z_high, (x_low, x_high), (c_low, c_high), 0)
+    fill(raw, own, z_low, z_high, (x_low, x_high))
     here_x, here_y, _, _ = spot()
 
     @pl.when(here_x == 0)
@@ -489,7 +454,7 @@
         )
         geo[WS, x] = total
         s_a, r_a, p, frac, r_b, q, m, _ = coefficients(
-            raw, 3, src_ref, 0, x, total, rx - H, ry - H
+            raw, 3, src_ref, step, x, total
         )
         coef[SA, x] = s_a
         coef[RA, x] = r_a
@@ -507,7 +472,7 @@
     finish(False, step, steps, wells, lin, own.at[7], table_ref, None, outs)
 
 
-def prepare_kernel(step, with_acc, *refs):
+def prepare_kernel(step, first, with_acc, *refs):
     src_ref, geo, own, z_low, z_high, x_low, x_high = refs[:7]
     if with_acc:
         coef, acc_out, raw = refs[7:]
@@ -515,11 +480,11 @@
         acc, coef, raw = refs[7:]
     rx, ry, nz = own.shape[1:]
     ex = rx + 2 * H
-    fill(raw, own, z_low, z_high, (x_low, x_high), (x_low, x_high), H)
+    fill(raw, own, z_low, z_high, (x_low, x_high), first)
 
     def prepare(x, _):
         s_a, r_a, p, frac, r_b, q, m, s_b = coefficients(
-            raw, 0, src_ref, step, x, geo[WS, x], rx - H, ry - H
+            raw, 0, src_ref, step, x, geo[WS, x]
         )
         coef[SA, x] = s_a
         coef[RA, x] = r_a
@@ -547,7 +512,7 @@
     now, fa0, fb0, fa1, fb1, lin = refs[-6:]
     rx, ry, nz = own.shape[1:]
     ex = rx + 2 * H
-    fill(lin, lam, z_low, z_high, (x_low, x_high), (x_low, x_high), H)
+    fill(lin, lam, z_low, z_high, (x_low, x_high))
 
     def begin(x, _):
         a, b = by_v(lin, (0,), x), by_v(lin, (1,), x)
@@ -598,28 +563,30 @@
     )(*small)
     table = lax.all_to_all(mine, ("gx", "gy"), 0, 0, tiled=True)
 
-    blocks, y_low, y_high, e_low, e_high = load(arrays, leads, dims, (table,))
+    blocks, y_low, y_high, token = load(arrays, leads, dims, (table,))
     z_got = sent(y_low, y_high, "gy")
-    x_got = sent(e_low, e_high, "gx")
-
-    def sources(wanted, after):
-        return call(
-            functools.partial(source_kernel, wanted, steps, wells, ry), [table, after],
-            [sds(len(wanted), 3 * rx, 3 * ry, nz)], "sources", 8, [VMEM, ANY],
-        )[0]
-
-    def others(step, after):
-        with_acc = step == top - 1
-        arrays = own + ([acc_p, acc_s] if with_acc else [])
-        leads = [step] * 8 + ([None] * 2 if with_acc else [])
-        held, low, high = more(arrays, leads, dims, (after,))
-        return held, sent(low, high, "gy"), low
-
-    ready = {top - 1: others(top - 1, blocks)}
-    corners = pack_corners("corners", *z_got, (*x_got, ready[top - 1][2]))
-    c_got = sent(*corners, "gx")
-    src = sources((top,), corners[0])
-    sides = {top - 1: sent(*widen(*ready[top - 1][:1], *ready[top - 1][1], (src,)), "gx")}
+    plan, places, sizes = [], {}, []
+    for h, step in enumerate(reversed(range(top))):
+        places[step] = len(plan)
+        plan += [(n, step, h, n) for n in range(8)]
+        if h == 0:
+            plan += [(8, None, h, 8), (9, None, h, 9)]
+        sizes.append(len(plan) - places[step])
+    *holders, m_low, m_high = more(own + [acc_p, acc_s], plan, sizes, dims, token)
+    m_z = sent(m_low, m_high, "gy")
+    held = dict(zip(reversed(range(top)), holders))
+
+    wide = widen(blocks, *z_got)
+    x_got = sent(*wide, "gx")
+    src = call(
+        functools.partial(source_kernel, steps, wells), [table, wide[0]],
+        [sds(steps, ex, ey, nz)], "sources", 8, [VMEM, ANY],
+    )[0]
+
+    def beside(step, after):
+        return sent(*widen(held[step], *m_z, (after,), places[step]), "gx")
+
+    sides = beside(top - 1, src)
 
     ext = (ex, V, 8, nz)
     lam_out = [sds(2, rx, ry, nz), sds(2, rx, H, nz), sds(2, rx, H, nz)]
@@ -628,24 +595,20 @@
 
     geo, lam, low, high, dense = call(
         functools.partial(first_kernel, top, steps, wells),
-        [table, src, blocks, *z_got, *x_got, *c_got],
+        [table, src, blocks, *z_got, *x_got],
         [sds(5, *ext)] + lam_out + [well_out], "step_top", 16,
         scratch=[pltpu.VMEM((split, ex, ey, nz), F32), pltpu.VMEM((7, *ext), F32)] + fields,
     )
 
     acc = None
-    src = None
     for step in reversed(range(top)):
         last = step == 0
         with_acc = step == top - 1
-        if src is None:
-            src = sources(tuple(range(top)), low)
-        held, m_z, _ = ready[step]
-        if step not in sides:
-            sides[step] = sent(*widen(held, *m_z, (low,)), "gx")
+        if not with_acc:
+            sides = beside(step, coef)
         made = call(
-            functools.partial(prepare_kernel, step, with_acc),
-            [src, geo, held, *m_z, *sides[step]] + ([] if with_acc else [acc]),
+            functools.partial(prepare_kernel, step, places[step], with_acc),
+            [src, geo, held[step], *m_z, *sides] + ([] if with_acc else [acc]),
             [sds(9, *ext)] + ([sds(2, *ext)] if with_acc else []), "prepare", 8,
             scratch=[pltpu.VMEM((10 if with_acc else 8, ex, ey, nz), F32)],
         )
@@ -653,14 +616,12 @@
         if with_acc:
             acc = made[1]
 
-        if not last:
-            ready[step - 1] = others(step - 1, low)
         l_z = sent(low, high, "gy")
         l_x = sent(*widen(lam, *l_z), "gx")
         outs = [sds(rx, ry, nz)] * 2 if last else lam_out
         outs = call(
             functools.partial(sweep_kernel, last, step, steps, wells),
-            [table, coef, geo, held, lam, *l_z, *l_x, dense],
+            [table, coef, geo, held[step], lam, *l_z, *l_x, dense],
             outs + [well_out], "step", 8, scratch=[pltpu.VMEM((2, *ext), F32)] + fields,
         )
         dense = outs[-1]

time: 151 us -> 148 us (0.980)
  waiting for transfers between devices: 26 us -> 49.3 us
  starting transfers between devices: 51.1 us -> 36.9 us
  Pallas kernels: 40.9 us -> 28.3 us
    ppermute x22 -> x18, waiting for transfers between devices: 26 us -> 49.3 us  [shifted(): return lax.ppermute(value, axis, pairs)]
    ppermute x22 -> x18, starting transfers between devices: 51.1 us -> 36.9 us  [shifted(): return lax.ppermute(value, axis, pairs)]
    pallas_call x14 -> x12, Pallas kernels: 35.6 us -> 23.4 us  [call(): pl.pallas_call(kernel, in_specs=specs or [VMEM] * len(ins), out_specs=[VM...]
  transfers between devices with their start and end apart: 22 -> 18, of which waited for: 8 -> 9; matrix products, arithmetic and copies ran while one was open for 0% -> 0% of each run, Pallas kernels for 19% -> 12%
where the time goes in v6:
time: 148 us; the launch traced here: 147 us
  waiting for transfers between devices  49.3 us (33%)
  starting transfers between devices  36.9 us (25%)
  blocking collectives  30 us (20%)
  Pallas kernels  28.3 us (19%)
    ppermute x18, waiting for transfers between devices, shifted(): return lax.ppermute(value, axis, pairs)  49.3 us
    ppermute x18, starting transfers between devices, shifted(): return lax.ppermute(value, axis, pairs)  36.9 us
    pallas_call x12, Pallas kernels, call(): pl.pallas_call(kernel, in_specs=specs or [VMEM] * len(ins), out_specs=[VM...  23.4 us
    all_to_all x1, blocking collectives, local(): parts = lax.all_to_all(dense[:, None, :], ('gx', 'gy'), 0, 0, tiled=True)  15.1 us
    all_to_all x1, blocking collectives, local(): table = lax.all_to_all(mine, ('gx', 'gy'), 0, 0, tiled=True)  14.9 us
    pallas_call x1, Pallas kernels, load(): pl.pallas_call(functools.partial(load_kernel, leads), in_specs=[HBM] * n...  3.33 us
  transfers between devices with their start and end apart: 18, of which 9 were waited for; matrix products, arithmetic and copies ran while one was open for 0% of the time, Pallas kernels for 12%

profile of v6, /device:TPU:0, one launch (start us, length us, event | category | flops | bytes accessed | tf_op | source)
XLA Modules:
  0.0 146.9 jit_solution(9774001388634251925)
XLA Ops:
  0.6 1.5 %table.1 = f32[32,4,128]{2,1,0:T(4,128)} custom-call(f32[2,3]{1,0:T(2,128)} %refs_0_.3, f32[2,3]{1,0:T(2,128)} %refs_1_.3, s32[2,3]{1,0:T(2,128)} %refs_2_.3, s32[1,128]{1,0:T(1,128)} %bitcast.8, s32[1,128]{1,0:T(1,128)} %bitcast.9, f32[1,128]{1,0:T(1,128)} %bitcast.10), custom_call_target="tpu_custom_call" | custom-call | tf_op jit(solution)/shard_map/table/pallas_call | solution.py:555
  2.1 14.9 %all_to_all.10.refs_11_.table_ref.refs_0_ = f32[32,4,128]{2,1,0:T(4,128)} all-to-all(f32[32,4,128]{2,1,0:T(4,128)} %table.1), channel_id=1, replica_groups=mesh['gx'=8,'gy'=4] {'gx','gy'}, dimensions={0} | all-to-all | bytes 131072 | tf_op jit(solution)/shard_map/all_to_all | solution.py:564
  17.1 0.0 copy-start.4
  17.1 0.0 copy-start.5
  17.1 0.0 copy-start.6
  17.1 0.0 copy-start.7
  17.1 0.0 copy-start.10
  17.1 0.0 copy-start.11
  17.1 3.3 %load.1 = (f32[11,16,16,128]{3,2,1,0:T(8,128)}, f32[11,16,8,128]{3,2,1,0:T(8,128)}, f32[11,16,8,128]{3,2,1,0:T(8,128)}, f32[8,128]{1,0:T(8,128)}) custom-call(f32[16,16,128]{2,1,0:T(8,128)} %refs_0_.4, f32[16,16,128]{2,1,0:T(8,128)} %refs_1_.4, f32[16,16,128]{2,1,0:T(8,128)} %refs_2_.4, f32[3,16,16,128]{3,2,1,0:T(8,128)} %refs_0_.5, ...), custom_call_target="tpu_custom_call" | custom-call | tf_op jit(solution)/shard_map/load/pallas_call | solution.py:93
  20.5 2.2 %collective-permute-start = (f32[11,16,8,128]{3,2,1,0:T(8,128)}, f32[11,16,8,128]{3,2,1,0:T(8,128)S(1)}, u32[]{:S(2)}, u32[]{:S(2)}) collective-permute-start(f32[11,16,8,128]{3,2,1,0:T(8,128)} %get-tuple-element.36), channel_id=1, source_target_pairs={{0,1},{1,2},{2,3},{4,5},{5,6},{6,7},{8,9},{9,10},{10,11},{12,13},{... | collective-permute-start | bytes 2162696 | tf_op jit(solution)/shard_map/ppermute | solution.py:59
  22.7 1.3 collective-permute-start.1
  24.0 0.0 copy-done
  24.0 0.0 copy-done.1
  24.0 0.0 copy-done.2
  24.0 0.0 copy-done.3
  24.1 0.0 copy-start.12
  24.1 0.7 copy-done.12
  24.8 0.3 more.1
  25.1 4.8 %collective-permute-start.4 = (f32[18,16,8,128]{3,2,1,0:T(8,128)S(1)}, f32[18,16,8,128]{3,2,1,0:T(8,128)S(1)}, u32[]{:S(2)}, u32[]{:S(2)}) collective-permute-start(f32[18,16,8,128]{3,2,1,0:T(8,128)S(1)} %get-tuple-element.43), channel_id=1, source_target_pairs={{0,1},{1,2},{2,3},{4,5},{5,6},{6,7},{8,9},{9,10},{10,11},{12,13},{... | collective-permute-start | bytes 3538952 | tf_op jit(solution)/shard_map/ppermute | solution.py:59
  29.9 1.3 collective-permute-start.5
  31.2 8.3 %collective-permute-done.z_low.refs_3_ = f32[11,16,8,128]{3,2,1,0:T(8,128)S(1)} collective-permute-done((f32[11,16,8,128]{3,2,1,0:T(8,128)}, f32[11,16,8,128]{3,2,1,0:T(8,128)S(1)}, u32[]{:S(2)}, u32[]{:S(2)}) %collective-permute-start) | collective-permute-done | bytes 720928 | tf_op jit(solution)/shard_map/ppermute | solution.py:59
  39.4 4.4 %collective-permute-done.1.z_high.refs_4_ = f32[11,16,8,128]{3,2,1,0:T(8,128)S(1)} collective-permute-done((f32[11,16,8,128]{3,2,1,0:T(8,128)}, f32[11,16,8,128]{3,2,1,0:T(8,128)S(1)}, u32[]{:S(2)}, u32[]{:S(2)}) %collective-permute-start.1) | collective-permute-done | bytes 720928 | tf_op jit(solution)/shard_map/ppermute | solution.py:59
  43.8 0.2 widen.5
  44.0 1.4 collective-permute-start.2
  45.4 1.3 collective-permute-start.3
  46.7 1.0 sources.1.refs_1_.refs_0_
  47.7 16.0 %collective-permute-done.4.z_low.refs_3_ = f32[18,16,8,128]{3,2,1,0:T(8,128)S(1)} collective-permute-done((f32[18,16,8,128]{3,2,1,0:T(8,128)S(1)}, f32[18,16,8,128]{3,2,1,0:T(8,128)S(1)}, u32[]{:S(2)}, u32[]{:S(2)}) %collective-permute-start.4) | collective-permute-done | bytes 1179680 | tf_op jit(solution)/shard_map/ppermute | solution.py:59
  63.8 4.2 %collective-permute-done.5.z_high.refs_4_ = f32[18,16,8,128]{3,2,1,0:T(8,128)S(1)} collective-permute-done((f32[18,16,8,128]{3,2,1,0:T(8,128)S(1)}, f32[18,16,8,128]{3,2,1,0:T(8,128)S(1)}, u32[]{:S(2)}, u32[]{:S(2)}) %collective-permute-start.5) | collective-permute-done | bytes 1179680 | tf_op jit(solution)/shard_map/ppermute | solution.py:59
  67.9 0.2 widen.6
  68.1 1.4 collective-permute-start.6
  69.5 1.3 collective-permute-start.7
  70.8 0.0 collective-permute-done.2.refs_5_
  70.8 0.0 collective-permute-done.3.refs_6_
  70.8 7.1 %step_top.1 = (f32[5,32,4,8,128]{4,3,2,1,0:T(8,128)S(1)}, f32[2,16,16,128]{3,2,1,0:T(8,128)S(1)}, f32[2,16,8,128]{3,2,1,0:T(8,128)S(1)}, f32[2,16,8,128]{3,2,1,0:T(8,128)S(1)}, f32[32,128]{1,0:T(8,128)S(1)}) custom-call(f32[32,4,128]{2,1,0:T(4,128)S(1)} %copy-done.9, f32[3,32,32,128]{3,2,1,0:T(8,128)S(1)} %sources.1.refs_1_.refs_0_, ...), custom_call_target="tpu_custom_call" | custom-call | flops 7000000000 | bytes 21000000 | tf_op jit(solution)/shard_map/step_top/pallas_call | solution.py:44
  77.9 2.2 %collective-permute-start.10 = (f32[2,16,8,128]{3,2,1,0:T(8,128)S(1)}, f32[2,16,8,128]{3,2,1,0:T(8,128)S(1)}, u32[]{:S(2)}, u32[]{:S(2)}) collective-permute-start(f32[2,16,8,128]{3,2,1,0:T(8,128)S(1)} %get-tuple-element.53), channel_id=1, source_target_pairs={{0,1},{1,2},{2,3},{4,5},{5,6},{6,7},{8,9},{9,10},{10,11},{12,13},{... | collective-permute-start | bytes 393224 | tf_op jit(solution)/shard_map/ppermute | solution.py:59
  80.1 1.3 collective-permute-start.11
  81.4 1.6 %collective-permute-done.10.z_low.refs_5_ = f32[2,16,8,128]{3,2,1,0:T(8,128)S(1)} collective-permute-done((f32[2,16,8,128]{3,2,1,0:T(8,128)S(1)}, f32[2,16,8,128]{3,2,1,0:T(8,128)S(1)}, u32[]{:S(2)}, u32[]{:S(2)}) %collective-permute-start.10) | collective-permute-done | bytes 131104 | tf_op jit(solution)/shard_map/ppermute | solution.py:59
  83.0 4.7 %collective-permute-done.11.z_high.refs_6_ = f32[2,16,8,128]{3,2,1,0:T(8,128)S(1)} collective-permute-done((f32[2,16,8,128]{3,2,1,0:T(8,128)S(1)}, f32[2,16,8,128]{3,2,1,0:T(8,128)S(1)}, u32[]{:S(2)}, u32[]{:S(2)}) %collective-permute-start.11) | collective-permute-done | bytes 131104 | tf_op jit(solution)/shard_map/ppermute | solution.py:59
  87.7 2.4 %collective-permute-start.12 = (f32[2,12,16,128]{3,2,1,0:T(8,128)S(1)}, f32[2,12,16,128]{3,2,1,0:T(8,128)S(1)}, u32[]{:S(2)}, u32[]{:S(2)}) collective-permute-start(f32[2,12,16,128]{3,2,1,0:T(8,128)S(1)} %get-tuple-element.55), channel_id=1, source_target_pairs={{0,4},{4,8},{8,12},{12,16},{16,20},{20,24},{24,28},{1,5},{5,9},{9,... | collective-permute-start | bytes 589832 | tf_op jit(solution)/shard_map/ppermute | solution.py:59
  90.2 1.3 collective-permute-start.13
  91.5 0.0 collective-permute-done.6.refs_5_
  91.5 0.0 collective-permute-done.7.refs_6_
  91.5 1.1 prepare.2
  92.5 0.1 widen.7
  92.7 5.1 %collective-permute-start.8 = (f32[8,12,16,128]{3,2,1,0:T(8,128)S(1)}, f32[8,12,16,128]{3,2,1,0:T(8,128)S(1)}, u32[]{:S(2)}, u32[]{:S(2)}) collective-permute-start(f32[8,12,16,128]{3,2,1,0:T(8,128)S(1)} %get-tuple-element.49), channel_id=1, source_target_pairs={{0,4},{4,8},{8,12},{12,16},{16,20},{20,24},{24,28},{1,5},{5,9},{9,... | collective-permute-start | bytes 2359304 | tf_op jit(solution)/shard_map/ppermute | solution.py:59
  97.8 1.3 collective-permute-start.9
  99.1 0.0 collective-permute-done.12.refs_7_
  99.1 0.0 collective-permute-done.13.refs_8_
  99.1 6.0 %step.2 = (f32[2,16,16,128]{3,2,1,0:T(8,128)S(1)}, f32[2,16,8,128]{3,2,1,0:T(8,128)S(1)}, f32[2,16,8,128]{3,2,1,0:T(8,128)S(1)}, f32[32,128]{1,0:T(8,128)S(1)}) custom-call(f32[32,4,128]{2,1,0:T(4,128)S(1)} %copy-done.9, f32[9,32,4,8,128]{4,3,2,1,0:T(8,128)S(1)} %get-tuple-element.48.refs_0_.refs_1_, ...), custom_call_target="tpu_custom_call" | custom-call | flops 6000000000 | bytes 18000000 | tf_op jit(solution)/shard_map/step/pallas_call | solution.py:44
  105.1 2.9 %collective-permute-start.14 = (f32[2,16,8,128]{3,2,1,0:T(8,128)S(1)}, f32[2,16,8,128]{3,2,1,0:T(8,128)S(1)}, u32[]{:S(2)}, u32[]{:S(2)}) collective-permute-start(f32[2,16,8,128]{3,2,1,0:T(8,128)S(1)} %get-tuple-element.59), channel_id=1, source_target_pairs={{0,1},{1,2},{2,3},{4,5},{5,6},{6,7},{8,9},{9,10},{10,11},{12,13},{... | collective-permute-start | bytes 393224 | tf_op jit(solution)/shard_map/ppermute | solution.py:59
  108.0 1.3 collective-permute-start.15
  109.3 1.2 collective-permute-done.14.z_low.refs_5_
  110.5 4.7 %collective-permute-done.15.z_high.refs_6_ = f32[2,16,8,128]{3,2,1,0:T(8,128)S(1)} collective-permute-done((f32[2,16,8,128]{3,2,1,0:T(8,128)S(1)}, f32[2,16,8,128]{3,2,1,0:T(8,128)S(1)}, u32[]{:S(2)}, u32[]{:S(2)}) %collective-permute-start.15) | collective-permute-done | bytes 131104 | tf_op jit(solution)/shard_map/ppermute | solution.py:59
  115.3 2.8 %collective-permute-start.16 = (f32[2,12,16,128]{3,2,1,0:T(8,128)S(1)}, f32[2,12,16,128]{3,2,1,0:T(8,128)S(1)}, u32[]{:S(2)}, u32[]{:S(2)}) collective-permute-start(f32[2,12,16,128]{3,2,1,0:T(8,128)S(1)} %get-tuple-element.61), channel_id=1, source_target_pairs={{0,4},{4,8},{8,12},{12,16},{16,20},{20,24},{24,28},{1,5},{5,9},{9,... | collective-permute-start | bytes 589832 | tf_op jit(solution)/shard_map/ppermute | solution.py:59
  118.1 1.5 %collective-permute-start.17 = (f32[2,12,16,128]{3,2,1,0:T(8,128)S(1)}, f32[2,12,16,128]{3,2,1,0:T(8,128)S(1)}, u32[]{:S(2)}, u32[]{:S(2)}) collective-permute-start(f32[2,12,16,128]{3,2,1,0:T(8,128)S(1)} %get-tuple-element.62), channel_id=1, source_target_pairs={{4,0},{8,4},{12,8},{16,12},{20,16},{24,20},{28,24},{5,1},{9,5},{13... | collective-permute-start | bytes 589832 | tf_op jit(solution)/shard_map/ppermute | solution.py:59
  119.6 0.0 collective-permute-done.8.refs_5_
  119.6 0.0 collective-permute-done.9.refs_6_
  119.6 1.0 prepare.3.refs_1_
  120.6 0.0 collective-permute-done.16.refs_7_
  120.6 4.2 %collective-permute-done.17.refs_8_ = f32[2,12,16,128]{3,2,1,0:T(8,128)S(1)} collective-permute-done((f32[2,12,16,128]{3,2,1,0:T(8,128)S(1)}, f32[2,12,16,128]{3,2,1,0:T(8,128)S(1)}, u32[]{:S(2)}, u32[]{:S(2)}) %collective-permute-start.17) | collective-permute-done | bytes 196640 | tf_op jit(solution)/shard_map/ppermute | solution.py:59
  124.8 6.3 %step.3 = (f32[16,16,128]{2,1,0:T(8,128)}, f32[16,16,128]{2,1,0:T(8,128)}, f32[32,128]{1,0:T(8,128)S(1)}) custom-call(f32[32,4,128]{2,1,0:T(4,128)S(1)} %copy-done.9, f32[9,32,4,8,128]{4,3,2,1,0:T(8,128)S(1)} %prepare.3.refs_1_, f32[5,32,4,8,128]{4,3,2,1,0:T(8,128)S(1)} %get-tuple-element.40.refs_1_.refs_2_, ...), custom_call_target="tpu_custom_call" | custom-call | flops 6000000000 | bytes 18000000 | tf_op jit(solution)/shard_map/step/pallas_call | solution.py:44
  131.2 15.1 %all_to_all.11 = f32[32,1,128]{2,1,0:T(1,128)S(1)} all-to-all(f32[32,1,128]{2,1,0:T(1,128)S(1)} %bitcast.7), channel_id=1, replica_groups=mesh['gx'=8,'gy'=4] {'gx','gy'}, dimensions={0} | all-to-all | bytes 32768 | tf_op jit(solution)/shard_map/all_to_all | solution.py:631
  146.2 0.1 reduce_sum.9
  146.3 0.6 reshape.9
  (16 shorter events, 0.1 us)
Async XLA Ops:
  17.1 6.9 %copy-start = (f32[3,16,16,128]{3,2,1,0:T(8,128)S(1)}, f32[3,16,16,128]{3,2,1,0:T(8,128)}, u32[]{:S(2)}) copy-start(f32[3,16,16,128]{3,2,1,0:T(8,128)} %refs_0_.5) | copy-start | bytes 1179652
  17.1 6.9 %copy-start.1 = (f32[3,16,16,128]{3,2,1,0:T(8,128)S(1)}, f32[3,16,16,128]{3,2,1,0:T(8,128)}, u32[]{:S(2)}) copy-start(f32[3,16,16,128]{3,2,1,0:T(8,128)} %refs_1_.5) | copy-start | bytes 1179652
  17.1 6.9 %copy-start.2 = (f32[3,16,16,128]{3,2,1,0:T(8,128)S(1)}, f32[3,16,16,128]{3,2,1,0:T(8,128)}, u32[]{:S(2)}) copy-start(f32[3,16,16,128]{3,2,1,0:T(8,128)} %refs_2_.5) | copy-start | bytes 1179652
  17.1 6.9 %copy-start.3 = (f32[3,16,16,128]{3,2,1,0:T(8,128)S(1)}, f32[3,16,16,128]{3,2,1,0:T(8,128)}, u32[]{:S(2)}) copy-start(f32[3,16,16,128]{3,2,1,0:T(8,128)} %refs_3_.3) | copy-start | bytes 1179652
  17.1 6.9 %copy-start.4 = (f32[3,16,16,128]{3,2,1,0:T(8,128)S(1)}, f32[3,16,16,128]{3,2,1,0:T(8,128)}, u32[]{:S(2)}) copy-start(f32[3,16,16,128]{3,2,1,0:T(8,128)} %refs_4_.3) | copy-start | bytes 1179652
  17.1 6.9 %copy-start.5 = (f32[3,16,16,128]{3,2,1,0:T(8,128)S(1)}, f32[3,16,16,128]{3,2,1,0:T(8,128)}, u32[]{:S(2)}) copy-start(f32[3,16,16,128]{3,2,1,0:T(8,128)} %refs_5_.3) | copy-start | bytes 1179652
  17.1 6.9 %copy-start.6 = (f32[3,16,16,128]{3,2,1,0:T(8,128)S(1)}, f32[3,16,16,128]{3,2,1,0:T(8,128)}, u32[]{:S(2)}) copy-start(f32[3,16,16,128]{3,2,1,0:T(8,128)} %refs_6_.3) | copy-start | bytes 1179652
  17.1 6.9 %copy-start.7 = (f32[3,16,16,128]{3,2,1,0:T(8,128)S(1)}, f32[3,16,16,128]{3,2,1,0:T(8,128)}, u32[]{:S(2)}) copy-start(f32[3,16,16,128]{3,2,1,0:T(8,128)} %refs_7_.3) | copy-start | bytes 1179652
  17.1 6.9 %copy-start.10 = (f32[16,16,128]{2,1,0:T(8,128)S(1)}, f32[16,16,128]{2,1,0:T(8,128)}, u32[]{:S(2)}) copy-start(f32[16,16,128]{2,1,0:T(8,128)} %refs_8_.3) | copy-start | bytes 393220
  17.1 6.9 %copy-start.11 = (f32[16,16,128]{2,1,0:T(8,128)S(1)}, f32[16,16,128]{2,1,0:T(8,128)}, u32[]{:S(2)}) copy-start(f32[16,16,128]{2,1,0:T(8,128)} %refs_9_.3) | copy-start | bytes 393220
  20.5 18.9 %collective-permute-start = (f32[11,16,8,128]{3,2,1,0:T(8,128)}, f32[11,16,8,128]{3,2,1,0:T(8,128)S(1)}, u32[]{:S(2)}, u32[]{:S(2)}) collective-permute-start(f32[11,16,8,128]{3,2,1,0:T(8,128)} %get-tuple-element.36), channel_id=1, source_target_pairs={{0,1},{1,2},{2,3},{4,5},{5,6},{6,7},{8,9},{9,10},{10,11},{12,13},{... | collective-permute-start | bytes 2162696 | tf_op jit(solution)/shard_map/ppermute | solution.py:59
  22.7 21.1 %collective-permute-start.1 = (f32[11,16,8,128]{3,2,1,0:T(8,128)}, f32[11,16,8,128]{3,2,1,0:T(8,128)S(1)}, u32[]{:S(2)}, u32[]{:S(2)}) collective-permute-start(f32[11,16,8,128]{3,2,1,0:T(8,128)} %get-tuple-element.37), channel_id=1, source_target_pairs={{1,0},{2,1},{3,2},{5,4},{6,5},{7,6},{9,8},{10,9},{11,10},{13,12},{... | collective-permute-start | bytes 2162696 | tf_op jit(solution)/shard_map/ppermute | solution.py:59
  24.1 0.7 copy-start.12
  24.8 19.0 %copy-start.8 = (f32[11,16,16,128]{3,2,1,0:T(8,128)S(1)}, f32[11,16,16,128]{3,2,1,0:T(8,128)}, u32[]{:S(2)}) copy-start(f32[11,16,16,128]{3,2,1,0:T(8,128)} %get-tuple-element.35.own.refs_2_) | copy-start | bytes 4325380
  25.1 38.7 %collective-permute-start.4 = (f32[18,16,8,128]{3,2,1,0:T(8,128)S(1)}, f32[18,16,8,128]{3,2,1,0:T(8,128)S(1)}, u32[]{:S(2)}, u32[]{:S(2)}) collective-permute-start(f32[18,16,8,128]{3,2,1,0:T(8,128)S(1)} %get-tuple-element.43), channel_id=1, source_target_pairs={{0,1},{1,2},{2,3},{4,5},{5,6},{6,7},{8,9},{9,10},{10,11},{12,13},{... | collective-permute-start | bytes 3538952 | tf_op jit(solution)/shard_map/ppermute | solution.py:59
  29.9 38.1 %collective-permute-start.5 = (f32[18,16,8,128]{3,2,1,0:T(8,128)S(1)}, f32[18,16,8,128]{3,2,1,0:T(8,128)S(1)}, u32[]{:S(2)}, u32[]{:S(2)}) collective-permute-start(f32[18,16,8,128]{3,2,1,0:T(8,128)S(1)} %get-tuple-element.44), channel_id=1, source_target_pairs={{1,0},{2,1},{3,2},{5,4},{6,5},{7,6},{9,8},{10,9},{11,10},{13,12},{... | collective-permute-start | bytes 3538952 | tf_op jit(solution)/shard_map/ppermute | solution.py:59
  43.8 2.9 %copy-start.9 = (f32[32,4,128]{2,1,0:T(4,128)S(1)}, f32[32,4,128]{2,1,0:T(4,128)}, u32[]{:S(2)}) copy-start(f32[32,4,128]{2,1,0:T(4,128)} %all_to_all.10.refs_11_.table_ref.refs_0_) | copy-start | bytes 196612
  44.0 26.8 %collective-permute-start.2 = (f32[11,12,16,128]{3,2,1,0:T(8,128)S(1)}, f32[11,12,16,128]{3,2,1,0:T(8,128)S(1)}, u32[]{:S(2)}, u32[]{:S(2)}) collective-permute-start(f32[11,12,16,128]{3,2,1,0:T(8,128)S(1)} %get-tuple-element.39), channel_id=1, source_target_pairs={{0,4},{4,8},{8,12},{12,16},{16,20},{20,24},{24,28},{1,5},{5,9},{9,... | collective-permute-start | bytes 3244040 | tf_op jit(solution)/shard_map/ppermute | solution.py:59
  45.4 25.4 %collective-permute-start.3 = (f32[11,12,16,128]{3,2,1,0:T(8,128)S(1)}, f32[11,12,16,128]{3,2,1,0:T(8,128)S(1)}, u32[]{:S(2)}, u32[]{:S(2)}) collective-permute-start(f32[11,12,16,128]{3,2,1,0:T(8,128)S(1)} %get-tuple-element.38._), channel_id=1, source_target_pairs={{4,0},{8,4},{12,8},{16,12},{20,16},{24,20},{28,24},{5,1},{9,5},{13... | collective-permute-start | bytes 3244040 | tf_op jit(solution)/shard_map/ppermute | solution.py:59
  68.1 23.3 %collective-permute-start.6 = (f32[10,12,16,128]{3,2,1,0:T(8,128)S(1)}, f32[10,12,16,128]{3,2,1,0:T(8,128)S(1)}, u32[]{:S(2)}, u32[]{:S(2)}) collective-permute-start(f32[10,12,16,128]{3,2,1,0:T(8,128)S(1)} %get-tuple-element.46), channel_id=1, source_target_pairs={{0,4},{4,8},{8,12},{12,16},{16,20},{20,24},{24,28},{1,5},{5,9},{9,... | collective-permute-start | bytes 2949128 | tf_op jit(solution)/shard_map/ppermute | solution.py:59
  69.5 22.0 %collective-permute-start.7 = (f32[10,12,16,128]{3,2,1,0:T(8,128)S(1)}, f32[10,12,16,128]{3,2,1,0:T(8,128)S(1)}, u32[]{:S(2)}, u32[]{:S(2)}) collective-permute-start(f32[10,12,16,128]{3,2,1,0:T(8,128)S(1)} %get-tuple-element.47), channel_id=1, source_target_pairs={{4,0},{8,4},{12,8},{16,12},{20,16},{24,20},{28,24},{5,1},{9,5},{13... | collective-permute-start | bytes 2949128 | tf_op jit(solution)/shard_map/ppermute | solution.py:59
  77.9 5.1 %collective-permute-start.10 = (f32[2,16,8,128]{3,2,1,0:T(8,128)S(1)}, f32[2,16,8,128]{3,2,1,0:T(8,128)S(1)}, u32[]{:S(2)}, u32[]{:S(2)}) collective-permute-start(f32[2,16,8,128]{3,2,1,0:T(8,128)S(1)} %get-tuple-element.53), channel_id=1, source_target_pairs={{0,1},{1,2},{2,3},{4,5},{5,6},{6,7},{8,9},{9,10},{10,11},{12,13},{... | collective-permute-start | bytes 393224 | tf_op jit(solution)/shard_map/ppermute | solution.py:59
  80.1 7.6 %collective-permute-start.11 = (f32[2,16,8,128]{3,2,1,0:T(8,128)S(1)}, f32[2,16,8,128]{3,2,1,0:T(8,128)S(1)}, u32[]{:S(2)}, u32[]{:S(2)}) collective-permute-start(f32[2,16,8,128]{3,2,1,0:T(8,128)S(1)} %get-tuple-element.54), channel_id=1, source_target_pairs={{1,0},{2,1},{3,2},{5,4},{6,5},{7,6},{9,8},{10,9},{11,10},{13,12},{... | collective-permute-start | bytes 393224 | tf_op jit(solution)/shard_map/ppermute | solution.py:59
  87.7 11.4 %collective-permute-start.12 = (f32[2,12,16,128]{3,2,1,0:T(8,128)S(1)}, f32[2,12,16,128]{3,2,1,0:T(8,128)S(1)}, u32[]{:S(2)}, u32[]{:S(2)}) collective-permute-start(f32[2,12,16,128]{3,2,1,0:T(8,128)S(1)} %get-tuple-element.55), channel_id=1, source_target_pairs={{0,4},{4,8},{8,12},{12,16},{16,20},{20,24},{24,28},{1,5},{5,9},{9,... | collective-permute-start | bytes 589832 | tf_op jit(solution)/shard_map/ppermute | solution.py:59
  90.2 9.0 %collective-permute-start.13 = (f32[2,12,16,128]{3,2,1,0:T(8,128)S(1)}, f32[2,12,16,128]{3,2,1,0:T(8,128)S(1)}, u32[]{:S(2)}, u32[]{:S(2)}) collective-permute-start(f32[2,12,16,128]{3,2,1,0:T(8,128)S(1)} %get-tuple-element.56), channel_id=1, source_target_pairs={{4,0},{8,4},{12,8},{16,12},{20,16},{24,20},{28,24},{5,1},{9,5},{13... | collective-permute-start | bytes 589832 | tf_op jit(solution)/shard_map/ppermute | solution.py:59
  92.7 26.9 %collective-permute-start.8 = (f32[8,12,16,128]{3,2,1,0:T(8,128)S(1)}, f32[8,12,16,128]{3,2,1,0:T(8,128)S(1)}, u32[]{:S(2)}, u32[]{:S(2)}) collective-permute-start(f32[8,12,16,128]{3,2,1,0:T(8,128)S(1)} %get-tuple-element.49), channel_id=1, source_target_pairs={{0,4},{4,8},{8,12},{12,16},{16,20},{20,24},{24,28},{1,5},{5,9},{9,... | collective-permute-start | bytes 2359304 | tf_op jit(solution)/shard_map/ppermute | solution.py:59
  97.8 21.8 %collective-permute-start.9 = (f32[8,12,16,128]{3,2,1,0:T(8,128)S(1)}, f32[8,12,16,128]{3,2,1,0:T(8,128)S(1)}, u32[]{:S(2)}, u32[]{:S(2)}) collective-permute-start(f32[8,12,16,128]{3,2,1,0:T(8,128)S(1)} %get-tuple-element.50), channel_id=1, source_target_pairs={{4,0},{8,4},{12,8},{16,12},{20,16},{24,20},{28,24},{5,1},{9,5},{13... | collective-permute-start | bytes 2359304 | tf_op jit(solution)/shard_map/ppermute | solution.py:59
  105.1 5.4 %collective-permute-start.14 = (f32[2,16,8,128]{3,2,1,0:T(8,128)S(1)}, f32[2,16,8,128]{3,2,1,0:T(8,128)S(1)}, u32[]{:S(2)}, u32[]{:S(2)}) collective-permute-start(f32[2,16,8,128]{3,2,1,0:T(8,128)S(1)} %get-tuple-element.59), channel_id=1, source_target_pairs={{0,1},{1,2},{2,3},{4,5},{5,6},{6,7},{8,9},{9,10},{10,11},{12,13},{... | collective-permute-start | bytes 393224 | tf_op jit(solution)/shard_map/ppermute | solution.py:59
  108.0 7.2 %collective-permute-start.15 = (f32[2,16,8,128]{3,2,1,0:T(8,128)S(1)}, f32[2,16,8,128]{3,2,1,0:T(8,128)S(1)}, u32[]{:S(2)}, u32[]{:S(2)}) collective-permute-start(f32[2,16,8,128]{3,2,1,0:T(8,128)S(1)} %get-tuple-element.60), channel_id=1, source_target_pairs={{1,0},{2,1},{3,2},{5,4},{6,5},{7,6},{9,8},{10,9},{11,10},{13,12},{... | collective-permute-start | bytes 393224 | tf_op jit(solution)/shard_map/ppermute | solution.py:59
  115.3 5.3 %collective-permute-start.16 = (f32[2,12,16,128]{3,2,1,0:T(8,128)S(1)}, f32[2,12,16,128]{3,2,1,0:T(8,128)S(1)}, u32[]{:S(2)}, u32[]{:S(2)}) collective-permute-start(f32[2,12,16,128]{3,2,1,0:T(8,128)S(1)} %get-tuple-element.61), channel_id=1, source_target_pairs={{0,4},{4,8},{8,12},{12,16},{16,20},{20,24},{24,28},{1,5},{5,9},{9,... | collective-permute-start | bytes 589832 | tf_op jit(solution)/shard_map/ppermute | solution.py:59
  118.1 6.8 %collective-permute-start.17 = (f32[2,12,16,128]{3,2,1,0:T(8,128)S(1)}, f32[2,12,16,128]{3,2,1,0:T(8,128)S(1)}, u32[]{:S(2)}, u32[]{:S(2)}) collective-permute-start(f32[2,12,16,128]{3,2,1,0:T(8,128)S(1)} %get-tuple-element.62), channel_id=1, source_target_pairs={{4,0},{8,4},{12,8},{16,12},{20,16},{24,20},{28,24},{5,1},{9,5},{13... | collective-permute-start | bytes 589832 | tf_op jit(solution)/shard_map/ppermute | solution.py:59

commit v7 on v6

--- a/solution.py
+++ b/solution.py
@@ -125,10 +125,18 @@
     )
 
 
-def fold(rows_of, high):
+def tiles_of(reach):
+    return reach // 2
+
+
+def rows_of_array(reach):
+    return reach + tiles_of(reach)
+
+
+def fold(row, reach, high):
     tiles = []
-    for dx in range(1, 5):
-        near, far = rows_of(dx), rows_of(8 - dx)
+    for dx in range(1, tiles_of(reach) + 1):
+        near, far = row(dx), row(reach - dx)
         sub = lax.broadcasted_iota(jnp.int32, near.shape, 0)
         if high:
             tiles.append(jnp.where(sub < 8 - dx, near, pltpu.roll(far, 8 - dx, 0)))
@@ -141,40 +149,45 @@
     return tile, pltpu.roll(tile, dx if high else 8 - dx, 0)
 
 
-def corner_tiles(n, z_low, z_high, put):
-    rx = z_low.shape[1]
-    for side in (0, 1):
-        for high, z in ((False, z_low), (True, z_high)):
-
-            def rows_of(dx):
-                return z[n, dx - 1 if side == 0 else rx - dx]
-
-            for t, tile in enumerate(fold(rows_of, high)):
-                put(side, int(high), t, tile)
-
-
-def widen_kernel(first, own, z_low, z_high, *refs):
+def parts_of(reaches):
+    parts, row = [], 0
+    for n, reach in enumerate(reaches):
+        if parts and parts[-1][2] == reach:
+            parts[-1][1] += 1
+        else:
+            parts.append([n, 1, reach, row])
+        row += rows_of_array(reach)
+    return parts, row
+
+
+def widen_kernel(reaches, first, own, z_low, z_high, *refs):
     outs = refs[-2:]
     rx = own.shape[1]
-
-    def one(n, _):
-        def put(side, y, t, tile):
-            outs[side][n, H + t, y * H : (y + 1) * H, :] = tile
-
-        corner_tiles(n + first, z_low, z_high, put)
-        outs[0][n, 0:H] = own[n, 0:H]
-        outs[1][n, 0:H] = own[n, rx - H :]
-        return 0
-
-    lax.fori_loop(0, own.shape[0], one, 0)
-
-
-def widen(own, z_low, z_high, after=(), first=0):
-    count, rx, ry, nz = own.shape
+    for begin, count, reach, base in parts_of(reaches)[0]:
+
+        def one(k, _):
+            n = begin + k
+            at = base + k * rows_of_array(reach)
+            for side in (0, 1):
+                start = 0 if side == 0 else rx - reach
+                outs[side][pl.ds(at, reach)] = own[n, start : start + reach]
+                for high, z in ((0, z_low), (1, z_high)):
+
+                    def row(dx):
+                        return z[n + first, dx - 1 if side == 0 else rx - dx]
+
+                    for t, tile in enumerate(fold(row, reach, high == 1)):
+                        outs[side][at + reach + t, high * H : (high + 1) * H, :] = tile
+            return 0
+
+        lax.fori_loop(0, count, one, 0)
+
+
+def widen(own, reaches, z_low, z_high, after=(), first=0):
+    _, rx, ry, nz = own.shape
     return call(
-        functools.partial(widen_kernel, first), [own, z_low, z_high, *after],
-        [sds(count, H + 4, ry, nz)] * 2, "widen", 4,
-        [VMEM] * 3 + [ANY] * len(after),
+        functools.partial(widen_kernel, reaches, first), [own, z_low, z_high, *after],
+        [sds(parts_of(reaches)[1], ry, nz)] * 2, "widen", 4, [VMEM] * 3 + [ANY] * len(after),
     )
 
 
@@ -270,29 +283,44 @@
     return pltpu.roll(value, by, 2)
 
 
-def fill(dst, own, z_low, z_high, sides, first=0):
-    count, (rx, ry, nz) = dst.shape[0], own.shape[1:]
-
-    def one(n, _):
-        dst[n, H : H + rx, 0:H, :] = z_low[n + first]
-        dst[n, H : H + rx, H : H + ry, :] = own[n]
-        dst[n, H : H + rx, H + ry : 2 * H + ry, :] = z_high[n + first]
-        for side in (0, 1):
-            at = side * (H + rx)
-            dst[n, at : at + H, H : H + ry, :] = sides[side][n, 0:H]
-            for y in (0, 1):
-                to = y * (H + ry)
-                for t in range(4):
-                    tile = sides[side][n, H + t, y * H : (y + 1) * H, :]
-                    near, far = unfold(tile, t + 1, y == 1)
-                    for dx, row in ((t + 1, near), (7 - t, far)):
-                        x = H - dx if side == 0 else H + rx + dx - 1
-                        dst[n, x, to : to + H, :] = row
-                x = 0 if side == 0 else 2 * H + rx - 1
-                dst[n, x, to : to + H, :] = jnp.zeros((H, nz), F32)
-        return 0
-
-    lax.fori_loop(0, count, one, 0)
+def fill(dst, own, reaches, z_low, z_high, sides, first=0):
+    rx, ry, nz = own.shape[1:]
+    for begin, count, reach, base in parts_of(reaches)[0]:
+
+        def one(k, _):
+            n = begin + k
+            row = base + k * rows_of_array(reach)
+            dst[n, H : H + rx, 0:H, :] = z_low[n + first]
+            dst[n, H : H + rx, H : H + ry, :] = own[n]
+            dst[n, H : H + rx, H + ry : 2 * H + ry, :] = z_high[n + first]
+            for side in (0, 1):
+                at = H - reach if side == 0 else H + rx
+                dst[n, at : at + reach, H : H + ry, :] = sides[side][pl.ds(row, reach)]
+                known = set()
+                for y in (0, 1):
+                    to = y * (H + ry)
+                    for t in range(tiles_of(reach)):
+                        tile = sides[side][row + reach + t, y * H : (y + 1) * H, :]
+                        near, far = unfold(tile, t + 1, y == 1)
+                        for dx, value in ((t + 1, near), (reach - t - 1, far)):
+                            x = H - dx if side == 0 else H + rx + dx - 1
+                            dst[n, x, to : to + H, :] = value
+                            known.add(dx)
+                for dx in range(1, H + 1):
+                    x = H - dx if side == 0 else H + rx + dx - 1
+                    if dx not in known:
+                        for y in (0, H + ry):
+                            dst[n, x, y : y + H, :] = jnp.zeros((H, nz), F32)
+                    if dx > reach:
+                        dst[n, x, H : H + ry, :] = jnp.zeros((ry, nz), F32)
+            return 0
+
+        lax.fori_loop(0, count, one, 0)
+
+
+GEO, COEF = 8, 7
+TOP_REACH = (GEO,) * 3 + (COEF,) * 8
+LAM_REACH = (GEO,) * 2
 
 
 SA, RA, PC, FR, RB, QC, MC, AA, AB = range(9)
@@ -421,7 +449,7 @@
     raw, coef, fa0, fb0, fa1, fb1, lin = refs[12:]
     rx, ry, nz = own.shape[1:]
     ex = rx + 2 * H
-    fill(raw, own, z_low, z_high, (x_low, x_high))
+    fill(raw, own, TOP_REACH, z_low, z_high, (x_low, x_high))
     here_x, here_y, _, _ = spot()
 
     @pl.when(here_x == 0)
@@ -480,7 +508,7 @@
         acc, coef, raw = refs[7:]
     rx, ry, nz = own.shape[1:]
     ex = rx + 2 * H
-    fill(raw, own, z_low, z_high, (x_low, x_high), first)
+    fill(raw, own, (COEF,) * own.shape[0], z_low, z_high, (x_low, x_high), first)
 
     def prepare(x, _):
         s_a, r_a, p, frac, r_b, q, m, s_b = coefficients(
@@ -512,7 +540,7 @@
     now, fa0, fb0, fa1, fb1, lin = refs[-6:]
     rx, ry, nz = own.shape[1:]
     ex = rx + 2 * H
-    fill(lin, lam, z_low, z_high, (x_low, x_high))
+    fill(lin, lam, LAM_REACH, z_low, z_high, (x_low, x_high))
 
     def begin(x, _):
         a, b = by_v(lin, (0,), x), by_v(lin, (1,), x)
@@ -561,10 +589,18 @@
         + [pltpu.SemaphoreType.DMA((6,))],
         name="table",
     )(*small)
+    blocks, y_low, y_high, token = load(arrays, leads, dims, (mine,))
+    z_got = sent(y_low, y_high, "gy")
+    mine, _ = lax.optimization_barrier((mine, token))
     table = lax.all_to_all(mine, ("gx", "gy"), 0, 0, tiled=True)
 
-    blocks, y_low, y_high, token = load(arrays, leads, dims, (table,))
-    z_got = sent(y_low, y_high, "gy")
+    wide = widen(blocks, TOP_REACH, *z_got, (table,))
+    x_got = sent(*wide, "gx")
+    src = call(
+        functools.partial(source_kernel, steps, wells), [table, wide[0]],
+        [sds(steps, ex, ey, nz)], "sources", 8, [VMEM, ANY],
+    )[0]
+
     plan, places, sizes = [], {}, []
     for h, step in enumerate(reversed(range(top))):
         places[step] = len(plan)
@@ -572,19 +608,15 @@
         if h == 0:
             plan += [(8, None, h, 8), (9, None, h, 9)]
         sizes.append(len(plan) - places[step])
-    *holders, m_low, m_high = more(own + [acc_p, acc_s], plan, sizes, dims, token)
+    *holders, m_low, m_high = more(own + [acc_p, acc_s], plan, sizes, dims, table)
     m_z = sent(m_low, m_high, "gy")
     held = dict(zip(reversed(range(top)), holders))
 
-    wide = widen(blocks, *z_got)
-    x_got = sent(*wide, "gx")
-    src = call(
-        functools.partial(source_kernel, steps, wells), [table, wide[0]],
-        [sds(steps, ex, ey, nz)], "sources", 8, [VMEM, ANY],
-    )[0]
-
     def beside(step, after):
-        return sent(*widen(held[step], *m_z, (after,), places[step]), "gx")
+        group = held[step]
+        return sent(
+            *widen(group, (COEF,) * group.shape[0], *m_z, (after,), places[step]), "gx"
+        )
 
     sides = beside(top - 1, src)
 
@@ -617,7 +649,7 @@
             acc = made[1]
 
         l_z = sent(low, high, "gy")
-        l_x = sent(*widen(lam, *l_z), "gx")
+        l_x = sent(*widen(lam, LAM_REACH, *l_z), "gx")
         outs = [sds(rx, ry, nz)] * 2 if last else lam_out
         outs = call(
             functools.partial(sweep_kernel, last, step, steps, wells),

time: 148 us -> 146 us (0.986)
  waiting for transfers between devices: 49.3 us -> 40.1 us
  blocking collectives: 30 us -> 38.2 us
    ppermute x18, waiting for transfers between devices: 49.3 us -> 40.1 us  [shifted(): return lax.ppermute(value, axis, pairs)]
    all_to_all x1, blocking collectives: 14.9 us -> 23.2 us  [local(): table = lax.all_to_all(mine, ('gx', 'gy'), 0, 0, tiled=True)]
  transfers between devices with their start and end apart: 18 -> 18, of which waited for: 9 -> 7; matrix products, arithmetic and copies ran while one was open for 0% -> 0% of each run, Pallas kernels for 12% -> 12%
where the time goes in v7:
time: 146 us
  waiting for transfers between devices  40.1 us (27%)
  blocking collectives  38.2 us (26%)
  starting transfers between devices  37.1 us (25%)
  Pallas kernels  28.3 us (19%)
    ppermute x18, waiting for transfers between devices, shifted(): return lax.ppermute(value, axis, pairs)  40.1 us
    ppermute x18, starting transfers between devices, shifted(): return lax.ppermute(value, axis, pairs)  37.1 us
    pallas_call x12, Pallas kernels, call(): pl.pallas_call(kernel, in_specs=specs or [VMEM] * len(ins), out_specs=[VM...  23.5 us
    all_to_all x1, blocking collectives, local(): table = lax.all_to_all(mine, ('gx', 'gy'), 0, 0, tiled=True)  23.2 us
    all_to_all x1, blocking collectives, local(): parts = lax.all_to_all(dense[:, None, :], ('gx', 'gy'), 0, 0, tiled=True)  15.1 us
    pallas_call x1, Pallas kernels, load(): pl.pallas_call(functools.partial(load_kernel, leads), in_specs=[HBM] * n...  3.34 us
  transfers between devices with their start and end apart: 18, of which 7 were waited for; matrix products, arithmetic and copies ran while one was open for 0% of the time, Pallas kernels for 12%

profile of v7, /device:TPU:0, one launch (start us, length us, event | category | flops | bytes accessed | tf_op | source)
XLA Modules:
  0.0 145.6 jit_solution(5425961013738987941)
XLA Ops:
  0.6 1.5 %table.1.refs_11_ = f32[32,4,128]{2,1,0:T(4,128)} custom-call(f32[2,3]{1,0:T(2,128)} %refs_0_.3, f32[2,3]{1,0:T(2,128)} %refs_1_.3, s32[2,3]{1,0:T(2,128)} %refs_2_.3, s32[1,128]{1,0:T(1,128)} %bitcast.8, s32[1,128]{1,0:T(1,128)} %bitcast.9, f32[1,128]{1,0:T(1,128)} %bitcast.10), custom_call_target="tpu_custom_call" | custom-call | tf_op jit(solution)/shard_map/table/pallas_call | solution.py:583
  2.1 0.0 copy-start.11
  2.2 0.0 copy-start
  2.2 0.0 copy-start.1
  2.2 0.0 copy-start.2
  2.2 0.0 copy-start.3
  2.2 0.0 copy-start.4
  2.2 0.0 copy-start.5
  2.2 0.0 copy-start.6
  2.2 0.0 copy-start.7
  2.3 0.0 copy-start.9
  2.3 0.0 copy-start.10
  2.3 3.3 %load.1 = (f32[11,16,16,128]{3,2,1,0:T(8,128)}, f32[11,16,8,128]{3,2,1,0:T(8,128)}, f32[11,16,8,128]{3,2,1,0:T(8,128)}, f32[8,128]{1,0:T(8,128)}) custom-call(f32[16,16,128]{2,1,0:T(8,128)} %refs_0_.4, f32[16,16,128]{2,1,0:T(8,128)} %refs_1_.4, f32[16,16,128]{2,1,0:T(8,128)} %refs_2_.4, f32[3,16,16,128]{3,2,1,0:T(8,128)} %refs_0_.5, ...), custom_call_target="tpu_custom_call" | custom-call | tf_op jit(solution)/shard_map/load/pallas_call | solution.py:93
  5.6 5.0 %collective-permute-start = (f32[11,16,8,128]{3,2,1,0:T(8,128)}, f32[11,16,8,128]{3,2,1,0:T(8,128)S(1)}, u32[]{:S(2)}, u32[]{:S(2)}) collective-permute-start(f32[11,16,8,128]{3,2,1,0:T(8,128)} %get-tuple-element.35), channel_id=1, source_target_pairs={{0,1},{1,2},{2,3},{4,5},{5,6},{6,7},{8,9},{9,10},{10,11},{12,13},{... | collective-permute-start | bytes 2162696 | tf_op jit(solution)/shard_map/ppermute | solution.py:59
  10.6 1.3 collective-permute-start.1
  11.9 0.0 copy-done.11
  11.9 23.2 %all_to_all.10.refs_0_.table_ref.refs_10_ = f32[32,4,128]{2,1,0:T(4,128)S(1)} all-to-all(f32[32,4,128]{2,1,0:T(4,128)S(1)} %copy-done.11), channel_id=1, replica_groups=mesh['gx'=8,'gy'=4] {'gx','gy'}, dimensions={0} | all-to-all | bytes 131072 | tf_op jit(solution)/shard_map/all_to_all | solution.py:595
  35.2 0.4 more.1
  35.6 2.2 %collective-permute-start.4 = (f32[18,16,8,128]{3,2,1,0:T(8,128)S(1)}, f32[18,16,8,128]{3,2,1,0:T(8,128)S(1)}, u32[]{:S(2)}, u32[]{:S(2)}) collective-permute-start(f32[18,16,8,128]{3,2,1,0:T(8,128)S(1)} %get-tuple-element.41), channel_id=1, source_target_pairs={{0,1},{1,2},{2,3},{4,5},{5,6},{6,7},{8,9},{9,10},{10,11},{12,13},{... | collective-permute-start | bytes 3538952 | tf_op jit(solution)/shard_map/ppermute | solution.py:59
  37.8 1.3 collective-permute-start.5
  39.1 0.0 collective-permute-done.z_low.refs_3_
  39.1 0.0 collective-permute-done.1.z_high.refs_4_
  39.2 0.2 widen.5
  39.4 1.8 %collective-permute-start.2 = (f32[116,16,128]{2,1,0:T(8,128)S(1)}, f32[116,16,128]{2,1,0:T(8,128)S(1)}, u32[]{:S(2)}, u32[]{:S(2)}) collective-permute-start(f32[116,16,128]{2,1,0:T(8,128)S(1)} %get-tuple-element.38), channel_id=1, source_target_pairs={{0,4},{4,8},{8,12},{12,16},{16,20},{20,24},{24,28},{1,5},{5,9},{9,... | collective-permute-start | bytes 2850824 | tf_op jit(solution)/shard_map/ppermute | solution.py:59
  41.2 1.3 collective-permute-start.3
  42.5 1.1 sources.1.refs_1_.refs_0_
  43.5 19.7 %collective-permute-done.4.z_low.refs_3_ = f32[18,16,8,128]{3,2,1,0:T(8,128)S(1)} collective-permute-done((f32[18,16,8,128]{3,2,1,0:T(8,128)S(1)}, f32[18,16,8,128]{3,2,1,0:T(8,128)S(1)}, u32[]{:S(2)}, u32[]{:S(2)}) %collective-permute-start.4) | collective-permute-done | bytes 1179680 | tf_op jit(solution)/shard_map/ppermute | solution.py:59
  63.2 4.2 %collective-permute-done.5.z_high.refs_4_ = f32[18,16,8,128]{3,2,1,0:T(8,128)S(1)} collective-permute-done((f32[18,16,8,128]{3,2,1,0:T(8,128)S(1)}, f32[18,16,8,128]{3,2,1,0:T(8,128)S(1)}, u32[]{:S(2)}, u32[]{:S(2)}) %collective-permute-start.5) | collective-permute-done | bytes 1179680 | tf_op jit(solution)/shard_map/ppermute | solution.py:59
  67.4 0.2 widen.6
  67.6 1.3 collective-permute-start.6
  68.9 1.3 collective-permute-start.7
  70.2 0.0 collective-permute-done.2.refs_5_
  70.3 0.0 collective-permute-done.3.refs_6_
  70.3 7.1 %step_top.1 = (f32[5,32,4,8,128]{4,3,2,1,0:T(8,128)S(1)}, f32[2,16,16,128]{3,2,1,0:T(8,128)S(1)}, f32[2,16,8,128]{3,2,1,0:T(8,128)S(1)}, f32[2,16,8,128]{3,2,1,0:T(8,128)S(1)}, f32[32,128]{1,0:T(8,128)S(1)}) custom-call(f32[32,4,128]{2,1,0:T(4,128)S(1)} %all_to_all.10.refs_0_.table_ref.refs_10_, f32[3,32,32,128]{3,2,1,0:T(8,128)S(1)} %sources.1.refs_1_.refs_0_, ...), custom_call_target="tpu_custom_call" | custom-call | flops 7000000000 | bytes 21000000 | tf_op jit(solution)/shard_map/step_top/pallas_call | solution.py:44
  77.4 2.0 %collective-permute-start.10 = (f32[2,16,8,128]{3,2,1,0:T(8,128)S(1)}, f32[2,16,8,128]{3,2,1,0:T(8,128)S(1)}, u32[]{:S(2)}, u32[]{:S(2)}) collective-permute-start(f32[2,16,8,128]{3,2,1,0:T(8,128)S(1)} %get-tuple-element.51), channel_id=1, source_target_pairs={{0,1},{1,2},{2,3},{4,5},{5,6},{6,7},{8,9},{9,10},{10,11},{12,13},{... | collective-permute-start | bytes 393224 | tf_op jit(solution)/shard_map/ppermute | solution.py:59
  79.4 1.3 collective-permute-start.11
  80.7 1.3 collective-permute-done.10.z_low.refs_5_
  82.0 4.7 %collective-permute-done.11.z_high.refs_6_ = f32[2,16,8,128]{3,2,1,0:T(8,128)S(1)} collective-permute-done((f32[2,16,8,128]{3,2,1,0:T(8,128)S(1)}, f32[2,16,8,128]{3,2,1,0:T(8,128)S(1)}, u32[]{:S(2)}, u32[]{:S(2)}) %collective-permute-start.11) | collective-permute-done | bytes 131104 | tf_op jit(solution)/shard_map/ppermute | solution.py:59
  86.8 2.6 %collective-permute-start.12 = (f32[24,16,128]{2,1,0:T(8,128)S(1)}, f32[24,16,128]{2,1,0:T(8,128)S(1)}, u32[]{:S(2)}, u32[]{:S(2)}) collective-permute-start(f32[24,16,128]{2,1,0:T(8,128)S(1)} %get-tuple-element.53), channel_id=1, source_target_pairs={{0,4},{4,8},{8,12},{12,16},{16,20},{20,24},{24,28},{1,5},{5,9},{9,... | collective-permute-start | bytes 589832 | tf_op jit(solution)/shard_map/ppermute | solution.py:59
  89.4 1.3 collective-permute-start.13
  90.7 0.0 collective-permute-done.6.refs_5_
  90.7 0.0 collective-permute-done.7.refs_6_
  90.7 1.1 prepare.2
  91.8 0.1 widen.7
  91.9 5.3 %collective-permute-start.8 = (f32[80,16,128]{2,1,0:T(8,128)S(1)}, f32[80,16,128]{2,1,0:T(8,128)S(1)}, u32[]{:S(2)}, u32[]{:S(2)}) collective-permute-start(f32[80,16,128]{2,1,0:T(8,128)S(1)} %get-tuple-element.47), channel_id=1, source_target_pairs={{0,4},{4,8},{8,12},{12,16},{16,20},{20,24},{24,28},{1,5},{5,9},{9,... | collective-permute-start | bytes 1966088 | tf_op jit(solution)/shard_map/ppermute | solution.py:59
  97.2 1.3 collective-permute-start.9
  98.5 0.0 collective-permute-done.12.refs_7_
  98.6 0.0 collective-permute-done.13.refs_8_
  98.6 6.0 %step.2 = (f32[2,16,16,128]{3,2,1,0:T(8,128)S(1)}, f32[2,16,8,128]{3,2,1,0:T(8,128)S(1)}, f32[2,16,8,128]{3,2,1,0:T(8,128)S(1)}, f32[32,128]{1,0:T(8,128)S(1)}) custom-call(f32[32,4,128]{2,1,0:T(4,128)S(1)} %all_to_all.10.refs_0_.table_ref.refs_10_, f32[9,32,4,8,128]{4,3,2,1,0:T(8,128)S(1)} %get-tuple-element.46.refs_0_.refs_1_, ...), custom_call_target="tpu_custom_call" | custom-call | flops 6000000000 | bytes 18000000 | tf_op jit(solution)/shard_map/step/pallas_call | solution.py:44
  104.5 2.2 %collective-permute-start.14 = (f32[2,16,8,128]{3,2,1,0:T(8,128)S(1)}, f32[2,16,8,128]{3,2,1,0:T(8,128)S(1)}, u32[]{:S(2)}, u32[]{:S(2)}) collective-permute-start(f32[2,16,8,128]{3,2,1,0:T(8,128)S(1)} %get-tuple-element.57), channel_id=1, source_target_pairs={{0,1},{1,2},{2,3},{4,5},{5,6},{6,7},{8,9},{9,10},{10,11},{12,13},{... | collective-permute-start | bytes 393224 | tf_op jit(solution)/shard_map/ppermute | solution.py:59
  106.7 1.3 collective-permute-start.15
  108.0 1.2 collective-permute-done.14.z_low.refs_5_
  109.2 4.7 %collective-permute-done.15.z_high.refs_6_ = f32[2,16,8,128]{3,2,1,0:T(8,128)S(1)} collective-permute-done((f32[2,16,8,128]{3,2,1,0:T(8,128)S(1)}, f32[2,16,8,128]{3,2,1,0:T(8,128)S(1)}, u32[]{:S(2)}, u32[]{:S(2)}) %collective-permute-start.15) | collective-permute-done | bytes 131104 | tf_op jit(solution)/shard_map/ppermute | solution.py:59
  114.0 2.8 %collective-permute-start.16 = (f32[24,16,128]{2,1,0:T(8,128)S(1)}, f32[24,16,128]{2,1,0:T(8,128)S(1)}, u32[]{:S(2)}, u32[]{:S(2)}) collective-permute-start(f32[24,16,128]{2,1,0:T(8,128)S(1)} %get-tuple-element.59), channel_id=1, source_target_pairs={{0,4},{4,8},{8,12},{12,16},{16,20},{20,24},{24,28},{1,5},{5,9},{9,... | collective-permute-start | bytes 589832 | tf_op jit(solution)/shard_map/ppermute | solution.py:59
  116.8 1.5 %collective-permute-start.17 = (f32[24,16,128]{2,1,0:T(8,128)S(1)}, f32[24,16,128]{2,1,0:T(8,128)S(1)}, u32[]{:S(2)}, u32[]{:S(2)}) collective-permute-start(f32[24,16,128]{2,1,0:T(8,128)S(1)} %get-tuple-element.60), channel_id=1, source_target_pairs={{4,0},{8,4},{12,8},{16,12},{20,16},{24,20},{28,24},{5,1},{9,5},{13... | collective-permute-start | bytes 589832 | tf_op jit(solution)/shard_map/ppermute | solution.py:59
  118.3 0.0 collective-permute-done.8.refs_5_
  118.3 0.0 collective-permute-done.9.refs_6_
  118.3 1.0 prepare.3.refs_1_
  119.3 0.0 collective-permute-done.16.refs_7_
  119.3 4.2 %collective-permute-done.17.refs_8_ = f32[24,16,128]{2,1,0:T(8,128)S(1)} collective-permute-done((f32[24,16,128]{2,1,0:T(8,128)S(1)}, f32[24,16,128]{2,1,0:T(8,128)S(1)}, u32[]{:S(2)}, u32[]{:S(2)}) %collective-permute-start.17) | collective-permute-done | bytes 196640 | tf_op jit(solution)/shard_map/ppermute | solution.py:59
  123.6 6.3 %step.3 = (f32[16,16,128]{2,1,0:T(8,128)}, f32[16,16,128]{2,1,0:T(8,128)}, f32[32,128]{1,0:T(8,128)S(1)}) custom-call(f32[32,4,128]{2,1,0:T(4,128)S(1)} %all_to_all.10.refs_0_.table_ref.refs_10_, f32[9,32,4,8,128]{4,3,2,1,0:T(8,128)S(1)} %prepare.3.refs_1_, f32[5,32,4,8,128]{4,3,2,1,0:T(8,128)S(1)} %get-tuple-element.39.refs_1_.refs_2_, ...), custom_call_target="tpu_custom_call" | custom-call | flops 6000000000 | bytes 18000000 | tf_op jit(solution)/shard_map/step/pallas_call | solution.py:44
  129.9 15.1 %all_to_all.11 = f32[32,1,128]{2,1,0:T(1,128)S(1)} all-to-all(f32[32,1,128]{2,1,0:T(1,128)S(1)} %bitcast.7), channel_id=1, replica_groups=mesh['gx'=8,'gy'=4] {'gx','gy'}, dimensions={0} | all-to-all | bytes 32768 | tf_op jit(solution)/shard_map/all_to_all | solution.py:663
  144.9 0.1 reduce_sum.9
  145.0 0.6 reshape.9
  (14 shorter events, 0.1 us)
Async XLA Ops:
  2.1 9.8 %copy-start.11 = (f32[32,4,128]{2,1,0:T(4,128)S(1)}, f32[32,4,128]{2,1,0:T(4,128)}, u32[]{:S(2)}) copy-start(f32[32,4,128]{2,1,0:T(4,128)} %table.1.refs_11_) | copy-start | bytes 196612
  2.2 32.9 %copy-start = (f32[3,16,16,128]{3,2,1,0:T(8,128)S(1)}, f32[3,16,16,128]{3,2,1,0:T(8,128)}, u32[]{:S(2)}) copy-start(f32[3,16,16,128]{3,2,1,0:T(8,128)} %refs_0_.5) | copy-start | bytes 1179652
  2.2 32.9 %copy-start.1 = (f32[3,16,16,128]{3,2,1,0:T(8,128)S(1)}, f32[3,16,16,128]{3,2,1,0:T(8,128)}, u32[]{:S(2)}) copy-start(f32[3,16,16,128]{3,2,1,0:T(8,128)} %refs_1_.5) | copy-start | bytes 1179652
  2.2 32.9 %copy-start.2 = (f32[3,16,16,128]{3,2,1,0:T(8,128)S(1)}, f32[3,16,16,128]{3,2,1,0:T(8,128)}, u32[]{:S(2)}) copy-start(f32[3,16,16,128]{3,2,1,0:T(8,128)} %refs_2_.5) | copy-start | bytes 1179652
  2.2 32.9 %copy-start.3 = (f32[3,16,16,128]{3,2,1,0:T(8,128)S(1)}, f32[3,16,16,128]{3,2,1,0:T(8,128)}, u32[]{:S(2)}) copy-start(f32[3,16,16,128]{3,2,1,0:T(8,128)} %refs_3_.3) | copy-start | bytes 1179652
  2.2 32.9 %copy-start.4 = (f32[3,16,16,128]{3,2,1,0:T(8,128)S(1)}, f32[3,16,16,128]{3,2,1,0:T(8,128)}, u32[]{:S(2)}) copy-start(f32[3,16,16,128]{3,2,1,0:T(8,128)} %refs_4_.3) | copy-start | bytes 1179652
  2.2 32.9 %copy-start.5 = (f32[3,16,16,128]{3,2,1,0:T(8,128)S(1)}, f32[3,16,16,128]{3,2,1,0:T(8,128)}, u32[]{:S(2)}) copy-start(f32[3,16,16,128]{3,2,1,0:T(8,128)} %refs_5_.3) | copy-start | bytes 1179652
  2.2 32.9 %copy-start.6 = (f32[3,16,16,128]{3,2,1,0:T(8,128)S(1)}, f32[3,16,16,128]{3,2,1,0:T(8,128)}, u32[]{:S(2)}) copy-start(f32[3,16,16,128]{3,2,1,0:T(8,128)} %refs_6_.3) | copy-start | bytes 1179652
  2.2 32.9 %copy-start.7 = (f32[3,16,16,128]{3,2,1,0:T(8,128)S(1)}, f32[3,16,16,128]{3,2,1,0:T(8,128)}, u32[]{:S(2)}) copy-start(f32[3,16,16,128]{3,2,1,0:T(8,128)} %refs_7_.3) | copy-start | bytes 1179652
  2.3 32.9 %copy-start.9 = (f32[16,16,128]{2,1,0:T(8,128)S(1)}, f32[16,16,128]{2,1,0:T(8,128)}, u32[]{:S(2)}) copy-start(f32[16,16,128]{2,1,0:T(8,128)} %refs_8_.3) | copy-start | bytes 393220
  2.3 32.9 %copy-start.10 = (f32[16,16,128]{2,1,0:T(8,128)S(1)}, f32[16,16,128]{2,1,0:T(8,128)}, u32[]{:S(2)}) copy-start(f32[16,16,128]{2,1,0:T(8,128)} %refs_9_.3) | copy-start | bytes 393220
  5.6 33.5 %collective-permute-start = (f32[11,16,8,128]{3,2,1,0:T(8,128)}, f32[11,16,8,128]{3,2,1,0:T(8,128)S(1)}, u32[]{:S(2)}, u32[]{:S(2)}) collective-permute-start(f32[11,16,8,128]{3,2,1,0:T(8,128)} %get-tuple-element.35), channel_id=1, source_target_pairs={{0,1},{1,2},{2,3},{4,5},{5,6},{6,7},{8,9},{9,10},{10,11},{12,13},{... | collective-permute-start | bytes 2162696 | tf_op jit(solution)/shard_map/ppermute | solution.py:59
  10.6 28.5 %collective-permute-start.1 = (f32[11,16,8,128]{3,2,1,0:T(8,128)}, f32[11,16,8,128]{3,2,1,0:T(8,128)S(1)}, u32[]{:S(2)}, u32[]{:S(2)}) collective-permute-start(f32[11,16,8,128]{3,2,1,0:T(8,128)} %get-tuple-element.36), channel_id=1, source_target_pairs={{1,0},{2,1},{3,2},{5,4},{6,5},{7,6},{9,8},{10,9},{11,10},{13,12},{... | collective-permute-start | bytes 2162696 | tf_op jit(solution)/shard_map/ppermute | solution.py:59
  35.2 4.0 %copy-start.8 = (f32[11,16,16,128]{3,2,1,0:T(8,128)S(1)}, f32[11,16,16,128]{3,2,1,0:T(8,128)}, u32[]{:S(2)}) copy-start(f32[11,16,16,128]{3,2,1,0:T(8,128)} %get-tuple-element.34.own.refs_2_) | copy-start | bytes 4325380
  35.6 27.6 %collective-permute-start.4 = (f32[18,16,8,128]{3,2,1,0:T(8,128)S(1)}, f32[18,16,8,128]{3,2,1,0:T(8,128)S(1)}, u32[]{:S(2)}, u32[]{:S(2)}) collective-permute-start(f32[18,16,8,128]{3,2,1,0:T(8,128)S(1)} %get-tuple-element.41), channel_id=1, source_target_pairs={{0,1},{1,2},{2,3},{4,5},{5,6},{6,7},{8,9},{9,10},{10,11},{12,13},{... | collective-permute-start | bytes 3538952 | tf_op jit(solution)/shard_map/ppermute | solution.py:59
  37.8 29.6 %collective-permute-start.5 = (f32[18,16,8,128]{3,2,1,0:T(8,128)S(1)}, f32[18,16,8,128]{3,2,1,0:T(8,128)S(1)}, u32[]{:S(2)}, u32[]{:S(2)}) collective-permute-start(f32[18,16,8,128]{3,2,1,0:T(8,128)S(1)} %get-tuple-element.42), channel_id=1, source_target_pairs={{1,0},{2,1},{3,2},{5,4},{6,5},{7,6},{9,8},{10,9},{11,10},{13,12},{... | collective-permute-start | bytes 3538952 | tf_op jit(solution)/shard_map/ppermute | solution.py:59
  39.4 30.9 %collective-permute-start.2 = (f32[116,16,128]{2,1,0:T(8,128)S(1)}, f32[116,16,128]{2,1,0:T(8,128)S(1)}, u32[]{:S(2)}, u32[]{:S(2)}) collective-permute-start(f32[116,16,128]{2,1,0:T(8,128)S(1)} %get-tuple-element.38), channel_id=1, source_target_pairs={{0,4},{4,8},{8,12},{12,16},{16,20},{20,24},{24,28},{1,5},{5,9},{9,... | collective-permute-start | bytes 2850824 | tf_op jit(solution)/shard_map/ppermute | solution.py:59
  41.2 29.1 %collective-permute-start.3 = (f32[116,16,128]{2,1,0:T(8,128)S(1)}, f32[116,16,128]{2,1,0:T(8,128)S(1)}, u32[]{:S(2)}, u32[]{:S(2)}) collective-permute-start(f32[116,16,128]{2,1,0:T(8,128)S(1)} %get-tuple-element.37._), channel_id=1, source_target_pairs={{4,0},{8,4},{12,8},{16,12},{20,16},{24,20},{28,24},{5,1},{9,5},{13... | collective-permute-start | bytes 2850824 | tf_op jit(solution)/shard_map/ppermute | solution.py:59
  67.6 23.1 %collective-permute-start.6 = (f32[100,16,128]{2,1,0:T(8,128)S(1)}, f32[100,16,128]{2,1,0:T(8,128)S(1)}, u32[]{:S(2)}, u32[]{:S(2)}) collective-permute-start(f32[100,16,128]{2,1,0:T(8,128)S(1)} %get-tuple-element.44), channel_id=1, source_target_pairs={{0,4},{4,8},{8,12},{12,16},{16,20},{20,24},{24,28},{1,5},{5,9},{9,... | collective-permute-start | bytes 2457608 | tf_op jit(solution)/shard_map/ppermute | solution.py:59
  68.9 21.8 %collective-permute-start.7 = (f32[100,16,128]{2,1,0:T(8,128)S(1)}, f32[100,16,128]{2,1,0:T(8,128)S(1)}, u32[]{:S(2)}, u32[]{:S(2)}) collective-permute-start(f32[100,16,128]{2,1,0:T(8,128)S(1)} %get-tuple-element.45), channel_id=1, source_target_pairs={{4,0},{8,4},{12,8},{16,12},{20,16},{24,20},{28,24},{5,1},{9,5},{13... | collective-permute-start | bytes 2457608 | tf_op jit(solution)/shard_map/ppermute | solution.py:59
  77.4 4.6 %collective-permute-start.10 = (f32[2,16,8,128]{3,2,1,0:T(8,128)S(1)}, f32[2,16,8,128]{3,2,1,0:T(8,128)S(1)}, u32[]{:S(2)}, u32[]{:S(2)}) collective-permute-start(f32[2,16,8,128]{3,2,1,0:T(8,128)S(1)} %get-tuple-element.51), channel_id=1, source_target_pairs={{0,1},{1,2},{2,3},{4,5},{5,6},{6,7},{8,9},{9,10},{10,11},{12,13},{... | collective-permute-start | bytes 393224 | tf_op jit(solution)/shard_map/ppermute | solution.py:59
  79.4 7.4 %collective-permute-start.11 = (f32[2,16,8,128]{3,2,1,0:T(8,128)S(1)}, f32[2,16,8,128]{3,2,1,0:T(8,128)S(1)}, u32[]{:S(2)}, u32[]{:S(2)}) collective-permute-start(f32[2,16,8,128]{3,2,1,0:T(8,128)S(1)} %get-tuple-element.52), channel_id=1, source_target_pairs={{1,0},{2,1},{3,2},{5,4},{6,5},{7,6},{9,8},{10,9},{11,10},{13,12},{... | collective-permute-start | bytes 393224 | tf_op jit(solution)/shard_map/ppermute | solution.py:59
  86.8 11.8 %collective-permute-start.12 = (f32[24,16,128]{2,1,0:T(8,128)S(1)}, f32[24,16,128]{2,1,0:T(8,128)S(1)}, u32[]{:S(2)}, u32[]{:S(2)}) collective-permute-start(f32[24,16,128]{2,1,0:T(8,128)S(1)} %get-tuple-element.53), channel_id=1, source_target_pairs={{0,4},{4,8},{8,12},{12,16},{16,20},{20,24},{24,28},{1,5},{5,9},{9,... | collective-permute-start | bytes 589832 | tf_op jit(solution)/shard_map/ppermute | solution.py:59
  89.4 9.1 %collective-permute-start.13 = (f32[24,16,128]{2,1,0:T(8,128)S(1)}, f32[24,16,128]{2,1,0:T(8,128)S(1)}, u32[]{:S(2)}, u32[]{:S(2)}) collective-permute-start(f32[24,16,128]{2,1,0:T(8,128)S(1)} %get-tuple-element.54), channel_id=1, source_target_pairs={{4,0},{8,4},{12,8},{16,12},{20,16},{24,20},{28,24},{5,1},{9,5},{13... | collective-permute-start | bytes 589832 | tf_op jit(solution)/shard_map/ppermute | solution.py:59
  91.9 26.4 %collective-permute-start.8 = (f32[80,16,128]{2,1,0:T(8,128)S(1)}, f32[80,16,128]{2,1,0:T(8,128)S(1)}, u32[]{:S(2)}, u32[]{:S(2)}) collective-permute-start(f32[80,16,128]{2,1,0:T(8,128)S(1)} %get-tuple-element.47), channel_id=1, source_target_pairs={{0,4},{4,8},{8,12},{12,16},{16,20},{20,24},{24,28},{1,5},{5,9},{9,... | collective-permute-start | bytes 1966088 | tf_op jit(solution)/shard_map/ppermute | solution.py:59
  97.2 21.0 %collective-permute-start.9 = (f32[80,16,128]{2,1,0:T(8,128)S(1)}, f32[80,16,128]{2,1,0:T(8,128)S(1)}, u32[]{:S(2)}, u32[]{:S(2)}) collective-permute-start(f32[80,16,128]{2,1,0:T(8,128)S(1)} %get-tuple-element.48), channel_id=1, source_target_pairs={{4,0},{8,4},{12,8},{16,12},{20,16},{24,20},{28,24},{5,1},{9,5},{13... | collective-permute-start | bytes 1966088 | tf_op jit(solution)/shard_map/ppermute | solution.py:59
  104.5 4.7 %collective-permute-start.14 = (f32[2,16,8,128]{3,2,1,0:T(8,128)S(1)}, f32[2,16,8,128]{3,2,1,0:T(8,128)S(1)}, u32[]{:S(2)}, u32[]{:S(2)}) collective-permute-start(f32[2,16,8,128]{3,2,1,0:T(8,128)S(1)} %get-tuple-element.57), channel_id=1, source_target_pairs={{0,1},{1,2},{2,3},{4,5},{5,6},{6,7},{8,9},{9,10},{10,11},{12,13},{... | collective-permute-start | bytes 393224 | tf_op jit(solution)/shard_map/ppermute | solution.py:59
  106.7 7.2 %collective-permute-start.15 = (f32[2,16,8,128]{3,2,1,0:T(8,128)S(1)}, f32[2,16,8,128]{3,2,1,0:T(8,128)S(1)}, u32[]{:S(2)}, u32[]{:S(2)}) collective-permute-start(f32[2,16,8,128]{3,2,1,0:T(8,128)S(1)} %get-tuple-element.58), channel_id=1, source_target_pairs={{1,0},{2,1},{3,2},{5,4},{6,5},{7,6},{9,8},{10,9},{11,10},{13,12},{... | collective-permute-start | bytes 393224 | tf_op jit(solution)/shard_map/ppermute | solution.py:59
  114.0 5.3 %collective-permute-start.16 = (f32[24,16,128]{2,1,0:T(8,128)S(1)}, f32[24,16,128]{2,1,0:T(8,128)S(1)}, u32[]{:S(2)}, u32[]{:S(2)}) collective-permute-start(f32[24,16,128]{2,1,0:T(8,128)S(1)} %get-tuple-element.59), channel_id=1, source_target_pairs={{0,4},{4,8},{8,12},{12,16},{16,20},{20,24},{24,28},{1,5},{5,9},{9,... | collective-permute-start | bytes 589832 | tf_op jit(solution)/shard_map/ppermute | solution.py:59
  116.8 6.8 %collective-permute-start.17 = (f32[24,16,128]{2,1,0:T(8,128)S(1)}, f32[24,16,128]{2,1,0:T(8,128)S(1)}, u32[]{:S(2)}, u32[]{:S(2)}) collective-permute-start(f32[24,16,128]{2,1,0:T(8,128)S(1)} %get-tuple-element.60), channel_id=1, source_target_pairs={{4,0},{8,4},{12,8},{16,12},{20,16},{24,20},{28,24},{5,1},{9,5},{13... | collective-permute-start | bytes 589832 | tf_op jit(solution)/shard_map/ppermute | solution.py:59

commit v8 on v7

--- a/solution.py
+++ b/solution.py
@@ -53,10 +53,24 @@
     )(*ins)
 
 
-def shifted(value, axis, by):
+def swaps(first, second, axis):
     length = lax.axis_size(axis)
-    pairs = [(i, i + by) for i in range(length) if 0 <= i + by < length]
-    return lax.ppermute(value, axis, pairs)
+    even = [(i, i ^ 1) for i in range(length) if i ^ 1 < length]
+    odd = [(i, i + 1) for i in range(1, length - 1, 2)]
+    odd += [(j, i) for i, j in odd]
+    return lax.ppermute(first, axis, even), lax.ppermute(second, axis, odd)
+
+
+def by_side(axis, work, first, second):
+    at = lax.axis_index(axis) % 2
+
+    @pl.when(at == 1)
+    def _():
+        work(first, second)
+
+    @pl.when(at == 0)
+    def _():
+        work(second, first)
 
 
 def load_kernel(leads, *refs):
@@ -73,7 +87,7 @@
         c.start()
     for c in copies:
         c.wait()
-    y_edges(own, y_low, y_high)
+    by_side("gy", lambda low, high: y_edges(own, low, high), y_low, y_high)
 
 
 def y_edges(own, low, high):
@@ -104,15 +118,18 @@
     ins, holders, (y_low, y_high) = refs[:count], refs[count + 1 : -2], refs[-2:]
     rx, ry = y_low.shape[1], holders[0].shape[2]
 
-    def row(x, _):
-        for n, (i, lead, h, m) in enumerate(plan):
-            value = ins[i][x] if lead is None else ins[i][lead, x]
-            holders[h][m, x] = value
-            y_low[n, x] = value[0:H]
-            y_high[n, x] = value[ry - H :]
-        return 0
-
-    lax.fori_loop(0, rx, row, 0)
+    def work(low, high):
+        def row(x, _):
+            for n, (i, lead, h, m) in enumerate(plan):
+                value = ins[i][x] if lead is None else ins[i][lead, x]
+                holders[h][m, x] = value
+                low[n, x] = value[0:H]
+                high[n, x] = value[ry - H :]
+            return 0
+
+        lax.fori_loop(0, rx, row, 0)
+
+    by_side("gy", work, y_low, y_high)
 
 
 def more(arrays, plan, sizes, dims, after):
@@ -160,27 +177,33 @@
     return parts, row
 
 
-def widen_kernel(reaches, first, own, z_low, z_high, *refs):
-    outs = refs[-2:]
+def widen_kernel(reaches, first, own, z_first, z_second, *refs):
     rx = own.shape[1]
-    for begin, count, reach, base in parts_of(reaches)[0]:
-
-        def one(k, _):
-            n = begin + k
-            at = base + k * rows_of_array(reach)
-            for side in (0, 1):
-                start = 0 if side == 0 else rx - reach
-                outs[side][pl.ds(at, reach)] = own[n, start : start + reach]
-                for high, z in ((0, z_low), (1, z_high)):
-
-                    def row(dx):
-                        return z[n + first, dx - 1 if side == 0 else rx - dx]
-
-                    for t, tile in enumerate(fold(row, reach, high == 1)):
-                        outs[side][at + reach + t, high * H : (high + 1) * H, :] = tile
-            return 0
-
-        lax.fori_loop(0, count, one, 0)
+
+    def work(z_low, z_high, outs):
+        for begin, count, reach, base in parts_of(reaches)[0]:
+
+            def one(k, _):
+                n = begin + k
+                at = base + k * rows_of_array(reach)
+                for side in (0, 1):
+                    start = 0 if side == 0 else rx - reach
+                    outs[side][pl.ds(at, reach)] = own[n, start : start + reach]
+                    for high, z in ((0, z_low), (1, z_high)):
+
+                        def row(dx):
+                            return z[n + first, dx - 1 if side == 0 else rx - dx]
+
+                        for t, tile in enumerate(fold(row, reach, high == 1)):
+                            outs[side][at + reach + t, high * H : (high + 1) * H, :] = tile
+                return 0
+
+            lax.fori_loop(0, count, one, 0)
+
+    def along_x(low, high):
+        by_side("gy", lambda a, b: work(a, b, (low, high)), z_first, z_second)
+
+    by_side("gx", along_x, *refs[-2:])
 
 
 def widen(own, reaches, z_low, z_high, after=(), first=0):
@@ -283,39 +306,51 @@
     return pltpu.roll(value, by, 2)
 
 
-def fill(dst, own, reaches, z_low, z_high, sides, first=0):
+def fill(dst, own, reaches, z_got, x_got, first=0):
     rx, ry, nz = own.shape[1:]
-    for begin, count, reach, base in parts_of(reaches)[0]:
-
-        def one(k, _):
-            n = begin + k
-            row = base + k * rows_of_array(reach)
+
+    def middle(z_low, z_high):
+        def one(n, _):
             dst[n, H : H + rx, 0:H, :] = z_low[n + first]
             dst[n, H : H + rx, H : H + ry, :] = own[n]
             dst[n, H : H + rx, H + ry : 2 * H + ry, :] = z_high[n + first]
-            for side in (0, 1):
-                at = H - reach if side == 0 else H + rx
-                dst[n, at : at + reach, H : H + ry, :] = sides[side][pl.ds(row, reach)]
-                known = set()
-                for y in (0, 1):
-                    to = y * (H + ry)
-                    for t in range(tiles_of(reach)):
-                        tile = sides[side][row + reach + t, y * H : (y + 1) * H, :]
-                        near, far = unfold(tile, t + 1, y == 1)
-                        for dx, value in ((t + 1, near), (reach - t - 1, far)):
-                            x = H - dx if side == 0 else H + rx + dx - 1
-                            dst[n, x, to : to + H, :] = value
-                            known.add(dx)
-                for dx in range(1, H + 1):
-                    x = H - dx if side == 0 else H + rx + dx - 1
-                    if dx not in known:
-                        for y in (0, H + ry):
-                            dst[n, x, y : y + H, :] = jnp.zeros((H, nz), F32)
-                    if dx > reach:
-                        dst[n, x, H : H + ry, :] = jnp.zeros((ry, nz), F32)
             return 0
 
-        lax.fori_loop(0, count, one, 0)
+        lax.fori_loop(0, len(reaches), one, 0)
+
+    def outer(x_low, x_high):
+        sides = (x_low, x_high)
+        for begin, count, reach, base in parts_of(reaches)[0]:
+
+            def one(k, _):
+                n = begin + k
+                row = base + k * rows_of_array(reach)
+                for side in (0, 1):
+                    at = H - reach if side == 0 else H + rx
+                    dst[n, at : at + reach, H : H + ry, :] = sides[side][pl.ds(row, reach)]
+                    known = set()
+                    for y in (0, 1):
+                        to = y * (H + ry)
+                        for t in range(tiles_of(reach)):
+                            tile = sides[side][row + reach + t, y * H : (y + 1) * H, :]
+                            near, far = unfold(tile, t + 1, y == 1)
+                            for dx, value in ((t + 1, near), (reach - t - 1, far)):
+                                x = H - dx if side == 0 else H + rx + dx - 1
+                                dst[n, x, to : to + H, :] = value
+                                known.add(dx)
+                    for dx in range(1, H + 1):
+                        x = H - dx if side == 0 else H + rx + dx - 1
+                        if dx not in known:
+                            for y in (0, H + ry):
+                                dst[n, x, y : y + H, :] = jnp.zeros((H, nz), F32)
+                        if dx > reach:
+                            dst[n, x, H : H + ry, :] = jnp.zeros((ry, nz), F32)
+                return 0
+
+            lax.fori_loop(0, count, one, 0)
+
+    by_side("gy", middle, *z_got)
+    by_side("gx", outer, *x_got)
 
 
 GEO, COEF = 8, 7
@@ -393,18 +428,24 @@
     rx, ry, nz = frac.shape[-3:]
     out_wells = outs[-1]
 
-    def copy(x, _):
-        for f in range(2):
-            row = lin[f, H + x, H : H + ry, :]
-            if last:
-                outs[f][x] = row
-            else:
-                outs[0][f, x] = row
-                outs[1][f, x] = row[0:H]
-                outs[2][f, x] = row[ry - H :]
-        return 0
-
-    lax.fori_loop(0, rx, copy, 0, unroll=2)
+    def copies(low, high):
+        def copy(x, _):
+            for f in range(2):
+                row = lin[f, H + x, H : H + ry, :]
+                if last:
+                    outs[f][x] = row
+                else:
+                    outs[0][f, x] = row
+                    low[f, x] = row[0:H]
+                    high[f, x] = row[ry - H :]
+            return 0
+
+        lax.fori_loop(0, rx, copy, 0, unroll=2)
+
+    if last:
+        copies(None, None)
+    else:
+        by_side("gy", copies, outs[1], outs[2])
     mix = lin[0, H : H + rx, H : H + ry, :] + frac[...] * lin[1, H : H + rx, H : H + ry, :]
     mix = mix.reshape(rx * ry, nz)
     here_x, here_y, _, n_y = spot()
@@ -449,7 +490,7 @@
     raw, coef, fa0, fb0, fa1, fb1, lin = refs[12:]
     rx, ry, nz = own.shape[1:]
     ex = rx + 2 * H
-    fill(raw, own, TOP_REACH, z_low, z_high, (x_low, x_high))
+    fill(raw, own, TOP_REACH, (z_low, z_high), (x_low, x_high))
     here_x, here_y, _, _ = spot()
 
     @pl.when(here_x == 0)
@@ -508,7 +549,7 @@
         acc, coef, raw = refs[7:]
     rx, ry, nz = own.shape[1:]
     ex = rx + 2 * H
-    fill(raw, own, (COEF,) * own.shape[0], z_low, z_high, (x_low, x_high), first)
+    fill(raw, own, (COEF,) * own.shape[0], (z_low, z_high), (x_low, x_high), first)
 
     def prepare(x, _):
         s_a, r_a, p, frac, r_b, q, m, s_b = coefficients(
@@ -540,7 +581,7 @@
     now, fa0, fb0, fa1, fb1, lin = refs[-6:]
     rx, ry, nz = own.shape[1:]
     ex = rx + 2 * H
-    fill(lin, lam, LAM_REACH, z_low, z_high, (x_low, x_high))
+    fill(lin, lam, LAM_REACH, (z_low, z_high), (x_low, x_high))
 
     def begin(x, _):
         a, b = by_v(lin, (0,), x), by_v(lin, (1,), x)
@@ -572,9 +613,6 @@
     devices = lax.axis_size("gx") * lax.axis_size("gy")
     own = [c_pp, c_ss, c_ps, c_sp, frac, mobility, grad_p, grad_s]
     top = steps - 1
-
-    def sent(low, high, axis):
-        return shifted(high, axis, 1), shifted(low, axis, -1)
 
     arrays = [trans_x, trans_y, trans_z] + own
     leads = [None] * 3 + [top] * 8
@@ -590,12 +628,12 @@
         name="table",
     )(*small)
     blocks, y_low, y_high, token = load(arrays, leads, dims, (mine,))
-    z_got = sent(y_low, y_high, "gy")
+    z_got = swaps(y_low, y_high, "gy")
     mine, _ = lax.optimization_barrier((mine, token))
     table = lax.all_to_all(mine, ("gx", "gy"), 0, 0, tiled=True)
 
     wide = widen(blocks, TOP_REACH, *z_got, (table,))
-    x_got = sent(*wide, "gx")
+    x_got = swaps(*wide, "gx")
     src = call(
         functools.partial(source_kernel, steps, wells), [table, wide[0]],
         [sds(steps, ex, ey, nz)], "sources", 8, [VMEM, ANY],
@@ -609,12 +647,12 @@
             plan += [(8, None, h, 8), (9, None, h, 9)]
         sizes.append(len(plan) - places[step])
     *holders, m_low, m_high = more(own + [acc_p, acc_s], plan, sizes, dims, table)
-    m_z = sent(m_low, m_high, "gy")
+    m_z = swaps(m_low, m_high, "gy")
     held = dict(zip(reversed(range(top)), holders))
 
     def beside(step, after):
         group = held[step]
-        return sent(
+        return swaps(
             *widen(group, (COEF,) * group.shape[0], *m_z, (after,), places[step]), "gx"
         )
 
@@ -648,8 +686,8 @@
         if with_acc:
             acc = made[1]
 
-        l_z = sent(low, high, "gy")
-        l_x = sent(*widen(lam, LAM_REACH, *l_z), "gx")
+        l_z = swaps(low, high, "gy")
+        l_x = swaps(*widen(lam, LAM_REACH, *l_z), "gx")
         outs = [sds(rx, ry, nz)] * 2 if last else lam_out
         outs = call(
             functools.partial(sweep_kernel, last, step, steps, wells),

time: 146 us -> 131 us (0.90)
  waiting for transfers between devices: 40.1 us -> 27.2 us
  starting transfers between devices: 37.1 us -> 27.9 us
  blocking collectives: 38.2 us -> 44.9 us
    ppermute x18, waiting for transfers between devices: 40.1 us -> 27.2 us  [swaps(): return (lax.ppermute(first, axis, even), lax.ppermute(second, axis, odd))]
    ppermute x18, starting transfers between devices: 37.1 us -> 27.9 us  [swaps(): return (lax.ppermute(first, axis, even), lax.ppermute(second, axis, odd))]
    all_to_all x1, blocking collectives: 15.1 us -> 22.1 us  [local(): parts = lax.all_to_all(dense[:, None, :], ('gx', 'gy'), 0, 0, tiled=True)]
  transfers between devices with their start and end apart: 18 -> 18, of which waited for: 7 -> 3; matrix products, arithmetic and copies ran while one was open for 0% -> 0% of each run, Pallas kernels for 12% -> 13%
where the time goes in v8:
time: 131 us
  blocking collectives  44.9 us (34%)
  Pallas kernels  28.7 us (22%)
  starting transfers between devices  27.9 us (21%)
  waiting for transfers between devices  27.2 us (21%)
    ppermute x18, starting transfers between devices, swaps(): return (lax.ppermute(first, axis, even), lax.ppermute(second, axis, odd))  27.9 us
    ppermute x18, waiting for transfers between devices, swaps(): return (lax.ppermute(first, axis, even), lax.ppermute(second, axis, odd))  27.2 us
    pallas_call x12, Pallas kernels, call(): pl.pallas_call(kernel, in_specs=specs or [VMEM] * len(ins), out_specs=[VM...  23.9 us
    all_to_all x1, blocking collectives, local(): table = lax.all_to_all(mine, ('gx', 'gy'), 0, 0, tiled=True)  22.8 us
    all_to_all x1, blocking collectives, local(): parts = lax.all_to_all(dense[:, None, :], ('gx', 'gy'), 0, 0, tiled=True)  22.1 us
    pallas_call x1, Pallas kernels, load(): pl.pallas_call(functools.partial(load_kernel, leads), in_specs=[HBM] * n...  3.35 us
  transfers between devices with their start and end apart: 18, of which 3 were waited for; matrix products, arithmetic and copies ran while one was open for 0% of the time, Pallas kernels for 13%

profile of v8, /device:TPU:0, one launch (start us, length us, event | category | flops | bytes accessed | tf_op | source)
XLA Modules:
  0.0 130.6 jit_solution(3039326437534665721)
XLA Ops:
  0.6 1.5 %table.1.refs_11_ = f32[32,4,128]{2,1,0:T(4,128)} custom-call(f32[2,3]{1,0:T(2,128)} %refs_0_.3, f32[2,3]{1,0:T(2,128)} %refs_1_.3, s32[2,3]{1,0:T(2,128)} %refs_2_.3, s32[1,128]{1,0:T(1,128)} %bitcast.8, s32[1,128]{1,0:T(1,128)} %bitcast.9, f32[1,128]{1,0:T(1,128)} %bitcast.10), custom_call_target="tpu_custom_call" | custom-call | tf_op jit(solution)/shard_map/table/pallas_call | solution.py:621
  2.1 0.0 copy-start.11
  2.2 0.0 copy-start
  2.2 0.0 copy-start.1
  2.2 0.0 copy-start.2
  2.2 0.0 copy-start.3
  2.2 0.0 copy-start.4
  2.2 0.0 copy-start.5
  2.2 0.0 copy-start.6
  2.2 0.0 copy-start.7
  2.3 0.0 copy-start.9
  2.3 0.0 copy-start.10
  2.3 3.4 %load.1 = (f32[11,16,16,128]{3,2,1,0:T(8,128)}, f32[11,16,8,128]{3,2,1,0:T(8,128)}, f32[11,16,8,128]{3,2,1,0:T(8,128)}, f32[8,128]{1,0:T(8,128)}) custom-call(f32[16,16,128]{2,1,0:T(8,128)} %refs_0_.4, f32[16,16,128]{2,1,0:T(8,128)} %refs_1_.4, f32[16,16,128]{2,1,0:T(8,128)} %refs_2_.4, f32[3,16,16,128]{3,2,1,0:T(8,128)} %refs_0_.5, ...), custom_call_target="tpu_custom_call" | custom-call | tf_op jit(solution)/shard_map/load/pallas_call | solution.py:107
  5.6 3.1 %collective-permute-start = (f32[11,16,8,128]{3,2,1,0:T(8,128)}, f32[11,16,8,128]{3,2,1,0:T(8,128)S(1)}, u32[]{:S(2)}, u32[]{:S(2)}) collective-permute-start(f32[11,16,8,128]{3,2,1,0:T(8,128)} %get-tuple-element.35), channel_id=1, source_target_pairs={{0,1},{1,0},{2,3},{3,2},{4,5},{5,4},{6,7},{7,6},{8,9},{9,8},{10,11... | collective-permute-start | bytes 2162696 | tf_op jit(solution)/shard_map/ppermute | solution.py:61
  8.7 0.7 collective-permute-start.1
  9.4 22.8 %all_to_all.10.refs_0_.table_ref.refs_10_ = f32[32,4,128]{2,1,0:T(4,128)S(1)} all-to-all(f32[32,4,128]{2,1,0:T(4,128)S(1)} %copy-done.11), channel_id=1, replica_groups=mesh['gx'=8,'gy'=4] {'gx','gy'}, dimensions={0} | all-to-all | bytes 131072 | tf_op jit(solution)/shard_map/all_to_all | solution.py:633
  32.3 0.0 copy-done
  32.3 0.4 more.1
  32.8 0.8 collective-permute-start.4
  33.5 0.7 collective-permute-start.5
  34.3 0.0 collective-permute-done.z_first.refs_3_
  34.3 0.0 collective-permute-done.1.z_second.refs_4_
  34.3 0.2 widen.5
  34.5 0.7 collective-permute-start.3
  35.3 2.0 %collective-permute-start.2 = (f32[116,16,128]{2,1,0:T(8,128)S(1)}, f32[116,16,128]{2,1,0:T(8,128)S(1)}, u32[]{:S(2)}, u32[]{:S(2)}) collective-permute-start(f32[116,16,128]{2,1,0:T(8,128)S(1)} %get-tuple-element.37._), channel_id=1, source_target_pairs={{0,4},{4,0},{8,12},{12,8},{16,20},{20,16},{24,28},{28,24},{1,5},{5... | collective-permute-start | bytes 2850824 | tf_op jit(solution)/shard_map/ppermute | solution.py:61
  37.3 1.0 sources.1.refs_1_.refs_0_
  38.3 22.5 %collective-permute-done.4.z_first.refs_3_ = f32[18,16,8,128]{3,2,1,0:T(8,128)S(1)} collective-permute-done((f32[18,16,8,128]{3,2,1,0:T(8,128)S(1)}, f32[18,16,8,128]{3,2,1,0:T(8,128)S(1)}, u32[]{:S(2)}, u32[]{:S(2)}) %collective-permute-start.4) | collective-permute-done | bytes 1179680 | tf_op jit(solution)/shard_map/ppermute | solution.py:61
  60.8 0.0 collective-permute-done.5.z_second.refs_4_
  60.8 0.2 widen.6
  61.0 0.1 collective-permute-start.6
  61.1 0.7 collective-permute-start.7
  61.8 0.0 collective-permute-done.3.refs_6_
  61.8 0.0 collective-permute-done.2.refs_5_
  61.8 7.1 %step_top.1 = (f32[5,32,4,8,128]{4,3,2,1,0:T(8,128)S(1)}, f32[2,16,16,128]{3,2,1,0:T(8,128)S(1)}, f32[2,16,8,128]{3,2,1,0:T(8,128)S(1)}, f32[2,16,8,128]{3,2,1,0:T(8,128)S(1)}, f32[32,128]{1,0:T(8,128)S(1)}) custom-call(f32[32,4,128]{2,1,0:T(4,128)S(1)} %all_to_all.10.refs_0_.table_ref.refs_10_, f32[3,32,32,128]{3,2,1,0:T(8,128)S(1)} %sources.1.refs_1_.refs_0_, ...), custom_call_target="tpu_custom_call" | custom-call | flops 7000000000 | bytes 21000000 | tf_op jit(solution)/shard_map/step_top/pallas_call | solution.py:44
  69.0 3.5 %collective-permute-start.10 = (f32[2,16,8,128]{3,2,1,0:T(8,128)S(1)}, f32[2,16,8,128]{3,2,1,0:T(8,128)S(1)}, u32[]{:S(2)}, u32[]{:S(2)}) collective-permute-start(f32[2,16,8,128]{3,2,1,0:T(8,128)S(1)} %get-tuple-element.51), channel_id=1, source_target_pairs={{0,1},{1,0},{2,3},{3,2},{4,5},{5,4},{6,7},{7,6},{8,9},{9,8},{10,11... | collective-permute-start | bytes 393224 | tf_op jit(solution)/shard_map/ppermute | solution.py:61
  72.4 0.7 collective-permute-start.11
  73.1 2.4 %collective-permute-done.10.z_first.refs_5_ = f32[2,16,8,128]{3,2,1,0:T(8,128)S(1)} collective-permute-done((f32[2,16,8,128]{3,2,1,0:T(8,128)S(1)}, f32[2,16,8,128]{3,2,1,0:T(8,128)S(1)}, u32[]{:S(2)}, u32[]{:S(2)}) %collective-permute-start.10) | collective-permute-done | bytes 131104 | tf_op jit(solution)/shard_map/ppermute | solution.py:61
  75.5 0.0 collective-permute-done.11.z_second.refs_6_
  75.5 1.2 collective-permute-start.12
  76.7 0.7 collective-permute-start.13
  77.4 0.0 collective-permute-done.6.refs_5_
  77.4 0.0 collective-permute-done.7.refs_6_
  77.4 1.1 prepare.2
  78.5 0.2 widen.7
  78.7 6.4 %collective-permute-start.8 = (f32[80,16,128]{2,1,0:T(8,128)S(1)}, f32[80,16,128]{2,1,0:T(8,128)S(1)}, u32[]{:S(2)}, u32[]{:S(2)}) collective-permute-start(f32[80,16,128]{2,1,0:T(8,128)S(1)} %get-tuple-element.47), channel_id=1, source_target_pairs={{0,4},{4,0},{8,12},{12,8},{16,20},{20,16},{24,28},{28,24},{1,5},{5... | collective-permute-start | bytes 1966088 | tf_op jit(solution)/shard_map/ppermute | solution.py:61
  85.1 0.7 collective-permute-start.9
  85.8 0.0 collective-permute-done.12.refs_7_
  85.8 0.0 collective-permute-done.13.refs_8_
  85.8 6.0 %step.2 = (f32[2,16,16,128]{3,2,1,0:T(8,128)S(1)}, f32[2,16,8,128]{3,2,1,0:T(8,128)S(1)}, f32[2,16,8,128]{3,2,1,0:T(8,128)S(1)}, f32[32,128]{1,0:T(8,128)S(1)}) custom-call(f32[32,4,128]{2,1,0:T(4,128)S(1)} %all_to_all.10.refs_0_.table_ref.refs_10_, f32[9,32,4,8,128]{4,3,2,1,0:T(8,128)S(1)} %get-tuple-element.46.refs_0_.refs_1_, ...), custom_call_target="tpu_custom_call" | custom-call | flops 6000000000 | bytes 18000000 | tf_op jit(solution)/shard_map/step/pallas_call | solution.py:44
  91.8 3.5 %collective-permute-start.14 = (f32[2,16,8,128]{3,2,1,0:T(8,128)S(1)}, f32[2,16,8,128]{3,2,1,0:T(8,128)S(1)}, u32[]{:S(2)}, u32[]{:S(2)}) collective-permute-start(f32[2,16,8,128]{3,2,1,0:T(8,128)S(1)} %get-tuple-element.57), channel_id=1, source_target_pairs={{0,1},{1,0},{2,3},{3,2},{4,5},{5,4},{6,7},{7,6},{8,9},{9,8},{10,11... | collective-permute-start | bytes 393224 | tf_op jit(solution)/shard_map/ppermute | solution.py:61
  95.2 0.7 collective-permute-start.15
  95.9 2.3 %collective-permute-done.14.z_first.refs_5_ = f32[2,16,8,128]{3,2,1,0:T(8,128)S(1)} collective-permute-done((f32[2,16,8,128]{3,2,1,0:T(8,128)S(1)}, f32[2,16,8,128]{3,2,1,0:T(8,128)S(1)}, u32[]{:S(2)}, u32[]{:S(2)}) %collective-permute-start.14) | collective-permute-done | bytes 131104 | tf_op jit(solution)/shard_map/ppermute | solution.py:61
  98.2 0.0 collective-permute-done.15.z_second.refs_6_
  98.2 1.3 collective-permute-start.16
  99.5 0.7 collective-permute-start.17
  100.2 0.0 collective-permute-done.8.refs_5_
  100.2 0.0 collective-permute-done.9.refs_6_
  100.2 1.0 prepare.3.refs_1_
  101.2 0.0 collective-permute-done.16.refs_7_
  101.2 0.0 collective-permute-done.17.refs_8_
  101.3 6.5 %step.3 = (f32[16,16,128]{2,1,0:T(8,128)}, f32[16,16,128]{2,1,0:T(8,128)}, f32[32,128]{1,0:T(8,128)S(1)}) custom-call(f32[32,4,128]{2,1,0:T(4,128)S(1)} %all_to_all.10.refs_0_.table_ref.refs_10_, f32[9,32,4,8,128]{4,3,2,1,0:T(8,128)S(1)} %prepare.3.refs_1_, f32[5,32,4,8,128]{4,3,2,1,0:T(8,128)S(1)} %get-tuple-element.39.refs_1_.refs_2_, ...), custom_call_target="tpu_custom_call" | custom-call | flops 6000000000 | bytes 18000000 | tf_op jit(solution)/shard_map/step/pallas_call | solution.py:44
  107.8 22.1 %all_to_all.11 = f32[32,1,128]{2,1,0:T(1,128)S(1)} all-to-all(f32[32,1,128]{2,1,0:T(1,128)S(1)} %bitcast.7), channel_id=1, replica_groups=mesh['gx'=8,'gy'=4] {'gx','gy'}, dimensions={0} | all-to-all | bytes 32768 | tf_op jit(solution)/shard_map/all_to_all | solution.py:701
  129.9 0.1 reduce_sum.9
  129.9 0.6 reshape.9
  (14 shorter events, 0.1 us)
Async XLA Ops:
  2.1 7.3 %copy-start.11 = (f32[32,4,128]{2,1,0:T(4,128)S(1)}, f32[32,4,128]{2,1,0:T(4,128)}, u32[]{:S(2)}) copy-start(f32[32,4,128]{2,1,0:T(4,128)} %table.1.refs_11_) | copy-start | bytes 196612
  2.2 30.1 %copy-start = (f32[3,16,16,128]{3,2,1,0:T(8,128)S(1)}, f32[3,16,16,128]{3,2,1,0:T(8,128)}, u32[]{:S(2)}) copy-start(f32[3,16,16,128]{3,2,1,0:T(8,128)} %refs_0_.5) | copy-start | bytes 1179652
  2.2 30.1 %copy-start.1 = (f32[3,16,16,128]{3,2,1,0:T(8,128)S(1)}, f32[3,16,16,128]{3,2,1,0:T(8,128)}, u32[]{:S(2)}) copy-start(f32[3,16,16,128]{3,2,1,0:T(8,128)} %refs_1_.5) | copy-start | bytes 1179652
  2.2 30.1 %copy-start.2 = (f32[3,16,16,128]{3,2,1,0:T(8,128)S(1)}, f32[3,16,16,128]{3,2,1,0:T(8,128)}, u32[]{:S(2)}) copy-start(f32[3,16,16,128]{3,2,1,0:T(8,128)} %refs_2_.5) | copy-start | bytes 1179652
  2.2 30.1 %copy-start.3 = (f32[3,16,16,128]{3,2,1,0:T(8,128)S(1)}, f32[3,16,16,128]{3,2,1,0:T(8,128)}, u32[]{:S(2)}) copy-start(f32[3,16,16,128]{3,2,1,0:T(8,128)} %refs_3_.3) | copy-start | bytes 1179652
  2.2 30.1 %copy-start.4 = (f32[3,16,16,128]{3,2,1,0:T(8,128)S(1)}, f32[3,16,16,128]{3,2,1,0:T(8,128)}, u32[]{:S(2)}) copy-start(f32[3,16,16,128]{3,2,1,0:T(8,128)} %refs_4_.3) | copy-start | bytes 1179652
  2.2 30.1 %copy-start.5 = (f32[3,16,16,128]{3,2,1,0:T(8,128)S(1)}, f32[3,16,16,128]{3,2,1,0:T(8,128)}, u32[]{:S(2)}) copy-start(f32[3,16,16,128]{3,2,1,0:T(8,128)} %refs_5_.3) | copy-start | bytes 1179652
  2.2 30.1 %copy-start.6 = (f32[3,16,16,128]{3,2,1,0:T(8,128)S(1)}, f32[3,16,16,128]{3,2,1,0:T(8,128)}, u32[]{:S(2)}) copy-start(f32[3,16,16,128]{3,2,1,0:T(8,128)} %refs_6_.3) | copy-start | bytes 1179652
  2.2 30.1 %copy-start.7 = (f32[3,16,16,128]{3,2,1,0:T(8,128)S(1)}, f32[3,16,16,128]{3,2,1,0:T(8,128)}, u32[]{:S(2)}) copy-start(f32[3,16,16,128]{3,2,1,0:T(8,128)} %refs_7_.3) | copy-start | bytes 1179652
  2.3 30.1 %copy-start.9 = (f32[16,16,128]{2,1,0:T(8,128)S(1)}, f32[16,16,128]{2,1,0:T(8,128)}, u32[]{:S(2)}) copy-start(f32[16,16,128]{2,1,0:T(8,128)} %refs_8_.3) | copy-start | bytes 393220
  2.3 30.1 %copy-start.10 = (f32[16,16,128]{2,1,0:T(8,128)S(1)}, f32[16,16,128]{2,1,0:T(8,128)}, u32[]{:S(2)}) copy-start(f32[16,16,128]{2,1,0:T(8,128)} %refs_9_.3) | copy-start | bytes 393220
  5.6 28.6 %collective-permute-start = (f32[11,16,8,128]{3,2,1,0:T(8,128)}, f32[11,16,8,128]{3,2,1,0:T(8,128)S(1)}, u32[]{:S(2)}, u32[]{:S(2)}) collective-permute-start(f32[11,16,8,128]{3,2,1,0:T(8,128)} %get-tuple-element.35), channel_id=1, source_target_pairs={{0,1},{1,0},{2,3},{3,2},{4,5},{5,4},{6,7},{7,6},{8,9},{9,8},{10,11... | collective-permute-start | bytes 2162696 | tf_op jit(solution)/shard_map/ppermute | solution.py:61
  8.7 25.6 %collective-permute-start.1 = (f32[11,16,8,128]{3,2,1,0:T(8,128)}, f32[11,16,8,128]{3,2,1,0:T(8,128)S(1)}, u32[]{:S(2)}, u32[]{:S(2)}) collective-permute-start(f32[11,16,8,128]{3,2,1,0:T(8,128)} %get-tuple-element.36), channel_id=1, source_target_pairs={{1,2},{2,1},{5,6},{6,5},{9,10},{10,9},{13,14},{14,13},{17,18},{18,... | collective-permute-start | bytes 2162696 | tf_op jit(solution)/shard_map/ppermute | solution.py:61
  32.3 2.0 %copy-start.8 = (f32[11,16,16,128]{3,2,1,0:T(8,128)S(1)}, f32[11,16,16,128]{3,2,1,0:T(8,128)}, u32[]{:S(2)}) copy-start(f32[11,16,16,128]{3,2,1,0:T(8,128)} %get-tuple-element.34.own.refs_2_) | copy-start | bytes 4325380
  32.8 28.1 %collective-permute-start.4 = (f32[18,16,8,128]{3,2,1,0:T(8,128)S(1)}, f32[18,16,8,128]{3,2,1,0:T(8,128)S(1)}, u32[]{:S(2)}, u32[]{:S(2)}) collective-permute-start(f32[18,16,8,128]{3,2,1,0:T(8,128)S(1)} %get-tuple-element.41), channel_id=1, source_target_pairs={{0,1},{1,0},{2,3},{3,2},{4,5},{5,4},{6,7},{7,6},{8,9},{9,8},{10,11... | collective-permute-start | bytes 3538952 | tf_op jit(solution)/shard_map/ppermute | solution.py:61
  33.5 27.3 %collective-permute-start.5 = (f32[18,16,8,128]{3,2,1,0:T(8,128)S(1)}, f32[18,16,8,128]{3,2,1,0:T(8,128)S(1)}, u32[]{:S(2)}, u32[]{:S(2)}) collective-permute-start(f32[18,16,8,128]{3,2,1,0:T(8,128)S(1)} %get-tuple-element.42), channel_id=1, source_target_pairs={{1,2},{2,1},{5,6},{6,5},{9,10},{10,9},{13,14},{14,13},{17,18},{18,... | collective-permute-start | bytes 3538952 | tf_op jit(solution)/shard_map/ppermute | solution.py:61
  34.5 27.3 %collective-permute-start.3 = (f32[116,16,128]{2,1,0:T(8,128)S(1)}, f32[116,16,128]{2,1,0:T(8,128)S(1)}, u32[]{:S(2)}, u32[]{:S(2)}) collective-permute-start(f32[116,16,128]{2,1,0:T(8,128)S(1)} %get-tuple-element.38), channel_id=1, source_target_pairs={{4,8},{12,16},{20,24},{8,4},{16,12},{24,20},{5,9},{13,17},{21,25},... | collective-permute-start | bytes 2850824 | tf_op jit(solution)/shard_map/ppermute | solution.py:61
  35.3 26.6 %collective-permute-start.2 = (f32[116,16,128]{2,1,0:T(8,128)S(1)}, f32[116,16,128]{2,1,0:T(8,128)S(1)}, u32[]{:S(2)}, u32[]{:S(2)}) collective-permute-start(f32[116,16,128]{2,1,0:T(8,128)S(1)} %get-tuple-element.37._), channel_id=1, source_target_pairs={{0,4},{4,0},{8,12},{12,8},{16,20},{20,16},{24,28},{28,24},{1,5},{5... | collective-permute-start | bytes 2850824 | tf_op jit(solution)/shard_map/ppermute | solution.py:61
  61.0 16.4 %collective-permute-start.6 = (f32[100,16,128]{2,1,0:T(8,128)S(1)}, f32[100,16,128]{2,1,0:T(8,128)S(1)}, u32[]{:S(2)}, u32[]{:S(2)}) collective-permute-start(f32[100,16,128]{2,1,0:T(8,128)S(1)} %get-tuple-element.44), channel_id=1, source_target_pairs={{0,4},{4,0},{8,12},{12,8},{16,20},{20,16},{24,28},{28,24},{1,5},{5... | collective-permute-start | bytes 2457608 | tf_op jit(solution)/shard_map/ppermute | solution.py:61
  61.1 16.3 %collective-permute-start.7 = (f32[100,16,128]{2,1,0:T(8,128)S(1)}, f32[100,16,128]{2,1,0:T(8,128)S(1)}, u32[]{:S(2)}, u32[]{:S(2)}) collective-permute-start(f32[100,16,128]{2,1,0:T(8,128)S(1)} %get-tuple-element.45), channel_id=1, source_target_pairs={{4,8},{12,16},{20,24},{8,4},{16,12},{24,20},{5,9},{13,17},{21,25},... | collective-permute-start | bytes 2457608 | tf_op jit(solution)/shard_map/ppermute | solution.py:61
  69.0 6.5 %collective-permute-start.10 = (f32[2,16,8,128]{3,2,1,0:T(8,128)S(1)}, f32[2,16,8,128]{3,2,1,0:T(8,128)S(1)}, u32[]{:S(2)}, u32[]{:S(2)}) collective-permute-start(f32[2,16,8,128]{3,2,1,0:T(8,128)S(1)} %get-tuple-element.51), channel_id=1, source_target_pairs={{0,1},{1,0},{2,3},{3,2},{4,5},{5,4},{6,7},{7,6},{8,9},{9,8},{10,11... | collective-permute-start | bytes 393224 | tf_op jit(solution)/shard_map/ppermute | solution.py:61
  72.4 3.0 %collective-permute-start.11 = (f32[2,16,8,128]{3,2,1,0:T(8,128)S(1)}, f32[2,16,8,128]{3,2,1,0:T(8,128)S(1)}, u32[]{:S(2)}, u32[]{:S(2)}) collective-permute-start(f32[2,16,8,128]{3,2,1,0:T(8,128)S(1)} %get-tuple-element.52), channel_id=1, source_target_pairs={{1,2},{2,1},{5,6},{6,5},{9,10},{10,9},{13,14},{14,13},{17,18},{18,... | collective-permute-start | bytes 393224 | tf_op jit(solution)/shard_map/ppermute | solution.py:61
  75.5 10.2 %collective-permute-start.12 = (f32[24,16,128]{2,1,0:T(8,128)S(1)}, f32[24,16,128]{2,1,0:T(8,128)S(1)}, u32[]{:S(2)}, u32[]{:S(2)}) collective-permute-start(f32[24,16,128]{2,1,0:T(8,128)S(1)} %get-tuple-element.53), channel_id=1, source_target_pairs={{0,4},{4,0},{8,12},{12,8},{16,20},{20,16},{24,28},{28,24},{1,5},{5... | collective-permute-start | bytes 589832 | tf_op jit(solution)/shard_map/ppermute | solution.py:61
  76.7 9.0 %collective-permute-start.13 = (f32[24,16,128]{2,1,0:T(8,128)S(1)}, f32[24,16,128]{2,1,0:T(8,128)S(1)}, u32[]{:S(2)}, u32[]{:S(2)}) collective-permute-start(f32[24,16,128]{2,1,0:T(8,128)S(1)} %get-tuple-element.54), channel_id=1, source_target_pairs={{4,8},{12,16},{20,24},{8,4},{16,12},{24,20},{5,9},{13,17},{21,25},... | collective-permute-start | bytes 589832 | tf_op jit(solution)/shard_map/ppermute | solution.py:61
  78.7 21.5 %collective-permute-start.8 = (f32[80,16,128]{2,1,0:T(8,128)S(1)}, f32[80,16,128]{2,1,0:T(8,128)S(1)}, u32[]{:S(2)}, u32[]{:S(2)}) collective-permute-start(f32[80,16,128]{2,1,0:T(8,128)S(1)} %get-tuple-element.47), channel_id=1, source_target_pairs={{0,4},{4,0},{8,12},{12,8},{16,20},{20,16},{24,28},{28,24},{1,5},{5... | collective-permute-start | bytes 1966088 | tf_op jit(solution)/shard_map/ppermute | solution.py:61
  85.1 15.2 %collective-permute-start.9 = (f32[80,16,128]{2,1,0:T(8,128)S(1)}, f32[80,16,128]{2,1,0:T(8,128)S(1)}, u32[]{:S(2)}, u32[]{:S(2)}) collective-permute-start(f32[80,16,128]{2,1,0:T(8,128)S(1)} %get-tuple-element.48), channel_id=1, source_target_pairs={{4,8},{12,16},{20,24},{8,4},{16,12},{24,20},{5,9},{13,17},{21,25},... | collective-permute-start | bytes 1966088 | tf_op jit(solution)/shard_map/ppermute | solution.py:61
  91.8 6.4 %collective-permute-start.14 = (f32[2,16,8,128]{3,2,1,0:T(8,128)S(1)}, f32[2,16,8,128]{3,2,1,0:T(8,128)S(1)}, u32[]{:S(2)}, u32[]{:S(2)}) collective-permute-start(f32[2,16,8,128]{3,2,1,0:T(8,128)S(1)} %get-tuple-element.57), channel_id=1, source_target_pairs={{0,1},{1,0},{2,3},{3,2},{4,5},{5,4},{6,7},{7,6},{8,9},{9,8},{10,11... | collective-permute-start | bytes 393224 | tf_op jit(solution)/shard_map/ppermute | solution.py:61
  95.2 2.9 %collective-permute-start.15 = (f32[2,16,8,128]{3,2,1,0:T(8,128)S(1)}, f32[2,16,8,128]{3,2,1,0:T(8,128)S(1)}, u32[]{:S(2)}, u32[]{:S(2)}) collective-permute-start(f32[2,16,8,128]{3,2,1,0:T(8,128)S(1)} %get-tuple-element.58), channel_id=1, source_target_pairs={{1,2},{2,1},{5,6},{6,5},{9,10},{10,9},{13,14},{14,13},{17,18},{18,... | collective-permute-start | bytes 393224 | tf_op jit(solution)/shard_map/ppermute | solution.py:61
  98.2 3.0 %collective-permute-start.16 = (f32[24,16,128]{2,1,0:T(8,128)S(1)}, f32[24,16,128]{2,1,0:T(8,128)S(1)}, u32[]{:S(2)}, u32[]{:S(2)}) collective-permute-start(f32[24,16,128]{2,1,0:T(8,128)S(1)} %get-tuple-element.59), channel_id=1, source_target_pairs={{0,4},{4,0},{8,12},{12,8},{16,20},{20,16},{24,28},{28,24},{1,5},{5... | collective-permute-start | bytes 589832 | tf_op jit(solution)/shard_map/ppermute | solution.py:61
  99.5 1.7 %collective-permute-start.17 = (f32[24,16,128]{2,1,0:T(8,128)S(1)}, f32[24,16,128]{2,1,0:T(8,128)S(1)}, u32[]{:S(2)}, u32[]{:S(2)}) collective-permute-start(f32[24,16,128]{2,1,0:T(8,128)S(1)} %get-tuple-element.60), channel_id=1, source_target_pairs={{4,8},{12,16},{20,24},{8,4},{16,12},{24,20},{5,9},{13,17},{21,25},... | collective-permute-start | bytes 589832 | tf_op jit(solution)/shard_map/ppermute | solution.py:61

commit v9 on v8

--- a/solution.py
+++ b/solution.py
@@ -114,31 +114,31 @@
     )(*arrays, *after)
 
 
-def more_kernel(plan, count, *refs):
-    ins, holders, (y_low, y_high) = refs[:count], refs[count + 1 : -2], refs[-2:]
-    rx, ry = y_low.shape[1], holders[0].shape[2]
-
-    def work(low, high):
+def more_kernel(plan, count, parts, *refs):
+    ins, outs = refs[:count], refs[count + 1 :]
+    holders, firsts, seconds = outs[:parts], outs[parts::2], outs[parts + 1 :: 2]
+    rx, ry = holders[0].shape[1:3]
+
+    def work(lows, highs):
         def row(x, _):
-            for n, (i, lead, h, m) in enumerate(plan):
+            for i, lead, h, m in plan:
                 value = ins[i][x] if lead is None else ins[i][lead, x]
                 holders[h][m, x] = value
-                low[n, x] = value[0:H]
-                high[n, x] = value[ry - H :]
+                lows[h][m, x] = value[0:H]
+                highs[h][m, x] = value[ry - H :]
             return 0
 
         lax.fori_loop(0, rx, row, 0)
 
-    by_side("gy", work, y_low, y_high)
+    by_side("gy", work, firsts, seconds)
 
 
 def more(arrays, plan, sizes, dims, after):
-    n = len(plan)
     rx, ry, nz = dims
     return call(
-        functools.partial(more_kernel, plan, len(arrays)), list(arrays) + [after],
-        [sds(m, *dims) for m in sizes] + [sds(n, rx, H, nz)] * 2, "more", 4,
-        [VMEM] * len(arrays) + [ANY],
+        functools.partial(more_kernel, plan, len(arrays), len(sizes)), list(arrays) + [after],
+        [sds(m, *dims) for m in sizes] + [sds(m, rx, H, nz) for m in sizes for _ in range(2)],
+        "more", 4, [VMEM] * len(arrays) + [ANY],
     )
 
 
@@ -639,24 +639,27 @@
         [sds(steps, ex, ey, nz)], "sources", 8, [VMEM, ANY],
     )[0]
 
-    plan, places, sizes = [], {}, []
+    plan, sizes = [], []
     for h, step in enumerate(reversed(range(top))):
-        places[step] = len(plan)
         plan += [(n, step, h, n) for n in range(8)]
         if h == 0:
             plan += [(8, None, h, 8), (9, None, h, 9)]
-        sizes.append(len(plan) - places[step])
-    *holders, m_low, m_high = more(own + [acc_p, acc_s], plan, sizes, dims, table)
-    m_z = swaps(m_low, m_high, "gy")
-    held = dict(zip(reversed(range(top)), holders))
+        sizes.append(10 if h == 0 else 8)
+    made = more(own + [acc_p, acc_s], plan, sizes, dims, table)
+    held = dict(zip(reversed(range(top)), made[:top]))
+    ends = {step: made[top + 2 * h : top + 2 * h + 2] for h, step in enumerate(reversed(range(top)))}
+    m_z = {}
 
     def beside(step, after):
         group = held[step]
-        return swaps(
-            *widen(group, (COEF,) * group.shape[0], *m_z, (after,), places[step]), "gx"
-        )
-
+        return widen(group, (COEF,) * group.shape[0], *m_z[step], (after,))
+
+    first, second = ends[top - 1]
+    first, second, _ = lax.optimization_barrier((first, second, src))
+    m_z[top - 1] = swaps(first, second, "gy")
     sides = beside(top - 1, src)
+    late = sides[0]
+    sides = swaps(*sides, "gx")
 
     ext = (ex, V, 8, nz)
     lam_out = [sds(2, rx, ry, nz), sds(2, rx, H, nz), sds(2, rx, H, nz)]
@@ -675,10 +678,14 @@
         last = step == 0
         with_acc = step == top - 1
         if not with_acc:
-            sides = beside(step, coef)
+            sides = swaps(*beside(step, coef), "gx")
+        else:
+            first, second, _ = lax.optimization_barrier((*ends[step - 1], late))
+            m_z[step - 1] = swaps(first, second, "gy")
+            low, high, *_ = lax.optimization_barrier((low, high, *m_z[step - 1]))
         made = call(
-            functools.partial(prepare_kernel, step, places[step], with_acc),
-            [src, geo, held[step], *m_z, *sides] + ([] if with_acc else [acc]),
+            functools.partial(prepare_kernel, step, 0, with_acc),
+            [src, geo, held[step], *m_z[step], *sides] + ([] if with_acc else [acc]),
             [sds(9, *ext)] + ([sds(2, *ext)] if with_acc else []), "prepare", 8,
             scratch=[pltpu.VMEM((10 if with_acc else 8, ex, ey, nz), F32)],
         )

time: 131 us -> 129 us (0.985)
  waiting for transfers between devices: 27.2 us -> 24.2 us
  starting transfers between devices: 27.9 us -> 29.9 us
    ppermute x18 -> x20, waiting for transfers between devices: 27.2 us -> 24.2 us  [swaps(): return (lax.ppermute(first, axis, even), lax.ppermute(second, axis, odd))]
    ppermute x18 -> x20, starting transfers between devices: 27.9 us -> 29.9 us  [swaps(): return (lax.ppermute(first, axis, even), lax.ppermute(second, axis, odd))]
  transfers between devices with their start and end apart: 18 -> 20, of which waited for: 3 -> 4; matrix products, arithmetic and copies ran while one was open for 0% -> 0% of each run, Pallas kernels for 13% -> 13%
where the time goes in v9:
time: 129 us
  blocking collectives  43.9 us (34%)
  starting transfers between devices  29.9 us (23%)
  Pallas kernels  28.7 us (22%)
  waiting for transfers between devices  24.2 us (19%)
    ppermute x20, starting transfers between devices, swaps(): return (lax.ppermute(first, axis, even), lax.ppermute(second, axis, odd))  29.9 us
    ppermute x20, waiting for transfers between devices, swaps(): return (lax.ppermute(first, axis, even), lax.ppermute(second, axis, odd))  24.2 us
    pallas_call x12, Pallas kernels, call(): pl.pallas_call(kernel, in_specs=specs or [VMEM] * len(ins), out_specs=[VM...  23.9 us
    all_to_all x1, blocking collectives, local(): table = lax.all_to_all(mine, ('gx', 'gy'), 0, 0, tiled=True)  22.8 us
    all_to_all x1, blocking collectives, local(): parts = lax.all_to_all(dense[:, None, :], ('gx', 'gy'), 0, 0, tiled=True)  21.1 us
    pallas_call x1, Pallas kernels, load(): pl.pallas_call(functools.partial(load_kernel, leads), in_specs=[HBM] * n...  3.2 us
  transfers between devices with their start and end apart: 20, of which 4 were waited for; matrix products, arithmetic and copies ran while one was open for 0% of the time, Pallas kernels for 13%

profile of v9, /device:TPU:0, one launch (start us, length us, event | category | flops | bytes accessed | tf_op | source)
XLA Modules:
  0.0 128.6 jit_solution(13026134363878853515)
XLA Ops:
  0.6 0.0 copy-start.5
  0.6 0.0 copy-start.4
  0.7 0.0 copy-start.3
  0.7 0.0 copy-start.2
  0.7 0.0 copy-start.1
  0.7 0.0 copy-start
  0.7 0.0 copy-start.7
  0.7 0.0 copy-start.6
  0.8 1.6 %table.1.refs_11_ = f32[32,4,128]{2,1,0:T(4,128)} custom-call(f32[2,3]{1,0:T(2,128)} %refs_0_.3, f32[2,3]{1,0:T(2,128)} %refs_1_.3, s32[2,3]{1,0:T(2,128)} %refs_2_.3, s32[1,128]{1,0:T(1,128)} %bitcast.8, s32[1,128]{1,0:T(1,128)} %bitcast.9, f32[1,128]{1,0:T(1,128)} %bitcast.10), custom_call_target="tpu_custom_call" | custom-call | tf_op jit(solution)/shard_map/table/pallas_call | solution.py:621
  2.4 0.0 copy-start.11
  2.4 3.2 %load.1 = (f32[11,16,16,128]{3,2,1,0:T(8,128)}, f32[11,16,8,128]{3,2,1,0:T(8,128)}, f32[11,16,8,128]{3,2,1,0:T(8,128)}, f32[8,128]{1,0:T(8,128)}) custom-call(f32[16,16,128]{2,1,0:T(8,128)} %refs_0_.4, f32[16,16,128]{2,1,0:T(8,128)} %refs_1_.4, f32[16,16,128]{2,1,0:T(8,128)} %refs_2_.4, f32[3,16,16,128]{3,2,1,0:T(8,128)} %refs_0_.5, ...), custom_call_target="tpu_custom_call" | custom-call | tf_op jit(solution)/shard_map/load/pallas_call | solution.py:107
  5.6 3.1 %collective-permute-start = (f32[11,16,8,128]{3,2,1,0:T(8,128)}, f32[11,16,8,128]{3,2,1,0:T(8,128)S(1)}, u32[]{:S(2)}, u32[]{:S(2)}) collective-permute-start(f32[11,16,8,128]{3,2,1,0:T(8,128)} %get-tuple-element.43), channel_id=1, source_target_pairs={{0,1},{1,0},{2,3},{3,2},{4,5},{5,4},{6,7},{7,6},{8,9},{9,8},{10,11... | collective-permute-start | bytes 2162696 | tf_op jit(solution)/shard_map/ppermute | solution.py:61
  8.7 0.7 collective-permute-start.1
  9.4 22.8 %all_to_all.10.refs_0_.table_ref.refs_10_ = f32[32,4,128]{2,1,0:T(4,128)S(1)} all-to-all(f32[32,4,128]{2,1,0:T(4,128)S(1)} %copy-done.11), channel_id=1, replica_groups=mesh['gx'=8,'gy'=4] {'gx','gy'}, dimensions={0} | all-to-all | bytes 131072 | tf_op jit(solution)/shard_map/all_to_all | solution.py:633
  32.3 0.5 more.1
  32.8 0.0 collective-permute-done.z_first.refs_3_
  32.8 0.0 collective-permute-done.1.z_second.refs_4_
  32.8 0.2 widen.5
  33.0 0.7 collective-permute-start.3
  33.7 2.0 %collective-permute-start.2 = (f32[116,16,128]{2,1,0:T(8,128)S(1)}, f32[116,16,128]{2,1,0:T(8,128)S(1)}, u32[]{:S(2)}, u32[]{:S(2)}) collective-permute-start(f32[116,16,128]{2,1,0:T(8,128)S(1)} %get-tuple-element.45._), channel_id=1, source_target_pairs={{0,4},{4,0},{8,12},{12,8},{16,20},{20,16},{24,28},{28,24},{1,5},{5... | collective-permute-start | bytes 2850824 | tf_op jit(solution)/shard_map/ppermute | solution.py:61
  35.7 1.0 sources.1.refs_1_.refs_0_
  36.8 0.8 collective-permute-start.4
  37.6 0.7 collective-permute-start.5
  38.3 15.3 %collective-permute-done.4.z_first.refs_3_ = f32[10,16,8,128]{3,2,1,0:T(8,128)S(1)} collective-permute-done((f32[10,16,8,128]{3,2,1,0:T(8,128)S(1)}, f32[10,16,8,128]{3,2,1,0:T(8,128)S(1)}, u32[]{:S(2)}, u32[]{:S(2)}) %collective-permute-start.4) | collective-permute-done | bytes 655392 | tf_op jit(solution)/shard_map/ppermute | solution.py:61
  53.5 0.0 collective-permute-done.5.z_second.refs_4_
  53.5 0.2 widen.6
  53.7 0.1 collective-permute-start.8
  53.8 3.9 %collective-permute-start.6 = (f32[8,16,8,128]{3,2,1,0:T(8,128)S(1)}, f32[8,16,8,128]{3,2,1,0:T(8,128)S(1)}, u32[]{:S(2)}, u32[]{:S(2)}) collective-permute-start(f32[8,16,8,128]{3,2,1,0:T(8,128)S(1)} %get-tuple-element.57), channel_id=1, source_target_pairs={{0,1},{1,0},{2,3},{3,2},{4,5},{5,4},{6,7},{7,6},{8,9},{9,8},{10,11... | collective-permute-start | bytes 1572872 | tf_op jit(solution)/shard_map/ppermute | solution.py:61
  57.7 0.7 collective-permute-start.7
  58.4 0.0 collective-permute-done.3.refs_6_
  58.4 0.7 collective-permute-start.9
  59.1 0.0 collective-permute-done.2.refs_5_
  59.1 7.1 %step_top.1 = (f32[5,32,4,8,128]{4,3,2,1,0:T(8,128)S(1)}, f32[2,16,16,128]{3,2,1,0:T(8,128)S(1)}, f32[2,16,8,128]{3,2,1,0:T(8,128)S(1)}, f32[2,16,8,128]{3,2,1,0:T(8,128)S(1)}, f32[32,128]{1,0:T(8,128)S(1)}) custom-call(f32[32,4,128]{2,1,0:T(4,128)S(1)} %all_to_all.10.refs_0_.table_ref.refs_10_, f32[3,32,32,128]{3,2,1,0:T(8,128)S(1)} %sources.1.refs_1_.refs_0_, ...), custom_call_target="tpu_custom_call" | custom-call | flops 7000000000 | bytes 21000000 | tf_op jit(solution)/shard_map/step_top/pallas_call | solution.py:44
  66.2 3.9 %collective-permute-done.6.z_first.refs_3_ = f32[8,16,8,128]{3,2,1,0:T(8,128)S(1)} collective-permute-done((f32[8,16,8,128]{3,2,1,0:T(8,128)S(1)}, f32[8,16,8,128]{3,2,1,0:T(8,128)S(1)}, u32[]{:S(2)}, u32[]{:S(2)}) %collective-permute-start.6) | collective-permute-done | bytes 524320 | tf_op jit(solution)/shard_map/ppermute | solution.py:61
  70.2 0.0 collective-permute-done.7.z_second.refs_4_
  70.2 3.6 %collective-permute-start.12 = (f32[2,16,8,128]{3,2,1,0:T(8,128)S(1)}, f32[2,16,8,128]{3,2,1,0:T(8,128)S(1)}, u32[]{:S(2)}, u32[]{:S(2)}) collective-permute-start(f32[2,16,8,128]{3,2,1,0:T(8,128)S(1)} %get-tuple-element.67), channel_id=1, source_target_pairs={{0,1},{1,0},{2,3},{3,2},{4,5},{5,4},{6,7},{7,6},{8,9},{9,8},{10,11... | collective-permute-start | bytes 393224 | tf_op jit(solution)/shard_map/ppermute | solution.py:61
  73.8 0.7 collective-permute-start.13
  74.5 2.6 %collective-permute-done.12.z_first.refs_5_ = f32[2,16,8,128]{3,2,1,0:T(8,128)S(1)} collective-permute-done((f32[2,16,8,128]{3,2,1,0:T(8,128)S(1)}, f32[2,16,8,128]{3,2,1,0:T(8,128)S(1)}, u32[]{:S(2)}, u32[]{:S(2)}) %collective-permute-start.12) | collective-permute-done | bytes 131104 | tf_op jit(solution)/shard_map/ppermute | solution.py:61
  77.1 0.0 collective-permute-done.13.z_second.refs_6_
  77.2 0.1 collective-permute-start.14
  77.2 0.7 collective-permute-start.15
  77.9 0.0 collective-permute-done.9.refs_6_
  77.9 0.0 collective-permute-done.8.refs_5_
  77.9 1.1 prepare.2
  79.0 0.2 widen.7
  79.2 2.9 %collective-permute-start.10 = (f32[80,16,128]{2,1,0:T(8,128)S(1)}, f32[80,16,128]{2,1,0:T(8,128)S(1)}, u32[]{:S(2)}, u32[]{:S(2)}) collective-permute-start(f32[80,16,128]{2,1,0:T(8,128)S(1)} %get-tuple-element.61), channel_id=1, source_target_pairs={{0,4},{4,0},{8,12},{12,8},{16,20},{20,16},{24,28},{28,24},{1,5},{5... | collective-permute-start | bytes 1966088 | tf_op jit(solution)/shard_map/ppermute | solution.py:61
  82.1 0.7 collective-permute-start.11
  82.8 0.0 collective-permute-done.14.refs_7_
  82.8 0.0 collective-permute-done.15.refs_8_
  82.8 6.0 %step.2 = (f32[2,16,16,128]{3,2,1,0:T(8,128)S(1)}, f32[2,16,8,128]{3,2,1,0:T(8,128)S(1)}, f32[2,16,8,128]{3,2,1,0:T(8,128)S(1)}, f32[32,128]{1,0:T(8,128)S(1)}) custom-call(f32[32,4,128]{2,1,0:T(4,128)S(1)} %all_to_all.10.refs_0_.table_ref.refs_10_, f32[9,32,4,8,128]{4,3,2,1,0:T(8,128)S(1)} %get-tuple-element.60.refs_0_.refs_1_, ...), custom_call_target="tpu_custom_call" | custom-call | flops 6000000000 | bytes 18000000 | tf_op jit(solution)/shard_map/step/pallas_call | solution.py:44
  88.8 3.6 %collective-permute-start.16 = (f32[2,16,8,128]{3,2,1,0:T(8,128)S(1)}, f32[2,16,8,128]{3,2,1,0:T(8,128)S(1)}, u32[]{:S(2)}, u32[]{:S(2)}) collective-permute-start(f32[2,16,8,128]{3,2,1,0:T(8,128)S(1)} %get-tuple-element.73), channel_id=1, source_target_pairs={{0,1},{1,0},{2,3},{3,2},{4,5},{5,4},{6,7},{7,6},{8,9},{9,8},{10,11... | collective-permute-start | bytes 393224 | tf_op jit(solution)/shard_map/ppermute | solution.py:61
  92.5 0.7 collective-permute-start.17
  93.1 2.3 %collective-permute-done.16.z_first.refs_5_ = f32[2,16,8,128]{3,2,1,0:T(8,128)S(1)} collective-permute-done((f32[2,16,8,128]{3,2,1,0:T(8,128)S(1)}, f32[2,16,8,128]{3,2,1,0:T(8,128)S(1)}, u32[]{:S(2)}, u32[]{:S(2)}) %collective-permute-start.16) | collective-permute-done | bytes 131104 | tf_op jit(solution)/shard_map/ppermute | solution.py:61
  95.4 0.0 collective-permute-done.17.z_second.refs_6_
  95.5 3.0 %collective-permute-start.18 = (f32[24,16,128]{2,1,0:T(8,128)S(1)}, f32[24,16,128]{2,1,0:T(8,128)S(1)}, u32[]{:S(2)}, u32[]{:S(2)}) collective-permute-start(f32[24,16,128]{2,1,0:T(8,128)S(1)} %get-tuple-element.75), channel_id=1, source_target_pairs={{0,4},{4,0},{8,12},{12,8},{16,20},{20,16},{24,28},{28,24},{1,5},{5... | collective-permute-start | bytes 589832 | tf_op jit(solution)/shard_map/ppermute | solution.py:61
  98.5 0.7 collective-permute-start.19
  99.2 0.0 collective-permute-done.11.refs_6_
  99.2 1.0 prepare.3.refs_1_
  100.2 0.0 collective-permute-done.18.refs_7_
  100.2 0.0 collective-permute-done.19.refs_8_
  100.2 6.5 %step.3 = (f32[16,16,128]{2,1,0:T(8,128)}, f32[16,16,128]{2,1,0:T(8,128)}, f32[32,128]{1,0:T(8,128)S(1)}) custom-call(f32[32,4,128]{2,1,0:T(4,128)S(1)} %all_to_all.10.refs_0_.table_ref.refs_10_, f32[9,32,4,8,128]{4,3,2,1,0:T(8,128)S(1)} %prepare.3.refs_1_, f32[5,32,4,8,128]{4,3,2,1,0:T(8,128)S(1)} %get-tuple-element.47.refs_1_.refs_2_, ...), custom_call_target="tpu_custom_call" | custom-call | flops 6000000000 | bytes 18000000 | tf_op jit(solution)/shard_map/step/pallas_call | solution.py:44
  106.7 21.1 %all_to_all.11 = f32[32,1,128]{2,1,0:T(1,128)S(1)} all-to-all(f32[32,1,128]{2,1,0:T(1,128)S(1)} %bitcast.7), channel_id=1, replica_groups=mesh['gx'=8,'gy'=4] {'gx','gy'}, dimensions={0} | all-to-all | bytes 32768 | tf_op jit(solution)/shard_map/all_to_all | solution.py:708
  127.9 0.1 reduce_sum.9
  127.9 0.6 reshape.9
  (18 shorter events, 0.1 us)
Async XLA Ops:
  0.6 31.6 %copy-start.5 = (f32[3,16,16,128]{3,2,1,0:T(8,128)S(1)}, f32[3,16,16,128]{3,2,1,0:T(8,128)}, u32[]{:S(2)}) copy-start(f32[3,16,16,128]{3,2,1,0:T(8,128)} %refs_5_.3) | copy-start | bytes 1179652
  0.6 31.6 %copy-start.4 = (f32[3,16,16,128]{3,2,1,0:T(8,128)S(1)}, f32[3,16,16,128]{3,2,1,0:T(8,128)}, u32[]{:S(2)}) copy-start(f32[3,16,16,128]{3,2,1,0:T(8,128)} %refs_4_.3) | copy-start | bytes 1179652
  0.7 31.6 %copy-start.3 = (f32[3,16,16,128]{3,2,1,0:T(8,128)S(1)}, f32[3,16,16,128]{3,2,1,0:T(8,128)}, u32[]{:S(2)}) copy-start(f32[3,16,16,128]{3,2,1,0:T(8,128)} %refs_3_.3) | copy-start | bytes 1179652
  0.7 31.6 %copy-start.2 = (f32[3,16,16,128]{3,2,1,0:T(8,128)S(1)}, f32[3,16,16,128]{3,2,1,0:T(8,128)}, u32[]{:S(2)}) copy-start(f32[3,16,16,128]{3,2,1,0:T(8,128)} %refs_2_.5) | copy-start | bytes 1179652
  0.7 31.6 %copy-start.1 = (f32[3,16,16,128]{3,2,1,0:T(8,128)S(1)}, f32[3,16,16,128]{3,2,1,0:T(8,128)}, u32[]{:S(2)}) copy-start(f32[3,16,16,128]{3,2,1,0:T(8,128)} %refs_1_.5) | copy-start | bytes 1179652
  0.7 31.6 %copy-start = (f32[3,16,16,128]{3,2,1,0:T(8,128)S(1)}, f32[3,16,16,128]{3,2,1,0:T(8,128)}, u32[]{:S(2)}) copy-start(f32[3,16,16,128]{3,2,1,0:T(8,128)} %refs_0_.5) | copy-start | bytes 1179652
  0.7 31.6 %copy-start.7 = (f32[3,16,16,128]{3,2,1,0:T(8,128)S(1)}, f32[3,16,16,128]{3,2,1,0:T(8,128)}, u32[]{:S(2)}) copy-start(f32[3,16,16,128]{3,2,1,0:T(8,128)} %refs_7_.3) | copy-start | bytes 1179652
  0.7 31.6 %copy-start.6 = (f32[3,16,16,128]{3,2,1,0:T(8,128)S(1)}, f32[3,16,16,128]{3,2,1,0:T(8,128)}, u32[]{:S(2)}) copy-start(f32[3,16,16,128]{3,2,1,0:T(8,128)} %refs_6_.3) | copy-start | bytes 1179652
  0.7 31.6 %copy-start.10 = (f32[16,16,128]{2,1,0:T(8,128)S(1)}, f32[16,16,128]{2,1,0:T(8,128)}, u32[]{:S(2)}) copy-start(f32[16,16,128]{2,1,0:T(8,128)} %refs_9_.3) | copy-start | bytes 393220
  0.7 31.6 %copy-start.9 = (f32[16,16,128]{2,1,0:T(8,128)S(1)}, f32[16,16,128]{2,1,0:T(8,128)}, u32[]{:S(2)}) copy-start(f32[16,16,128]{2,1,0:T(8,128)} %refs_8_.3) | copy-start | bytes 393220
  2.4 7.0 %copy-start.11 = (f32[32,4,128]{2,1,0:T(4,128)S(1)}, f32[32,4,128]{2,1,0:T(4,128)}, u32[]{:S(2)}) copy-start(f32[32,4,128]{2,1,0:T(4,128)} %table.1.refs_11_) | copy-start | bytes 196612
  5.6 27.2 %copy-start.8 = (f32[11,16,16,128]{3,2,1,0:T(8,128)S(1)}, f32[11,16,16,128]{3,2,1,0:T(8,128)}, u32[]{:S(2)}) copy-start(f32[11,16,16,128]{3,2,1,0:T(8,128)} %get-tuple-element.42.own.refs_2_) | copy-start | bytes 4325380
  5.6 27.2 %collective-permute-start = (f32[11,16,8,128]{3,2,1,0:T(8,128)}, f32[11,16,8,128]{3,2,1,0:T(8,128)S(1)}, u32[]{:S(2)}, u32[]{:S(2)}) collective-permute-start(f32[11,16,8,128]{3,2,1,0:T(8,128)} %get-tuple-element.43), channel_id=1, source_target_pairs={{0,1},{1,0},{2,3},{3,2},{4,5},{5,4},{6,7},{7,6},{8,9},{9,8},{10,11... | collective-permute-start | bytes 2162696 | tf_op jit(solution)/shard_map/ppermute | solution.py:61
  8.7 24.1 %collective-permute-start.1 = (f32[11,16,8,128]{3,2,1,0:T(8,128)}, f32[11,16,8,128]{3,2,1,0:T(8,128)S(1)}, u32[]{:S(2)}, u32[]{:S(2)}) collective-permute-start(f32[11,16,8,128]{3,2,1,0:T(8,128)} %get-tuple-element.44), channel_id=1, source_target_pairs={{1,2},{2,1},{5,6},{6,5},{9,10},{10,9},{13,14},{14,13},{17,18},{18,... | collective-permute-start | bytes 2162696 | tf_op jit(solution)/shard_map/ppermute | solution.py:61
  33.0 25.3 %collective-permute-start.3 = (f32[116,16,128]{2,1,0:T(8,128)S(1)}, f32[116,16,128]{2,1,0:T(8,128)S(1)}, u32[]{:S(2)}, u32[]{:S(2)}) collective-permute-start(f32[116,16,128]{2,1,0:T(8,128)S(1)} %get-tuple-element.46), channel_id=1, source_target_pairs={{4,8},{12,16},{20,24},{8,4},{16,12},{24,20},{5,9},{13,17},{21,25},... | collective-permute-start | bytes 2850824 | tf_op jit(solution)/shard_map/ppermute | solution.py:61
  33.7 25.3 %collective-permute-start.2 = (f32[116,16,128]{2,1,0:T(8,128)S(1)}, f32[116,16,128]{2,1,0:T(8,128)S(1)}, u32[]{:S(2)}, u32[]{:S(2)}) collective-permute-start(f32[116,16,128]{2,1,0:T(8,128)S(1)} %get-tuple-element.45._), channel_id=1, source_target_pairs={{0,4},{4,0},{8,12},{12,8},{16,20},{20,16},{24,28},{28,24},{1,5},{5... | collective-permute-start | bytes 2850824 | tf_op jit(solution)/shard_map/ppermute | solution.py:61
  36.8 16.7 %collective-permute-start.4 = (f32[10,16,8,128]{3,2,1,0:T(8,128)S(1)}, f32[10,16,8,128]{3,2,1,0:T(8,128)S(1)}, u32[]{:S(2)}, u32[]{:S(2)}) collective-permute-start(f32[10,16,8,128]{3,2,1,0:T(8,128)S(1)} %get-tuple-element.54), channel_id=1, source_target_pairs={{0,1},{1,0},{2,3},{3,2},{4,5},{5,4},{6,7},{7,6},{8,9},{9,8},{10,11... | collective-permute-start | bytes 1966088 | tf_op jit(solution)/shard_map/ppermute | solution.py:61
  37.6 16.0 %collective-permute-start.5 = (f32[10,16,8,128]{3,2,1,0:T(8,128)S(1)}, f32[10,16,8,128]{3,2,1,0:T(8,128)S(1)}, u32[]{:S(2)}, u32[]{:S(2)}) collective-permute-start(f32[10,16,8,128]{3,2,1,0:T(8,128)S(1)} %get-tuple-element.55), channel_id=1, source_target_pairs={{1,2},{2,1},{5,6},{6,5},{9,10},{10,9},{13,14},{14,13},{17,18},{18,... | collective-permute-start | bytes 1966088 | tf_op jit(solution)/shard_map/ppermute | solution.py:61
  53.7 24.3 %collective-permute-start.8 = (f32[100,16,128]{2,1,0:T(8,128)S(1)}, f32[100,16,128]{2,1,0:T(8,128)S(1)}, u32[]{:S(2)}, u32[]{:S(2)}) collective-permute-start(f32[100,16,128]{2,1,0:T(8,128)S(1)} %get-tuple-element.56), channel_id=1, source_target_pairs={{0,4},{4,0},{8,12},{12,8},{16,20},{20,16},{24,28},{28,24},{1,5},{5... | collective-permute-start | bytes 2457608 | tf_op jit(solution)/shard_map/ppermute | solution.py:61
  53.8 16.4 %collective-permute-start.6 = (f32[8,16,8,128]{3,2,1,0:T(8,128)S(1)}, f32[8,16,8,128]{3,2,1,0:T(8,128)S(1)}, u32[]{:S(2)}, u32[]{:S(2)}) collective-permute-start(f32[8,16,8,128]{3,2,1,0:T(8,128)S(1)} %get-tuple-element.57), channel_id=1, source_target_pairs={{0,1},{1,0},{2,3},{3,2},{4,5},{5,4},{6,7},{7,6},{8,9},{9,8},{10,11... | collective-permute-start | bytes 1572872 | tf_op jit(solution)/shard_map/ppermute | solution.py:61
  57.7 12.5 %collective-permute-start.7 = (f32[8,16,8,128]{3,2,1,0:T(8,128)S(1)}, f32[8,16,8,128]{3,2,1,0:T(8,128)S(1)}, u32[]{:S(2)}, u32[]{:S(2)}) collective-permute-start(f32[8,16,8,128]{3,2,1,0:T(8,128)S(1)} %get-tuple-element.58), channel_id=1, source_target_pairs={{1,2},{2,1},{5,6},{6,5},{9,10},{10,9},{13,14},{14,13},{17,18},{18,... | collective-permute-start | bytes 1572872 | tf_op jit(solution)/shard_map/ppermute | solution.py:61
  58.4 19.6 %collective-permute-start.9 = (f32[100,16,128]{2,1,0:T(8,128)S(1)}, f32[100,16,128]{2,1,0:T(8,128)S(1)}, u32[]{:S(2)}, u32[]{:S(2)}) collective-permute-start(f32[100,16,128]{2,1,0:T(8,128)S(1)} %get-tuple-element.59), channel_id=1, source_target_pairs={{4,8},{12,16},{20,24},{8,4},{16,12},{24,20},{5,9},{13,17},{21,25},... | collective-permute-start | bytes 2457608 | tf_op jit(solution)/shard_map/ppermute | solution.py:61
  70.2 6.9 %collective-permute-start.12 = (f32[2,16,8,128]{3,2,1,0:T(8,128)S(1)}, f32[2,16,8,128]{3,2,1,0:T(8,128)S(1)}, u32[]{:S(2)}, u32[]{:S(2)}) collective-permute-start(f32[2,16,8,128]{3,2,1,0:T(8,128)S(1)} %get-tuple-element.67), channel_id=1, source_target_pairs={{0,1},{1,0},{2,3},{3,2},{4,5},{5,4},{6,7},{7,6},{8,9},{9,8},{10,11... | collective-permute-start | bytes 393224 | tf_op jit(solution)/shard_map/ppermute | solution.py:61
  73.8 3.3 %collective-permute-start.13 = (f32[2,16,8,128]{3,2,1,0:T(8,128)S(1)}, f32[2,16,8,128]{3,2,1,0:T(8,128)S(1)}, u32[]{:S(2)}, u32[]{:S(2)}) collective-permute-start(f32[2,16,8,128]{3,2,1,0:T(8,128)S(1)} %get-tuple-element.68), channel_id=1, source_target_pairs={{1,2},{2,1},{5,6},{6,5},{9,10},{10,9},{13,14},{14,13},{17,18},{18,... | collective-permute-start | bytes 393224 | tf_op jit(solution)/shard_map/ppermute | solution.py:61
  77.2 5.6 %collective-permute-start.14 = (f32[24,16,128]{2,1,0:T(8,128)S(1)}, f32[24,16,128]{2,1,0:T(8,128)S(1)}, u32[]{:S(2)}, u32[]{:S(2)}) collective-permute-start(f32[24,16,128]{2,1,0:T(8,128)S(1)} %get-tuple-element.69), channel_id=1, source_target_pairs={{0,4},{4,0},{8,12},{12,8},{16,20},{20,16},{24,28},{28,24},{1,5},{5... | collective-permute-start | bytes 589832 | tf_op jit(solution)/shard_map/ppermute | solution.py:61
  77.2 5.6 %collective-permute-start.15 = (f32[24,16,128]{2,1,0:T(8,128)S(1)}, f32[24,16,128]{2,1,0:T(8,128)S(1)}, u32[]{:S(2)}, u32[]{:S(2)}) collective-permute-start(f32[24,16,128]{2,1,0:T(8,128)S(1)} %get-tuple-element.70), channel_id=1, source_target_pairs={{4,8},{12,16},{20,24},{8,4},{16,12},{24,20},{5,9},{13,17},{21,25},... | collective-permute-start | bytes 589832 | tf_op jit(solution)/shard_map/ppermute | solution.py:61
  79.2 20.0 %collective-permute-start.10 = (f32[80,16,128]{2,1,0:T(8,128)S(1)}, f32[80,16,128]{2,1,0:T(8,128)S(1)}, u32[]{:S(2)}, u32[]{:S(2)}) collective-permute-start(f32[80,16,128]{2,1,0:T(8,128)S(1)} %get-tuple-element.61), channel_id=1, source_target_pairs={{0,4},{4,0},{8,12},{12,8},{16,20},{20,16},{24,28},{28,24},{1,5},{5... | collective-permute-start | bytes 1966088 | tf_op jit(solution)/shard_map/ppermute | solution.py:61
  82.1 17.1 %collective-permute-start.11 = (f32[80,16,128]{2,1,0:T(8,128)S(1)}, f32[80,16,128]{2,1,0:T(8,128)S(1)}, u32[]{:S(2)}, u32[]{:S(2)}) collective-permute-start(f32[80,16,128]{2,1,0:T(8,128)S(1)} %get-tuple-element.62), channel_id=1, source_target_pairs={{4,8},{12,16},{20,24},{8,4},{16,12},{24,20},{5,9},{13,17},{21,25},... | collective-permute-start | bytes 1966088 | tf_op jit(solution)/shard_map/ppermute | solution.py:61
  88.8 6.6 %collective-permute-start.16 = (f32[2,16,8,128]{3,2,1,0:T(8,128)S(1)}, f32[2,16,8,128]{3,2,1,0:T(8,128)S(1)}, u32[]{:S(2)}, u32[]{:S(2)}) collective-permute-start(f32[2,16,8,128]{3,2,1,0:T(8,128)S(1)} %get-tuple-element.73), channel_id=1, source_target_pairs={{0,1},{1,0},{2,3},{3,2},{4,5},{5,4},{6,7},{7,6},{8,9},{9,8},{10,11... | collective-permute-start | bytes 393224 | tf_op jit(solution)/shard_map/ppermute | solution.py:61
  92.5 2.9 %collective-permute-start.17 = (f32[2,16,8,128]{3,2,1,0:T(8,128)S(1)}, f32[2,16,8,128]{3,2,1,0:T(8,128)S(1)}, u32[]{:S(2)}, u32[]{:S(2)}) collective-permute-start(f32[2,16,8,128]{3,2,1,0:T(8,128)S(1)} %get-tuple-element.74), channel_id=1, source_target_pairs={{1,2},{2,1},{5,6},{6,5},{9,10},{10,9},{13,14},{14,13},{17,18},{18,... | collective-permute-start | bytes 393224 | tf_op jit(solution)/shard_map/ppermute | solution.py:61
  95.5 4.7 %collective-permute-start.18 = (f32[24,16,128]{2,1,0:T(8,128)S(1)}, f32[24,16,128]{2,1,0:T(8,128)S(1)}, u32[]{:S(2)}, u32[]{:S(2)}) collective-permute-start(f32[24,16,128]{2,1,0:T(8,128)S(1)} %get-tuple-element.75), channel_id=1, source_target_pairs={{0,4},{4,0},{8,12},{12,8},{16,20},{20,16},{24,28},{28,24},{1,5},{5... | collective-permute-start | bytes 589832 | tf_op jit(solution)/shard_map/ppermute | solution.py:61
  98.5 1.7 %collective-permute-start.19 = (f32[24,16,128]{2,1,0:T(8,128)S(1)}, f32[24,16,128]{2,1,0:T(8,128)S(1)}, u32[]{:S(2)}, u32[]{:S(2)}) collective-permute-start(f32[24,16,128]{2,1,0:T(8,128)S(1)} %get-tuple-element.76), channel_id=1, source_target_pairs={{4,8},{12,16},{20,24},{8,4},{16,12},{24,20},{5,9},{13,17},{21,25},... | collective-permute-start | bytes 589832 | tf_op jit(solution)/shard_map/ppermute | solution.py:61

commit v10 on v9

--- a/solution.py
+++ b/solution.py
@@ -457,7 +457,6 @@
         return jnp.sum(jnp.where(diagonal, row, 0.0), axis=1, keepdims=True)
 
     cell = upright(slot[1:2, :]).astype(jnp.int32)
-    well = upright(slot[2:3, :]).astype(jnp.int32)
     wi = upright(slot[3:4, :])
     by_row = jnp.where(
         lax.broadcasted_iota(jnp.int32, (128, rx * ry), 1) == (cell >> 7), 1.0, 0.0
@@ -470,12 +469,11 @@
         picked = add if picked is None else picked + add
     values = jnp.sum(jnp.where(lane == (cell & 127), picked, 0.0), axis=1, keepdims=True)
     values = values * wi
-    owner = well // wells
-    spread = jnp.where(lane == (well - owner * wells) * steps + step, values, 0.0)
-    flat = slot[2:3, :].astype(jnp.int32) // wells
-    count = table_ref.shape[0]
+    spread = jnp.where(lane == step, values, 0.0)
+    well = slot[2:3, :].astype(jnp.int32)
+    count = table_ref.shape[0] * wells
     hot = jnp.where(
-        lax.broadcasted_iota(jnp.int32, (count, 128), 0) == flat, 1.0, 0.0
+        lax.broadcasted_iota(jnp.int32, (count, 128), 0) == well, 1.0, 0.0
     ).astype(F32)
     dense = jnp.dot(hot, spread, precision=HIGHEST, preferred_element_type=F32)
     if before is not None:
@@ -627,7 +625,7 @@
         + [pltpu.SemaphoreType.DMA((6,))],
         name="table",
     )(*small)
-    blocks, y_low, y_high, token = load(arrays, leads, dims, (mine,))
+    blocks, y_low, y_high, token = load(arrays, leads, dims, ())
     z_got = swaps(y_low, y_high, "gy")
     mine, _ = lax.optimization_barrier((mine, token))
     table = lax.all_to_all(mine, ("gx", "gy"), 0, 0, tiled=True)
@@ -663,7 +661,7 @@
 
     ext = (ex, V, 8, nz)
     lam_out = [sds(2, rx, ry, nz), sds(2, rx, H, nz), sds(2, rx, H, nz)]
-    well_out = sds(devices, 128)
+    well_out = sds(devices * wells, 128)
     fields = [pltpu.VMEM(ext, F32)] * 4 + [pltpu.VMEM((2, ex, ey, nz), F32)]
 
     geo, lam, low, high, dense = call(
@@ -705,8 +703,9 @@
         if not last:
             lam, low, high = outs[:3]
 
-    parts = lax.all_to_all(dense[:, None, :], ("gx", "gy"), 0, 0, tiled=True)
-    well_grad = jnp.sum(parts, axis=(0, 1))[: wells * steps].reshape(wells, steps)
+    dense = dense.reshape(devices, wells, 128)
+    parts = lax.all_to_all(dense, ("gx", "gy"), 0, 0, tiled=True)
+    well_grad = jnp.sum(parts, axis=0)[:, :steps]
     return outs[0], outs[1], well_grad
 
 

time: 129 us -> 129 us (level)
  Pallas kernels: 28.7 us -> 31.3 us
  blocking collectives: 43.9 us -> 41.7 us
  waiting for transfers between devices: 24.2 us -> 22.8 us
    pallas_call x12, Pallas kernels: 23.9 us -> 26.5 us  [call(): pl.pallas_call(kernel, in_specs=specs or [VMEM] * len(ins), out_specs=[VM...]
    all_to_all x1, blocking collectives: 22.8 us -> 20.5 us  [local(): table = lax.all_to_all(mine, ('gx', 'gy'), 0, 0, tiled=True)]
    ppermute x20, waiting for transfers between devices: 24.2 us -> 22.8 us  [swaps(): return (lax.ppermute(first, axis, even), lax.ppermute(second, axis, odd))]
  transfers between devices with their start and end apart: 20 -> 20, of which waited for: 4 -> 4; matrix products, arithmetic and copies ran while one was open for 0% -> 0% of each run, Pallas kernels for 13% -> 16%
where the time goes in v10:
time: 129 us; the launch traced here: 128 us
  blocking collectives  41.7 us (32%)
  Pallas kernels  31.3 us (24%)
  starting transfers between devices  30.8 us (24%)
  waiting for transfers between devices  22.8 us (18%)
    ppermute x20, starting transfers between devices, swaps(): return (lax.ppermute(first, axis, even), lax.ppermute(second, axis, odd))  30.8 us
    pallas_call x12, Pallas kernels, call(): pl.pallas_call(kernel, in_specs=specs or [VMEM] * len(ins), out_specs=[VM...  26.5 us
    ppermute x20, waiting for transfers between devices, swaps(): return (lax.ppermute(first, axis, even), lax.ppermute(second, axis, odd))  22.8 us
    all_to_all x1, blocking collectives, local(): parts = lax.all_to_all(dense, ('gx', 'gy'), 0, 0, tiled=True)  21.2 us
    all_to_all x1, blocking collectives, local(): table = lax.all_to_all(mine, ('gx', 'gy'), 0, 0, tiled=True)  20.5 us
    pallas_call x1, Pallas kernels, load(): pl.pallas_call(functools.partial(load_kernel, leads), in_specs=[HBM] * n...  3.34 us
  transfers between devices with their start and end apart: 20, of which 4 were waited for; matrix products, arithmetic and copies ran while one was open for 0% of the time, Pallas kernels for 16%

profile of v10, /device:TPU:0, one launch (start us, length us, event | category | flops | bytes accessed | tf_op | source)
XLA Modules:
  0.0 128.4 jit_solution(606491215937402734)
XLA Ops:
  0.6 0.0 copy-start.5
  0.6 0.0 copy-start.4
  0.7 0.0 copy-start.3
  0.7 0.0 copy-start.2
  0.7 0.0 copy-start.1
  0.7 0.0 copy-start
  0.7 0.0 copy-start.7
  0.7 0.0 copy-start.6
  0.7 0.0 copy-start.10
  0.7 3.3 %load.1 = (f32[11,16,16,128]{3,2,1,0:T(8,128)}, f32[11,16,8,128]{3,2,1,0:T(8,128)}, f32[11,16,8,128]{3,2,1,0:T(8,128)}, f32[8,128]{1,0:T(8,128)}) custom-call(f32[16,16,128]{2,1,0:T(8,128)} %refs_0_.4, f32[16,16,128]{2,1,0:T(8,128)} %refs_1_.4, f32[16,16,128]{2,1,0:T(8,128)} %refs_2_.4, f32[3,16,16,128]{3,2,1,0:T(8,128)} %refs_0_.5, ...), custom_call_target="tpu_custom_call" | custom-call | tf_op jit(solution)/shard_map/load/pallas_call | solution.py:107
  4.1 3.1 %collective-permute-start = (f32[11,16,8,128]{3,2,1,0:T(8,128)}, f32[11,16,8,128]{3,2,1,0:T(8,128)}, u32[]{:S(2)}, u32[]{:S(2)}) collective-permute-start(f32[11,16,8,128]{3,2,1,0:T(8,128)} %get-tuple-element.43), channel_id=1, source_target_pairs={{0,1},{1,0},{2,3},{3,2},{4,5},{5,4},{6,7},{7,6},{8,9},{9,8},{10,11... | collective-permute-start | bytes 2162696 | tf_op jit(solution)/shard_map/ppermute | solution.py:61
  7.2 1.5 %collective-permute-start.1 = (f32[11,16,8,128]{3,2,1,0:T(8,128)}, f32[11,16,8,128]{3,2,1,0:T(8,128)}, u32[]{:S(2)}, u32[]{:S(2)}) collective-permute-start(f32[11,16,8,128]{3,2,1,0:T(8,128)} %get-tuple-element.44), channel_id=1, source_target_pairs={{1,2},{2,1},{5,6},{6,5},{9,10},{10,9},{13,14},{14,13},{17,18},{18,... | collective-permute-start | bytes 2162696 | tf_op jit(solution)/shard_map/ppermute | solution.py:61
  8.7 1.5 %table.1 = f32[32,4,128]{2,1,0:T(4,128)} custom-call(f32[2,3]{1,0:T(2,128)} %refs_0_.3, f32[2,3]{1,0:T(2,128)} %refs_1_.3, s32[2,3]{1,0:T(2,128)} %refs_2_.3, s32[1,128]{1,0:T(1,128)} %bitcast.7, s32[1,128]{1,0:T(1,128)} %bitcast.8, f32[1,128]{1,0:T(1,128)} %bitcast.9), custom_call_target="tpu_custom_call" | custom-call | tf_op jit(solution)/shard_map/table/pallas_call | solution.py:619
  10.2 20.5 %all_to_all.10.refs_0_.table_ref.refs_10_ = f32[32,4,128]{2,1,0:T(4,128)S(1)} all-to-all(f32[32,4,128]{2,1,0:T(4,128)} %table.1), channel_id=1, replica_groups=mesh['gx'=8,'gy'=4] {'gx','gy'}, dimensions={0} | all-to-all | bytes 131072 | tf_op jit(solution)/shard_map/all_to_all | solution.py:631
  30.8 0.4 more.1
  31.2 0.0 collective-permute-done.z_first.refs_3_
  31.2 0.0 collective-permute-done.1.z_second.refs_4_
  31.3 1.5 %widen.5 = (f32[116,16,128]{2,1,0:T(8,128)S(1)}, f32[116,16,128]{2,1,0:T(8,128)S(1)}) custom-call(f32[11,16,16,128]{3,2,1,0:T(8,128)S(1)} %copy-done.8, f32[11,16,8,128]{3,2,1,0:T(8,128)} %collective-permute-done.z_first.refs_3_, f32[11,16,8,128]{3,2,1,0:T(8,128)} %collective-permute-done.1.z_second.refs_4_, ...), custom_call_target="tpu_custom_call" | custom-call | flops 500000000 | bytes 1500000 | tf_op jit(solution)/shard_map/widen/pallas_call | solution.py:44
  32.8 0.7 collective-permute-start.3
  33.5 2.0 %collective-permute-start.2 = (f32[116,16,128]{2,1,0:T(8,128)S(1)}, f32[116,16,128]{2,1,0:T(8,128)S(1)}, u32[]{:S(2)}, u32[]{:S(2)}) collective-permute-start(f32[116,16,128]{2,1,0:T(8,128)S(1)} %get-tuple-element.45._), channel_id=1, source_target_pairs={{0,4},{4,0},{8,12},{12,8},{16,20},{20,16},{24,28},{28,24},{1,5},{5... | collective-permute-start | bytes 2850824 | tf_op jit(solution)/shard_map/ppermute | solution.py:61
  35.5 1.0 sources.1.refs_1_.refs_0_
  36.6 0.8 collective-permute-start.4
  37.3 0.7 collective-permute-start.5
  38.0 15.3 %collective-permute-done.4.z_first.refs_3_ = f32[10,16,8,128]{3,2,1,0:T(8,128)S(1)} collective-permute-done((f32[10,16,8,128]{3,2,1,0:T(8,128)S(1)}, f32[10,16,8,128]{3,2,1,0:T(8,128)S(1)}, u32[]{:S(2)}, u32[]{:S(2)}) %collective-permute-start.4) | collective-permute-done | bytes 655392 | tf_op jit(solution)/shard_map/ppermute | solution.py:61
  53.3 0.0 collective-permute-done.5.z_second.refs_4_
  53.3 0.2 widen.6
  53.4 0.1 collective-permute-start.8
  53.5 3.9 %collective-permute-start.6 = (f32[8,16,8,128]{3,2,1,0:T(8,128)S(1)}, f32[8,16,8,128]{3,2,1,0:T(8,128)S(1)}, u32[]{:S(2)}, u32[]{:S(2)}) collective-permute-start(f32[8,16,8,128]{3,2,1,0:T(8,128)S(1)} %get-tuple-element.57), channel_id=1, source_target_pairs={{0,1},{1,0},{2,3},{3,2},{4,5},{5,4},{6,7},{7,6},{8,9},{9,8},{10,11... | collective-permute-start | bytes 1572872 | tf_op jit(solution)/shard_map/ppermute | solution.py:61
  57.4 0.7 collective-permute-start.7
  58.1 0.0 collective-permute-done.3.refs_6_
  58.1 0.7 collective-permute-start.9
  58.8 0.0 collective-permute-done.2.refs_5_
  58.8 8.5 %step_top.1 = (f32[5,32,4,8,128]{4,3,2,1,0:T(8,128)S(1)}, f32[2,16,16,128]{3,2,1,0:T(8,128)S(1)}, f32[2,16,8,128]{3,2,1,0:T(8,128)S(1)}, f32[2,16,8,128]{3,2,1,0:T(8,128)S(1)}, f32[64,128]{1,0:T(8,128)S(1)}) custom-call(f32[32,4,128]{2,1,0:T(4,128)S(1)} %all_to_all.10.refs_0_.table_ref.refs_10_, f32[3,32,32,128]{3,2,1,0:T(8,128)S(1)} %sources.1.refs_1_.refs_0_, ...), custom_call_target="tpu_custom_call" | custom-call | flops 7000000000 | bytes 21000000 | tf_op jit(solution)/shard_map/step_top/pallas_call | solution.py:44
  67.3 2.6 %collective-permute-done.6.z_first.refs_3_ = f32[8,16,8,128]{3,2,1,0:T(8,128)S(1)} collective-permute-done((f32[8,16,8,128]{3,2,1,0:T(8,128)S(1)}, f32[8,16,8,128]{3,2,1,0:T(8,128)S(1)}, u32[]{:S(2)}, u32[]{:S(2)}) %collective-permute-start.6) | collective-permute-done | bytes 524320 | tf_op jit(solution)/shard_map/ppermute | solution.py:61
  69.9 0.0 collective-permute-done.7.z_second.refs_4_
  69.9 3.6 %collective-permute-start.12 = (f32[2,16,8,128]{3,2,1,0:T(8,128)S(1)}, f32[2,16,8,128]{3,2,1,0:T(8,128)S(1)}, u32[]{:S(2)}, u32[]{:S(2)}) collective-permute-start(f32[2,16,8,128]{3,2,1,0:T(8,128)S(1)} %get-tuple-element.67), channel_id=1, source_target_pairs={{0,1},{1,0},{2,3},{3,2},{4,5},{5,4},{6,7},{7,6},{8,9},{9,8},{10,11... | collective-permute-start | bytes 393224 | tf_op jit(solution)/shard_map/ppermute | solution.py:61
  73.6 0.7 collective-permute-start.13
  74.2 2.6 %collective-permute-done.12.z_first.refs_5_ = f32[2,16,8,128]{3,2,1,0:T(8,128)S(1)} collective-permute-done((f32[2,16,8,128]{3,2,1,0:T(8,128)S(1)}, f32[2,16,8,128]{3,2,1,0:T(8,128)S(1)}, u32[]{:S(2)}, u32[]{:S(2)}) %collective-permute-start.12) | collective-permute-done | bytes 131104 | tf_op jit(solution)/shard_map/ppermute | solution.py:61
  76.9 0.0 collective-permute-done.13.z_second.refs_6_
  76.9 0.1 collective-permute-start.14
  77.0 0.7 collective-permute-start.15
  77.7 0.0 collective-permute-done.9.refs_6_
  77.7 0.0 collective-permute-done.8.refs_5_
  77.7 1.1 prepare.2
  78.8 0.2 widen.7
  79.0 2.9 %collective-permute-start.10 = (f32[80,16,128]{2,1,0:T(8,128)S(1)}, f32[80,16,128]{2,1,0:T(8,128)S(1)}, u32[]{:S(2)}, u32[]{:S(2)}) collective-permute-start(f32[80,16,128]{2,1,0:T(8,128)S(1)} %get-tuple-element.61), channel_id=1, source_target_pairs={{0,4},{4,0},{8,12},{12,8},{16,20},{20,16},{24,28},{28,24},{1,5},{5... | collective-permute-start | bytes 1966088 | tf_op jit(solution)/shard_map/ppermute | solution.py:61
  81.9 0.7 collective-permute-start.11
  82.6 0.0 collective-permute-done.14.refs_7_
  82.6 0.0 collective-permute-done.15.refs_8_
  82.6 6.0 %step.2 = (f32[2,16,16,128]{3,2,1,0:T(8,128)S(1)}, f32[2,16,8,128]{3,2,1,0:T(8,128)S(1)}, f32[2,16,8,128]{3,2,1,0:T(8,128)S(1)}, f32[64,128]{1,0:T(8,128)S(1)}) custom-call(f32[32,4,128]{2,1,0:T(4,128)S(1)} %all_to_all.10.refs_0_.table_ref.refs_10_, f32[9,32,4,8,128]{4,3,2,1,0:T(8,128)S(1)} %get-tuple-element.60.refs_0_.refs_1_, ...), custom_call_target="tpu_custom_call" | custom-call | flops 6000000000 | bytes 18000000 | tf_op jit(solution)/shard_map/step/pallas_call | solution.py:44
  88.6 3.7 %collective-permute-start.16 = (f32[2,16,8,128]{3,2,1,0:T(8,128)S(1)}, f32[2,16,8,128]{3,2,1,0:T(8,128)S(1)}, u32[]{:S(2)}, u32[]{:S(2)}) collective-permute-start(f32[2,16,8,128]{3,2,1,0:T(8,128)S(1)} %get-tuple-element.73), channel_id=1, source_target_pairs={{0,1},{1,0},{2,3},{3,2},{4,5},{5,4},{6,7},{7,6},{8,9},{9,8},{10,11... | collective-permute-start | bytes 393224 | tf_op jit(solution)/shard_map/ppermute | solution.py:61
  92.3 0.7 collective-permute-start.17
  93.0 2.3 %collective-permute-done.16.z_first.refs_5_ = f32[2,16,8,128]{3,2,1,0:T(8,128)S(1)} collective-permute-done((f32[2,16,8,128]{3,2,1,0:T(8,128)S(1)}, f32[2,16,8,128]{3,2,1,0:T(8,128)S(1)}, u32[]{:S(2)}, u32[]{:S(2)}) %collective-permute-start.16) | collective-permute-done | bytes 131104 | tf_op jit(solution)/shard_map/ppermute | solution.py:61
  95.2 0.0 collective-permute-done.17.z_second.refs_6_
  95.3 3.0 %collective-permute-start.18 = (f32[24,16,128]{2,1,0:T(8,128)S(1)}, f32[24,16,128]{2,1,0:T(8,128)S(1)}, u32[]{:S(2)}, u32[]{:S(2)}) collective-permute-start(f32[24,16,128]{2,1,0:T(8,128)S(1)} %get-tuple-element.75), channel_id=1, source_target_pairs={{0,4},{4,0},{8,12},{12,8},{16,20},{20,16},{24,28},{28,24},{1,5},{5... | collective-permute-start | bytes 589832 | tf_op jit(solution)/shard_map/ppermute | solution.py:61
  98.3 0.7 collective-permute-start.19
  99.0 0.0 collective-permute-done.10.refs_5_
  99.0 0.0 collective-permute-done.11.refs_6_
  99.0 1.0 prepare.3.refs_1_
  100.0 0.0 collective-permute-done.18.refs_7_
  100.0 0.0 collective-permute-done.19.refs_8_
  100.0 6.5 %step.3 = (f32[16,16,128]{2,1,0:T(8,128)}, f32[16,16,128]{2,1,0:T(8,128)}, f32[64,128]{1,0:T(8,128)S(1)}) custom-call(f32[32,4,128]{2,1,0:T(4,128)S(1)} %all_to_all.10.refs_0_.table_ref.refs_10_, f32[9,32,4,8,128]{4,3,2,1,0:T(8,128)S(1)} %prepare.3.refs_1_, f32[5,32,4,8,128]{4,3,2,1,0:T(8,128)S(1)} %get-tuple-element.47.refs_1_.refs_2_, ...), custom_call_target="tpu_custom_call" | custom-call | flops 6000000000 | bytes 18000000 | tf_op jit(solution)/shard_map/step/pallas_call | solution.py:44
  106.6 21.2 %all_to_all.11 = f32[32,2,128]{2,1,0:T(2,128)S(1)} all-to-all(f32[32,2,128]{2,1,0:T(2,128)S(1)} %bitcast.5), channel_id=1, replica_groups=mesh['gx'=8,'gy'=4] {'gx','gy'}, dimensions={0} | all-to-all | bytes 65536 | tf_op jit(solution)/shard_map/all_to_all | solution.py:707
  127.8 0.6 reduce_sum.9
  (15 shorter events, 0.1 us)
Async XLA Ops:
  0.6 30.1 %copy-start.5 = (f32[3,16,16,128]{3,2,1,0:T(8,128)S(1)}, f32[3,16,16,128]{3,2,1,0:T(8,128)}, u32[]{:S(2)}) copy-start(f32[3,16,16,128]{3,2,1,0:T(8,128)} %refs_5_.3) | copy-start | bytes 1179652
  0.6 30.1 %copy-start.4 = (f32[3,16,16,128]{3,2,1,0:T(8,128)S(1)}, f32[3,16,16,128]{3,2,1,0:T(8,128)}, u32[]{:S(2)}) copy-start(f32[3,16,16,128]{3,2,1,0:T(8,128)} %refs_4_.3) | copy-start | bytes 1179652
  0.7 30.1 %copy-start.3 = (f32[3,16,16,128]{3,2,1,0:T(8,128)S(1)}, f32[3,16,16,128]{3,2,1,0:T(8,128)}, u32[]{:S(2)}) copy-start(f32[3,16,16,128]{3,2,1,0:T(8,128)} %refs_3_.3) | copy-start | bytes 1179652
  0.7 30.0 %copy-start.2 = (f32[3,16,16,128]{3,2,1,0:T(8,128)S(1)}, f32[3,16,16,128]{3,2,1,0:T(8,128)}, u32[]{:S(2)}) copy-start(f32[3,16,16,128]{3,2,1,0:T(8,128)} %refs_2_.5) | copy-start | bytes 1179652
  0.7 30.0 %copy-start.1 = (f32[3,16,16,128]{3,2,1,0:T(8,128)S(1)}, f32[3,16,16,128]{3,2,1,0:T(8,128)}, u32[]{:S(2)}) copy-start(f32[3,16,16,128]{3,2,1,0:T(8,128)} %refs_1_.5) | copy-start | bytes 1179652
  0.7 30.0 %copy-start = (f32[3,16,16,128]{3,2,1,0:T(8,128)S(1)}, f32[3,16,16,128]{3,2,1,0:T(8,128)}, u32[]{:S(2)}) copy-start(f32[3,16,16,128]{3,2,1,0:T(8,128)} %refs_0_.5) | copy-start | bytes 1179652
  0.7 30.0 %copy-start.7 = (f32[3,16,16,128]{3,2,1,0:T(8,128)S(1)}, f32[3,16,16,128]{3,2,1,0:T(8,128)}, u32[]{:S(2)}) copy-start(f32[3,16,16,128]{3,2,1,0:T(8,128)} %refs_7_.3) | copy-start | bytes 1179652
  0.7 30.0 %copy-start.6 = (f32[3,16,16,128]{3,2,1,0:T(8,128)S(1)}, f32[3,16,16,128]{3,2,1,0:T(8,128)}, u32[]{:S(2)}) copy-start(f32[3,16,16,128]{3,2,1,0:T(8,128)} %refs_6_.3) | copy-start | bytes 1179652
  0.7 30.0 %copy-start.10 = (f32[16,16,128]{2,1,0:T(8,128)S(1)}, f32[16,16,128]{2,1,0:T(8,128)}, u32[]{:S(2)}) copy-start(f32[16,16,128]{2,1,0:T(8,128)} %refs_9_.3) | copy-start | bytes 393220
  0.7 30.0 %copy-start.9 = (f32[16,16,128]{2,1,0:T(8,128)S(1)}, f32[16,16,128]{2,1,0:T(8,128)}, u32[]{:S(2)}) copy-start(f32[16,16,128]{2,1,0:T(8,128)} %refs_8_.3) | copy-start | bytes 393220
  4.1 27.2 %collective-permute-start = (f32[11,16,8,128]{3,2,1,0:T(8,128)}, f32[11,16,8,128]{3,2,1,0:T(8,128)}, u32[]{:S(2)}, u32[]{:S(2)}) collective-permute-start(f32[11,16,8,128]{3,2,1,0:T(8,128)} %get-tuple-element.43), channel_id=1, source_target_pairs={{0,1},{1,0},{2,3},{3,2},{4,5},{5,4},{6,7},{7,6},{8,9},{9,8},{10,11... | collective-permute-start | bytes 2162696 | tf_op jit(solution)/shard_map/ppermute | solution.py:61
  7.2 24.1 %collective-permute-start.1 = (f32[11,16,8,128]{3,2,1,0:T(8,128)}, f32[11,16,8,128]{3,2,1,0:T(8,128)}, u32[]{:S(2)}, u32[]{:S(2)}) collective-permute-start(f32[11,16,8,128]{3,2,1,0:T(8,128)} %get-tuple-element.44), channel_id=1, source_target_pairs={{1,2},{2,1},{5,6},{6,5},{9,10},{10,9},{13,14},{14,13},{17,18},{18,... | collective-permute-start | bytes 2162696 | tf_op jit(solution)/shard_map/ppermute | solution.py:61
  10.2 21.1 %copy-start.8 = (f32[11,16,16,128]{3,2,1,0:T(8,128)S(1)}, f32[11,16,16,128]{3,2,1,0:T(8,128)}, u32[]{:S(2)}) copy-start(f32[11,16,16,128]{3,2,1,0:T(8,128)} %get-tuple-element.42.own.refs_2_) | copy-start | bytes 4325380
  32.8 25.3 %collective-permute-start.3 = (f32[116,16,128]{2,1,0:T(8,128)S(1)}, f32[116,16,128]{2,1,0:T(8,128)S(1)}, u32[]{:S(2)}, u32[]{:S(2)}) collective-permute-start(f32[116,16,128]{2,1,0:T(8,128)S(1)} %get-tuple-element.46), channel_id=1, source_target_pairs={{4,8},{12,16},{20,24},{8,4},{16,12},{24,20},{5,9},{13,17},{21,25},... | collective-permute-start | bytes 2850824 | tf_op jit(solution)/shard_map/ppermute | solution.py:61
  33.5 25.3 %collective-permute-start.2 = (f32[116,16,128]{2,1,0:T(8,128)S(1)}, f32[116,16,128]{2,1,0:T(8,128)S(1)}, u32[]{:S(2)}, u32[]{:S(2)}) collective-permute-start(f32[116,16,128]{2,1,0:T(8,128)S(1)} %get-tuple-element.45._), channel_id=1, source_target_pairs={{0,4},{4,0},{8,12},{12,8},{16,20},{20,16},{24,28},{28,24},{1,5},{5... | collective-permute-start | bytes 2850824 | tf_op jit(solution)/shard_map/ppermute | solution.py:61
  36.6 16.7 %collective-permute-start.4 = (f32[10,16,8,128]{3,2,1,0:T(8,128)S(1)}, f32[10,16,8,128]{3,2,1,0:T(8,128)S(1)}, u32[]{:S(2)}, u32[]{:S(2)}) collective-permute-start(f32[10,16,8,128]{3,2,1,0:T(8,128)S(1)} %get-tuple-element.54), channel_id=1, source_target_pairs={{0,1},{1,0},{2,3},{3,2},{4,5},{5,4},{6,7},{7,6},{8,9},{9,8},{10,11... | collective-permute-start | bytes 1966088 | tf_op jit(solution)/shard_map/ppermute | solution.py:61
  37.3 16.0 %collective-permute-start.5 = (f32[10,16,8,128]{3,2,1,0:T(8,128)S(1)}, f32[10,16,8,128]{3,2,1,0:T(8,128)S(1)}, u32[]{:S(2)}, u32[]{:S(2)}) collective-permute-start(f32[10,16,8,128]{3,2,1,0:T(8,128)S(1)} %get-tuple-element.55), channel_id=1, source_target_pairs={{1,2},{2,1},{5,6},{6,5},{9,10},{10,9},{13,14},{14,13},{17,18},{18,... | collective-permute-start | bytes 1966088 | tf_op jit(solution)/shard_map/ppermute | solution.py:61
  53.4 24.3 %collective-permute-start.8 = (f32[100,16,128]{2,1,0:T(8,128)S(1)}, f32[100,16,128]{2,1,0:T(8,128)S(1)}, u32[]{:S(2)}, u32[]{:S(2)}) collective-permute-start(f32[100,16,128]{2,1,0:T(8,128)S(1)} %get-tuple-element.56), channel_id=1, source_target_pairs={{0,4},{4,0},{8,12},{12,8},{16,20},{20,16},{24,28},{28,24},{1,5},{5... | collective-permute-start | bytes 2457608 | tf_op jit(solution)/shard_map/ppermute | solution.py:61
  53.5 16.4 %collective-permute-start.6 = (f32[8,16,8,128]{3,2,1,0:T(8,128)S(1)}, f32[8,16,8,128]{3,2,1,0:T(8,128)S(1)}, u32[]{:S(2)}, u32[]{:S(2)}) collective-permute-start(f32[8,16,8,128]{3,2,1,0:T(8,128)S(1)} %get-tuple-element.57), channel_id=1, source_target_pairs={{0,1},{1,0},{2,3},{3,2},{4,5},{5,4},{6,7},{7,6},{8,9},{9,8},{10,11... | collective-permute-start | bytes 1572872 | tf_op jit(solution)/shard_map/ppermute | solution.py:61
  57.4 12.5 %collective-permute-start.7 = (f32[8,16,8,128]{3,2,1,0:T(8,128)S(1)}, f32[8,16,8,128]{3,2,1,0:T(8,128)S(1)}, u32[]{:S(2)}, u32[]{:S(2)}) collective-permute-start(f32[8,16,8,128]{3,2,1,0:T(8,128)S(1)} %get-tuple-element.58), channel_id=1, source_target_pairs={{1,2},{2,1},{5,6},{6,5},{9,10},{10,9},{13,14},{14,13},{17,18},{18,... | collective-permute-start | bytes 1572872 | tf_op jit(solution)/shard_map/ppermute | solution.py:61
  58.1 19.6 %collective-permute-start.9 = (f32[100,16,128]{2,1,0:T(8,128)S(1)}, f32[100,16,128]{2,1,0:T(8,128)S(1)}, u32[]{:S(2)}, u32[]{:S(2)}) collective-permute-start(f32[100,16,128]{2,1,0:T(8,128)S(1)} %get-tuple-element.59), channel_id=1, source_target_pairs={{4,8},{12,16},{20,24},{8,4},{16,12},{24,20},{5,9},{13,17},{21,25},... | collective-permute-start | bytes 2457608 | tf_op jit(solution)/shard_map/ppermute | solution.py:61
  69.9 6.9 %collective-permute-start.12 = (f32[2,16,8,128]{3,2,1,0:T(8,128)S(1)}, f32[2,16,8,128]{3,2,1,0:T(8,128)S(1)}, u32[]{:S(2)}, u32[]{:S(2)}) collective-permute-start(f32[2,16,8,128]{3,2,1,0:T(8,128)S(1)} %get-tuple-element.67), channel_id=1, source_target_pairs={{0,1},{1,0},{2,3},{3,2},{4,5},{5,4},{6,7},{7,6},{8,9},{9,8},{10,11... | collective-permute-start | bytes 393224 | tf_op jit(solution)/shard_map/ppermute | solution.py:61
  73.6 3.3 %collective-permute-start.13 = (f32[2,16,8,128]{3,2,1,0:T(8,128)S(1)}, f32[2,16,8,128]{3,2,1,0:T(8,128)S(1)}, u32[]{:S(2)}, u32[]{:S(2)}) collective-permute-start(f32[2,16,8,128]{3,2,1,0:T(8,128)S(1)} %get-tuple-element.68), channel_id=1, source_target_pairs={{1,2},{2,1},{5,6},{6,5},{9,10},{10,9},{13,14},{14,13},{17,18},{18,... | collective-permute-start | bytes 393224 | tf_op jit(solution)/shard_map/ppermute | solution.py:61
  76.9 5.7 %collective-permute-start.14 = (f32[24,16,128]{2,1,0:T(8,128)S(1)}, f32[24,16,128]{2,1,0:T(8,128)S(1)}, u32[]{:S(2)}, u32[]{:S(2)}) collective-permute-start(f32[24,16,128]{2,1,0:T(8,128)S(1)} %get-tuple-element.69), channel_id=1, source_target_pairs={{0,4},{4,0},{8,12},{12,8},{16,20},{20,16},{24,28},{28,24},{1,5},{5... | collective-permute-start | bytes 589832 | tf_op jit(solution)/shard_map/ppermute | solution.py:61
  77.0 5.6 %collective-permute-start.15 = (f32[24,16,128]{2,1,0:T(8,128)S(1)}, f32[24,16,128]{2,1,0:T(8,128)S(1)}, u32[]{:S(2)}, u32[]{:S(2)}) collective-permute-start(f32[24,16,128]{2,1,0:T(8,128)S(1)} %get-tuple-element.70), channel_id=1, source_target_pairs={{4,8},{12,16},{20,24},{8,4},{16,12},{24,20},{5,9},{13,17},{21,25},... | collective-permute-start | bytes 589832 | tf_op jit(solution)/shard_map/ppermute | solution.py:61
  79.0 20.0 %collective-permute-start.10 = (f32[80,16,128]{2,1,0:T(8,128)S(1)}, f32[80,16,128]{2,1,0:T(8,128)S(1)}, u32[]{:S(2)}, u32[]{:S(2)}) collective-permute-start(f32[80,16,128]{2,1,0:T(8,128)S(1)} %get-tuple-element.61), channel_id=1, source_target_pairs={{0,4},{4,0},{8,12},{12,8},{16,20},{20,16},{24,28},{28,24},{1,5},{5... | collective-permute-start | bytes 1966088 | tf_op jit(solution)/shard_map/ppermute | solution.py:61
  81.9 17.1 %collective-permute-start.11 = (f32[80,16,128]{2,1,0:T(8,128)S(1)}, f32[80,16,128]{2,1,0:T(8,128)S(1)}, u32[]{:S(2)}, u32[]{:S(2)}) collective-permute-start(f32[80,16,128]{2,1,0:T(8,128)S(1)} %get-tuple-element.62), channel_id=1, source_target_pairs={{4,8},{12,16},{20,24},{8,4},{16,12},{24,20},{5,9},{13,17},{21,25},... | collective-permute-start | bytes 1966088 | tf_op jit(solution)/shard_map/ppermute | solution.py:61
  88.6 6.6 %collective-permute-start.16 = (f32[2,16,8,128]{3,2,1,0:T(8,128)S(1)}, f32[2,16,8,128]{3,2,1,0:T(8,128)S(1)}, u32[]{:S(2)}, u32[]{:S(2)}) collective-permute-start(f32[2,16,8,128]{3,2,1,0:T(8,128)S(1)} %get-tuple-element.73), channel_id=1, source_target_pairs={{0,1},{1,0},{2,3},{3,2},{4,5},{5,4},{6,7},{7,6},{8,9},{9,8},{10,11... | collective-permute-start | bytes 393224 | tf_op jit(solution)/shard_map/ppermute | solution.py:61
  92.3 3.0 %collective-permute-start.17 = (f32[2,16,8,128]{3,2,1,0:T(8,128)S(1)}, f32[2,16,8,128]{3,2,1,0:T(8,128)S(1)}, u32[]{:S(2)}, u32[]{:S(2)}) collective-permute-start(f32[2,16,8,128]{3,2,1,0:T(8,128)S(1)} %get-tuple-element.74), channel_id=1, source_target_pairs={{1,2},{2,1},{5,6},{6,5},{9,10},{10,9},{13,14},{14,13},{17,18},{18,... | collective-permute-start | bytes 393224 | tf_op jit(solution)/shard_map/ppermute | solution.py:61
  95.3 4.7 %collective-permute-start.18 = (f32[24,16,128]{2,1,0:T(8,128)S(1)}, f32[24,16,128]{2,1,0:T(8,128)S(1)}, u32[]{:S(2)}, u32[]{:S(2)}) collective-permute-start(f32[24,16,128]{2,1,0:T(8,128)S(1)} %get-tuple-element.75), channel_id=1, source_target_pairs={{0,4},{4,0},{8,12},{12,8},{16,20},{20,16},{24,28},{28,24},{1,5},{5... | collective-permute-start | bytes 589832 | tf_op jit(solution)/shard_map/ppermute | solution.py:61
  98.3 1.7 %collective-permute-start.19 = (f32[24,16,128]{2,1,0:T(8,128)S(1)}, f32[24,16,128]{2,1,0:T(8,128)S(1)}, u32[]{:S(2)}, u32[]{:S(2)}) collective-permute-start(f32[24,16,128]{2,1,0:T(8,128)S(1)} %get-tuple-element.76), channel_id=1, source_target_pairs={{4,8},{12,16},{20,24},{8,4},{16,12},{24,20},{5,9},{13,17},{21,25},... | collective-permute-start | bytes 589832 | tf_op jit(solution)/shard_map/ppermute | solution.py:61

commit v11 on v10

--- a/solution.py
+++ b/solution.py
@@ -215,13 +215,8 @@
 
 
 def table_kernel(steps, *refs):
-    ins, out, held, sems = refs[:6], refs[6], refs[7:13], refs[13]
-    copies = [pltpu.make_async_copy(i, h, sems.at[n]) for n, (i, h) in enumerate(zip(ins, held))]
-    for c in copies:
-        c.start()
-    for c in copies:
-        c.wait()
-    rate, bhp, control, perf_well, perf_cell, perf_wi = [h[...] for h in held]
+    rate, bhp, control, perf_well, perf_cell, perf_wi = [r[...] for r in refs[:6]]
+    out = refs[-1]
     wells = rate.shape[0]
     effective = jnp.where(control == 1, rate, bhp)
     lane = lax.broadcasted_iota(jnp.int32, (1, 128), 1)
@@ -616,15 +611,9 @@
     leads = [None] * 3 + [top] * 8
     split = len(arrays)
     small = [rate_mis, bhp_mis, control] + [p[None] for p in (perf_well, perf_cell, perf_wi)]
-    mine = pl.pallas_call(
-        functools.partial(table_kernel, steps),
-        in_specs=[HBM] * 6,
-        out_specs=VMEM,
-        out_shape=sds(devices, 4, 128),
-        scratch_shapes=[pltpu.VMEM(p.shape, p.dtype) for p in small]
-        + [pltpu.SemaphoreType.DMA((6,))],
-        name="table",
-    )(*small)
+    mine = call(
+        functools.partial(table_kernel, steps), small, [sds(devices, 4, 128)], "table", 4
+    )[0]
     blocks, y_low, y_high, token = load(arrays, leads, dims, ())
     z_got = swaps(y_low, y_high, "gy")
     mine, _ = lax.optimization_barrier((mine, token))

time: 129 us -> 128 us (level)
  Pallas kernels: 31.3 us -> 27.3 us
  blocking collectives: 41.7 us -> 43.9 us
  waiting for transfers between devices: 22.8 us -> 24.2 us
    pallas_call x12 -> x13, Pallas kernels: 26.5 us -> 24 us  [call(): pl.pallas_call(kernel, in_specs=specs or [VMEM] * len(ins), out_specs=[VM...]
    all_to_all x1, blocking collectives: 20.5 us -> 22.7 us  [local(): table = lax.all_to_all(mine, ('gx', 'gy'), 0, 0, tiled=True)]
    pallas_call x1 -> x0, Pallas kernels: 1.5 us -> none  [local(): pl.pallas_call(functools.partial(table_kernel, steps), in_specs=[HBM] * 6...]
    ppermute x20, waiting for transfers between devices: 22.8 us -> 24.2 us  [swaps(): return (lax.ppermute(first, axis, even), lax.ppermute(second, axis, odd))]
  transfers between devices with their start and end apart: 20 -> 20, of which waited for: 4 -> 4; matrix products, arithmetic and copies ran while one was open for 0% -> 0% of each run, Pallas kernels for 16% -> 14%
where the time goes in v11:
time: 128 us; the launch traced here: 127 us
  blocking collectives  43.9 us (34%)
  starting transfers between devices  30 us (23%)
  Pallas kernels  27.3 us (21%)
  waiting for transfers between devices  24.2 us (19%)
    ppermute x20, starting transfers between devices, swaps(): return (lax.ppermute(first, axis, even), lax.ppermute(second, axis, odd))  30 us
    ppermute x20, waiting for transfers between devices, swaps(): return (lax.ppermute(first, axis, even), lax.ppermute(second, axis, odd))  24.2 us
    pallas_call x13, Pallas kernels, call(): pl.pallas_call(kernel, in_specs=specs or [VMEM] * len(ins), out_specs=[VM...  24 us
    all_to_all x1, blocking collectives, local(): table = lax.all_to_all(mine, ('gx', 'gy'), 0, 0, tiled=True)  22.7 us
    all_to_all x1, blocking collectives, local(): parts = lax.all_to_all(dense, ('gx', 'gy'), 0, 0, tiled=True)  21.2 us
    pallas_call x1, Pallas kernels, load(): pl.pallas_call(functools.partial(load_kernel, leads), in_specs=[HBM] * n...  3.33 us
  transfers between devices with their start and end apart: 20, of which 4 were waited for; matrix products, arithmetic and copies ran while one was open for 0% of the time, Pallas kernels for 14%

profile of v11, /device:TPU:0, one launch (start us, length us, event | category | flops | bytes accessed | tf_op | source)
XLA Modules:
  0.0 127.2 jit_solution(3449436848420189210)
XLA Ops:
  0.8 3.3 %load.1 = (f32[11,16,16,128]{3,2,1,0:T(8,128)}, f32[11,16,8,128]{3,2,1,0:T(8,128)}, f32[11,16,8,128]{3,2,1,0:T(8,128)}, f32[8,128]{1,0:T(8,128)}) custom-call(f32[16,16,128]{2,1,0:T(8,128)} %refs_0_.4, f32[16,16,128]{2,1,0:T(8,128)} %refs_1_.4, f32[16,16,128]{2,1,0:T(8,128)} %refs_2_.4, f32[3,16,16,128]{3,2,1,0:T(8,128)} %refs_0_.5, ...), custom_call_target="tpu_custom_call" | custom-call | tf_op jit(solution)/shard_map/load/pallas_call | solution.py:107
  4.1 3.1 %collective-permute-start = (f32[11,16,8,128]{3,2,1,0:T(8,128)}, f32[11,16,8,128]{3,2,1,0:T(8,128)S(1)}, u32[]{:S(2)}, u32[]{:S(2)}) collective-permute-start(f32[11,16,8,128]{3,2,1,0:T(8,128)} %get-tuple-element.43), channel_id=1, source_target_pairs={{0,1},{1,0},{2,3},{3,2},{4,5},{5,4},{6,7},{7,6},{8,9},{9,8},{10,11... | collective-permute-start | bytes 2162696 | tf_op jit(solution)/shard_map/ppermute | solution.py:61
  7.2 0.7 collective-permute-start.1
  7.9 0.0 copy-done.16
  7.9 0.0 copy-done.15
  7.9 0.0 copy-done.14
  8.0 0.0 copy-done.13
  8.0 0.0 copy-done.12
  8.0 0.0 copy-done.11
  8.0 0.0 copy-start.8
  8.0 0.1 table.1
  8.1 22.7 %all_to_all.10.refs_0_.table_ref.refs_10_ = f32[32,4,128]{2,1,0:T(4,128)S(1)} all-to-all(f32[32,4,128]{2,1,0:T(4,128)S(1)} %table.1), channel_id=1, replica_groups=mesh['gx'=8,'gy'=4] {'gx','gy'}, dimensions={0} | all-to-all | bytes 131072 | tf_op jit(solution)/shard_map/all_to_all | solution.py:620
  30.8 0.0 copy-done.4
  30.8 0.4 more.1
  31.3 0.0 collective-permute-done.z_first.refs_3_
  31.3 0.0 collective-permute-done.1.z_second.refs_4_
  31.3 0.0 copy-done.8
  31.3 0.2 widen.5
  31.5 0.7 collective-permute-start.3
  32.3 2.0 %collective-permute-start.2 = (f32[116,16,128]{2,1,0:T(8,128)S(1)}, f32[116,16,128]{2,1,0:T(8,128)S(1)}, u32[]{:S(2)}, u32[]{:S(2)}) collective-permute-start(f32[116,16,128]{2,1,0:T(8,128)S(1)} %get-tuple-element.45._), channel_id=1, source_target_pairs={{0,4},{4,0},{8,12},{12,8},{16,20},{20,16},{24,28},{28,24},{1,5},{5... | collective-permute-start | bytes 2850824 | tf_op jit(solution)/shard_map/ppermute | solution.py:61
  34.3 1.1 sources.1.refs_1_.refs_0_
  35.3 0.8 collective-permute-start.4
  36.1 0.7 collective-permute-start.5
  36.8 15.3 %collective-permute-done.4.z_first.refs_3_ = f32[10,16,8,128]{3,2,1,0:T(8,128)S(1)} collective-permute-done((f32[10,16,8,128]{3,2,1,0:T(8,128)S(1)}, f32[10,16,8,128]{3,2,1,0:T(8,128)S(1)}, u32[]{:S(2)}, u32[]{:S(2)}) %collective-permute-start.4) | collective-permute-done | bytes 655392 | tf_op jit(solution)/shard_map/ppermute | solution.py:61
  52.0 0.0 collective-permute-done.5.z_second.refs_4_
  52.0 0.2 widen.6
  52.2 0.1 collective-permute-start.8
  52.3 3.9 %collective-permute-start.6 = (f32[8,16,8,128]{3,2,1,0:T(8,128)S(1)}, f32[8,16,8,128]{3,2,1,0:T(8,128)S(1)}, u32[]{:S(2)}, u32[]{:S(2)}) collective-permute-start(f32[8,16,8,128]{3,2,1,0:T(8,128)S(1)} %get-tuple-element.57), channel_id=1, source_target_pairs={{0,1},{1,0},{2,3},{3,2},{4,5},{5,4},{6,7},{7,6},{8,9},{9,8},{10,11... | collective-permute-start | bytes 1572872 | tf_op jit(solution)/shard_map/ppermute | solution.py:61
  56.2 0.7 collective-permute-start.7
  56.9 0.0 collective-permute-done.3.refs_6_
  56.9 0.7 collective-permute-start.9
  57.6 0.0 collective-permute-done.2.refs_5_
  57.6 7.1 %step_top.1 = (f32[5,32,4,8,128]{4,3,2,1,0:T(8,128)S(1)}, f32[2,16,16,128]{3,2,1,0:T(8,128)S(1)}, f32[2,16,8,128]{3,2,1,0:T(8,128)S(1)}, f32[2,16,8,128]{3,2,1,0:T(8,128)S(1)}, f32[64,128]{1,0:T(8,128)S(1)}) custom-call(f32[32,4,128]{2,1,0:T(4,128)S(1)} %all_to_all.10.refs_0_.table_ref.refs_10_, f32[3,32,32,128]{3,2,1,0:T(8,128)S(1)} %sources.1.refs_1_.refs_0_, ...), custom_call_target="tpu_custom_call" | custom-call | flops 7000000000 | bytes 21000000 | tf_op jit(solution)/shard_map/step_top/pallas_call | solution.py:44
  64.8 3.9 %collective-permute-done.6.z_first.refs_3_ = f32[8,16,8,128]{3,2,1,0:T(8,128)S(1)} collective-permute-done((f32[8,16,8,128]{3,2,1,0:T(8,128)S(1)}, f32[8,16,8,128]{3,2,1,0:T(8,128)S(1)}, u32[]{:S(2)}, u32[]{:S(2)}) %collective-permute-start.6) | collective-permute-done | bytes 524320 | tf_op jit(solution)/shard_map/ppermute | solution.py:61
  68.7 0.0 collective-permute-done.7.z_second.refs_4_
  68.7 3.6 %collective-permute-start.12 = (f32[2,16,8,128]{3,2,1,0:T(8,128)S(1)}, f32[2,16,8,128]{3,2,1,0:T(8,128)S(1)}, u32[]{:S(2)}, u32[]{:S(2)}) collective-permute-start(f32[2,16,8,128]{3,2,1,0:T(8,128)S(1)} %get-tuple-element.67), channel_id=1, source_target_pairs={{0,1},{1,0},{2,3},{3,2},{4,5},{5,4},{6,7},{7,6},{8,9},{9,8},{10,11... | collective-permute-start | bytes 393224 | tf_op jit(solution)/shard_map/ppermute | solution.py:61
  72.3 0.7 collective-permute-start.13
  73.0 2.6 %collective-permute-done.12.z_first.refs_5_ = f32[2,16,8,128]{3,2,1,0:T(8,128)S(1)} collective-permute-done((f32[2,16,8,128]{3,2,1,0:T(8,128)S(1)}, f32[2,16,8,128]{3,2,1,0:T(8,128)S(1)}, u32[]{:S(2)}, u32[]{:S(2)}) %collective-permute-start.12) | collective-permute-done | bytes 131104 | tf_op jit(solution)/shard_map/ppermute | solution.py:61
  75.6 0.0 collective-permute-done.13.z_second.refs_6_
  75.7 0.1 collective-permute-start.14
  75.8 0.7 collective-permute-start.15
  76.4 0.0 collective-permute-done.9.refs_6_
  76.5 0.0 collective-permute-done.8.refs_5_
  76.5 1.1 prepare.2
  77.6 0.2 widen.7
  77.7 2.9 %collective-permute-start.10 = (f32[80,16,128]{2,1,0:T(8,128)S(1)}, f32[80,16,128]{2,1,0:T(8,128)S(1)}, u32[]{:S(2)}, u32[]{:S(2)}) collective-permute-start(f32[80,16,128]{2,1,0:T(8,128)S(1)} %get-tuple-element.61), channel_id=1, source_target_pairs={{0,4},{4,0},{8,12},{12,8},{16,20},{20,16},{24,28},{28,24},{1,5},{5... | collective-permute-start | bytes 1966088 | tf_op jit(solution)/shard_map/ppermute | solution.py:61
  80.6 0.7 collective-permute-start.11
  81.3 0.0 collective-permute-done.14.refs_7_
  81.3 0.0 collective-permute-done.15.refs_8_
  81.3 6.0 %step.2 = (f32[2,16,16,128]{3,2,1,0:T(8,128)S(1)}, f32[2,16,8,128]{3,2,1,0:T(8,128)S(1)}, f32[2,16,8,128]{3,2,1,0:T(8,128)S(1)}, f32[64,128]{1,0:T(8,128)S(1)}) custom-call(f32[32,4,128]{2,1,0:T(4,128)S(1)} %all_to_all.10.refs_0_.table_ref.refs_10_, f32[9,32,4,8,128]{4,3,2,1,0:T(8,128)S(1)} %get-tuple-element.60.refs_0_.refs_1_, ...), custom_call_target="tpu_custom_call" | custom-call | flops 6000000000 | bytes 18000000 | tf_op jit(solution)/shard_map/step/pallas_call | solution.py:44
  87.4 3.7 %collective-permute-start.16 = (f32[2,16,8,128]{3,2,1,0:T(8,128)S(1)}, f32[2,16,8,128]{3,2,1,0:T(8,128)S(1)}, u32[]{:S(2)}, u32[]{:S(2)}) collective-permute-start(f32[2,16,8,128]{3,2,1,0:T(8,128)S(1)} %get-tuple-element.73), channel_id=1, source_target_pairs={{0,1},{1,0},{2,3},{3,2},{4,5},{5,4},{6,7},{7,6},{8,9},{9,8},{10,11... | collective-permute-start | bytes 393224 | tf_op jit(solution)/shard_map/ppermute | solution.py:61
  91.1 0.7 collective-permute-start.17
  91.7 2.3 %collective-permute-done.16.z_first.refs_5_ = f32[2,16,8,128]{3,2,1,0:T(8,128)S(1)} collective-permute-done((f32[2,16,8,128]{3,2,1,0:T(8,128)S(1)}, f32[2,16,8,128]{3,2,1,0:T(8,128)S(1)}, u32[]{:S(2)}, u32[]{:S(2)}) %collective-permute-start.16) | collective-permute-done | bytes 131104 | tf_op jit(solution)/shard_map/ppermute | solution.py:61
  94.0 0.0 collective-permute-done.17.z_second.refs_6_
  94.0 3.0 %collective-permute-start.18 = (f32[24,16,128]{2,1,0:T(8,128)S(1)}, f32[24,16,128]{2,1,0:T(8,128)S(1)}, u32[]{:S(2)}, u32[]{:S(2)}) collective-permute-start(f32[24,16,128]{2,1,0:T(8,128)S(1)} %get-tuple-element.75), channel_id=1, source_target_pairs={{0,4},{4,0},{8,12},{12,8},{16,20},{20,16},{24,28},{28,24},{1,5},{5... | collective-permute-start | bytes 589832 | tf_op jit(solution)/shard_map/ppermute | solution.py:61
  97.1 0.7 collective-permute-start.19
  97.7 0.0 collective-permute-done.10.refs_5_
  97.7 0.0 collective-permute-done.11.refs_6_
  97.8 1.0 prepare.3.refs_1_
  98.8 0.0 collective-permute-done.18.refs_7_
  98.8 0.0 collective-permute-done.19.refs_8_
  98.8 6.5 %step.3 = (f32[16,16,128]{2,1,0:T(8,128)}, f32[16,16,128]{2,1,0:T(8,128)}, f32[64,128]{1,0:T(8,128)S(1)}) custom-call(f32[32,4,128]{2,1,0:T(4,128)S(1)} %all_to_all.10.refs_0_.table_ref.refs_10_, f32[9,32,4,8,128]{4,3,2,1,0:T(8,128)S(1)} %prepare.3.refs_1_, f32[5,32,4,8,128]{4,3,2,1,0:T(8,128)S(1)} %get-tuple-element.47.refs_1_.refs_2_, ...), custom_call_target="tpu_custom_call" | custom-call | flops 6000000000 | bytes 18000000 | tf_op jit(solution)/shard_map/step/pallas_call | solution.py:44
  105.3 21.2 %all_to_all.11 = f32[32,2,128]{2,1,0:T(2,128)S(1)} all-to-all(f32[32,2,128]{2,1,0:T(2,128)S(1)} %bitcast.5), channel_id=1, replica_groups=mesh['gx'=8,'gy'=4] {'gx','gy'}, dimensions={0} | all-to-all | bytes 65536 | tf_op jit(solution)/shard_map/all_to_all | solution.py:696
  126.6 0.6 reduce_sum.9
  (27 shorter events, 0.1 us)
Async XLA Ops:
  0.6 30.1 %copy-start.5 = (f32[3,16,16,128]{3,2,1,0:T(8,128)S(1)}, f32[3,16,16,128]{3,2,1,0:T(8,128)}, u32[]{:S(2)}) copy-start(f32[3,16,16,128]{3,2,1,0:T(8,128)} %refs_5_.3) | copy-start | bytes 1179652
  0.6 30.1 %copy-start.4 = (f32[3,16,16,128]{3,2,1,0:T(8,128)S(1)}, f32[3,16,16,128]{3,2,1,0:T(8,128)}, u32[]{:S(2)}) copy-start(f32[3,16,16,128]{3,2,1,0:T(8,128)} %refs_4_.3) | copy-start | bytes 1179652
  0.7 30.1 %copy-start.3 = (f32[3,16,16,128]{3,2,1,0:T(8,128)S(1)}, f32[3,16,16,128]{3,2,1,0:T(8,128)}, u32[]{:S(2)}) copy-start(f32[3,16,16,128]{3,2,1,0:T(8,128)} %refs_3_.3) | copy-start | bytes 1179652
  0.7 30.1 %copy-start.2 = (f32[3,16,16,128]{3,2,1,0:T(8,128)S(1)}, f32[3,16,16,128]{3,2,1,0:T(8,128)}, u32[]{:S(2)}) copy-start(f32[3,16,16,128]{3,2,1,0:T(8,128)} %refs_2_.5) | copy-start | bytes 1179652
  0.7 30.1 %copy-start.1 = (f32[3,16,16,128]{3,2,1,0:T(8,128)S(1)}, f32[3,16,16,128]{3,2,1,0:T(8,128)}, u32[]{:S(2)}) copy-start(f32[3,16,16,128]{3,2,1,0:T(8,128)} %refs_1_.5) | copy-start | bytes 1179652
  0.7 30.1 %copy-start = (f32[3,16,16,128]{3,2,1,0:T(8,128)S(1)}, f32[3,16,16,128]{3,2,1,0:T(8,128)}, u32[]{:S(2)}) copy-start(f32[3,16,16,128]{3,2,1,0:T(8,128)} %refs_0_.5) | copy-start | bytes 1179652
  0.7 30.1 %copy-start.7 = (f32[3,16,16,128]{3,2,1,0:T(8,128)S(1)}, f32[3,16,16,128]{3,2,1,0:T(8,128)}, u32[]{:S(2)}) copy-start(f32[3,16,16,128]{3,2,1,0:T(8,128)} %refs_7_.3) | copy-start | bytes 1179652
  0.7 30.1 %copy-start.6 = (f32[3,16,16,128]{3,2,1,0:T(8,128)S(1)}, f32[3,16,16,128]{3,2,1,0:T(8,128)}, u32[]{:S(2)}) copy-start(f32[3,16,16,128]{3,2,1,0:T(8,128)} %refs_6_.3) | copy-start | bytes 1179652
  0.7 7.2 %copy-start.16 = (f32[128]{0:T(128)S(1)}, f32[128]{0:T(128)}, u32[]{:S(2)}) copy-start(f32[128]{0:T(128)} %param.37) | copy-start | bytes 1540
  0.7 7.2 %copy-start.15 = (s32[128]{0:T(128)S(1)}, s32[128]{0:T(128)}, u32[]{:S(2)}) copy-start(s32[128]{0:T(128)} %param.36) | copy-start | bytes 1540
  0.7 7.2 %copy-start.14 = (s32[128]{0:T(128)S(1)}, s32[128]{0:T(128)}, u32[]{:S(2)}) copy-start(s32[128]{0:T(128)} %param.35) | copy-start | bytes 1540
  0.7 7.2 %copy-start.13 = (s32[2,3]{1,0:T(2,128)S(1)}, s32[2,3]{1,0:T(2,128)}, u32[]{:S(2)}) copy-start(s32[2,3]{1,0:T(2,128)} %refs_2_.3) | copy-start | bytes 76
  0.8 7.2 %copy-start.12 = (f32[2,3]{1,0:T(2,128)S(1)}, f32[2,3]{1,0:T(2,128)}, u32[]{:S(2)}) copy-start(f32[2,3]{1,0:T(2,128)} %refs_1_.3) | copy-start | bytes 76
  0.8 7.2 %copy-start.11 = (f32[2,3]{1,0:T(2,128)S(1)}, f32[2,3]{1,0:T(2,128)}, u32[]{:S(2)}) copy-start(f32[2,3]{1,0:T(2,128)} %refs_0_.3) | copy-start | bytes 76
  0.8 30.0 %copy-start.10 = (f32[16,16,128]{2,1,0:T(8,128)S(1)}, f32[16,16,128]{2,1,0:T(8,128)}, u32[]{:S(2)}) copy-start(f32[16,16,128]{2,1,0:T(8,128)} %refs_9_.3) | copy-start | bytes 393220
  0.8 30.0 %copy-start.9 = (f32[16,16,128]{2,1,0:T(8,128)S(1)}, f32[16,16,128]{2,1,0:T(8,128)}, u32[]{:S(2)}) copy-start(f32[16,16,128]{2,1,0:T(8,128)} %refs_8_.3) | copy-start | bytes 393220
  4.1 27.2 %collective-permute-start = (f32[11,16,8,128]{3,2,1,0:T(8,128)}, f32[11,16,8,128]{3,2,1,0:T(8,128)S(1)}, u32[]{:S(2)}, u32[]{:S(2)}) collective-permute-start(f32[11,16,8,128]{3,2,1,0:T(8,128)} %get-tuple-element.43), channel_id=1, source_target_pairs={{0,1},{1,0},{2,3},{3,2},{4,5},{5,4},{6,7},{7,6},{8,9},{9,8},{10,11... | collective-permute-start | bytes 2162696 | tf_op jit(solution)/shard_map/ppermute | solution.py:61
  7.2 24.1 %collective-permute-start.1 = (f32[11,16,8,128]{3,2,1,0:T(8,128)}, f32[11,16,8,128]{3,2,1,0:T(8,128)S(1)}, u32[]{:S(2)}, u32[]{:S(2)}) collective-permute-start(f32[11,16,8,128]{3,2,1,0:T(8,128)} %get-tuple-element.44), channel_id=1, source_target_pairs={{1,2},{2,1},{5,6},{6,5},{9,10},{10,9},{13,14},{14,13},{17,18},{18,... | collective-permute-start | bytes 2162696 | tf_op jit(solution)/shard_map/ppermute | solution.py:61
  8.0 23.3 %copy-start.8 = (f32[11,16,16,128]{3,2,1,0:T(8,128)S(1)}, f32[11,16,16,128]{3,2,1,0:T(8,128)}, u32[]{:S(2)}) copy-start(f32[11,16,16,128]{3,2,1,0:T(8,128)} %get-tuple-element.42.own.refs_2_) | copy-start | bytes 4325380
  31.5 25.3 %collective-permute-start.3 = (f32[116,16,128]{2,1,0:T(8,128)S(1)}, f32[116,16,128]{2,1,0:T(8,128)S(1)}, u32[]{:S(2)}, u32[]{:S(2)}) collective-permute-start(f32[116,16,128]{2,1,0:T(8,128)S(1)} %get-tuple-element.46), channel_id=1, source_target_pairs={{4,8},{12,16},{20,24},{8,4},{16,12},{24,20},{5,9},{13,17},{21,25},... | collective-permute-start | bytes 2850824 | tf_op jit(solution)/shard_map/ppermute | solution.py:61
  32.3 25.3 %collective-permute-start.2 = (f32[116,16,128]{2,1,0:T(8,128)S(1)}, f32[116,16,128]{2,1,0:T(8,128)S(1)}, u32[]{:S(2)}, u32[]{:S(2)}) collective-permute-start(f32[116,16,128]{2,1,0:T(8,128)S(1)} %get-tuple-element.45._), channel_id=1, source_target_pairs={{0,4},{4,0},{8,12},{12,8},{16,20},{20,16},{24,28},{28,24},{1,5},{5... | collective-permute-start | bytes 2850824 | tf_op jit(solution)/shard_map/ppermute | solution.py:61
  35.3 16.7 %collective-permute-start.4 = (f32[10,16,8,128]{3,2,1,0:T(8,128)S(1)}, f32[10,16,8,128]{3,2,1,0:T(8,128)S(1)}, u32[]{:S(2)}, u32[]{:S(2)}) collective-permute-start(f32[10,16,8,128]{3,2,1,0:T(8,128)S(1)} %get-tuple-element.54), channel_id=1, source_target_pairs={{0,1},{1,0},{2,3},{3,2},{4,5},{5,4},{6,7},{7,6},{8,9},{9,8},{10,11... | collective-permute-start | bytes 1966088 | tf_op jit(solution)/shard_map/ppermute | solution.py:61
  36.1 16.0 %collective-permute-start.5 = (f32[10,16,8,128]{3,2,1,0:T(8,128)S(1)}, f32[10,16,8,128]{3,2,1,0:T(8,128)S(1)}, u32[]{:S(2)}, u32[]{:S(2)}) collective-permute-start(f32[10,16,8,128]{3,2,1,0:T(8,128)S(1)} %get-tuple-element.55), channel_id=1, source_target_pairs={{1,2},{2,1},{5,6},{6,5},{9,10},{10,9},{13,14},{14,13},{17,18},{18,... | collective-permute-start | bytes 1966088 | tf_op jit(solution)/shard_map/ppermute | solution.py:61
  52.2 24.3 %collective-permute-start.8 = (f32[100,16,128]{2,1,0:T(8,128)S(1)}, f32[100,16,128]{2,1,0:T(8,128)S(1)}, u32[]{:S(2)}, u32[]{:S(2)}) collective-permute-start(f32[100,16,128]{2,1,0:T(8,128)S(1)} %get-tuple-element.56), channel_id=1, source_target_pairs={{0,4},{4,0},{8,12},{12,8},{16,20},{20,16},{24,28},{28,24},{1,5},{5... | collective-permute-start | bytes 2457608 | tf_op jit(solution)/shard_map/ppermute | solution.py:61
  52.3 16.4 %collective-permute-start.6 = (f32[8,16,8,128]{3,2,1,0:T(8,128)S(1)}, f32[8,16,8,128]{3,2,1,0:T(8,128)S(1)}, u32[]{:S(2)}, u32[]{:S(2)}) collective-permute-start(f32[8,16,8,128]{3,2,1,0:T(8,128)S(1)} %get-tuple-element.57), channel_id=1, source_target_pairs={{0,1},{1,0},{2,3},{3,2},{4,5},{5,4},{6,7},{7,6},{8,9},{9,8},{10,11... | collective-permute-start | bytes 1572872 | tf_op jit(solution)/shard_map/ppermute | solution.py:61
  56.2 12.5 %collective-permute-start.7 = (f32[8,16,8,128]{3,2,1,0:T(8,128)S(1)}, f32[8,16,8,128]{3,2,1,0:T(8,128)S(1)}, u32[]{:S(2)}, u32[]{:S(2)}) collective-permute-start(f32[8,16,8,128]{3,2,1,0:T(8,128)S(1)} %get-tuple-element.58), channel_id=1, source_target_pairs={{1,2},{2,1},{5,6},{6,5},{9,10},{10,9},{13,14},{14,13},{17,18},{18,... | collective-permute-start | bytes 1572872 | tf_op jit(solution)/shard_map/ppermute | solution.py:61
  56.9 19.6 %collective-permute-start.9 = (f32[100,16,128]{2,1,0:T(8,128)S(1)}, f32[100,16,128]{2,1,0:T(8,128)S(1)}, u32[]{:S(2)}, u32[]{:S(2)}) collective-permute-start(f32[100,16,128]{2,1,0:T(8,128)S(1)} %get-tuple-element.59), channel_id=1, source_target_pairs={{4,8},{12,16},{20,24},{8,4},{16,12},{24,20},{5,9},{13,17},{21,25},... | collective-permute-start | bytes 2457608 | tf_op jit(solution)/shard_map/ppermute | solution.py:61
  68.7 6.9 %collective-permute-start.12 = (f32[2,16,8,128]{3,2,1,0:T(8,128)S(1)}, f32[2,16,8,128]{3,2,1,0:T(8,128)S(1)}, u32[]{:S(2)}, u32[]{:S(2)}) collective-permute-start(f32[2,16,8,128]{3,2,1,0:T(8,128)S(1)} %get-tuple-element.67), channel_id=1, source_target_pairs={{0,1},{1,0},{2,3},{3,2},{4,5},{5,4},{6,7},{7,6},{8,9},{9,8},{10,11... | collective-permute-start | bytes 393224 | tf_op jit(solution)/shard_map/ppermute | solution.py:61
  72.3 3.3 %collective-permute-start.13 = (f32[2,16,8,128]{3,2,1,0:T(8,128)S(1)}, f32[2,16,8,128]{3,2,1,0:T(8,128)S(1)}, u32[]{:S(2)}, u32[]{:S(2)}) collective-permute-start(f32[2,16,8,128]{3,2,1,0:T(8,128)S(1)} %get-tuple-element.68), channel_id=1, source_target_pairs={{1,2},{2,1},{5,6},{6,5},{9,10},{10,9},{13,14},{14,13},{17,18},{18,... | collective-permute-start | bytes 393224 | tf_op jit(solution)/shard_map/ppermute | solution.py:61
  75.7 5.6 %collective-permute-start.14 = (f32[24,16,128]{2,1,0:T(8,128)S(1)}, f32[24,16,128]{2,1,0:T(8,128)S(1)}, u32[]{:S(2)}, u32[]{:S(2)}) collective-permute-start(f32[24,16,128]{2,1,0:T(8,128)S(1)} %get-tuple-element.69), channel_id=1, source_target_pairs={{0,4},{4,0},{8,12},{12,8},{16,20},{20,16},{24,28},{28,24},{1,5},{5... | collective-permute-start | bytes 589832 | tf_op jit(solution)/shard_map/ppermute | solution.py:61
  75.8 5.6 %collective-permute-start.15 = (f32[24,16,128]{2,1,0:T(8,128)S(1)}, f32[24,16,128]{2,1,0:T(8,128)S(1)}, u32[]{:S(2)}, u32[]{:S(2)}) collective-permute-start(f32[24,16,128]{2,1,0:T(8,128)S(1)} %get-tuple-element.70), channel_id=1, source_target_pairs={{4,8},{12,16},{20,24},{8,4},{16,12},{24,20},{5,9},{13,17},{21,25},... | collective-permute-start | bytes 589832 | tf_op jit(solution)/shard_map/ppermute | solution.py:61
  77.7 20.0 %collective-permute-start.10 = (f32[80,16,128]{2,1,0:T(8,128)S(1)}, f32[80,16,128]{2,1,0:T(8,128)S(1)}, u32[]{:S(2)}, u32[]{:S(2)}) collective-permute-start(f32[80,16,128]{2,1,0:T(8,128)S(1)} %get-tuple-element.61), channel_id=1, source_target_pairs={{0,4},{4,0},{8,12},{12,8},{16,20},{20,16},{24,28},{28,24},{1,5},{5... | collective-permute-start | bytes 1966088 | tf_op jit(solution)/shard_map/ppermute | solution.py:61
  80.6 17.1 %collective-permute-start.11 = (f32[80,16,128]{2,1,0:T(8,128)S(1)}, f32[80,16,128]{2,1,0:T(8,128)S(1)}, u32[]{:S(2)}, u32[]{:S(2)}) collective-permute-start(f32[80,16,128]{2,1,0:T(8,128)S(1)} %get-tuple-element.62), channel_id=1, source_target_pairs={{4,8},{12,16},{20,24},{8,4},{16,12},{24,20},{5,9},{13,17},{21,25},... | collective-permute-start | bytes 1966088 | tf_op jit(solution)/shard_map/ppermute | solution.py:61
  87.4 6.6 %collective-permute-start.16 = (f32[2,16,8,128]{3,2,1,0:T(8,128)S(1)}, f32[2,16,8,128]{3,2,1,0:T(8,128)S(1)}, u32[]{:S(2)}, u32[]{:S(2)}) collective-permute-start(f32[2,16,8,128]{3,2,1,0:T(8,128)S(1)} %get-tuple-element.73), channel_id=1, source_target_pairs={{0,1},{1,0},{2,3},{3,2},{4,5},{5,4},{6,7},{7,6},{8,9},{9,8},{10,11... | collective-permute-start | bytes 393224 | tf_op jit(solution)/shard_map/ppermute | solution.py:61
  91.1 3.0 %collective-permute-start.17 = (f32[2,16,8,128]{3,2,1,0:T(8,128)S(1)}, f32[2,16,8,128]{3,2,1,0:T(8,128)S(1)}, u32[]{:S(2)}, u32[]{:S(2)}) collective-permute-start(f32[2,16,8,128]{3,2,1,0:T(8,128)S(1)} %get-tuple-element.74), channel_id=1, source_target_pairs={{1,2},{2,1},{5,6},{6,5},{9,10},{10,9},{13,14},{14,13},{17,18},{18,... | collective-permute-start | bytes 393224 | tf_op jit(solution)/shard_map/ppermute | solution.py:61
  94.0 4.7 %collective-permute-start.18 = (f32[24,16,128]{2,1,0:T(8,128)S(1)}, f32[24,16,128]{2,1,0:T(8,128)S(1)}, u32[]{:S(2)}, u32[]{:S(2)}) collective-permute-start(f32[24,16,128]{2,1,0:T(8,128)S(1)} %get-tuple-element.75), channel_id=1, source_target_pairs={{0,4},{4,0},{8,12},{12,8},{16,20},{20,16},{24,28},{28,24},{1,5},{5... | collective-permute-start | bytes 589832 | tf_op jit(solution)/shard_map/ppermute | solution.py:61
  97.1 1.7 %collective-permute-start.19 = (f32[24,16,128]{2,1,0:T(8,128)S(1)}, f32[24,16,128]{2,1,0:T(8,128)S(1)}, u32[]{:S(2)}, u32[]{:S(2)}) collective-permute-start(f32[24,16,128]{2,1,0:T(8,128)S(1)} %get-tuple-element.76), channel_id=1, source_target_pairs={{4,8},{12,16},{20,24},{8,4},{16,12},{24,20},{5,9},{13,17},{21,25},... | collective-permute-start | bytes 589832 | tf_op jit(solution)/shard_map/ppermute | solution.py:61

commit v12 on v11

--- a/solution.py
+++ b/solution.py
@@ -565,7 +565,7 @@
         coef[AB, x] = s_b * b
         return 0
 
-    lax.fori_loop(0, ex - 1, prepare, 0)
+    lax.fori_loop(0, ex, prepare, 0, unroll=4)
 
 
 def sweep_kernel(last, step, steps, wells, *refs):

time: 128 us -> 128 us (level)
  transfers between devices with their start and end apart: 20 -> 20, of which waited for: 4 -> 4; matrix products, arithmetic and copies ran while one was open for 0% -> 0% of each run, Pallas kernels for 14% -> 13%
where the time goes in v12:
time: 128 us; the launch traced here: 127 us
  blocking collectives  44.1 us (34%)
  starting transfers between devices  30.1 us (24%)
  Pallas kernels  27 us (21%)
  waiting for transfers between devices  24.2 us (19%)
    ppermute x20, starting transfers between devices, swaps(): return (lax.ppermute(first, axis, even), lax.ppermute(second, axis, odd))  30.1 us
    ppermute x20, waiting for transfers between devices, swaps(): return (lax.ppermute(first, axis, even), lax.ppermute(second, axis, odd))  24.2 us
    pallas_call x13, Pallas kernels, call(): pl.pallas_call(kernel, in_specs=specs or [VMEM] * len(ins), out_specs=[VM...  23.7 us
    all_to_all x1, blocking collectives, local(): table = lax.all_to_all(mine, ('gx', 'gy'), 0, 0, tiled=True)  22.7 us
    all_to_all x1, blocking collectives, local(): parts = lax.all_to_all(dense, ('gx', 'gy'), 0, 0, tiled=True)  21.4 us
    pallas_call x1, Pallas kernels, load(): pl.pallas_call(functools.partial(load_kernel, leads), in_specs=[HBM] * n...  3.33 us
  transfers between devices with their start and end apart: 20, of which 4 were waited for; matrix products, arithmetic and copies ran while one was open for 0% of the time, Pallas kernels for 13%

profile of v12, /device:TPU:0, one launch (start us, length us, event | category | flops | bytes accessed | tf_op | source)
XLA Modules:
  0.0 127.2 jit_solution(13270405817747804730)
XLA Ops:
  0.8 3.3 %load.1 = (f32[11,16,16,128]{3,2,1,0:T(8,128)}, f32[11,16,8,128]{3,2,1,0:T(8,128)}, f32[11,16,8,128]{3,2,1,0:T(8,128)}, f32[8,128]{1,0:T(8,128)}) custom-call(f32[16,16,128]{2,1,0:T(8,128)} %refs_0_.4, f32[16,16,128]{2,1,0:T(8,128)} %refs_1_.4, f32[16,16,128]{2,1,0:T(8,128)} %refs_2_.4, f32[3,16,16,128]{3,2,1,0:T(8,128)} %refs_0_.5, ...), custom_call_target="tpu_custom_call" | custom-call | tf_op jit(solution)/shard_map/load/pallas_call | solution.py:107
  4.1 3.1 %collective-permute-start = (f32[11,16,8,128]{3,2,1,0:T(8,128)}, f32[11,16,8,128]{3,2,1,0:T(8,128)S(1)}, u32[]{:S(2)}, u32[]{:S(2)}) collective-permute-start(f32[11,16,8,128]{3,2,1,0:T(8,128)} %get-tuple-element.43), channel_id=1, source_target_pairs={{0,1},{1,0},{2,3},{3,2},{4,5},{5,4},{6,7},{7,6},{8,9},{9,8},{10,11... | collective-permute-start | bytes 2162696 | tf_op jit(solution)/shard_map/ppermute | solution.py:61
  7.2 0.7 collective-permute-start.1
  7.9 0.0 copy-done.16
  7.9 0.0 copy-done.15
  7.9 0.0 copy-done.14
  8.0 0.0 copy-done.13
  8.0 0.0 copy-done.12
  8.0 0.0 copy-done.11
  8.0 0.0 copy-start.8
  8.0 0.1 table.1
  8.1 22.7 %all_to_all.10.refs_0_.table_ref.refs_10_ = f32[32,4,128]{2,1,0:T(4,128)S(1)} all-to-all(f32[32,4,128]{2,1,0:T(4,128)S(1)} %table.1), channel_id=1, replica_groups=mesh['gx'=8,'gy'=4] {'gx','gy'}, dimensions={0} | all-to-all | bytes 131072 | tf_op jit(solution)/shard_map/all_to_all | solution.py:620
  30.8 0.0 copy-done.4
  30.8 0.4 more.1
  31.3 0.0 collective-permute-done.z_first.refs_3_
  31.3 0.0 collective-permute-done.1.z_second.refs_4_
  31.3 0.0 copy-done.8
  31.3 0.2 widen.5
  31.5 0.7 collective-permute-start.3
  32.3 2.0 %collective-permute-start.2 = (f32[116,16,128]{2,1,0:T(8,128)S(1)}, f32[116,16,128]{2,1,0:T(8,128)S(1)}, u32[]{:S(2)}, u32[]{:S(2)}) collective-permute-start(f32[116,16,128]{2,1,0:T(8,128)S(1)} %get-tuple-element.45._), channel_id=1, source_target_pairs={{0,4},{4,0},{8,12},{12,8},{16,20},{20,16},{24,28},{28,24},{1,5},{5... | collective-permute-start | bytes 2850824 | tf_op jit(solution)/shard_map/ppermute | solution.py:61
  34.3 1.1 sources.1.refs_1_.refs_0_
  35.3 0.8 collective-permute-start.4
  36.1 0.7 collective-permute-start.5
  36.8 15.3 %collective-permute-done.4.z_first.refs_3_ = f32[10,16,8,128]{3,2,1,0:T(8,128)S(1)} collective-permute-done((f32[10,16,8,128]{3,2,1,0:T(8,128)S(1)}, f32[10,16,8,128]{3,2,1,0:T(8,128)S(1)}, u32[]{:S(2)}, u32[]{:S(2)}) %collective-permute-start.4) | collective-permute-done | bytes 655392 | tf_op jit(solution)/shard_map/ppermute | solution.py:61
  52.0 0.0 collective-permute-done.5.z_second.refs_4_
  52.0 0.2 widen.6
  52.2 0.1 collective-permute-start.8
  52.3 3.9 %collective-permute-start.6 = (f32[8,16,8,128]{3,2,1,0:T(8,128)S(1)}, f32[8,16,8,128]{3,2,1,0:T(8,128)S(1)}, u32[]{:S(2)}, u32[]{:S(2)}) collective-permute-start(f32[8,16,8,128]{3,2,1,0:T(8,128)S(1)} %get-tuple-element.57), channel_id=1, source_target_pairs={{0,1},{1,0},{2,3},{3,2},{4,5},{5,4},{6,7},{7,6},{8,9},{9,8},{10,11... | collective-permute-start | bytes 1572872 | tf_op jit(solution)/shard_map/ppermute | solution.py:61
  56.2 0.7 collective-permute-start.7
  56.9 0.0 collective-permute-done.3.refs_6_
  56.9 0.7 collective-permute-start.9
  57.6 0.0 collective-permute-done.2.refs_5_
  57.6 7.1 %step_top.1 = (f32[5,32,4,8,128]{4,3,2,1,0:T(8,128)S(1)}, f32[2,16,16,128]{3,2,1,0:T(8,128)S(1)}, f32[2,16,8,128]{3,2,1,0:T(8,128)S(1)}, f32[2,16,8,128]{3,2,1,0:T(8,128)S(1)}, f32[64,128]{1,0:T(8,128)S(1)}) custom-call(f32[32,4,128]{2,1,0:T(4,128)S(1)} %all_to_all.10.refs_0_.table_ref.refs_10_, f32[3,32,32,128]{3,2,1,0:T(8,128)S(1)} %sources.1.refs_1_.refs_0_, ...), custom_call_target="tpu_custom_call" | custom-call | flops 7000000000 | bytes 21000000 | tf_op jit(solution)/shard_map/step_top/pallas_call | solution.py:44
  64.8 3.9 %collective-permute-done.6.z_first.refs_3_ = f32[8,16,8,128]{3,2,1,0:T(8,128)S(1)} collective-permute-done((f32[8,16,8,128]{3,2,1,0:T(8,128)S(1)}, f32[8,16,8,128]{3,2,1,0:T(8,128)S(1)}, u32[]{:S(2)}, u32[]{:S(2)}) %collective-permute-start.6) | collective-permute-done | bytes 524320 | tf_op jit(solution)/shard_map/ppermute | solution.py:61
  68.7 0.0 collective-permute-done.7.z_second.refs_4_
  68.7 3.6 %collective-permute-start.12 = (f32[2,16,8,128]{3,2,1,0:T(8,128)S(1)}, f32[2,16,8,128]{3,2,1,0:T(8,128)S(1)}, u32[]{:S(2)}, u32[]{:S(2)}) collective-permute-start(f32[2,16,8,128]{3,2,1,0:T(8,128)S(1)} %get-tuple-element.67), channel_id=1, source_target_pairs={{0,1},{1,0},{2,3},{3,2},{4,5},{5,4},{6,7},{7,6},{8,9},{9,8},{10,11... | collective-permute-start | bytes 393224 | tf_op jit(solution)/shard_map/ppermute | solution.py:61
  72.3 0.7 collective-permute-start.13
  73.0 2.6 %collective-permute-done.12.z_first.refs_5_ = f32[2,16,8,128]{3,2,1,0:T(8,128)S(1)} collective-permute-done((f32[2,16,8,128]{3,2,1,0:T(8,128)S(1)}, f32[2,16,8,128]{3,2,1,0:T(8,128)S(1)}, u32[]{:S(2)}, u32[]{:S(2)}) %collective-permute-start.12) | collective-permute-done | bytes 131104 | tf_op jit(solution)/shard_map/ppermute | solution.py:61
  75.6 0.0 collective-permute-done.13.z_second.refs_6_
  75.7 0.1 collective-permute-start.14
  75.8 0.7 collective-permute-start.15
  76.4 0.0 collective-permute-done.9.refs_6_
  76.5 0.0 collective-permute-done.8.refs_5_
  76.5 1.0 prepare.2
  77.4 0.2 widen.7
  77.6 2.9 %collective-permute-start.10 = (f32[80,16,128]{2,1,0:T(8,128)S(1)}, f32[80,16,128]{2,1,0:T(8,128)S(1)}, u32[]{:S(2)}, u32[]{:S(2)}) collective-permute-start(f32[80,16,128]{2,1,0:T(8,128)S(1)} %get-tuple-element.61), channel_id=1, source_target_pairs={{0,4},{4,0},{8,12},{12,8},{16,20},{20,16},{24,28},{28,24},{1,5},{5... | collective-permute-start | bytes 1966088 | tf_op jit(solution)/shard_map/ppermute | solution.py:61
  80.5 0.7 collective-permute-start.11
  81.2 0.0 collective-permute-done.14.refs_7_
  81.2 0.0 collective-permute-done.15.refs_8_
  81.2 6.0 %step.2 = (f32[2,16,16,128]{3,2,1,0:T(8,128)S(1)}, f32[2,16,8,128]{3,2,1,0:T(8,128)S(1)}, f32[2,16,8,128]{3,2,1,0:T(8,128)S(1)}, f32[64,128]{1,0:T(8,128)S(1)}) custom-call(f32[32,4,128]{2,1,0:T(4,128)S(1)} %all_to_all.10.refs_0_.table_ref.refs_10_, f32[9,32,4,8,128]{4,3,2,1,0:T(8,128)S(1)} %get-tuple-element.60.refs_0_.refs_1_, ...), custom_call_target="tpu_custom_call" | custom-call | flops 6000000000 | bytes 18000000 | tf_op jit(solution)/shard_map/step/pallas_call | solution.py:44
  87.3 3.7 %collective-permute-start.16 = (f32[2,16,8,128]{3,2,1,0:T(8,128)S(1)}, f32[2,16,8,128]{3,2,1,0:T(8,128)S(1)}, u32[]{:S(2)}, u32[]{:S(2)}) collective-permute-start(f32[2,16,8,128]{3,2,1,0:T(8,128)S(1)} %get-tuple-element.73), channel_id=1, source_target_pairs={{0,1},{1,0},{2,3},{3,2},{4,5},{5,4},{6,7},{7,6},{8,9},{9,8},{10,11... | collective-permute-start | bytes 393224 | tf_op jit(solution)/shard_map/ppermute | solution.py:61
  90.9 0.7 collective-permute-start.17
  91.6 2.3 %collective-permute-done.16.z_first.refs_5_ = f32[2,16,8,128]{3,2,1,0:T(8,128)S(1)} collective-permute-done((f32[2,16,8,128]{3,2,1,0:T(8,128)S(1)}, f32[2,16,8,128]{3,2,1,0:T(8,128)S(1)}, u32[]{:S(2)}, u32[]{:S(2)}) %collective-permute-start.16) | collective-permute-done | bytes 131104 | tf_op jit(solution)/shard_map/ppermute | solution.py:61
  93.9 0.0 collective-permute-done.17.z_second.refs_6_
  93.9 3.1 %collective-permute-start.18 = (f32[24,16,128]{2,1,0:T(8,128)S(1)}, f32[24,16,128]{2,1,0:T(8,128)S(1)}, u32[]{:S(2)}, u32[]{:S(2)}) collective-permute-start(f32[24,16,128]{2,1,0:T(8,128)S(1)} %get-tuple-element.75), channel_id=1, source_target_pairs={{0,4},{4,0},{8,12},{12,8},{16,20},{20,16},{24,28},{28,24},{1,5},{5... | collective-permute-start | bytes 589832 | tf_op jit(solution)/shard_map/ppermute | solution.py:61
  97.1 0.7 collective-permute-start.19
  97.7 0.0 collective-permute-done.10.refs_5_
  97.7 0.0 collective-permute-done.11.refs_6_
  97.8 0.8 prepare.3.refs_1_
  98.6 0.0 collective-permute-done.18.refs_7_
  98.6 0.0 collective-permute-done.19.refs_8_
  98.6 6.5 %step.3 = (f32[16,16,128]{2,1,0:T(8,128)}, f32[16,16,128]{2,1,0:T(8,128)}, f32[64,128]{1,0:T(8,128)S(1)}) custom-call(f32[32,4,128]{2,1,0:T(4,128)S(1)} %all_to_all.10.refs_0_.table_ref.refs_10_, f32[9,32,4,8,128]{4,3,2,1,0:T(8,128)S(1)} %prepare.3.refs_1_, f32[5,32,4,8,128]{4,3,2,1,0:T(8,128)S(1)} %get-tuple-element.47.refs_1_.refs_2_, ...), custom_call_target="tpu_custom_call" | custom-call | flops 6000000000 | bytes 18000000 | tf_op jit(solution)/shard_map/step/pallas_call | solution.py:44
  105.2 21.4 %all_to_all.11 = f32[32,2,128]{2,1,0:T(2,128)S(1)} all-to-all(f32[32,2,128]{2,1,0:T(2,128)S(1)} %bitcast.5), channel_id=1, replica_groups=mesh['gx'=8,'gy'=4] {'gx','gy'}, dimensions={0} | all-to-all | bytes 65536 | tf_op jit(solution)/shard_map/all_to_all | solution.py:696
  126.6 0.6 reduce_sum.9
  (27 shorter events, 0.1 us)
Async XLA Ops:
  0.6 30.1 %copy-start.5 = (f32[3,16,16,128]{3,2,1,0:T(8,128)S(1)}, f32[3,16,16,128]{3,2,1,0:T(8,128)}, u32[]{:S(2)}) copy-start(f32[3,16,16,128]{3,2,1,0:T(8,128)} %refs_5_.3) | copy-start | bytes 1179652
  0.6 30.1 %copy-start.4 = (f32[3,16,16,128]{3,2,1,0:T(8,128)S(1)}, f32[3,16,16,128]{3,2,1,0:T(8,128)}, u32[]{:S(2)}) copy-start(f32[3,16,16,128]{3,2,1,0:T(8,128)} %refs_4_.3) | copy-start | bytes 1179652
  0.7 30.1 %copy-start.3 = (f32[3,16,16,128]{3,2,1,0:T(8,128)S(1)}, f32[3,16,16,128]{3,2,1,0:T(8,128)}, u32[]{:S(2)}) copy-start(f32[3,16,16,128]{3,2,1,0:T(8,128)} %refs_3_.3) | copy-start | bytes 1179652
  0.7 30.1 %copy-start.2 = (f32[3,16,16,128]{3,2,1,0:T(8,128)S(1)}, f32[3,16,16,128]{3,2,1,0:T(8,128)}, u32[]{:S(2)}) copy-start(f32[3,16,16,128]{3,2,1,0:T(8,128)} %refs_2_.5) | copy-start | bytes 1179652
  0.7 30.1 %copy-start.1 = (f32[3,16,16,128]{3,2,1,0:T(8,128)S(1)}, f32[3,16,16,128]{3,2,1,0:T(8,128)}, u32[]{:S(2)}) copy-start(f32[3,16,16,128]{3,2,1,0:T(8,128)} %refs_1_.5) | copy-start | bytes 1179652
  0.7 30.1 %copy-start = (f32[3,16,16,128]{3,2,1,0:T(8,128)S(1)}, f32[3,16,16,128]{3,2,1,0:T(8,128)}, u32[]{:S(2)}) copy-start(f32[3,16,16,128]{3,2,1,0:T(8,128)} %refs_0_.5) | copy-start | bytes 1179652
  0.7 30.1 %copy-start.7 = (f32[3,16,16,128]{3,2,1,0:T(8,128)S(1)}, f32[3,16,16,128]{3,2,1,0:T(8,128)}, u32[]{:S(2)}) copy-start(f32[3,16,16,128]{3,2,1,0:T(8,128)} %refs_7_.3) | copy-start | bytes 1179652
  0.7 30.1 %copy-start.6 = (f32[3,16,16,128]{3,2,1,0:T(8,128)S(1)}, f32[3,16,16,128]{3,2,1,0:T(8,128)}, u32[]{:S(2)}) copy-start(f32[3,16,16,128]{3,2,1,0:T(8,128)} %refs_6_.3) | copy-start | bytes 1179652
  0.7 7.2 %copy-start.16 = (f32[128]{0:T(128)S(1)}, f32[128]{0:T(128)}, u32[]{:S(2)}) copy-start(f32[128]{0:T(128)} %param.37) | copy-start | bytes 1540
  0.7 7.2 %copy-start.15 = (s32[128]{0:T(128)S(1)}, s32[128]{0:T(128)}, u32[]{:S(2)}) copy-start(s32[128]{0:T(128)} %param.36) | copy-start | bytes 1540
  0.7 7.2 %copy-start.14 = (s32[128]{0:T(128)S(1)}, s32[128]{0:T(128)}, u32[]{:S(2)}) copy-start(s32[128]{0:T(128)} %param.35) | copy-start | bytes 1540
  0.7 7.2 %copy-start.13 = (s32[2,3]{1,0:T(2,128)S(1)}, s32[2,3]{1,0:T(2,128)}, u32[]{:S(2)}) copy-start(s32[2,3]{1,0:T(2,128)} %refs_2_.3) | copy-start | bytes 76
  0.8 7.2 %copy-start.12 = (f32[2,3]{1,0:T(2,128)S(1)}, f32[2,3]{1,0:T(2,128)}, u32[]{:S(2)}) copy-start(f32[2,3]{1,0:T(2,128)} %refs_1_.3) | copy-start | bytes 76
  0.8 7.2 %copy-start.11 = (f32[2,3]{1,0:T(2,128)S(1)}, f32[2,3]{1,0:T(2,128)}, u32[]{:S(2)}) copy-start(f32[2,3]{1,0:T(2,128)} %refs_0_.3) | copy-start | bytes 76
  0.8 30.0 %copy-start.10 = (f32[16,16,128]{2,1,0:T(8,128)S(1)}, f32[16,16,128]{2,1,0:T(8,128)}, u32[]{:S(2)}) copy-start(f32[16,16,128]{2,1,0:T(8,128)} %refs_9_.3) | copy-start | bytes 393220
  0.8 30.0 %copy-start.9 = (f32[16,16,128]{2,1,0:T(8,128)S(1)}, f32[16,16,128]{2,1,0:T(8,128)}, u32[]{:S(2)}) copy-start(f32[16,16,128]{2,1,0:T(8,128)} %refs_8_.3) | copy-start | bytes 393220
  4.1 27.2 %collective-permute-start = (f32[11,16,8,128]{3,2,1,0:T(8,128)}, f32[11,16,8,128]{3,2,1,0:T(8,128)S(1)}, u32[]{:S(2)}, u32[]{:S(2)}) collective-permute-start(f32[11,16,8,128]{3,2,1,0:T(8,128)} %get-tuple-element.43), channel_id=1, source_target_pairs={{0,1},{1,0},{2,3},{3,2},{4,5},{5,4},{6,7},{7,6},{8,9},{9,8},{10,11... | collective-permute-start | bytes 2162696 | tf_op jit(solution)/shard_map/ppermute | solution.py:61
  7.2 24.1 %collective-permute-start.1 = (f32[11,16,8,128]{3,2,1,0:T(8,128)}, f32[11,16,8,128]{3,2,1,0:T(8,128)S(1)}, u32[]{:S(2)}, u32[]{:S(2)}) collective-permute-start(f32[11,16,8,128]{3,2,1,0:T(8,128)} %get-tuple-element.44), channel_id=1, source_target_pairs={{1,2},{2,1},{5,6},{6,5},{9,10},{10,9},{13,14},{14,13},{17,18},{18,... | collective-permute-start | bytes 2162696 | tf_op jit(solution)/shard_map/ppermute | solution.py:61
  8.0 23.3 %copy-start.8 = (f32[11,16,16,128]{3,2,1,0:T(8,128)S(1)}, f32[11,16,16,128]{3,2,1,0:T(8,128)}, u32[]{:S(2)}) copy-start(f32[11,16,16,128]{3,2,1,0:T(8,128)} %get-tuple-element.42.own.refs_2_) | copy-start | bytes 4325380
  31.5 25.3 %collective-permute-start.3 = (f32[116,16,128]{2,1,0:T(8,128)S(1)}, f32[116,16,128]{2,1,0:T(8,128)S(1)}, u32[]{:S(2)}, u32[]{:S(2)}) collective-permute-start(f32[116,16,128]{2,1,0:T(8,128)S(1)} %get-tuple-element.46), channel_id=1, source_target_pairs={{4,8},{12,16},{20,24},{8,4},{16,12},{24,20},{5,9},{13,17},{21,25},... | collective-permute-start | bytes 2850824 | tf_op jit(solution)/shard_map/ppermute | solution.py:61
  32.3 25.3 %collective-permute-start.2 = (f32[116,16,128]{2,1,0:T(8,128)S(1)}, f32[116,16,128]{2,1,0:T(8,128)S(1)}, u32[]{:S(2)}, u32[]{:S(2)}) collective-permute-start(f32[116,16,128]{2,1,0:T(8,128)S(1)} %get-tuple-element.45._), channel_id=1, source_target_pairs={{0,4},{4,0},{8,12},{12,8},{16,20},{20,16},{24,28},{28,24},{1,5},{5... | collective-permute-start | bytes 2850824 | tf_op jit(solution)/shard_map/ppermute | solution.py:61
  35.3 16.7 %collective-permute-start.4 = (f32[10,16,8,128]{3,2,1,0:T(8,128)S(1)}, f32[10,16,8,128]{3,2,1,0:T(8,128)S(1)}, u32[]{:S(2)}, u32[]{:S(2)}) collective-permute-start(f32[10,16,8,128]{3,2,1,0:T(8,128)S(1)} %get-tuple-element.54), channel_id=1, source_target_pairs={{0,1},{1,0},{2,3},{3,2},{4,5},{5,4},{6,7},{7,6},{8,9},{9,8},{10,11... | collective-permute-start | bytes 1966088 | tf_op jit(solution)/shard_map/ppermute | solution.py:61
  36.1 16.0 %collective-permute-start.5 = (f32[10,16,8,128]{3,2,1,0:T(8,128)S(1)}, f32[10,16,8,128]{3,2,1,0:T(8,128)S(1)}, u32[]{:S(2)}, u32[]{:S(2)}) collective-permute-start(f32[10,16,8,128]{3,2,1,0:T(8,128)S(1)} %get-tuple-element.55), channel_id=1, source_target_pairs={{1,2},{2,1},{5,6},{6,5},{9,10},{10,9},{13,14},{14,13},{17,18},{18,... | collective-permute-start | bytes 1966088 | tf_op jit(solution)/shard_map/ppermute | solution.py:61
  52.2 24.3 %collective-permute-start.8 = (f32[100,16,128]{2,1,0:T(8,128)S(1)}, f32[100,16,128]{2,1,0:T(8,128)S(1)}, u32[]{:S(2)}, u32[]{:S(2)}) collective-permute-start(f32[100,16,128]{2,1,0:T(8,128)S(1)} %get-tuple-element.56), channel_id=1, source_target_pairs={{0,4},{4,0},{8,12},{12,8},{16,20},{20,16},{24,28},{28,24},{1,5},{5... | collective-permute-start | bytes 2457608 | tf_op jit(solution)/shard_map/ppermute | solution.py:61
  52.3 16.4 %collective-permute-start.6 = (f32[8,16,8,128]{3,2,1,0:T(8,128)S(1)}, f32[8,16,8,128]{3,2,1,0:T(8,128)S(1)}, u32[]{:S(2)}, u32[]{:S(2)}) collective-permute-start(f32[8,16,8,128]{3,2,1,0:T(8,128)S(1)} %get-tuple-element.57), channel_id=1, source_target_pairs={{0,1},{1,0},{2,3},{3,2},{4,5},{5,4},{6,7},{7,6},{8,9},{9,8},{10,11... | collective-permute-start | bytes 1572872 | tf_op jit(solution)/shard_map/ppermute | solution.py:61
  56.2 12.5 %collective-permute-start.7 = (f32[8,16,8,128]{3,2,1,0:T(8,128)S(1)}, f32[8,16,8,128]{3,2,1,0:T(8,128)S(1)}, u32[]{:S(2)}, u32[]{:S(2)}) collective-permute-start(f32[8,16,8,128]{3,2,1,0:T(8,128)S(1)} %get-tuple-element.58), channel_id=1, source_target_pairs={{1,2},{2,1},{5,6},{6,5},{9,10},{10,9},{13,14},{14,13},{17,18},{18,... | collective-permute-start | bytes 1572872 | tf_op jit(solution)/shard_map/ppermute | solution.py:61
  56.9 19.6 %collective-permute-start.9 = (f32[100,16,128]{2,1,0:T(8,128)S(1)}, f32[100,16,128]{2,1,0:T(8,128)S(1)}, u32[]{:S(2)}, u32[]{:S(2)}) collective-permute-start(f32[100,16,128]{2,1,0:T(8,128)S(1)} %get-tuple-element.59), channel_id=1, source_target_pairs={{4,8},{12,16},{20,24},{8,4},{16,12},{24,20},{5,9},{13,17},{21,25},... | collective-permute-start | bytes 2457608 | tf_op jit(solution)/shard_map/ppermute | solution.py:61
  68.7 6.9 %collective-permute-start.12 = (f32[2,16,8,128]{3,2,1,0:T(8,128)S(1)}, f32[2,16,8,128]{3,2,1,0:T(8,128)S(1)}, u32[]{:S(2)}, u32[]{:S(2)}) collective-permute-start(f32[2,16,8,128]{3,2,1,0:T(8,128)S(1)} %get-tuple-element.67), channel_id=1, source_target_pairs={{0,1},{1,0},{2,3},{3,2},{4,5},{5,4},{6,7},{7,6},{8,9},{9,8},{10,11... | collective-permute-start | bytes 393224 | tf_op jit(solution)/shard_map/ppermute | solution.py:61
  72.3 3.3 %collective-permute-start.13 = (f32[2,16,8,128]{3,2,1,0:T(8,128)S(1)}, f32[2,16,8,128]{3,2,1,0:T(8,128)S(1)}, u32[]{:S(2)}, u32[]{:S(2)}) collective-permute-start(f32[2,16,8,128]{3,2,1,0:T(8,128)S(1)} %get-tuple-element.68), channel_id=1, source_target_pairs={{1,2},{2,1},{5,6},{6,5},{9,10},{10,9},{13,14},{14,13},{17,18},{18,... | collective-permute-start | bytes 393224 | tf_op jit(solution)/shard_map/ppermute | solution.py:61
  75.7 5.5 %collective-permute-start.14 = (f32[24,16,128]{2,1,0:T(8,128)S(1)}, f32[24,16,128]{2,1,0:T(8,128)S(1)}, u32[]{:S(2)}, u32[]{:S(2)}) collective-permute-start(f32[24,16,128]{2,1,0:T(8,128)S(1)} %get-tuple-element.69), channel_id=1, source_target_pairs={{0,4},{4,0},{8,12},{12,8},{16,20},{20,16},{24,28},{28,24},{1,5},{5... | collective-permute-start | bytes 589832 | tf_op jit(solution)/shard_map/ppermute | solution.py:61
  75.8 5.5 %collective-permute-start.15 = (f32[24,16,128]{2,1,0:T(8,128)S(1)}, f32[24,16,128]{2,1,0:T(8,128)S(1)}, u32[]{:S(2)}, u32[]{:S(2)}) collective-permute-start(f32[24,16,128]{2,1,0:T(8,128)S(1)} %get-tuple-element.70), channel_id=1, source_target_pairs={{4,8},{12,16},{20,24},{8,4},{16,12},{24,20},{5,9},{13,17},{21,25},... | collective-permute-start | bytes 589832 | tf_op jit(solution)/shard_map/ppermute | solution.py:61
  77.6 20.1 %collective-permute-start.10 = (f32[80,16,128]{2,1,0:T(8,128)S(1)}, f32[80,16,128]{2,1,0:T(8,128)S(1)}, u32[]{:S(2)}, u32[]{:S(2)}) collective-permute-start(f32[80,16,128]{2,1,0:T(8,128)S(1)} %get-tuple-element.61), channel_id=1, source_target_pairs={{0,4},{4,0},{8,12},{12,8},{16,20},{20,16},{24,28},{28,24},{1,5},{5... | collective-permute-start | bytes 1966088 | tf_op jit(solution)/shard_map/ppermute | solution.py:61
  80.5 17.2 %collective-permute-start.11 = (f32[80,16,128]{2,1,0:T(8,128)S(1)}, f32[80,16,128]{2,1,0:T(8,128)S(1)}, u32[]{:S(2)}, u32[]{:S(2)}) collective-permute-start(f32[80,16,128]{2,1,0:T(8,128)S(1)} %get-tuple-element.62), channel_id=1, source_target_pairs={{4,8},{12,16},{20,24},{8,4},{16,12},{24,20},{5,9},{13,17},{21,25},... | collective-permute-start | bytes 1966088 | tf_op jit(solution)/shard_map/ppermute | solution.py:61
  87.3 6.6 %collective-permute-start.16 = (f32[2,16,8,128]{3,2,1,0:T(8,128)S(1)}, f32[2,16,8,128]{3,2,1,0:T(8,128)S(1)}, u32[]{:S(2)}, u32[]{:S(2)}) collective-permute-start(f32[2,16,8,128]{3,2,1,0:T(8,128)S(1)} %get-tuple-element.73), channel_id=1, source_target_pairs={{0,1},{1,0},{2,3},{3,2},{4,5},{5,4},{6,7},{7,6},{8,9},{9,8},{10,11... | collective-permute-start | bytes 393224 | tf_op jit(solution)/shard_map/ppermute | solution.py:61
  90.9 3.0 %collective-permute-start.17 = (f32[2,16,8,128]{3,2,1,0:T(8,128)S(1)}, f32[2,16,8,128]{3,2,1,0:T(8,128)S(1)}, u32[]{:S(2)}, u32[]{:S(2)}) collective-permute-start(f32[2,16,8,128]{3,2,1,0:T(8,128)S(1)} %get-tuple-element.74), channel_id=1, source_target_pairs={{1,2},{2,1},{5,6},{6,5},{9,10},{10,9},{13,14},{14,13},{17,18},{18,... | collective-permute-start | bytes 393224 | tf_op jit(solution)/shard_map/ppermute | solution.py:61
  93.9 4.7 %collective-permute-start.18 = (f32[24,16,128]{2,1,0:T(8,128)S(1)}, f32[24,16,128]{2,1,0:T(8,128)S(1)}, u32[]{:S(2)}, u32[]{:S(2)}) collective-permute-start(f32[24,16,128]{2,1,0:T(8,128)S(1)} %get-tuple-element.75), channel_id=1, source_target_pairs={{0,4},{4,0},{8,12},{12,8},{16,20},{20,16},{24,28},{28,24},{1,5},{5... | collective-permute-start | bytes 589832 | tf_op jit(solution)/shard_map/ppermute | solution.py:61
  97.1 1.6 %collective-permute-start.19 = (f32[24,16,128]{2,1,0:T(8,128)S(1)}, f32[24,16,128]{2,1,0:T(8,128)S(1)}, u32[]{:S(2)}, u32[]{:S(2)}) collective-permute-start(f32[24,16,128]{2,1,0:T(8,128)S(1)} %get-tuple-element.76), channel_id=1, source_target_pairs={{4,8},{12,16},{20,24},{8,4},{16,12},{24,20},{5,9},{13,17},{21,25},... | collective-permute-start | bytes 589832 | tf_op jit(solution)/shard_map/ppermute | solution.py:61
